TPU v7x, 128 devices: a whole 4x4x4 slice. The times are simulated.
128 devices in a mesh: dp: 2 (over core), pipe: 2 (over x_hi), expert: 32 (over z, y, x_lo).
Axes of the slice: x: 4 (x_hi: 2, x_lo: 2; x = x_hi * 2 + x_lo), y: 4, z: 4, core: 2. Of those that a mesh axis runs over, the one named last changes fastest.
Arguments:
- saved_inputs: bfloat16 [2, 4, 128, 3072], P('pipe', None, 'dp'), may hold values from -6 to 6
- top_grad: bfloat16 [4, 128, 3072], P(None, 'dp'), may hold values from -6 to 6
- routes: int32 [2, 4, 128, 2], P('pipe', None, 'dp'), may hold values from 0 to 3, all different within a row; in each aligned block of 64 rows (0 to 63, 64 to 127, ..., all dimensions but the last counted through in order) at most 48 rows name the same one
- mix_weights: float32 [2, 4, 128, 2], P('pipe', None, 'dp'), may hold values from 0.2 to 0.8
- w_gate: bfloat16 [2, 32, 1, 3072, 1024], P('pipe', 'expert', None, None, 'dp'), may hold values from -0.109375 to 0.109375
- w_up: bfloat16 [2, 32, 1, 3072, 1024], P('pipe', 'expert', None, None, 'dp'), may hold values from -0.109375 to 0.109375
- w_down: bfloat16 [2, 32, 1, 1024, 3072], P('pipe', 'expert', None, 'dp'), may hold values from -0.0625 to 0.0625
- q_prev: float32 [2, 32, 1, 3, 1024, 64], P('pipe', 'expert', None, None, 'dp'), may hold values from -6 to 6
Outputs:
- input_grads: bfloat16 [2, 4, 128, 3072], P('pipe', None, 'dp')
- basis: float32 [2, 32, 1, 3072, 64], P('pipe', 'expert', None, 'dp')
- q_next: float32 [2, 32, 1, 3, 1024, 64], P('pipe', 'expert', None, None, 'dp')
Inputs may be any that keep to these rules, and one draw needn't show every extreme that they name: For every section, microbatch and aligned block of 64 tokens (the tokens of one index of dp), each expert is named by at most 48 routes, a bound that some block reaches; a token's 2 routes name different experts.
All inputs are finite; a program needn't handle non-finite values.
Results may differ from a plain program's by a relative error of at most 0.015.
Values may be sent and summed in bfloat16 or wider, within the bound.
No kernel may reach another device: no remote copies, remote signals or barrier semaphores. Data moves between devices by JAX's collectives and lax.ppermute only.
A program may use at most 128 MiB of HBM per device.

v0:
```python
import math

import jax
import jax.numpy as jnp
from jax import lax
from jax.sharding import PartitionSpec as P

D = 3072
EXPERTS = 4
R = 64
MICRO = 4

BF = jnp.bfloat16
F32 = jnp.float32


def swap_cores(value):
    return lax.ppermute(value, "dp", [(0, 1), (1, 0)])


def exchange(pieces, groups=None):
    return lax.all_to_all(pieces, "expert", 0, 0, tiled=True, axis_index_groups=groups)


def times(a, b, ca=1, cb=0, precision=None):
    return lax.dot_general(
        a, b, (((ca,), (cb,)), ((), ())), preferred_element_type=F32, precision=precision
    )


def shards(saved_inputs, top_grad, routes, mix_weights, w_gate, w_up, w_down, q_prev):
    sections = lax.axis_size("pipe")
    section_index = lax.axis_index("pipe")
    peers = lax.axis_size("expert")
    expert_index = lax.axis_index("expert")
    replicas = lax.axis_size("dp")
    dp_index = lax.axis_index("dp")
    gate, up, down = (w_gate[0, 0, 0], w_up[0, 0, 0], w_down[0, 0, 0])
    right = q_prev[0, 0, 0]
    copies = peers // EXPERTS
    token_count = saved_inputs.shape[2]
    rows = MICRO * token_count
    rows_each = rows // peers
    plane = [[c * copies + i for i in range(copies)] for c in range(EXPERTS)]
    own_expert = expert_index // copies

    own_inputs = saved_inputs[0].reshape(rows, D)
    top_rows = top_grad.reshape(rows, D)
    hits = routes[0].reshape(rows, 2) == own_expert
    own_weight = jnp.sum(jnp.where(hits, mix_weights[0].reshape(rows, 2), 0.0), axis=1)
    weight = jnp.concatenate([own_weight, swap_cores(own_weight)])[:, None]
    inputs = jnp.concatenate([own_inputs, swap_cores(own_inputs)])

    pre_gate = times(inputs, gate)
    pre_up = times(inputs, up)
    sigmoid_gate = jax.nn.sigmoid(pre_gate)
    silu_gate = pre_gate * sigmoid_gate
    hidden = (silu_gate * pre_up).astype(BF)
    slope = pre_up * sigmoid_gate * (1.0 + pre_gate * (1.0 - sigmoid_gate))

    def phase(arriving):
        both = jnp.concatenate([arriving, swap_cores(arriving)])
        grad_rows = (weight * both.astype(F32)).astype(BF)
        grad_hidden = times(grad_rows, down, 1, 1)
        grad_gate = (grad_hidden * slope).astype(BF)
        grad_up = (grad_hidden * silu_gate).astype(BF)
        partial = times(grad_gate, gate, 1, 1) + times(grad_up, up, 1, 1)
        mine = partial[:rows] + swap_cores(partial[rows:].astype(BF)).astype(F32)
        pieces = exchange(mine.astype(BF).reshape(peers, rows_each, D))
        share = jnp.sum(pieces.astype(F32), axis=0)
        base = lax.dynamic_slice_in_dim(arriving, expert_index * rows_each, rows_each, 0)
        return (base.astype(F32) + share).astype(BF), grad_rows, grad_gate, grad_up

    def gathered(part):
        return exchange(jnp.broadcast_to(part, (peers, rows_each, D))).reshape(rows, D)

    part, _, _, _ = phase(top_rows)
    incoming = gathered(lax.ppermute(part, "pipe", [(i, i - 1) for i in range(1, sections)]))
    arriving = jnp.where(section_index == sections - 1, top_rows, incoming)
    part, grad_rows, grad_gate, grad_up = phase(arriving)
    produced = gathered(part)

    right16 = right.astype(BF)
    sums = jnp.concatenate(
        [times(grad_gate, right16[0]) + times(grad_up, right16[1]), times(hidden, right16[2])],
        axis=1,
    )
    other = swap_cores(sums)
    sums = sums + jnp.concatenate([other[rows:], other[:rows]])
    pieces = exchange(sums.reshape(copies, replicas * rows // copies, 2 * R), plane)
    piece = jnp.sum(pieces, axis=0)
    sums = exchange(jnp.broadcast_to(piece, (copies, *piece.shape)), plane)
    sums = sums.reshape(replicas * rows, 2 * R).astype(BF)
    factor = times(inputs, sums[:, :R], 0, 0) + times(grad_rows, sums[:, R:], 0, 0)
    gram_matrix = times(factor, factor, 0, 0, lax.Precision.HIGHEST)
    lower_factor = jnp.linalg.cholesky(gram_matrix)
    ortho = jax.scipy.linalg.solve_triangular(lower_factor, factor.T, lower=True).T
    ortho16 = ortho.astype(BF)
    along_inputs = times(inputs, ortho16).astype(BF)
    along_grads = times(grad_rows, ortho16).astype(BF)
    scale = 1.0 / math.sqrt(float(replicas * rows))
    q_next = jnp.stack(
        [
            times(grad_gate, along_inputs, 0, 0),
            times(grad_up, along_inputs, 0, 0),
            times(hidden, along_grads, 0, 0),
        ]
    )
    row_count = D // replicas
    basis = lax.dynamic_slice_in_dim(ortho, dp_index * row_count, row_count, 0)
    return (
        produced.reshape(1, MICRO, token_count, D),
        (basis * math.sqrt(float(D)))[None, None, None],
        (q_next * scale)[None, None, None],
    )


def solution(mesh):
    placed = (
        P("pipe", None, "dp", None),
        P(None, "dp", None),
        P("pipe", None, "dp", None),
        P("pipe", None, "dp", None),
        P("pipe", "expert", None, None, "dp"),
        P("pipe", "expert", None, None, "dp"),
        P("pipe", "expert", None, "dp", None),
        P("pipe", "expert", None, None, "dp", None),
    )
    return jax.shard_map(
        shards,
        mesh=mesh,
        in_specs=placed,
        out_specs=(
            P("pipe", None, "dp", None),
            P("pipe", "expert", None, "dp", None),
            P("pipe", "expert", None, None, "dp", None),
        ),
        check_vma=False,
    )
```

profile of v0, /device:TPU:0, one launch (start us, length us, event | category | flops | bytes accessed | tf_op | source)
XLA Modules:
  0.0 203.5 jit_solution(849431742204199565)
XLA Ops:
  1.2 1.0 fusion.37
  2.4 4.4 %collective-permute-done = f32[256]{0:T(256)S(1)} collective-permute-done((f32[256]{0:T(256)S(1)}, f32[256]{0:T(256)S(1)}, u32[]{:S(2)}, u32[]{:S(2)}) %collective-permute-start) | collective-permute-done | bytes 1056 | tf_op jit(solution)/shard_map/ppermute | solution.py:18
  6.8 3.8 %fusion.10 = f32[512,512]{1,0:T(8,128)S(1)} fusion(bf16[1,1,1,3072,512]{4,3,2,1,0:T(8,128)(2,1)S(1)} %copy-done, bf16[256,3072]{1,0:T(8,128)(2,1)} %collective-permute-done.2, bf16[256,3072]{1,0:T(8,128)(2,1)} %bitcast.83), kind=kOutput, calls=%fused_computation.20 | convolution fusion | flops 1616904192 | bytes 7340032 | tf_op jit(solution)/shard_map/dot_general | solution.py:26
  10.6 3.6 %fusion.14 = f32[512,512]{1,0:T(8,128)S(1)} fusion(bf16[1,1,1,3072,512]{4,3,2,1,0:T(8,128)(2,1)S(1)} %copy-done.3, bf16[256,3072]{1,0:T(8,128)(2,1)} %collective-permute-done.2, bf16[256,3072]{1,0:T(8,128)(2,1)S(1)} %bitcast.85), kind=kOutput, calls=%fused_computation.24 | convolution fusion | flops 1616904192 | bytes 7340032 | tf_op jit(solution)/shard_map/dot_general | solution.py:26
  14.3 3.7 %fusion = f32[512,512]{1,0:T(8,128)S(1)} fusion(bf16[256,3072]{1,0:T(8,128)(2,1)} %collective-permute-done.1, bf16[256,3072]{1,0:T(8,128)(2,1)S(1)} %bitcast.76, bf16[1,1,1,512,3072]{4,3,2,1,0:T(8,128)(2,1)S(1)} %copy-done.18, f32[512]{0:T(512)S(1)} %pad_maximum_fusion.3), kind=kOutput, calls=%fused_computation.5 | convolution fusion | flops 1620049920 | bytes 7342080 | tf_op jit(solution)/shard_map/dot_general | solution.py:26
  18.0 2.1 %fusion.8 = f32[512,3072]{1,0:T(8,128)S(1)} fusion(bf16[1,1,1,3072,512]{4,3,2,1,0:T(8,128)(2,1)S(1)} %copy-done, f32[512,512]{1,0:T(8,128)S(1)} %fusion, f32[512,512]{1,0:T(8,128)S(1)} %fusion.10, f32[512,512]{1,0:T(8,128)S(1)} %fusion.14), kind=kOutput, calls=%fused_computation.18 | convolution fusion | flops 1613234176 | bytes 12582912 | tf_op jit(solution)/shard_map/dot_general | solution.py:26
  20.1 1.9 convolution_add_fusion.1
  22.4 3.3 %collective-permute-done.3 = bf16[256,3072]{1,0:T(8,128)(2,1)S(1)} collective-permute-done((bf16[256,3072]{1,0:T(8,128)(2,1)S(1)}, bf16[256,3072]{1,0:T(8,128)(2,1)S(1)}, u32[]{:S(2)}, u32[]{:S(2)}) %collective-permute-start.3) | collective-permute-done | bytes 1572896 | tf_op jit(solution)/shard_map/ppermute | solution.py:18
  25.7 1.6 fusion.20
  27.3 9.5 %all-to-all-start = ((bf16[32,8,3072]{2,1,0:T(8,128)(2,1)}), bf16[32,8,3072]{2,1,0:T(8,128)(2,1)}, u32[]{:S(2)}, u32[]{:S(2)}) async-start(bf16[32,8,3072]{2,1,0:T(8,128)(2,1)} %fusion.20), calls=%async_computation | async-start | bytes 3145728 | tf_op jit(solution)/shard_map/all_to_all | solution.py:22
  36.8 23.8 %all-to-all-done = bf16[32,8,3072]{2,1,0:T(8,128)(2,1)} async-done(((bf16[32,8,3072]{2,1,0:T(8,128)(2,1)}), bf16[32,8,3072]{2,1,0:T(8,128)(2,1)}, u32[]{:S(2)}, u32[]{:S(2)}) %all-to-all-start) | async-done | bytes 1572896 | tf_op jit(solution)/shard_map/all_to_all | solution.py:22
  60.7 1.6 convert_reduce_fusion.1
  63.1 1.3 collective-permute-start.4
  64.4 6.2 %collective-permute-done.4 = bf16[8,3072]{1,0:T(8,128)(2,1)S(1)} collective-permute-done((bf16[8,3072]{1,0:T(8,128)(2,1)S(1)}, bf16[8,3072]{1,0:T(8,128)(2,1)S(1)}, u32[]{:S(2)}, u32[]{:S(2)}) %collective-permute-start.4) | collective-permute-done | bytes 49184 | tf_op jit(solution)/shard_map/ppermute | solution.py:78
  70.6 1.3 broadcast_in_dim.21
  71.9 4.7 %all-to-all-start.1 = ((bf16[32,8,3072]{2,1,0:T(8,128)(2,1)}), bf16[32,8,3072]{2,1,0:T(8,128)(2,1)}, u32[]{:S(2)}, u32[]{:S(2)}) async-start(bf16[32,8,3072]{2,1,0:T(8,128)(2,1)} %broadcast_in_dim.21), calls=%async_computation.1 | async-start | bytes 3145728 | tf_op jit(solution)/shard_map/all_to_all | solution.py:22
  76.7 21.5 %all-to-all-done.1 = bf16[32,8,3072]{2,1,0:T(8,128)(2,1)} async-done(((bf16[32,8,3072]{2,1,0:T(8,128)(2,1)}), bf16[32,8,3072]{2,1,0:T(8,128)(2,1)}, u32[]{:S(2)}, u32[]{:S(2)}) %all-to-all-start.1) | async-done | bytes 1572896 | tf_op jit(solution)/shard_map/all_to_all | solution.py:22
  98.1 2.2 %bitcast_select_fusion = bf16[256,3072]{1,0:T(8,128)(2,1)S(1)} fusion(bf16[32,8,3072]{2,1,0:T(8,128)(2,1)} %all-to-all-done.1, pred[]{:T(512)S(6)} %eq.10, bf16[4,64,3072]{2,1,0:T(8,128)(2,1)} %param.9), kind=kLoop, calls=%fused_computation.34 | loop fusion | flops 786432 | bytes 4718593 | tf_op jit(solution)/shard_map/jit(_where)/select_n | solution.py:79
  100.7 3.4 %collective-permute-done.5 = bf16[256,3072]{1,0:T(8,128)(2,1)S(1)} collective-permute-done((bf16[256,3072]{1,0:T(8,128)(2,1)S(1)}, bf16[256,3072]{1,0:T(8,128)(2,1)S(1)}, u32[]{:S(2)}, u32[]{:S(2)}) %collective-permute-start.5) | collective-permute-done | bytes 1572896 | tf_op jit(solution)/shard_map/ppermute | solution.py:18
  104.0 4.7 %multiply_convert_fusion.3 = (bf16[512,512]{1,0:T(8,128)(2,1)S(1)}, bf16[512,512]{1,0:T(8,128)(2,1)S(1)}, bf16[512,512]{1,0:T(8,128)(2,1)S(1)}) fusion(f32[512,512]{1,0:T(8,128)S(1)} %copy-done.12, f32[512,512]{1,0:T(8,128)S(1)} %copy-done.6, bf16[1,1,1,512,3072]{4,3,2,1,0:T(8,128)(2,1)} %param.14, bf16[256,3072]{1,0:T(8,128)(2,1)S(1)} %collective-permute-done.5, ...), kind=kOutput, calls=%fused_computation.42 | convolution fusion | flops 1623982080 | bytes 9963520 | tf_op jit(solution)/shard_map/dot_general | solution.py:26
  108.8 1.8 fusion.6
  111.2 1.8 convolution_add_fusion
  113.1 2.6 %copy-done.2 = f32[512,3072]{1,0:T(8,128)} copy-done((f32[512,3072]{1,0:T(8,128)}, f32[512,3072]{1,0:T(8,128)S(1)}, u32[]{:S(2)}) %copy-start.2) | copy-done | bytes 6291480
  117.8 0.8 copy.16
  118.6 0.8 copy.17
  119.9 1.0 fusion.40
  120.9 0.8 copy.14
  121.8 1.9 maximum_add_fusion
  123.7 3.4 %all-to-all-start.4 = ((f32[8,64,128]{2,1,0:T(8,128)}), f32[8,64,128]{2,1,0:T(8,128)S(1)}, u32[]{:S(2)}, u32[]{:S(2)}) async-start(f32[8,64,128]{2,1,0:T(8,128)} %maximum_add_fusion), calls=%async_computation.4 | async-start | bytes 524288 | tf_op jit(solution)/shard_map/all_to_all | solution.py:22
  127.1 7.8 %all-to-all-done.4 = f32[8,64,128]{2,1,0:T(8,128)S(1)} async-done(((f32[8,64,128]{2,1,0:T(8,128)}), f32[8,64,128]{2,1,0:T(8,128)S(1)}, u32[]{:S(2)}, u32[]{:S(2)}) %all-to-all-start.4) | async-done | bytes 262176 | tf_op jit(solution)/shard_map/all_to_all | solution.py:22
  135.6 3.4 %all-to-all-start.5 = ((bf16[8,64,128]{2,1,0:T(8,128)(2,1)}), bf16[8,64,128]{2,1,0:T(8,128)(2,1)S(1)}, u32[]{:S(2)}, u32[]{:S(2)}) async-start(bf16[8,64,128]{2,1,0:T(8,128)(2,1)} %broadcast_in_dim.23), calls=%async_computation.5 | async-start | bytes 262144 | tf_op jit(solution)/shard_map/all_to_all | solution.py:22
  139.0 3.5 %fusion.21 = bf16[32,8,3072]{2,1,0:T(8,128)(2,1)} fusion(bf16[256,3072]{1,0:T(8,128)(2,1)S(1)} %collective-permute-done.6, f32[512,3072]{1,0:T(8,128)} %copy-done.2), kind=kLoop, calls=%fused_computation.33 | loop fusion | flops 2359296 | bytes 6291456 | tf_op jit(solution)/shard_map/reshape | solution.py:69
  142.5 3.2 %all-to-all-done.5 = bf16[8,64,128]{2,1,0:T(8,128)(2,1)S(1)} async-done(((bf16[8,64,128]{2,1,0:T(8,128)(2,1)}), bf16[8,64,128]{2,1,0:T(8,128)(2,1)S(1)}, u32[]{:S(2)}, u32[]{:S(2)}) %all-to-all-start.5) | async-done | bytes 131104 | tf_op jit(solution)/shard_map/all_to_all | solution.py:22
  145.6 4.0 %all-to-all-start.2 = ((bf16[32,8,3072]{2,1,0:T(8,128)(2,1)}), bf16[32,8,3072]{2,1,0:T(8,128)(2,1)S(1)}, u32[]{:S(2)}, u32[]{:S(2)}) async-start(bf16[32,8,3072]{2,1,0:T(8,128)(2,1)} %fusion.21), calls=%async_computation.2 | async-start | bytes 3145728 | tf_op jit(solution)/shard_map/all_to_all | solution.py:22
  149.6 2.9 %fusion.28 = f32[3072,64]{0,1:T(8,128)S(1)} fusion(bf16[512,128]{1,0:T(8,128)(2,1)S(1)} %bitcast.80, bf16[256,3072]{1,0:T(8,128)(2,1)} %copy-done.21, bf16[256,3072]{1,0:T(8,128)(2,1)} %copy-done.15, f32[512]{0:T(512)S(1)} %pad_maximum_fusion.3), kind=kOutput, calls=%fused_computation.57 | convolution fusion | flops 210763776 | bytes 4065280 | tf_op jit(solution)/shard_map/dot_general | solution.py:26
  152.5 2.1 %convolution_add_fusion.2 = f32[3072,64]{0,1:T(8,128)S(1)} fusion(f32[3072,64]{0,1:T(8,128)S(1)} %fusion.28, bf16[512,128]{1,0:T(8,128)(2,1)S(1)} %bitcast.81, bf16[256,3072]{1,0:T(8,128)(2,1)} %collective-permute-done.2, bf16[256,3072]{1,0:T(8,128)(2,1)S(1)} %bitcast.86), kind=kOutput, calls=%fused_computation.4 | convolution fusion | flops 207814656 | bytes 4849664 | tf_op jit(solution)/shard_map/dot_general | solution.py:26
  155.5 5.8 %cholesky.16 = f32[64,64]{1,0:T(8,128)S(1)} custom-call(f32[64,64]{1,0:T(8,128)S(1)} %fusion.36), custom_call_target="Cholesky" | custom-call | tf_op jit(solution)/shard_map/jit(cholesky)/cholesky | solution.py:96
  162.7 4.9 %custom-call.7 = f32[1,64,64]{1,2,0:T(8,128)S(1)} custom-call(f32[1,64,64]{2,1,0:T(8,128)S(1)} %fusion.33), custom_call_target="InvertDiagBlocksLowerTriangular" | custom-call | tf_op jit(solution)/shard_map/jit(_solve_triangular)/triangular_solve | solution.py:97
  167.6 4.1 %all-to-all-done.2 = bf16[32,8,3072]{2,1,0:T(8,128)(2,1)S(1)} async-done(((bf16[32,8,3072]{2,1,0:T(8,128)(2,1)}), bf16[32,8,3072]{2,1,0:T(8,128)(2,1)S(1)}, u32[]{:S(2)}, u32[]{:S(2)}) %all-to-all-start.2) | async-done | bytes 1572896 | tf_op jit(solution)/shard_map/all_to_all | solution.py:22
  171.9 0.8 add_convert_fusion
  172.7 1.3 broadcast_in_dim.22
  174.1 4.9 %all-to-all-start.3 = ((bf16[32,8,3072]{2,1,0:T(8,128)(2,1)}), bf16[32,8,3072]{2,1,0:T(8,128)(2,1)}, u32[]{:S(2)}, u32[]{:S(2)}) async-start(bf16[32,8,3072]{2,1,0:T(8,128)(2,1)} %broadcast_in_dim.22), calls=%async_computation.3 | async-start | bytes 3145728 | tf_op jit(solution)/shard_map/all_to_all | solution.py:22
  179.0 0.8 fusion.34
  179.8 3.3 %convolution_convert_fusion.1 = bf16[512,64]{0,1:T(8,128)(2,1)S(1)} fusion(f32[3072,64]{0,1:T(8,128)S(1)} %fusion.34, bf16[256,3072]{1,0:T(8,128)(2,1)} %collective-permute-done.2, bf16[256,3072]{1,0:T(8,128)(2,1)} %bitcast.84), kind=kOutput, calls=%fused_computation.41 | convolution fusion | flops 207847424 | bytes 3997696 | tf_op jit(solution)/shard_map/dot_general | solution.py:26
  183.5 3.7 %fusion.23 = f32[1,1,1,1,512,64]{4,5,3,2,1,0:T(8,128)S(1)} fusion(bf16[512,512]{1,0:T(8,128)(2,1)} %copy-done.16, f32[3072,64]{0,1:T(8,128)} %copy-done.13, bf16[256,3072]{1,0:T(8,128)(2,1)} %copy-done.21, bf16[256,3072]{1,0:T(8,128)(2,1)} %copy-done.15, f32[512]{0:T(512)S(1)} %pad_maximum_fusion.3), kind=kOutput, calls=%fused_computation.40 | convolution fusion | flops 244547584 | bytes 4589568 | tf_op jit(solution)/shard_map/dot_general | solution.py:26
  188.0 1.8 multiply_bitcast_fusion
  189.8 11.1 %all-to-all-done.3 = bf16[32,8,3072]{2,1,0:T(8,128)(2,1)} async-done(((bf16[32,8,3072]{2,1,0:T(8,128)(2,1)}), bf16[32,8,3072]{2,1,0:T(8,128)(2,1)}, u32[]{:S(2)}, u32[]{:S(2)}) %all-to-all-start.3) | async-done | bytes 1572896 | tf_op jit(solution)/shard_map/all_to_all | solution.py:22
  200.9 2.7 %copy.19 = bf16[1,4,64,3072]{3,2,1,0:T(8,128)(2,1)} copy(bf16[1,4,64,3072]{3,2,1,0:T(8,128)(2,1)} %bitcast.8) | data formatting | bytes 3145728
  (77 shorter events, 9.7 us)
Async XLA Ops:
  0.6 6.1 %copy-start = (bf16[1,1,1,3072,512]{4,3,2,1,0:T(8,128)(2,1)S(1)}, bf16[1,1,1,3072,512]{4,3,2,1,0:T(8,128)(2,1)}, u32[]{:S(2)}) copy-start(bf16[1,1,1,3072,512]{4,3,2,1,0:T(8,128)(2,1)} %param.12) | copy-start | bytes 9437188
  0.6 6.1 %collective-permute-start.2 = (bf16[256,3072]{1,0:T(8,128)(2,1)}, bf16[256,3072]{1,0:T(8,128)(2,1)}, u32[]{:S(2)}, u32[]{:S(2)}) collective-permute-start(bf16[256,3072]{1,0:T(8,128)(2,1)} %bitcast.82), channel_id=1, source_target_pairs={{0,64},{64,0},{1,65},{65,1},{2,66},{66,2},{3,67},{67,3},{4,68},{68... | collective-permute-start | bytes 4718600 | tf_op jit(solution)/shard_map/ppermute | solution.py:18
  0.7 13.5 %collective-permute-start.1 = (bf16[256,3072]{1,0:T(8,128)(2,1)}, bf16[256,3072]{1,0:T(8,128)(2,1)}, u32[]{:S(2)}, u32[]{:S(2)}) collective-permute-start(bf16[256,3072]{1,0:T(8,128)(2,1)} %bitcast.74), channel_id=1, source_target_pairs={{0,64},{64,0},{1,65},{65,1},{2,66},{66,2},{3,67},{67,3},{4,68},{68... | collective-permute-start | bytes 4718600 | tf_op jit(solution)/shard_map/ppermute | solution.py:18
  2.3 4.4 %collective-permute-start = (f32[256]{0:T(256)S(1)}, f32[256]{0:T(256)S(1)}, u32[]{:S(2)}, u32[]{:S(2)}) collective-permute-start(f32[256]{0:T(256)S(1)} %reduce_sum.39), channel_id=1, source_target_pairs={{0,64},{64,0},{1,65},{65,1},{2,66},{66,2},{3,67},{67,3},{4,68},{68... | collective-permute-start | bytes 3080 | tf_op jit(solution)/shard_map/ppermute | solution.py:18
  6.7 3.9 %copy-start.3 = (bf16[1,1,1,3072,512]{4,3,2,1,0:T(8,128)(2,1)S(1)}, bf16[1,1,1,3072,512]{4,3,2,1,0:T(8,128)(2,1)}, u32[]{:S(2)}) copy-start(bf16[1,1,1,3072,512]{4,3,2,1,0:T(8,128)(2,1)} %param.13) | copy-start | bytes 9437188
  6.7 3.9 %copy-start.19 = (bf16[1,4,64,3072]{3,2,1,0:T(8,128)(2,1)S(1)}, bf16[1,4,64,3072]{3,2,1,0:T(8,128)(2,1)}, u32[]{:S(2)}) copy-start(bf16[1,4,64,3072]{3,2,1,0:T(8,128)(2,1)} %param.8) | copy-start | bytes 4718596
  10.6 9.5 %copy-start.5 = (f32[512,512]{1,0:T(8,128)}, f32[512,512]{1,0:T(8,128)S(1)}, u32[]{:S(2)}) copy-start(f32[512,512]{1,0:T(8,128)S(1)} %fusion.10) | copy-start | bytes 3145732
  10.6 3.7 %copy-start.14 = (bf16[4,64,3072]{2,1,0:T(8,128)(2,1)S(1)}, bf16[4,64,3072]{2,1,0:T(8,128)(2,1)}, u32[]{:S(2)}) copy-start(bf16[4,64,3072]{2,1,0:T(8,128)(2,1)} %param.9) | copy-start | bytes 4718596
  10.6 3.7 %copy-start.18 = (bf16[1,1,1,512,3072]{4,3,2,1,0:T(8,128)(2,1)S(1)}, bf16[1,1,1,512,3072]{4,3,2,1,0:T(8,128)(2,1)}, u32[]{:S(2)}) copy-start(bf16[1,1,1,512,3072]{4,3,2,1,0:T(8,128)(2,1)} %param.14) | copy-start | bytes 9437188
  14.3 3.7 %copy-start.11 = (f32[512,512]{1,0:T(8,128)}, f32[512,512]{1,0:T(8,128)S(1)}, u32[]{:S(2)}) copy-start(f32[512,512]{1,0:T(8,128)S(1)} %fusion.14) | copy-start | bytes 3145732
  22.2 3.5 %collective-permute-start.3 = (bf16[256,3072]{1,0:T(8,128)(2,1)S(1)}, bf16[256,3072]{1,0:T(8,128)(2,1)S(1)}, u32[]{:S(2)}, u32[]{:S(2)}) collective-permute-start(bf16[256,3072]{1,0:T(8,128)(2,1)S(1)} %slice.95), channel_id=1, source_target_pairs={{0,64},{64,0},{1,65},{65,1},{2,66},{66,2},{3,67},{67,3},{4,68},{68... | collective-permute-start | bytes 4718600 | tf_op jit(solution)/shard_map/ppermute | solution.py:18
  27.3 33.3 %all-to-all-start = ((bf16[32,8,3072]{2,1,0:T(8,128)(2,1)}), bf16[32,8,3072]{2,1,0:T(8,128)(2,1)}, u32[]{:S(2)}, u32[]{:S(2)}) async-start(bf16[32,8,3072]{2,1,0:T(8,128)(2,1)} %fusion.20), calls=%async_computation | async-start | bytes 3145728 | tf_op jit(solution)/shard_map/all_to_all | solution.py:22
  63.1 7.5 %collective-permute-start.4 = (bf16[8,3072]{1,0:T(8,128)(2,1)S(1)}, bf16[8,3072]{1,0:T(8,128)(2,1)S(1)}, u32[]{:S(2)}, u32[]{:S(2)}) collective-permute-start(bf16[8,3072]{1,0:T(8,128)(2,1)S(1)} %add_convert_fusion.1), channel_id=1, source_target_pairs={{32,0},{33,1},{34,2},{35,3},{36,4},{37,5},{38,6},{39,7},{40,8},{41... | collective-permute-start | bytes 147464 | tf_op jit(solution)/shard_map/ppermute | solution.py:78
  71.9 26.2 %all-to-all-start.1 = ((bf16[32,8,3072]{2,1,0:T(8,128)(2,1)}), bf16[32,8,3072]{2,1,0:T(8,128)(2,1)}, u32[]{:S(2)}, u32[]{:S(2)}) async-start(bf16[32,8,3072]{2,1,0:T(8,128)(2,1)} %broadcast_in_dim.21), calls=%async_computation.1 | async-start | bytes 3145728 | tf_op jit(solution)/shard_map/all_to_all | solution.py:22
  76.6 24.0 %copy-start.17 = (f32[1,1,1,3,512,64]{4,5,3,2,1,0:T(8,128)S(1)}, f32[1,1,1,3,512,64]{4,5,3,2,1,0:T(8,128)}, u32[]{:S(2)}) copy-start(f32[1,1,1,3,512,64]{4,5,3,2,1,0:T(8,128)} %param.15) | copy-start | bytes 1179652
  98.1 5.9 %copy-start.6 = (f32[512,512]{1,0:T(8,128)S(1)}, f32[512,512]{1,0:T(8,128)}, u32[]{:S(2)}) copy-start(f32[512,512]{1,0:T(8,128)} %copy-done.5) | copy-start | bytes 3145732
  98.1 5.9 %copy-start.12 = (f32[512,512]{1,0:T(8,128)S(1)}, f32[512,512]{1,0:T(8,128)}, u32[]{:S(2)}) copy-start(f32[512,512]{1,0:T(8,128)} %copy-done.11) | copy-start | bytes 3145732
  100.3 8.4 %copy-start.15 = (bf16[256,3072]{1,0:T(8,128)(2,1)}, bf16[256,3072]{1,0:T(8,128)(2,1)S(1)}, u32[]{:S(2)}) copy-start(bf16[256,3072]{1,0:T(8,128)(2,1)S(1)} %bitcast_select_fusion) | copy-start | bytes 4718596
  100.4 3.7 %collective-permute-start.5 = (bf16[256,3072]{1,0:T(8,128)(2,1)S(1)}, bf16[256,3072]{1,0:T(8,128)(2,1)S(1)}, u32[]{:S(2)}, u32[]{:S(2)}) collective-permute-start(bf16[256,3072]{1,0:T(8,128)(2,1)S(1)} %bitcast_select_fusion), channel_id=1, source_target_pairs={{0,64},{64,0},{1,65},{65,1},{2,66},{66,2},{3,67},{67,3},{4,68},{68... | collective-permute-start | bytes 4718600 | tf_op jit(solution)/shard_map/ppermute | solution.py:18
  104.0 4.7 %copy-start.21 = (bf16[256,3072]{1,0:T(8,128)(2,1)}, bf16[256,3072]{1,0:T(8,128)(2,1)S(1)}, u32[]{:S(2)}) copy-start(bf16[256,3072]{1,0:T(8,128)(2,1)S(1)} %collective-permute-done.5) | copy-start | bytes 4718596
  108.7 1.9 copy-start.9
  108.7 7.4 %copy-start.16 = (bf16[512,512]{1,0:T(8,128)(2,1)}, bf16[512,512]{1,0:T(8,128)(2,1)S(1)}, u32[]{:S(2)}) copy-start(bf16[512,512]{1,0:T(8,128)(2,1)S(1)} %get-tuple-element.3) | copy-start | bytes 1572868
  108.7 7.7 %copy-start.7 = (bf16[512,512]{1,0:T(8,128)(2,1)}, bf16[512,512]{1,0:T(8,128)(2,1)S(1)}, u32[]{:S(2)}) copy-start(bf16[512,512]{1,0:T(8,128)(2,1)S(1)} %get-tuple-element.5) | copy-start | bytes 1572868
  108.8 2.4 %copy-start.4 = (bf16[1,1,1,3072,512]{4,3,2,1,0:T(8,128)(2,1)S(1)}, bf16[1,1,1,3072,512]{4,3,2,1,0:T(8,128)(2,1)}, u32[]{:S(2)}) copy-start(bf16[1,1,1,3072,512]{4,3,2,1,0:T(8,128)(2,1)} %param.13) | copy-start | bytes 9437188
  113.0 2.7 %copy-start.2 = (f32[512,3072]{1,0:T(8,128)}, f32[512,3072]{1,0:T(8,128)S(1)}, u32[]{:S(2)}) copy-start(f32[512,3072]{1,0:T(8,128)S(1)} %convolution_add_fusion) | copy-start | bytes 18874372
  115.9 23.1 %collective-permute-start.6 = (bf16[256,3072]{1,0:T(8,128)(2,1)S(1)}, bf16[256,3072]{1,0:T(8,128)(2,1)S(1)}, u32[]{:S(2)}, u32[]{:S(2)}) collective-permute-start(bf16[256,3072]{1,0:T(8,128)(2,1)S(1)} %slice.94), channel_id=1, source_target_pairs={{0,64},{64,0},{1,65},{65,1},{2,66},{66,2},{3,67},{67,3},{4,68},{68... | collective-permute-start | bytes 4718600 | tf_op jit(solution)/shard_map/ppermute | solution.py:18
  117.4 2.5 %collective-permute-start.7 = (f32[512,128]{0,1:T(8,128)}, f32[512,128]{0,1:T(8,128)}, u32[]{:S(2)}, u32[]{:S(2)}) collective-permute-start(f32[512,128]{0,1:T(8,128)} %pad_maximum_fusion.1), channel_id=1, source_target_pairs={{0,64},{64,0},{1,65},{65,1},{2,66},{66,2},{3,67},{67,3},{4,68},{68... | collective-permute-start | bytes 786440 | tf_op jit(solution)/shard_map/ppermute | solution.py:18
  123.7 11.2 %all-to-all-start.4 = ((f32[8,64,128]{2,1,0:T(8,128)}), f32[8,64,128]{2,1,0:T(8,128)S(1)}, u32[]{:S(2)}, u32[]{:S(2)}) async-start(f32[8,64,128]{2,1,0:T(8,128)} %maximum_add_fusion), calls=%async_computation.4 | async-start | bytes 524288 | tf_op jit(solution)/shard_map/all_to_all | solution.py:22
  135.6 10.0 %all-to-all-start.5 = ((bf16[8,64,128]{2,1,0:T(8,128)(2,1)}), bf16[8,64,128]{2,1,0:T(8,128)(2,1)S(1)}, u32[]{:S(2)}, u32[]{:S(2)}) async-start(bf16[8,64,128]{2,1,0:T(8,128)(2,1)} %broadcast_in_dim.23), calls=%async_computation.5 | async-start | bytes 262144 | tf_op jit(solution)/shard_map/all_to_all | solution.py:22
  145.6 26.1 %all-to-all-start.2 = ((bf16[32,8,3072]{2,1,0:T(8,128)(2,1)}), bf16[32,8,3072]{2,1,0:T(8,128)(2,1)S(1)}, u32[]{:S(2)}, u32[]{:S(2)}) async-start(bf16[32,8,3072]{2,1,0:T(8,128)(2,1)} %fusion.21), calls=%async_computation.2 | async-start | bytes 3145728 | tf_op jit(solution)/shard_map/all_to_all | solution.py:22
  149.6 2.9 %copy-start.20 = (bf16[1,4,64,3072]{3,2,1,0:T(8,128)(2,1)S(1)}, bf16[1,4,64,3072]{3,2,1,0:T(8,128)(2,1)}, u32[]{:S(2)}) copy-start(bf16[1,4,64,3072]{3,2,1,0:T(8,128)(2,1)} %param.8) | copy-start | bytes 4718596
  174.1 26.8 %all-to-all-start.3 = ((bf16[32,8,3072]{2,1,0:T(8,128)(2,1)}), bf16[32,8,3072]{2,1,0:T(8,128)(2,1)}, u32[]{:S(2)}, u32[]{:S(2)}) async-start(bf16[32,8,3072]{2,1,0:T(8,128)(2,1)} %broadcast_in_dim.22), calls=%async_computation.3 | async-start | bytes 3145728 | tf_op jit(solution)/shard_map/all_to_all | solution.py:22
  179.8 3.5 %copy-start.13 = (f32[3072,64]{0,1:T(8,128)}, f32[3072,64]{0,1:T(8,128)S(1)}, u32[]{:S(2)}) copy-start(f32[3072,64]{0,1:T(8,128)S(1)} %fusion.34) | copy-start | bytes 2359300
  179.8 3.3 %copy-start.10 = (bf16[512,512]{1,0:T(8,128)(2,1)S(1)}, bf16[512,512]{1,0:T(8,128)(2,1)}, u32[]{:S(2)}) copy-start(bf16[512,512]{1,0:T(8,128)(2,1)} %copy-done.9) | copy-start | bytes 1572868
  179.8 3.5 %copy-start.8 = (bf16[512,512]{1,0:T(8,128)(2,1)S(1)}, bf16[512,512]{1,0:T(8,128)(2,1)}, u32[]{:S(2)}) copy-start(bf16[512,512]{1,0:T(8,128)(2,1)} %copy-done.7) | copy-start | bytes 1572868
  183.5 20.0 %copy-start.1 = (bf16[1,1,1,3072,512]{4,3,2,1,0:T(8,128)(2,1)S(1)}, bf16[1,1,1,3072,512]{4,3,2,1,0:T(8,128)(2,1)}, u32[]{:S(2)}) copy-start(bf16[1,1,1,3072,512]{4,3,2,1,0:T(8,128)(2,1)} %param.12) | copy-start | bytes 9437188
where the time goes:
time: 205 us; the launch traced here: 204 us
  waiting for transfers between devices  89.1 us (43%)
  matrix products  38.1 us (19%)
  starting transfers between devices  32.8 us (16%)
  other arithmetic  29.2 us (14%)
  local copies, waits for them, and re-layouts  13.1 us (6%)
    all_to_all x6, waiting for transfers between devices, exchange(): lax.all_to_all(pieces, 'expert', 0, 0, tiled=True, axis_index_groups=groups)  71.5 us
    dot_general x18, matrix products, times(): lax.dot_general(a, b, (((ca,), (cb,)), ((), ())), preferred_element_type=...  37.3 us
    all_to_all x6, starting transfers between devices, exchange(): lax.all_to_all(pieces, 'expert', 0, 0, tiled=True, axis_index_groups=groups)  29.9 us
    ppermute x7, waiting for transfers between devices, swap_cores(): return lax.ppermute(value, 'dp', [(0, 1), (1, 0)])  11.4 us
    another operation x3, other arithmetic, shards(): lower_factor = jnp.linalg.cholesky(gram_matrix)  6.52 us
    ppermute x1, waiting for transfers between devices, shards(): lax.ppermute(part, 'pipe', [(i, i - 1) for i in range(1, sections)])  6.19 us
    unnamed x45, local copies, waits for them, and re-layouts  5.72 us
    another operation x2, other arithmetic, shards(): jax.scipy.linalg.solve_triangular(lower_factor, factor.T, lower=True)  5.55 us
  transfers between devices with their start and end apart: 14, of which 11 were waited for; matrix products, arithmetic and copies ran while one was open for 24% of the time, Pallas kernels for 0%

commit v1 on v0

v1 whole, which is shorter than its diff:
```python
import math

import jax
import jax.numpy as jnp
from jax import lax
from jax.sharding import PartitionSpec as P

D = 3072
EXPERTS = 4
R = 64
MICRO = 4
CAP = 48

BF = jnp.bfloat16
F32 = jnp.float32


def swap_cores(value):
    return lax.ppermute(value, "dp", [(0, 1), (1, 0)])


def exchange(pieces):
    return lax.all_to_all(pieces, "expert", 0, 0, tiled=True)


def times(a, b, ca=1, cb=0, precision=None):
    return lax.dot_general(
        a, b, (((ca,), (cb,)), ((), ())), preferred_element_type=F32, precision=precision
    )


def slots_of(route_rows):
    flat = route_rows.reshape(MICRO, -1)
    count = flat.shape[1]
    earlier = lax.broadcasted_iota(jnp.int32, (count, count), 1) < lax.broadcasted_iota(
        jnp.int32, (count, count), 0
    )
    same = (flat[:, :, None] == flat[:, None, :]) & earlier[None]
    return jnp.sum(same.astype(jnp.int32), axis=2).reshape(route_rows.shape)


def hit_table(ids, count):
    rows = lax.broadcasted_iota(jnp.int32, (count, ids.shape[0]), 0)
    return rows == ids[None, :, 0], rows == ids[None, :, 1]


def add_copies(values, copies):
    def x_pair(i):
        return i ^ 1

    def y_pair(i):
        return i ^ 2

    def y_cross(i):
        y = i // 2 % 4
        return i + (((3 - y) % 4) - y) * 2

    for partner in (x_pair, y_pair, y_cross):
        route = [(i, partner(i)) for i in range(copies * EXPERTS)]
        values = values + lax.ppermute(values, "expert", route)
    return values


def shards(saved_inputs, top_grad, routes, mix_weights, w_gate, w_up, w_down, q_prev):
    sections = lax.axis_size("pipe")
    last = lax.axis_index("pipe") == sections - 1
    peers = lax.axis_size("expert")
    expert_index = lax.axis_index("expert")
    replicas = lax.axis_size("dp")
    dp_index = lax.axis_index("dp")
    gate, up, down = (w_gate[0, 0, 0], w_up[0, 0, 0], w_down[0, 0, 0])
    right = q_prev[0, 0, 0].astype(BF)
    copies = peers // EXPERTS
    tokens = saved_inputs.shape[2]
    rows = MICRO * tokens
    slots = MICRO * CAP
    columns = D // copies
    major, minor = (expert_index // copies, expert_index % copies)

    own_inputs = saved_inputs[0].reshape(rows, D)
    top_rows = top_grad.reshape(rows, D)
    rank = slots_of(routes[0])
    mix = mix_weights[0].reshape(rows, 2)
    micro_start = (jnp.arange(MICRO, dtype=jnp.int32) * CAP)[:, None, None]
    own_ids = jnp.where(routes[0] == major, micro_start + rank, -1).reshape(rows, 2)
    first, second = hit_table(own_ids, slots)
    own_pick = (first | second).astype(BF)
    weight = jnp.sum(
        jnp.where(first, mix[None, :, 0], 0.0) + jnp.where(second, mix[None, :, 1], 0.0),
        axis=1,
        keepdims=True,
    )
    part_ids = lax.dynamic_index_in_dim(routes[0] * CAP + rank, major, 0, keepdims=False)
    first, second = hit_table(part_ids, EXPERTS * CAP)
    part_pick = (first | second).astype(BF)

    def both_cores(own):
        return jnp.concatenate([own, swap_cores(own)])

    inputs = both_cores(times(own_pick, own_inputs).astype(BF))
    pre_gate = times(inputs, gate)
    pre_up = times(inputs, up)
    sigmoid_gate = jax.nn.sigmoid(pre_gate)
    silu_gate = pre_gate * sigmoid_gate
    hidden = (silu_gate * pre_up).astype(BF)
    slope = pre_up * sigmoid_gate * (1.0 + pre_gate * (1.0 - sigmoid_gate))

    def phase(own_rows, base):
        grad_rows = both_cores((weight * own_rows).astype(BF))
        grad_hidden = times(grad_rows, down, 1, 1)
        grad_gate = (grad_hidden * slope).astype(BF)
        grad_up = (grad_hidden * silu_gate).astype(BF)
        partial = times(grad_gate, gate, 1, 1) + times(grad_up, up, 1, 1)
        mine = partial[:slots] + swap_cores(partial[slots:].astype(BF)).astype(F32)
        mine = mine.astype(BF).reshape(MICRO, CAP, copies, columns).transpose(0, 2, 1, 3)
        pieces = exchange(mine.reshape(peers, CAP, columns))
        summed = jnp.sum(pieces.astype(F32).reshape(EXPERTS, copies, CAP, columns), axis=1)
        share = times(
            part_pick.astype(F32),
            summed.reshape(EXPERTS * CAP, columns),
            0,
            0,
            lax.Precision.HIGHEST,
        )
        return (base.astype(F32) + share).astype(BF), grad_rows, grad_gate, grad_up

    top_part = lax.dynamic_slice(
        top_grad, (major, 0, minor * columns), (1, tokens, columns)
    ).reshape(tokens, columns)
    part, _, _, _ = phase(times(own_pick, top_rows), top_part)
    incoming = lax.ppermute(part, "pipe", [(i, i - 1) for i in range(1, sections)])
    base = jnp.where(last, top_part, incoming)
    listed = times(part_pick, base).astype(BF).reshape(EXPERTS, 1, CAP, columns)
    pieces = jnp.broadcast_to(listed, (EXPERTS, copies, CAP, columns))
    own_rows = exchange(pieces.reshape(peers, CAP, columns))
    own_rows = own_rows.reshape(MICRO, copies, CAP, columns).transpose(0, 2, 1, 3)
    part, grad_rows, grad_gate, grad_up = phase(own_rows.reshape(slots, D).astype(F32), base)
    produced = exchange(jnp.broadcast_to(part, (peers, tokens, columns)))
    produced = produced.reshape(MICRO, copies, tokens, columns).transpose(0, 2, 1, 3)

    sums = jnp.concatenate(
        [times(grad_gate, right[0]) + times(grad_up, right[1]), times(hidden, right[2])], axis=1
    )
    other = swap_cores(sums)
    sums = sums + jnp.concatenate([other[slots:], other[:slots]])
    sums = add_copies(sums, copies).astype(BF)
    factor = times(inputs, sums[:, :R], 0, 0) + times(grad_rows, sums[:, R:], 0, 0)
    gram_matrix = times(factor, factor, 0, 0, lax.Precision.HIGHEST)
    lower_factor = jnp.linalg.cholesky(gram_matrix)
    ortho = jax.scipy.linalg.solve_triangular(lower_factor, factor.T, lower=True).T
    ortho16 = ortho.astype(BF)
    along_inputs = times(inputs, ortho16).astype(BF)
    along_grads = times(grad_rows, ortho16).astype(BF)
    scale = 1.0 / math.sqrt(float(replicas * rows))
    q_next = jnp.stack(
        [
            times(grad_gate, along_inputs, 0, 0),
            times(grad_up, along_inputs, 0, 0),
            times(hidden, along_grads, 0, 0),
        ]
    )
    row_count = D // replicas
    basis = lax.dynamic_slice_in_dim(ortho, dp_index * row_count, row_count, 0)
    return (
        produced.reshape(1, MICRO, tokens, D),
        (basis * math.sqrt(float(D)))[None, None, None],
        (q_next * scale)[None, None, None],
    )


def solution(mesh):
    placed = (
        P("pipe", None, "dp", None),
        P(None, "dp", None),
        P("pipe", None, "dp", None),
        P("pipe", None, "dp", None),
        P("pipe", "expert", None, None, "dp"),
        P("pipe", "expert", None, None, "dp"),
        P("pipe", "expert", None, "dp", None),
        P("pipe", "expert", None, None, "dp", None),
    )
    return jax.shard_map(
        shards,
        mesh=mesh,
        in_specs=placed,
        out_specs=(
            P("pipe", None, "dp", None),
            P("pipe", "expert", None, "dp", None),
            P("pipe", "expert", None, None, "dp", None),
        ),
        check_vma=False,
    )
```

time: 205 us -> 190 us (0.927)
  waiting for transfers between devices: 89.1 us -> 48.6 us
  blocking collectives: 0 us -> 20.8 us
  local copies, waits for them, and re-layouts: 13.1 us -> 19 us
  starting transfers between devices: 32.8 us -> 28.4 us
    all_to_all x6 -> x3, waiting for transfers between devices: 71.5 us -> 19.4 us  [exchange(): return lax.all_to_all(pieces, 'expert', 0, 0, tiled=True)]
    all_to_all x0 -> x1, blocking collectives: none -> 20.8 us  [exchange(): return lax.all_to_all(pieces, 'expert', 0, 0, tiled=True)]
    ppermute x0 -> x3, waiting for transfers between devices: none -> 17.9 us  [add_copies(): values = values + lax.ppermute(values, 'expert', route)]
    all_to_all x6 -> x3, starting transfers between devices: 29.9 us -> 22.7 us  [exchange(): return lax.all_to_all(pieces, 'expert', 0, 0, tiled=True)]
    ppermute x7 -> x6, waiting for transfers between devices: 11.4 us -> 5.04 us  [swap_cores(): return lax.ppermute(value, 'dp', [(0, 1), (1, 0)])]
    reshape x0 -> x5, local copies, waits for them, and re-layouts: none -> 6.25 us  [the longest x1 3.68 us: shards(): produced.reshape(1, MICRO, tokens, D)]
    reshape x2 -> x0, other arithmetic: 5.09 us -> none  [phase(): pieces = exchange(mine.astype(BF).reshape(peers, rows_each, D))]
    transpose x0 -> x1, local copies, waits for them, and re-layouts: none -> 3.48 us  [shards(): produced.reshape(MICRO, copies, tokens, columns).transpose(0, 2, 1, 3)]
  transfers between devices with their start and end apart: 14 -> 13, of which waited for: 11 -> 9; matrix products, arithmetic and copies ran while one was open for 24% -> 28% of each run, Pallas kernels for 0% -> 0%
where the time goes in v1:
time: 190 us; the launch traced here: 189 us
  waiting for transfers between devices  48.6 us (26%)
  matrix products  39.6 us (21%)
  other arithmetic  30.8 us (16%)
  starting transfers between devices  28.4 us (15%)
  blocking collectives  20.8 us (11%)
  local copies, waits for them, and re-layouts  19 us (10%)
    dot_general x23, matrix products, times(): lax.dot_general(a, b, (((ca,), (cb,)), ((), ())), preferred_element_type=...  37.6 us
    all_to_all x3, starting transfers between devices, exchange(): return lax.all_to_all(pieces, 'expert', 0, 0, tiled=True)  22.7 us
    all_to_all x1, blocking collectives, exchange(): return lax.all_to_all(pieces, 'expert', 0, 0, tiled=True)  20.8 us
    all_to_all x3, waiting for transfers between devices, exchange(): return lax.all_to_all(pieces, 'expert', 0, 0, tiled=True)  19.4 us
    ppermute x3, waiting for transfers between devices, add_copies(): values = values + lax.ppermute(values, 'expert', route)  17.9 us
    another operation x3, other arithmetic, shards(): lower_factor = jnp.linalg.cholesky(gram_matrix)  8.73 us
    another operation x2, other arithmetic, shards(): jax.scipy.linalg.solve_triangular(lower_factor, factor.T, lower=True)  8.35 us
    ppermute x1, waiting for transfers between devices, shards(): lax.ppermute(part, 'pipe', [(i, i - 1) for i in range(1, sections)])  6.18 us
  transfers between devices with their start and end apart: 13, of which 9 were waited for; matrix products, arithmetic and copies ran while one was open for 28% of the time, Pallas kernels for 0%

profile of v1, /device:TPU:0, one launch (start us, length us, event | category | flops | bytes accessed | tf_op | source)
XLA Modules:
  0.0 188.5 jit_solution(14504454296458241629)
XLA Ops:
  0.7 0.9 copy.39
  3.2 2.9 %convolution_convert_fusion = bf16[192,3072]{1,0:T(8,128)(2,1)} fusion(bf16[256,3072]{1,0:T(8,128)(2,1)} %bitcast.134, s32[256]{0:T(256)S(1)} %bitcast.143, s32[256]{0:T(256)S(1)} %bitcast.140), kind=kOutput, calls=%fused_computation.4 | convolution fusion | flops 302727168 | bytes 2754560 | tf_op jit(solution)/shard_map/dot_general | solution.py:27
  6.4 1.9 %fusion = bf16[192,3072]{1,0:T(8,128)(2,1)S(1)} fusion(bf16[256,3072]{1,0:T(8,128)(2,1)} %bitcast.133, f32[192]{0:T(256)S(1)} %add_reduce_fusion, s32[256]{0:T(256)S(1)} %bitcast.145, s32[256]{0:T(256)S(1)} %bitcast.142), kind=kOutput, calls=%fused_computation.3 | convolution fusion | flops 303316992 | bytes 2755328 | tf_op jit(solution)/shard_map/dot_general | solution.py:27
  9.3 3.0 %fusion.5 = f32[384,512]{1,0:T(8,128)S(1)} fusion(bf16[1,1,1,3072,512]{4,3,2,1,0:T(8,128)(2,1)S(1)} %copy-done, bf16[192,3072]{1,0:T(8,128)(2,1)} %collective-permute-done.1, bf16[192,3072]{1,0:T(8,128)(2,1)} %convolution_convert_fusion), kind=kOutput, calls=%fused_computation.10 | convolution fusion | flops 1212678144 | bytes 6291456 | tf_op jit(solution)/shard_map/dot_general | solution.py:27
  12.4 3.4 %fusion.9 = f32[384,512]{1,0:T(8,128)S(1)} fusion(bf16[1,1,1,3072,512]{4,3,2,1,0:T(8,128)(2,1)S(1)} %copy-done.2, bf16[192,3072]{1,0:T(8,128)(2,1)} %collective-permute-done.1, bf16[192,3072]{1,0:T(8,128)(2,1)} %convolution_convert_fusion), kind=kOutput, calls=%fused_computation.14 | convolution fusion | flops 1212678144 | bytes 6291456 | tf_op jit(solution)/shard_map/dot_general | solution.py:27
  15.8 1.4 fusion.13
  17.2 1.5 fusion.3
  18.7 1.5 convolution_add_fusion.1
  20.9 2.5 %collective-permute-done.2 = bf16[192,3072]{1,0:T(8,128)(2,1)S(1)} collective-permute-done((bf16[192,3072]{1,0:T(8,128)(2,1)S(1)}, bf16[192,3072]{1,0:T(8,128)(2,1)S(1)}, u32[]{:S(2)}, u32[]{:S(2)}) %collective-permute-start.2) | collective-permute-done | bytes 1179680 | tf_op jit(solution)/shard_map/ppermute | solution.py:19
  23.9 1.2 copy.48
  25.1 9.5 %all-to-all-start = ((bf16[32,48,384]{2,1,0:T(8,128)(2,1)}), bf16[32,48,384]{2,1,0:T(8,128)(2,1)}, u32[]{:S(2)}, u32[]{:S(2)}) async-start(bf16[32,48,384]{2,1,0:T(8,128)(2,1)} %bitcast.126), calls=%async_computation | async-start | bytes 2359296 | tf_op jit(solution)/shard_map/all_to_all | solution.py:23
  35.0 19.3 %all-to-all-done = bf16[32,48,384]{2,1,0:T(8,128)(2,1)} async-done(((bf16[32,48,384]{2,1,0:T(8,128)(2,1)}), bf16[32,48,384]{2,1,0:T(8,128)(2,1)}, u32[]{:S(2)}, u32[]{:S(2)}) %all-to-all-start) | async-done | bytes 1179680 | tf_op jit(solution)/shard_map/all_to_all | solution.py:23
  54.3 1.5 convert_reduce_fusion.1
  55.8 1.1 fusion.20
  56.9 1.3 collective-permute-start.3
  58.2 6.2 %collective-permute-done.3 = bf16[64,384]{1,0:T(8,128)(2,1)S(1)} collective-permute-done((bf16[64,384]{1,0:T(8,128)(2,1)S(1)}, bf16[64,384]{1,0:T(8,128)(2,1)S(1)}, u32[]{:S(2)}, u32[]{:S(2)}) %collective-permute-start.3) | collective-permute-done | bytes 49184 | tf_op jit(solution)/shard_map/ppermute | solution.py:131
  64.4 1.0 convolution_convert_fusion.1
  65.5 20.8 %all_to_all.20 = bf16[32,48,384]{2,1,0:T(8,128)(2,1)S(1)} all-to-all(bf16[32,48,384]{2,1,0:T(8,128)(2,1)S(1)} %bitcast.129), channel_id=1, replica_groups=mesh['dp'=2,'pipe'=2,'expert'=32] {'expert'}, dimensions={0} | all-to-all | bytes 2359296 | tf_op jit(solution)/shard_map/all_to_all | solution.py:23
  89.0 2.1 %collective-permute-done.4 = bf16[192,3072]{1,0:T(8,128)(2,1)S(1)} collective-permute-done((bf16[192,3072]{1,0:T(8,128)(2,1)S(1)}, bf16[192,3072]{1,0:T(8,128)(2,1)S(1)}, u32[]{:S(2)}, u32[]{:S(2)}) %collective-permute-start.4) | collective-permute-done | bytes 1179680 | tf_op jit(solution)/shard_map/ppermute | solution.py:19
  91.1 1.7 multiply_convert_fusion.1
  92.8 1.4 fusion.1
  95.3 1.6 convolution_add_fusion
  96.9 1.3 slice.120
  99.6 6.2 %collective-permute-done.7 = f32[384,128]{0,1:T(8,128)S(1)} collective-permute-done((f32[384,128]{0,1:T(8,128)S(1)}, f32[384,128]{0,1:T(8,128)S(1)}, u32[]{:S(2)}, u32[]{:S(2)}) %collective-permute-start.7) | collective-permute-done | bytes 196640 | tf_op jit(solution)/shard_map/ppermute | solution.py:60
  106.6 5.4 %collective-permute-done.8 = f32[384,128]{0,1:T(8,128)S(1)} collective-permute-done((f32[384,128]{0,1:T(8,128)S(1)}, f32[384,128]{0,1:T(8,128)S(1)}, u32[]{:S(2)}, u32[]{:S(2)}) %collective-permute-start.8) | collective-permute-done | bytes 196640 | tf_op jit(solution)/shard_map/ppermute | solution.py:60
  113.6 6.3 %collective-permute-done.9 = f32[384,128]{0,1:T(8,128)} collective-permute-done((f32[384,128]{0,1:T(8,128)}, f32[384,128]{0,1:T(8,128)}, u32[]{:S(2)}, u32[]{:S(2)}) %collective-permute-start.9) | collective-permute-done | bytes 196640 | tf_op jit(solution)/shard_map/ppermute | solution.py:60
  119.9 1.7 add_convert_fusion
  121.6 2.2 %fusion.15 = bf16[192,3072]{1,0:T(8,128)(2,1)S(1)} fusion(f32[384,3072]{1,0:T(8,128)} %copy-done.1, bf16[192,3072]{1,0:T(8,128)(2,1)} %collective-permute-done.5), kind=kLoop, calls=%fused_computation.22 | loop fusion | flops 1769472 | bytes 4718592 | tf_op jit(solution)/shard_map/convert_element_type | solution.py:115
  124.1 1.2 copy.50
  125.2 4.7 %all-to-all-start.2 = ((bf16[32,48,384]{2,1,0:T(8,128)(2,1)}), bf16[32,48,384]{2,1,0:T(8,128)(2,1)}, u32[]{:S(2)}, u32[]{:S(2)}) async-start(bf16[32,48,384]{2,1,0:T(8,128)(2,1)} %bitcast.127), calls=%async_computation.2 | async-start | bytes 2359296 | tf_op jit(solution)/shard_map/all_to_all | solution.py:23
  129.9 2.2 %fusion.22 = f32[3072,64]{0,1:T(8,128)S(1)} fusion(bf16[192,3072]{1,0:T(8,128)(2,1)} %copy-done.22, bf16[192,3072]{1,0:T(8,128)(2,1)} %copy-done.12, bf16[384,128]{0,1:T(8,128)(2,1)} %add_convert_fusion), kind=kOutput, calls=%fused_computation.52 | convolution fusion | flops 155713536 | bytes 3194880 | tf_op jit(solution)/shard_map/dot_general | solution.py:27
  132.2 2.2 %convolution_add_fusion.2 = f32[3072,64]{0,1:T(8,128)S(1)} fusion(f32[3072,64]{0,1:T(8,128)S(1)} %fusion.22, bf16[384,128]{0,1:T(8,128)(2,1)S(1)} %copy-done.17, bf16[192,3072]{1,0:T(8,128)(2,1)} %collective-permute-done.1, bf16[192,3072]{1,0:T(8,128)(2,1)} %convolution_convert_fusion), kind=kOutput, calls=%fused_computation.5 | convolution fusion | flops 155910144 | bytes 3981312 | tf_op jit(solution)/shard_map/dot_general | solution.py:27
  135.2 1.4 fusion.64
  136.6 1.4 copy.52
  138.1 1.4 fusion.53
  139.5 7.2 %cholesky.16 = f32[64,64]{1,0:T(8,128)} custom-call(f32[64,64]{1,0:T(8,128)} %fusion.53), custom_call_target="Cholesky" | custom-call | tf_op jit(solution)/shard_map/jit(cholesky)/cholesky | solution.py:149
  148.2 1.5 convert_reduce_fusion
  149.7 1.1 add_convert_fusion.1
  150.8 1.4 broadcast_in_dim.53
  152.2 8.6 %all-to-all-start.3 = ((bf16[32,64,384]{2,1,0:T(8,128)(2,1)}), bf16[32,64,384]{2,1,0:T(8,128)(2,1)}, u32[]{:S(2)}, u32[]{:S(2)}) async-start(bf16[32,64,384]{2,1,0:T(8,128)(2,1)} %broadcast_in_dim.53), calls=%async_computation.3 | async-start | bytes 3145728 | tf_op jit(solution)/shard_map/all_to_all | solution.py:23
  160.7 2.1 %fusion.50 = f32[1,64,64]{2,1,0:T(8,128)} fusion(f32[64,64]{1,0:T(8,128)} %cholesky.16, pred[]{:T(512)} %compare_reduce_fusion), kind=kLoop, calls=%fused_computation.92 | loop fusion | flops 16384 | bytes 32769 | tf_op jit(solution)/shard_map/jit(_solve_triangular)/triangular_solve | solution.py:150
  162.8 6.3 %custom-call.7 = f32[1,64,64]{1,2,0:T(8,128)} custom-call(f32[1,64,64]{2,1,0:T(8,128)} %fusion.50), custom_call_target="InvertDiagBlocksLowerTriangular" | custom-call | tf_op jit(solution)/shard_map/jit(_solve_triangular)/triangular_solve | solution.py:150
  169.1 2.0 %fusion.51 = f32[3072,64]{0,1:T(8,128)S(1)} fusion(f32[3072,64]{0,1:T(8,128)} %copy-done.4, f32[1,64,64]{1,2,0:T(8,128)} %custom-call.7), kind=kOutput, calls=%fused_computation.93 | convolution fusion | flops 150994944 | bytes 1589248 | tf_op jit(solution)/shard_map/jit(_solve_triangular)/triangular_solve | solution.py:150
  171.1 2.8 %convolution_convert_fusion.3 = bf16[384,64]{0,1:T(8,128)(2,1)S(1)} fusion(f32[3072,64]{0,1:T(8,128)S(1)} %fusion.51, bf16[192,3072]{1,0:T(8,128)(2,1)} %collective-permute-done.1, bf16[192,3072]{1,0:T(8,128)(2,1)} %convolution_convert_fusion), kind=kOutput, calls=%fused_computation.42 | convolution fusion | flops 155934720 | bytes 3194880 | tf_op jit(solution)/shard_map/dot_general | solution.py:27
  175.6 3.1 %convolution_bitcast_fusion = f32[1,1,1,1,512,64]{4,5,3,2,1,0:T(8,128)S(1)} fusion(bf16[384,512]{1,0:T(8,128)(2,1)} %copy-done.16, bf16[192,3072]{1,0:T(8,128)(2,1)} %copy-done.22, bf16[192,3072]{1,0:T(8,128)(2,1)} %copy-done.12, f32[3072,64]{0,1:T(8,128)} %copy-done.9), kind=kOutput, calls=%fused_computation.36 | convolution fusion | flops 181100544 | bytes 3670016 | tf_op jit(solution)/shard_map/dot_general | solution.py:27
  179.4 1.8 multiply_bitcast_fusion
  181.4 3.5 %copy.51 = bf16[4,64,8,384]{3,2,1,0:T(8,128)(2,1)} copy(bf16[4,64,8,384]{3,1,2,0:T(8,128)(2,1)} %bitcast.29) | data formatting | bytes 3145728 | tf_op jit(solution)/shard_map/transpose | solution.py:139
  184.8 3.7 %reshape.170 = bf16[1,4,64,3072]{3,2,1,0:T(8,128)(2,1)} reshape(bf16[4,64,8,384]{3,2,1,0:T(8,128)(2,1)} %copy.51) | data formatting | bytes 3145728 | tf_op jit(solution)/shard_map/reshape | solution.py:165
  (106 shorter events, 17.2 us)
Async XLA Ops:
  0.6 8.7 %copy-start = (bf16[1,1,1,3072,512]{4,3,2,1,0:T(8,128)(2,1)S(1)}, bf16[1,1,1,3072,512]{4,3,2,1,0:T(8,128)(2,1)}, u32[]{:S(2)}) copy-start(bf16[1,1,1,3072,512]{4,3,2,1,0:T(8,128)(2,1)} %param.12) | copy-start | bytes 9437188
  0.6 5.5 %copy-start.19 = (f32[1,4,64,2]{2,3,1,0:T(2,128)S(1)}, f32[1,4,64,2]{2,3,1,0:T(2,128)}, u32[]{:S(2)}) copy-start(f32[1,4,64,2]{2,3,1,0:T(2,128)} %param.11) | copy-start | bytes 6148
  6.1 3.2 %collective-permute-start.1 = (bf16[192,3072]{1,0:T(8,128)(2,1)}, bf16[192,3072]{1,0:T(8,128)(2,1)}, u32[]{:S(2)}, u32[]{:S(2)}) collective-permute-start(bf16[192,3072]{1,0:T(8,128)(2,1)} %convolution_convert_fusion), channel_id=1, source_target_pairs={{0,64},{64,0},{1,65},{65,1},{2,66},{66,2},{3,67},{67,3},{4,68},{68... | collective-permute-start | bytes 3538952 | tf_op jit(solution)/shard_map/ppermute | solution.py:19
  8.3 4.1 %copy-start.2 = (bf16[1,1,1,3072,512]{4,3,2,1,0:T(8,128)(2,1)S(1)}, bf16[1,1,1,3072,512]{4,3,2,1,0:T(8,128)(2,1)}, u32[]{:S(2)}) copy-start(bf16[1,1,1,3072,512]{4,3,2,1,0:T(8,128)(2,1)} %param.13) | copy-start | bytes 9437188
  8.3 7.5 %collective-permute-start = (bf16[192,3072]{1,0:T(8,128)(2,1)S(1)}, bf16[192,3072]{1,0:T(8,128)(2,1)S(1)}, u32[]{:S(2)}, u32[]{:S(2)}) collective-permute-start(bf16[192,3072]{1,0:T(8,128)(2,1)S(1)} %fusion), channel_id=1, source_target_pairs={{0,64},{64,0},{1,65},{65,1},{2,66},{66,2},{3,67},{67,3},{4,68},{68... | collective-permute-start | bytes 3538952 | tf_op jit(solution)/shard_map/ppermute | solution.py:19
  12.3 6.4 %copy-start.7 = (f32[384,512]{1,0:T(8,128)}, f32[384,512]{1,0:T(8,128)S(1)}, u32[]{:S(2)}) copy-start(f32[384,512]{1,0:T(8,128)S(1)} %fusion.5) | copy-start | bytes 2359300
  12.3 3.4 %copy-start.20 = (bf16[1,1,1,512,3072]{4,3,2,1,0:T(8,128)(2,1)S(1)}, bf16[1,1,1,512,3072]{4,3,2,1,0:T(8,128)(2,1)}, u32[]{:S(2)}) copy-start(bf16[1,1,1,512,3072]{4,3,2,1,0:T(8,128)(2,1)} %param.14) | copy-start | bytes 9437188
  15.7 1.5 copy-start.10
  20.4 2.9 %collective-permute-start.2 = (bf16[192,3072]{1,0:T(8,128)(2,1)S(1)}, bf16[192,3072]{1,0:T(8,128)(2,1)S(1)}, u32[]{:S(2)}, u32[]{:S(2)}) collective-permute-start(bf16[192,3072]{1,0:T(8,128)(2,1)S(1)} %slice.121), channel_id=1, source_target_pairs={{0,64},{64,0},{1,65},{65,1},{2,66},{66,2},{3,67},{67,3},{4,68},{68... | collective-permute-start | bytes 3538952 | tf_op jit(solution)/shard_map/ppermute | solution.py:19
  25.1 29.3 %all-to-all-start = ((bf16[32,48,384]{2,1,0:T(8,128)(2,1)}), bf16[32,48,384]{2,1,0:T(8,128)(2,1)}, u32[]{:S(2)}, u32[]{:S(2)}) async-start(bf16[32,48,384]{2,1,0:T(8,128)(2,1)} %bitcast.126), calls=%async_computation | async-start | bytes 2359296 | tf_op jit(solution)/shard_map/all_to_all | solution.py:23
  56.9 7.5 %collective-permute-start.3 = (bf16[64,384]{1,0:T(8,128)(2,1)S(1)}, bf16[64,384]{1,0:T(8,128)(2,1)S(1)}, u32[]{:S(2)}, u32[]{:S(2)}) collective-permute-start(bf16[64,384]{1,0:T(8,128)(2,1)S(1)} %fusion.20), channel_id=1, source_target_pairs={{32,0},{33,1},{34,2},{35,3},{36,4},{37,5},{38,6},{39,7},{40,8},{41... | collective-permute-start | bytes 147464 | tf_op jit(solution)/shard_map/ppermute | solution.py:131
  64.4 22.1 %copy-start.18 = (bf16[64,384]{1,0:T(8,128)(2,1)}, bf16[64,384]{1,0:T(8,128)(2,1)S(1)}, u32[]{:S(2)}) copy-start(bf16[64,384]{1,0:T(8,128)(2,1)S(1)} %collective-permute-done.3) | copy-start | bytes 147460
  87.2 3.8 %copy-start.21 = (bf16[1,1,1,512,3072]{4,3,2,1,0:T(8,128)(2,1)S(1)}, bf16[1,1,1,512,3072]{4,3,2,1,0:T(8,128)(2,1)}, u32[]{:S(2)}) copy-start(bf16[1,1,1,512,3072]{4,3,2,1,0:T(8,128)(2,1)} %param.14) | copy-start | bytes 9437188
  87.7 1.3 copy-start.15
  87.7 3.4 %copy-start.8 = (f32[384,512]{1,0:T(8,128)S(1)}, f32[384,512]{1,0:T(8,128)}, u32[]{:S(2)}) copy-start(f32[384,512]{1,0:T(8,128)} %copy-done.7) | copy-start | bytes 2359300
  87.7 3.4 %copy-start.11 = (f32[384,512]{1,0:T(8,128)S(1)}, f32[384,512]{1,0:T(8,128)}, u32[]{:S(2)}) copy-start(f32[384,512]{1,0:T(8,128)} %copy-done.10) | copy-start | bytes 2359300
  88.0 4.8 %copy-start.12 = (bf16[192,3072]{1,0:T(8,128)(2,1)}, bf16[192,3072]{1,0:T(8,128)(2,1)S(1)}, u32[]{:S(2)}) copy-start(bf16[192,3072]{1,0:T(8,128)(2,1)S(1)} %multiply_convert_fusion) | copy-start | bytes 3538948
  88.0 3.1 %collective-permute-start.4 = (bf16[192,3072]{1,0:T(8,128)(2,1)S(1)}, bf16[192,3072]{1,0:T(8,128)(2,1)S(1)}, u32[]{:S(2)}, u32[]{:S(2)}) collective-permute-start(bf16[192,3072]{1,0:T(8,128)(2,1)S(1)} %multiply_convert_fusion), channel_id=1, source_target_pairs={{0,64},{64,0},{1,65},{65,1},{2,66},{66,2},{3,67},{67,3},{4,68},{68... | collective-permute-start | bytes 3538952 | tf_op jit(solution)/shard_map/ppermute | solution.py:19
  91.1 1.7 copy-start.22
  92.8 1.5 copy-start.5
  92.8 1.7 copy-start.16
  92.8 2.5 %copy-start.3 = (bf16[1,1,1,3072,512]{4,3,2,1,0:T(8,128)(2,1)S(1)}, bf16[1,1,1,3072,512]{4,3,2,1,0:T(8,128)(2,1)}, u32[]{:S(2)}) copy-start(bf16[1,1,1,3072,512]{4,3,2,1,0:T(8,128)(2,1)} %param.13) | copy-start | bytes 9437188
  95.1 3.5 %collective-permute-start.6 = (f32[384,128]{0,1:T(8,128)S(1)}, f32[384,128]{0,1:T(8,128)S(1)}, u32[]{:S(2)}, u32[]{:S(2)}) collective-permute-start(f32[384,128]{0,1:T(8,128)S(1)} %pad_maximum_fusion.6), channel_id=1, source_target_pairs={{0,64},{64,0},{1,65},{65,1},{2,66},{66,2},{3,67},{67,3},{4,68},{68... | collective-permute-start | bytes 589832 | tf_op jit(solution)/shard_map/ppermute | solution.py:19
  96.9 15.8 %copy-start.1 = (f32[384,3072]{1,0:T(8,128)}, f32[384,3072]{1,0:T(8,128)S(1)}, u32[]{:S(2)}) copy-start(f32[384,3072]{1,0:T(8,128)S(1)} %convolution_add_fusion) | copy-start | bytes 14155780
  98.2 23.4 %collective-permute-start.5 = (bf16[192,3072]{1,0:T(8,128)(2,1)}, bf16[192,3072]{1,0:T(8,128)(2,1)}, u32[]{:S(2)}, u32[]{:S(2)}) collective-permute-start(bf16[192,3072]{1,0:T(8,128)(2,1)} %slice.120), channel_id=1, source_target_pairs={{0,64},{64,0},{1,65},{65,1},{2,66},{66,2},{3,67},{67,3},{4,68},{68... | collective-permute-start | bytes 3538952 | tf_op jit(solution)/shard_map/ppermute | solution.py:19
  98.8 7.0 %collective-permute-start.7 = (f32[384,128]{0,1:T(8,128)S(1)}, f32[384,128]{0,1:T(8,128)S(1)}, u32[]{:S(2)}, u32[]{:S(2)}) collective-permute-start(f32[384,128]{0,1:T(8,128)S(1)} %maximum_add_fusion), channel_id=1, source_target_pairs={{0,1},{1,0},{2,3},{3,2},{4,5},{5,4},{6,7},{7,6},{8,9},{9,8},{10,11... | collective-permute-start | bytes 589832 | tf_op jit(solution)/shard_map/ppermute | solution.py:60
  105.8 6.2 %collective-permute-start.8 = (f32[384,128]{0,1:T(8,128)S(1)}, f32[384,128]{0,1:T(8,128)S(1)}, u32[]{:S(2)}, u32[]{:S(2)}) collective-permute-start(f32[384,128]{0,1:T(8,128)S(1)} %add.108), channel_id=1, source_target_pairs={{0,2},{1,3},{2,0},{3,1},{4,6},{5,7},{6,4},{7,5},{8,10},{9,11},{10,... | collective-permute-start | bytes 589832 | tf_op jit(solution)/shard_map/ppermute | solution.py:60
  112.7 7.2 %collective-permute-start.9 = (f32[384,128]{0,1:T(8,128)}, f32[384,128]{0,1:T(8,128)}, u32[]{:S(2)}, u32[]{:S(2)}) collective-permute-start(f32[384,128]{0,1:T(8,128)} %add.109), channel_id=1, source_target_pairs={{0,6},{1,7},{2,4},{3,5},{4,2},{5,3},{6,0},{7,1},{8,14},{9,15},{10,... | collective-permute-start | bytes 589832 | tf_op jit(solution)/shard_map/ppermute | solution.py:60
  125.2 23.0 %all-to-all-start.2 = ((bf16[32,48,384]{2,1,0:T(8,128)(2,1)}), bf16[32,48,384]{2,1,0:T(8,128)(2,1)}, u32[]{:S(2)}, u32[]{:S(2)}) async-start(bf16[32,48,384]{2,1,0:T(8,128)(2,1)} %bitcast.127), calls=%async_computation.2 | async-start | bytes 2359296 | tf_op jit(solution)/shard_map/all_to_all | solution.py:23
  129.9 2.2 %copy-start.17 = (bf16[384,128]{0,1:T(8,128)(2,1)S(1)}, bf16[384,128]{0,1:T(8,128)(2,1)}, u32[]{:S(2)}) copy-start(bf16[384,128]{0,1:T(8,128)(2,1)} %add_convert_fusion) | copy-start | bytes 294916
  134.4 0.9 copy-start.4
  152.2 29.2 %all-to-all-start.3 = ((bf16[32,64,384]{2,1,0:T(8,128)(2,1)}), bf16[32,64,384]{2,1,0:T(8,128)(2,1)}, u32[]{:S(2)}, u32[]{:S(2)}) async-start(bf16[32,64,384]{2,1,0:T(8,128)(2,1)} %broadcast_in_dim.53), calls=%async_computation.3 | async-start | bytes 3145728 | tf_op jit(solution)/shard_map/all_to_all | solution.py:23
  171.1 3.6 %copy-start.9 = (f32[3072,64]{0,1:T(8,128)}, f32[3072,64]{0,1:T(8,128)S(1)}, u32[]{:S(2)}) copy-start(f32[3072,64]{0,1:T(8,128)S(1)} %fusion.51) | copy-start | bytes 2359300
  171.1 2.8 %copy-start.6 = (bf16[384,512]{1,0:T(8,128)(2,1)S(1)}, bf16[384,512]{1,0:T(8,128)(2,1)}, u32[]{:S(2)}) copy-start(bf16[384,512]{1,0:T(8,128)(2,1)} %copy-done.5) | copy-start | bytes 1179652
  175.6 3.1 %copy-start.13 = (f32[1,1,1,1,512,64]{4,5,3,2,1,0:T(8,128)S(1)}, f32[1,1,1,1,512,64]{4,5,3,2,1,0:T(8,128)}, u32[]{:S(2)}) copy-start(f32[1,1,1,1,512,64]{4,5,3,2,1,0:T(8,128)} %convolution_bitcast_fusion.2) | copy-start | bytes 393220
  175.6 3.1 %copy-start.14 = (f32[1,1,1,1,512,64]{4,5,3,2,1,0:T(8,128)S(1)}, f32[1,1,1,1,512,64]{4,5,3,2,1,0:T(8,128)}, u32[]{:S(2)}) copy-start(f32[1,1,1,1,512,64]{4,5,3,2,1,0:T(8,128)} %convolution_bitcast_fusion.1) | copy-start | bytes 393220

commit v2 on v1

--- a/solution.py
+++ b/solution.py
@@ -3,6 +3,8 @@
 import jax
 import jax.numpy as jnp
 from jax import lax
+from jax.experimental import pallas as pl
+from jax.experimental.pallas import tpu as pltpu
 from jax.sharding import PartitionSpec as P
 
 D = 3072
@@ -59,6 +61,58 @@
         route = [(i, partner(i)) for i in range(copies * EXPERTS)]
         values = values + lax.ppermute(values, "expert", route)
     return values
+
+
+def eliminate(gram_ref, inverse_ref):
+    height = 8
+    lanes = lax.broadcasted_iota(jnp.int32, (height, 2 * R), 1)
+    depth = lax.broadcasted_iota(jnp.int32, (height, 2 * R), 0)
+    blocks = []
+    for b in range(R // height):
+        held = jnp.concatenate([jnp.zeros((height, R), F32), gram_ref[pl.ds(b * height, height), :]], 1)
+        blocks.append(jnp.where(lanes == depth + b * height, 1.0, held))
+    for k in range(R):
+        at, row = divmod(k, height)
+        pivot_row = blocks[at][row : row + 1, :]
+        pivot_row = pivot_row * (1.0 / pivot_row[:, R + k : R + k + 1])
+        for b in range((k + 1) // height, R // height):
+            below = blocks[b] - blocks[b][:, R + k : R + k + 1] * pivot_row
+            blocks[b] = jnp.where(depth + b * height > k, below, blocks[b]) if b == at else below
+    for b in range(R // height):
+        diagonal = jnp.where(lanes == depth + R + b * height, blocks[b], 0.0)
+        pivots = jnp.sum(diagonal, axis=1, keepdims=True)
+        inverse_ref[pl.ds(b * height, height), :] = (blocks[b] * lax.rsqrt(pivots))[:, :R]
+
+
+def inverse_lower(gram_matrix):
+    return pl.pallas_call(
+        eliminate, out_shape=jax.ShapeDtypeStruct((R, R), F32), name="inverse_lower"
+    )(gram_matrix)
+
+
+def side_by_side(pieces):
+    micro, copies, tokens, columns = pieces.shape
+
+    def kernel(pieces_ref, out_ref, done):
+        moves = [
+            pltpu.make_async_copy(
+                pieces_ref.at[:, c], out_ref.at[:, :, pl.ds(c * columns, columns)], done.at[c]
+            )
+            for c in range(copies)
+        ]
+        for move in moves:
+            move.start()
+        for move in moves:
+            move.wait()
+
+    return pl.pallas_call(
+        kernel,
+        out_shape=jax.ShapeDtypeStruct((micro, tokens, copies * columns), pieces.dtype),
+        in_specs=[pl.BlockSpec(memory_space=pl.ANY)],
+        out_specs=pl.BlockSpec(memory_space=pl.ANY),
+        scratch_shapes=[pltpu.SemaphoreType.DMA((copies,))],
+        name="side_by_side",
+    )(pieces)
 
 
 def shards(saved_inputs, top_grad, routes, mix_weights, w_gate, w_up, w_down, q_prev):
@@ -111,7 +165,8 @@
         grad_gate = (grad_hidden * slope).astype(BF)
         grad_up = (grad_hidden * silu_gate).astype(BF)
         partial = times(grad_gate, gate, 1, 1) + times(grad_up, up, 1, 1)
-        mine = partial[:slots] + swap_cores(partial[slots:].astype(BF)).astype(F32)
+        other = swap_cores(partial[slots:].astype(BF))
+        mine = partial[:slots] + other.astype(F32)
         mine = mine.astype(BF).reshape(MICRO, CAP, copies, columns).transpose(0, 2, 1, 3)
         pieces = exchange(mine.reshape(peers, CAP, columns))
         summed = jnp.sum(pieces.astype(F32).reshape(EXPERTS, copies, CAP, columns), axis=1)
@@ -122,7 +177,8 @@
             0,
             lax.Precision.HIGHEST,
         )
-        return (base.astype(F32) + share).astype(BF), grad_rows, grad_gate, grad_up
+        part = (base.astype(F32) + share).astype(BF)
+        return part, grad_rows, grad_gate, grad_up
 
     top_part = lax.dynamic_slice(
         top_grad, (major, 0, minor * columns), (1, tokens, columns)
@@ -136,7 +192,7 @@
     own_rows = own_rows.reshape(MICRO, copies, CAP, columns).transpose(0, 2, 1, 3)
     part, grad_rows, grad_gate, grad_up = phase(own_rows.reshape(slots, D).astype(F32), base)
     produced = exchange(jnp.broadcast_to(part, (peers, tokens, columns)))
-    produced = produced.reshape(MICRO, copies, tokens, columns).transpose(0, 2, 1, 3)
+    produced = side_by_side(produced.reshape(MICRO, copies, tokens, columns))
 
     sums = jnp.concatenate(
         [times(grad_gate, right[0]) + times(grad_up, right[1]), times(hidden, right[2])], axis=1
@@ -146,8 +202,8 @@
     sums = add_copies(sums, copies).astype(BF)
     factor = times(inputs, sums[:, :R], 0, 0) + times(grad_rows, sums[:, R:], 0, 0)
     gram_matrix = times(factor, factor, 0, 0, lax.Precision.HIGHEST)
-    lower_factor = jnp.linalg.cholesky(gram_matrix)
-    ortho = jax.scipy.linalg.solve_triangular(lower_factor, factor.T, lower=True).T
+    inverse = inverse_lower(gram_matrix)
+    ortho = times(factor, inverse, 1, 1, lax.Precision.HIGHEST)
     ortho16 = ortho.astype(BF)
     along_inputs = times(inputs, ortho16).astype(BF)
     along_grads = times(grad_rows, ortho16).astype(BF)

time: 190 us -> 226 us (1.19)
  Pallas kernels: 0 us -> 55.6 us
  other arithmetic: 30.8 us -> 11.4 us
  local copies, waits for them, and re-layouts: 19 us -> 9.08 us
  waiting for transfers between devices: 48.6 us -> 54.9 us
    pallas_call x0 -> x2, Pallas kernels: none -> 55.6 us  [the longest x1 48.8 us: side_by_side(): pl.pallas_call(kernel, out_shape=jax.ShapeDtypeStruct((micro, tokens, cop...]
    another operation x5 -> x0, other arithmetic: 17.1 us -> none  [the longest x3 8.73 us: shards(): lower_factor = jnp.linalg.cholesky(gram_matrix)]
    dot_general x23 -> x24, matrix products: 37.6 us -> 41.8 us  [times(): lax.dot_general(a, b, (((ca,), (cb,)), ((), ())), preferred_element_type=...]
    ppermute x3, waiting for transfers between devices: 17.9 us -> 21.7 us  [add_copies(): values = values + lax.ppermute(values, 'expert', route)]
    reshape x1 -> x0, local copies, waits for them, and re-layouts: 3.68 us -> none  [shards(): produced.reshape(1, MICRO, tokens, D)]
    transpose x1 -> x0, local copies, waits for them, and re-layouts: 3.48 us -> none  [shards(): produced.reshape(MICRO, copies, tokens, columns).transpose(0, 2, 1, 3)]
  transfers between devices with their start and end apart: 13 -> 13, of which waited for: 9 -> 10; matrix products, arithmetic and copies ran while one was open for 28% -> 16% of each run, Pallas kernels for 0% -> 3%
where the time goes in v2:
time: 226 us; the launch traced here: 225 us
  Pallas kernels  55.6 us (25%)
  waiting for transfers between devices  54.9 us (24%)
  matrix products  41.8 us (18%)
  starting transfers between devices  30.2 us (13%)
  blocking collectives  20.8 us (9%)
  other arithmetic  11.4 us (5%)
  local copies, waits for them, and re-layouts  9.08 us (4%)
    pallas_call x1, Pallas kernels, side_by_side(): pl.pallas_call(kernel, out_shape=jax.ShapeDtypeStruct((micro, tokens, cop...  48.8 us
    dot_general x24, matrix products, times(): lax.dot_general(a, b, (((ca,), (cb,)), ((), ())), preferred_element_type=...  41.8 us
    all_to_all x3, starting transfers between devices, exchange(): return lax.all_to_all(pieces, 'expert', 0, 0, tiled=True)  22.5 us
    ppermute x3, waiting for transfers between devices, add_copies(): values = values + lax.ppermute(values, 'expert', route)  21.7 us
    all_to_all x1, blocking collectives, exchange(): return lax.all_to_all(pieces, 'expert', 0, 0, tiled=True)  20.8 us
    all_to_all x3, waiting for transfers between devices, exchange(): return lax.all_to_all(pieces, 'expert', 0, 0, tiled=True)  20.2 us
    pallas_call x1, Pallas kernels, inverse_lower(): pl.pallas_call(eliminate, out_shape=jax.ShapeDtypeStruct((R, R), F32), na...  6.81 us
    ppermute x6, waiting for transfers between devices, swap_cores(): return lax.ppermute(value, 'dp', [(0, 1), (1, 0)])  6.72 us
  transfers between devices with their start and end apart: 13, of which 10 were waited for; matrix products, arithmetic and copies ran while one was open for 16% of the time, Pallas kernels for 3%

profile of v2, /device:TPU:0, one launch (start us, length us, event | category | flops | bytes accessed | tf_op | source)
XLA Modules:
  0.0 225.3 jit_solution(4195382998940917431)
XLA Ops:
  0.7 0.9 copy.23
  3.2 2.9 %convolution_convert_fusion = bf16[192,3072]{1,0:T(8,128)(2,1)} fusion(bf16[256,3072]{1,0:T(8,128)(2,1)} %bitcast.123, s32[256]{0:T(256)S(1)} %bitcast.133, s32[256]{0:T(256)S(1)} %bitcast.130), kind=kOutput, calls=%fused_computation.4 | convolution fusion | flops 302727168 | bytes 2754560 | tf_op jit(solution)/shard_map/dot_general | solution.py:29
  6.3 1.9 fusion
  9.3 3.0 %fusion.5 = f32[384,512]{1,0:T(8,128)S(1)} fusion(bf16[1,1,1,3072,512]{4,3,2,1,0:T(8,128)(2,1)S(1)} %copy-done, bf16[192,3072]{1,0:T(8,128)(2,1)} %collective-permute-done.1, bf16[192,3072]{1,0:T(8,128)(2,1)} %convolution_convert_fusion), kind=kOutput, calls=%fused_computation.10 | convolution fusion | flops 1212678144 | bytes 6291456 | tf_op jit(solution)/shard_map/dot_general | solution.py:29
  12.3 3.4 %fusion.9 = f32[384,512]{1,0:T(8,128)S(1)} fusion(bf16[1,1,1,3072,512]{4,3,2,1,0:T(8,128)(2,1)S(1)} %copy-done.1, bf16[192,3072]{1,0:T(8,128)(2,1)} %collective-permute-done.1, bf16[192,3072]{1,0:T(8,128)(2,1)} %convolution_convert_fusion), kind=kOutput, calls=%fused_computation.14 | convolution fusion | flops 1212678144 | bytes 6291456 | tf_op jit(solution)/shard_map/dot_general | solution.py:29
  15.7 1.4 fusion.13
  17.2 1.5 fusion.3
  18.7 1.5 convolution_add_fusion.1
  20.8 2.5 %collective-permute-done.2 = bf16[192,3072]{1,0:T(8,128)(2,1)S(1)} collective-permute-done((bf16[192,3072]{1,0:T(8,128)(2,1)S(1)}, bf16[192,3072]{1,0:T(8,128)(2,1)S(1)}, u32[]{:S(2)}, u32[]{:S(2)}) %collective-permute-start.2) | collective-permute-done | bytes 1179680 | tf_op jit(solution)/shard_map/ppermute | solution.py:21
  23.9 1.2 copy.32
  25.0 9.5 %all-to-all-start = ((bf16[32,48,384]{2,1,0:T(8,128)(2,1)}), bf16[32,48,384]{2,1,0:T(8,128)(2,1)}, u32[]{:S(2)}, u32[]{:S(2)}) async-start(bf16[32,48,384]{2,1,0:T(8,128)(2,1)} %bitcast.116), calls=%async_computation | async-start | bytes 2359296 | tf_op jit(solution)/shard_map/all_to_all | solution.py:25
  35.0 19.3 %all-to-all-done = bf16[32,48,384]{2,1,0:T(8,128)(2,1)} async-done(((bf16[32,48,384]{2,1,0:T(8,128)(2,1)}), bf16[32,48,384]{2,1,0:T(8,128)(2,1)}, u32[]{:S(2)}, u32[]{:S(2)}) %all-to-all-start) | async-done | bytes 1179680 | tf_op jit(solution)/shard_map/all_to_all | solution.py:25
  54.3 1.5 convert_reduce_fusion.1
  55.8 1.1 fusion.20
  56.9 1.3 collective-permute-start.3
  58.2 6.2 %collective-permute-done.3 = bf16[64,384]{1,0:T(8,128)(2,1)S(1)} collective-permute-done((bf16[64,384]{1,0:T(8,128)(2,1)S(1)}, bf16[64,384]{1,0:T(8,128)(2,1)S(1)}, u32[]{:S(2)}, u32[]{:S(2)}) %collective-permute-start.3) | collective-permute-done | bytes 49184 | tf_op jit(solution)/shard_map/ppermute | solution.py:187
  64.4 1.0 convolution_convert_fusion.1
  65.5 20.8 %all_to_all.20 = bf16[32,48,384]{2,1,0:T(8,128)(2,1)S(1)} all-to-all(bf16[32,48,384]{2,1,0:T(8,128)(2,1)S(1)} %bitcast.118), channel_id=1, replica_groups=mesh['dp'=2,'pipe'=2,'expert'=32] {'expert'}, dimensions={0} | all-to-all | bytes 2359296 | tf_op jit(solution)/shard_map/all_to_all | solution.py:25
  89.0 2.1 collective-permute-done.4
  91.1 1.7 multiply_convert_fusion.1
  92.8 1.5 fusion.1
  95.0 1.6 convolution_add_fusion
  98.2 1.7 collective-permute-done.6
  100.0 0.8 maximum_add_fusion
  102.1 1.2 copy.34
  103.2 4.7 %all-to-all-start.2 = ((bf16[32,48,384]{2,1,0:T(8,128)(2,1)}), bf16[32,48,384]{2,1,0:T(8,128)(2,1)}, u32[]{:S(2)}, u32[]{:S(2)}) async-start(bf16[32,48,384]{2,1,0:T(8,128)(2,1)} %bitcast.115), calls=%async_computation.2 | async-start | bytes 2359296 | tf_op jit(solution)/shard_map/all_to_all | solution.py:25
  108.1 1.0 add.96
  109.1 1.6 collective-permute-start.8
  110.7 16.2 %collective-permute-done.8 = f32[384,128]{0,1:T(8,128)S(1)} collective-permute-done((f32[384,128]{0,1:T(8,128)S(1)}, f32[384,128]{0,1:T(8,128)S(1)}, u32[]{:S(2)}, u32[]{:S(2)}) %collective-permute-start.8) | collective-permute-done | bytes 196640 | tf_op jit(solution)/shard_map/ppermute | solution.py:62
  127.6 2.1 collective-permute-start.9
  129.7 5.4 %collective-permute-done.9 = f32[384,128]{0,1:T(8,128)} collective-permute-done((f32[384,128]{0,1:T(8,128)}, f32[384,128]{0,1:T(8,128)}, u32[]{:S(2)}, u32[]{:S(2)}) %collective-permute-start.9) | collective-permute-done | bytes 196640 | tf_op jit(solution)/shard_map/ppermute | solution.py:62
  135.1 1.0 add_convert_fusion
  136.2 2.2 fusion.22
  138.3 3.1 %convolution_add_fusion.2 = f32[3072,64]{0,1:T(8,128)} fusion(f32[3072,64]{0,1:T(8,128)S(1)} %fusion.22, bf16[384,128]{0,1:T(8,128)(2,1)S(1)} %add_convert_fusion, bf16[192,3072]{1,0:T(8,128)(2,1)} %collective-permute-done.1, bf16[192,3072]{1,0:T(8,128)(2,1)} %convolution_convert_fusion), kind=kOutput, calls=%fused_computation.5 | convolution fusion | flops 155910144 | bytes 3981312 | tf_op jit(solution)/shard_map/dot_general | solution.py:29
  141.4 1.5 convert_reduce_fusion
  142.9 1.1 add_convert_fusion.1
  144.0 1.4 broadcast_in_dim.51
  145.4 8.3 %all-to-all-start.3 = ((bf16[32,64,384]{2,1,0:T(8,128)(2,1)}), bf16[32,64,384]{2,1,0:T(8,128)(2,1)}, u32[]{:S(2)}, u32[]{:S(2)}) async-start(bf16[32,64,384]{2,1,0:T(8,128)(2,1)} %broadcast_in_dim.51), calls=%async_computation.3 | async-start | bytes 3145728 | tf_op jit(solution)/shard_map/all_to_all | solution.py:25
  153.7 2.7 %fusion.60.gram_ref = f32[64,64]{1,0:T(8,128)} fusion(f32[3072,64]{0,1:T(8,128)} %convolution_add_fusion.2), kind=kOutput, calls=%fused_computation.104 | convolution fusion | flops 150994944 | bytes 802816 | tf_op jit(solution)/shard_map/dot_general | solution.py:29
  156.5 6.8 %inverse_lower.1 = f32[64,64]{1,0:T(8,128)} custom-call(f32[64,64]{1,0:T(8,128)} %fusion.60.gram_ref), custom_call_target="tpu_custom_call" | custom-call | tf_op jit(solution)/shard_map/inverse_lower/pallas_call | solution.py:88
  163.3 2.0 fusion.61
  165.3 2.8 %convolution_convert_fusion.3 = bf16[384,64]{0,1:T(8,128)(2,1)S(1)} fusion(f32[3072,64]{0,1:T(8,128)S(1)} %fusion.61, bf16[192,3072]{1,0:T(8,128)(2,1)} %collective-permute-done.1, bf16[192,3072]{1,0:T(8,128)(2,1)} %convolution_convert_fusion), kind=kOutput, calls=%fused_computation.42 | convolution fusion | flops 155934720 | bytes 3194880 | tf_op jit(solution)/shard_map/dot_general | solution.py:29
  168.0 0.8 convolution_bitcast_fusion.2
  168.9 0.8 convolution_bitcast_fusion.1
  169.7 3.1 %convolution_bitcast_fusion = f32[1,1,1,1,512,64]{4,5,3,2,1,0:T(8,128)S(1)} fusion(bf16[384,512]{1,0:T(8,128)(2,1)} %copy-done.14, bf16[192,3072]{1,0:T(8,128)(2,1)} %copy-done.19, bf16[192,3072]{1,0:T(8,128)(2,1)} %copy-done.10, f32[3072,64]{0,1:T(8,128)} %copy-done.7), kind=kOutput, calls=%fused_computation.36 | convolution fusion | flops 181100544 | bytes 3670016 | tf_op jit(solution)/shard_map/dot_general | solution.py:29
  173.6 1.8 multiply_bitcast_fusion
  175.4 0.9 all-to-all-done.3
  176.3 48.8 %side_by_side.1 = bf16[4,64,3072]{2,1,0:T(8,128)(2,1)} custom-call(bf16[4,8,64,384]{3,2,1,0:T(8,128)(2,1)} %bitcast.28.pieces_ref), custom_call_target="tpu_custom_call" | custom-call | tf_op jit(solution)/shard_map/side_by_side/pallas_call | solution.py:108
  (93 shorter events, 12.5 us)
Async XLA Ops:
  0.6 8.7 %copy-start = (bf16[1,1,1,3072,512]{4,3,2,1,0:T(8,128)(2,1)S(1)}, bf16[1,1,1,3072,512]{4,3,2,1,0:T(8,128)(2,1)}, u32[]{:S(2)}) copy-start(bf16[1,1,1,3072,512]{4,3,2,1,0:T(8,128)(2,1)} %param.12) | copy-start | bytes 9437188
  0.6 5.5 %copy-start.16 = (f32[1,4,64,2]{2,3,1,0:T(2,128)S(1)}, f32[1,4,64,2]{2,3,1,0:T(2,128)}, u32[]{:S(2)}) copy-start(f32[1,4,64,2]{2,3,1,0:T(2,128)} %param.11) | copy-start | bytes 6148
  6.1 3.2 %collective-permute-start.1 = (bf16[192,3072]{1,0:T(8,128)(2,1)}, bf16[192,3072]{1,0:T(8,128)(2,1)}, u32[]{:S(2)}, u32[]{:S(2)}) collective-permute-start(bf16[192,3072]{1,0:T(8,128)(2,1)} %convolution_convert_fusion), channel_id=1, source_target_pairs={{0,64},{64,0},{1,65},{65,1},{2,66},{66,2},{3,67},{67,3},{4,68},{68... | collective-permute-start | bytes 3538952 | tf_op jit(solution)/shard_map/ppermute | solution.py:21
  8.2 4.1 %copy-start.1 = (bf16[1,1,1,3072,512]{4,3,2,1,0:T(8,128)(2,1)S(1)}, bf16[1,1,1,3072,512]{4,3,2,1,0:T(8,128)(2,1)}, u32[]{:S(2)}) copy-start(bf16[1,1,1,3072,512]{4,3,2,1,0:T(8,128)(2,1)} %param.13) | copy-start | bytes 9437188
  8.3 7.5 %collective-permute-start = (bf16[192,3072]{1,0:T(8,128)(2,1)S(1)}, bf16[192,3072]{1,0:T(8,128)(2,1)S(1)}, u32[]{:S(2)}, u32[]{:S(2)}) collective-permute-start(bf16[192,3072]{1,0:T(8,128)(2,1)S(1)} %fusion), channel_id=1, source_target_pairs={{0,64},{64,0},{1,65},{65,1},{2,66},{66,2},{3,67},{67,3},{4,68},{68... | collective-permute-start | bytes 3538952 | tf_op jit(solution)/shard_map/ppermute | solution.py:21
  12.3 6.4 %copy-start.5 = (f32[384,512]{1,0:T(8,128)}, f32[384,512]{1,0:T(8,128)S(1)}, u32[]{:S(2)}) copy-start(f32[384,512]{1,0:T(8,128)S(1)} %fusion.5) | copy-start | bytes 2359300
  12.3 3.4 %copy-start.17 = (bf16[1,1,1,512,3072]{4,3,2,1,0:T(8,128)(2,1)S(1)}, bf16[1,1,1,512,3072]{4,3,2,1,0:T(8,128)(2,1)}, u32[]{:S(2)}) copy-start(bf16[1,1,1,512,3072]{4,3,2,1,0:T(8,128)(2,1)} %param.14) | copy-start | bytes 9437188
  15.7 1.5 copy-start.8
  20.4 2.9 %collective-permute-start.2 = (bf16[192,3072]{1,0:T(8,128)(2,1)S(1)}, bf16[192,3072]{1,0:T(8,128)(2,1)S(1)}, u32[]{:S(2)}, u32[]{:S(2)}) collective-permute-start(bf16[192,3072]{1,0:T(8,128)(2,1)S(1)} %slice.109), channel_id=1, source_target_pairs={{0,64},{64,0},{1,65},{65,1},{2,66},{66,2},{3,67},{67,3},{4,68},{68... | collective-permute-start | bytes 3538952 | tf_op jit(solution)/shard_map/ppermute | solution.py:21
  25.0 29.3 %all-to-all-start = ((bf16[32,48,384]{2,1,0:T(8,128)(2,1)}), bf16[32,48,384]{2,1,0:T(8,128)(2,1)}, u32[]{:S(2)}, u32[]{:S(2)}) async-start(bf16[32,48,384]{2,1,0:T(8,128)(2,1)} %bitcast.116), calls=%async_computation | async-start | bytes 2359296 | tf_op jit(solution)/shard_map/all_to_all | solution.py:25
  56.9 7.5 %collective-permute-start.3 = (bf16[64,384]{1,0:T(8,128)(2,1)S(1)}, bf16[64,384]{1,0:T(8,128)(2,1)S(1)}, u32[]{:S(2)}, u32[]{:S(2)}) collective-permute-start(bf16[64,384]{1,0:T(8,128)(2,1)S(1)} %fusion.20), channel_id=1, source_target_pairs={{32,0},{33,1},{34,2},{35,3},{36,4},{37,5},{38,6},{39,7},{40,8},{41... | collective-permute-start | bytes 147464 | tf_op jit(solution)/shard_map/ppermute | solution.py:187
  64.4 22.1 %copy-start.15 = (bf16[64,384]{1,0:T(8,128)(2,1)}, bf16[64,384]{1,0:T(8,128)(2,1)S(1)}, u32[]{:S(2)}) copy-start(bf16[64,384]{1,0:T(8,128)(2,1)S(1)} %collective-permute-done.3) | copy-start | bytes 147460
  87.2 3.8 %copy-start.18 = (bf16[1,1,1,512,3072]{4,3,2,1,0:T(8,128)(2,1)S(1)}, bf16[1,1,1,512,3072]{4,3,2,1,0:T(8,128)(2,1)}, u32[]{:S(2)}) copy-start(bf16[1,1,1,512,3072]{4,3,2,1,0:T(8,128)(2,1)} %param.14) | copy-start | bytes 9437188
  87.7 1.3 copy-start.13
  87.7 3.4 %copy-start.6 = (f32[384,512]{1,0:T(8,128)S(1)}, f32[384,512]{1,0:T(8,128)}, u32[]{:S(2)}) copy-start(f32[384,512]{1,0:T(8,128)} %copy-done.5) | copy-start | bytes 2359300
  87.7 3.4 %copy-start.9 = (f32[384,512]{1,0:T(8,128)S(1)}, f32[384,512]{1,0:T(8,128)}, u32[]{:S(2)}) copy-start(f32[384,512]{1,0:T(8,128)} %copy-done.8) | copy-start | bytes 2359300
  88.0 4.8 %copy-start.10 = (bf16[192,3072]{1,0:T(8,128)(2,1)}, bf16[192,3072]{1,0:T(8,128)(2,1)S(1)}, u32[]{:S(2)}) copy-start(bf16[192,3072]{1,0:T(8,128)(2,1)S(1)} %multiply_convert_fusion) | copy-start | bytes 3538948
  88.0 3.1 %collective-permute-start.4 = (bf16[192,3072]{1,0:T(8,128)(2,1)S(1)}, bf16[192,3072]{1,0:T(8,128)(2,1)S(1)}, u32[]{:S(2)}, u32[]{:S(2)}) collective-permute-start(bf16[192,3072]{1,0:T(8,128)(2,1)S(1)} %multiply_convert_fusion), channel_id=1, source_target_pairs={{0,64},{64,0},{1,65},{65,1},{2,66},{66,2},{3,67},{67,3},{4,68},{68... | collective-permute-start | bytes 3538952 | tf_op jit(solution)/shard_map/ppermute | solution.py:21
  91.1 1.7 copy-start.19
  92.8 4.1 %copy-start.3 = (bf16[384,512]{1,0:T(8,128)(2,1)}, bf16[384,512]{1,0:T(8,128)(2,1)S(1)}, u32[]{:S(2)}) copy-start(bf16[384,512]{1,0:T(8,128)(2,1)S(1)} %get-tuple-element.4) | copy-start | bytes 1179652
  92.8 4.4 %copy-start.14 = (bf16[384,512]{1,0:T(8,128)(2,1)}, bf16[384,512]{1,0:T(8,128)(2,1)S(1)}, u32[]{:S(2)}) copy-start(bf16[384,512]{1,0:T(8,128)(2,1)S(1)} %get-tuple-element.3) | copy-start | bytes 1179652
  92.8 2.2 copy-start.2
  96.7 4.9 %collective-permute-start.5 = (bf16[192,3072]{1,0:T(8,128)(2,1)S(1)}, bf16[192,3072]{1,0:T(8,128)(2,1)S(1)}, u32[]{:S(2)}, u32[]{:S(2)}) collective-permute-start(bf16[192,3072]{1,0:T(8,128)(2,1)S(1)} %slice.108), channel_id=1, source_target_pairs={{0,64},{64,0},{1,65},{65,1},{2,66},{66,2},{3,67},{67,3},{4,68},{68... | collective-permute-start | bytes 3538952 | tf_op jit(solution)/shard_map/ppermute | solution.py:21
  97.8 2.1 collective-permute-start.6
  100.8 7.3 %collective-permute-start.7 = (f32[384,128]{0,1:T(8,128)}, f32[384,128]{0,1:T(8,128)}, u32[]{:S(2)}, u32[]{:S(2)}) collective-permute-start(f32[384,128]{0,1:T(8,128)} %maximum_add_fusion), channel_id=1, source_target_pairs={{0,1},{1,0},{2,3},{3,2},{4,5},{5,4},{6,7},{7,6},{8,9},{9,8},{10,11... | collective-permute-start | bytes 589832 | tf_op jit(solution)/shard_map/ppermute | solution.py:62
  103.2 38.2 %all-to-all-start.2 = ((bf16[32,48,384]{2,1,0:T(8,128)(2,1)}), bf16[32,48,384]{2,1,0:T(8,128)(2,1)}, u32[]{:S(2)}, u32[]{:S(2)}) async-start(bf16[32,48,384]{2,1,0:T(8,128)(2,1)} %bitcast.115), calls=%async_computation.2 | async-start | bytes 2359296 | tf_op jit(solution)/shard_map/all_to_all | solution.py:25
  109.1 17.7 %collective-permute-start.8 = (f32[384,128]{0,1:T(8,128)S(1)}, f32[384,128]{0,1:T(8,128)S(1)}, u32[]{:S(2)}, u32[]{:S(2)}) collective-permute-start(f32[384,128]{0,1:T(8,128)S(1)} %add.96), channel_id=1, source_target_pairs={{0,2},{1,3},{2,0},{3,1},{4,6},{5,7},{6,4},{7,5},{8,10},{9,11},{10,... | collective-permute-start | bytes 589832 | tf_op jit(solution)/shard_map/ppermute | solution.py:62
  127.6 7.5 %collective-permute-start.9 = (f32[384,128]{0,1:T(8,128)}, f32[384,128]{0,1:T(8,128)}, u32[]{:S(2)}, u32[]{:S(2)}) collective-permute-start(f32[384,128]{0,1:T(8,128)} %add.97), channel_id=1, source_target_pairs={{0,6},{1,7},{2,4},{3,5},{4,2},{5,3},{6,0},{7,1},{8,14},{9,15},{10,... | collective-permute-start | bytes 589832 | tf_op jit(solution)/shard_map/ppermute | solution.py:62
  145.4 30.9 %all-to-all-start.3 = ((bf16[32,64,384]{2,1,0:T(8,128)(2,1)}), bf16[32,64,384]{2,1,0:T(8,128)(2,1)}, u32[]{:S(2)}, u32[]{:S(2)}) async-start(bf16[32,64,384]{2,1,0:T(8,128)(2,1)} %broadcast_in_dim.51), calls=%async_computation.3 | async-start | bytes 3145728 | tf_op jit(solution)/shard_map/all_to_all | solution.py:25
  165.2 3.6 %copy-start.7 = (f32[3072,64]{0,1:T(8,128)}, f32[3072,64]{0,1:T(8,128)S(1)}, u32[]{:S(2)}) copy-start(f32[3072,64]{0,1:T(8,128)S(1)} %fusion.61) | copy-start | bytes 2359300
  165.3 2.8 %copy-start.4 = (bf16[384,512]{1,0:T(8,128)(2,1)S(1)}, bf16[384,512]{1,0:T(8,128)(2,1)}, u32[]{:S(2)}) copy-start(bf16[384,512]{1,0:T(8,128)(2,1)} %copy-done.3) | copy-start | bytes 1179652
  169.7 3.1 %copy-start.11 = (f32[1,1,1,1,512,64]{4,5,3,2,1,0:T(8,128)S(1)}, f32[1,1,1,1,512,64]{4,5,3,2,1,0:T(8,128)}, u32[]{:S(2)}) copy-start(f32[1,1,1,1,512,64]{4,5,3,2,1,0:T(8,128)} %convolution_bitcast_fusion.2) | copy-start | bytes 393220
  169.7 3.1 %copy-start.12 = (f32[1,1,1,1,512,64]{4,5,3,2,1,0:T(8,128)S(1)}, f32[1,1,1,1,512,64]{4,5,3,2,1,0:T(8,128)}, u32[]{:S(2)}) copy-start(f32[1,1,1,1,512,64]{4,5,3,2,1,0:T(8,128)} %convolution_bitcast_fusion.1) | copy-start | bytes 393220

commit v3 on v2

--- a/solution.py
+++ b/solution.py
@@ -59,17 +59,20 @@
 
     for partner in (x_pair, y_pair, y_cross):
         route = [(i, partner(i)) for i in range(copies * EXPERTS)]
-        values = values + lax.ppermute(values, "expert", route)
+        rounded = values.astype(BF)
+        other = lax.ppermute(rounded, "expert", route)
+        values = rounded.astype(F32) + other.astype(F32)
     return values
 
 
-def eliminate(gram_ref, inverse_ref):
+def inverse_lower(gram):
     height = 8
     lanes = lax.broadcasted_iota(jnp.int32, (height, 2 * R), 1)
     depth = lax.broadcasted_iota(jnp.int32, (height, 2 * R), 0)
     blocks = []
     for b in range(R // height):
-        held = jnp.concatenate([jnp.zeros((height, R), F32), gram_ref[pl.ds(b * height, height), :]], 1)
+        rows = gram[b * height : (b + 1) * height, :]
+        held = jnp.concatenate([jnp.zeros((height, R), F32), rows], 1)
         blocks.append(jnp.where(lanes == depth + b * height, 1.0, held))
     for k in range(R):
         at, row = divmod(k, height)
@@ -81,36 +84,111 @@
     for b in range(R // height):
         diagonal = jnp.where(lanes == depth + R + b * height, blocks[b], 0.0)
         pivots = jnp.sum(diagonal, axis=1, keepdims=True)
-        inverse_ref[pl.ds(b * height, height), :] = (blocks[b] * lax.rsqrt(pivots))[:, :R]
-
-
-def inverse_lower(gram_matrix):
-    return pl.pallas_call(
-        eliminate, out_shape=jax.ShapeDtypeStruct((R, R), F32), name="inverse_lower"
-    )(gram_matrix)
-
-
-def side_by_side(pieces):
-    micro, copies, tokens, columns = pieces.shape
-
-    def kernel(pieces_ref, out_ref, done):
+        blocks[b] = (blocks[b] * lax.rsqrt(pivots))[:, :R]
+    return jnp.concatenate(blocks, axis=0)
+
+
+def halves(value):
+    high = value.astype(BF)
+    return high, (value - high.astype(F32)).astype(BF)
+
+
+def finish(dp_index, sums, squares, rows16, grads, token_total):
+    wide = rows16[0].shape[1]
+    half = wide // 2
+    count = sums.shape[0]
+    units = grads[0].shape[1]
+    height = rows16[0].shape[0]
+
+    def kernel(dp_ref, sums_ref, *refs):
+        squares_hbm, rows_hbm, grads_hbm = (refs[:3], refs[3:7], refs[7:10])
+        q_ref, basis_ref = refs[10:12]
+        squares_ref, rows_ref, grads_ref, done = refs[12:]
         moves = [
+            pltpu.make_async_copy(squares_hbm[i], squares_ref.at[i], done.at[i]) for i in range(3)
+        ]
+        moves += [
+            pltpu.make_async_copy(grads_hbm[i], grads_ref.at[i], done.at[3 + i]) for i in range(3)
+        ]
+        start = pl.multiple_of(dp_ref[0] * half, half)
+        moves += [
             pltpu.make_async_copy(
-                pieces_ref.at[:, c], out_ref.at[:, :, pl.ds(c * columns, columns)], done.at[c]
+                rows_hbm[i].at[:, pl.ds(start, half)],
+                rows_ref.at[pl.ds(i * height, height)],
+                done.at[6 + i],
             )
-            for c in range(copies)
+            for i in range(4)
         ]
         for move in moves:
             move.start()
-        for move in moves:
+        turned = sums_ref[...].T
+        of_inputs, of_grads = (turned[:R].astype(BF), turned[R:].astype(BF))
+        for move in moves[:3]:
             move.wait()
 
+        def twice(left, right, cb):
+            high, low = halves(right)
+            return times(left, high, 1, cb) + times(left, low, 1, cb)
+
+        inputs_inputs, grads_inputs, grads_grads = (squares_ref[i] for i in range(3))
+        along_inputs = twice(of_inputs, inputs_inputs, 0) + twice(of_grads, grads_inputs, 0)
+        along_grads = twice(of_inputs, grads_inputs, 1) + twice(of_grads, grads_grads, 0)
+        gram = twice(of_inputs, along_inputs, 1) + twice(of_grads, along_grads, 1)
+        inverse = inverse_lower(0.5 * (gram + gram.T))
+        exact = lax.Precision.HIGHEST
+        weights = jnp.concatenate(
+            [
+                times(inverse, of_inputs.astype(F32), 1, 0, exact),
+                times(inverse, of_grads.astype(F32), 1, 0, exact),
+            ],
+            axis=1,
+        ).astype(BF)
+        scale = 1.0 / math.sqrt(float(token_total))
+        along_inputs = times(inverse, along_inputs, 1, 0, exact).astype(BF)
+        along_grads = times(inverse, along_grads, 1, 0, exact).astype(BF)
+        for move in moves[3:]:
+            move.wait()
+        q_ref[0] = times(along_inputs, grads_ref[0]) * scale
+        q_ref[1] = times(along_inputs, grads_ref[1]) * scale
+        q_ref[2] = times(along_grads, grads_ref[2]) * scale
+        basis_ref[...] = times(weights, rows_ref[...]) * math.sqrt(float(wide))
+
+    anywhere = pl.BlockSpec(memory_space=pl.ANY)
     return pl.pallas_call(
         kernel,
+        out_shape=(
+            jax.ShapeDtypeStruct((3, R, units), F32),
+            jax.ShapeDtypeStruct((R, half), F32),
+        ),
+        in_specs=[
+            pl.BlockSpec(memory_space=pltpu.SMEM),
+            pl.BlockSpec(memory_space=pltpu.VMEM),
+            *[anywhere] * 10,
+        ],
+        scratch_shapes=[
+            pltpu.VMEM((3, count, count), F32),
+            pltpu.VMEM((4 * height, half), BF),
+            pltpu.VMEM((3, count, units), BF),
+            pltpu.SemaphoreType.DMA((10,)),
+        ],
+        compiler_params=pltpu.CompilerParams(vmem_limit_bytes=32 << 20),
+        name="finish",
+    )(dp_index.reshape(1), sums, *squares, *rows16, *grads)
+
+
+def side_by_side(pieces):
+    micro, copies, tokens, columns = pieces.shape
+
+    def kernel(pieces_ref, out_ref):
+        for c in range(copies):
+            out_ref[0, :, c * columns : (c + 1) * columns] = pieces_ref[0, c]
+
+    return pl.pallas_call(
+        kernel,
+        grid=(micro,),
         out_shape=jax.ShapeDtypeStruct((micro, tokens, copies * columns), pieces.dtype),
-        in_specs=[pl.BlockSpec(memory_space=pl.ANY)],
-        out_specs=pl.BlockSpec(memory_space=pl.ANY),
-        scratch_shapes=[pltpu.SemaphoreType.DMA((copies,))],
+        in_specs=[pl.BlockSpec((1, copies, tokens, columns), lambda m: (m, 0, 0, 0))],
+        out_specs=pl.BlockSpec((1, tokens, copies * columns), lambda m: (m, 0, 0)),
         name="side_by_side",
     )(pieces)
 
@@ -148,10 +226,9 @@
     first, second = hit_table(part_ids, EXPERTS * CAP)
     part_pick = (first | second).astype(BF)
 
-    def both_cores(own):
-        return jnp.concatenate([own, swap_cores(own)])
-
-    inputs = both_cores(times(own_pick, own_inputs).astype(BF))
+    own_slots = times(own_pick, own_inputs).astype(BF)
+    inputs_both = (own_slots, swap_cores(own_slots))
+    inputs = jnp.concatenate(inputs_both)
     pre_gate = times(inputs, gate)
     pre_up = times(inputs, up)
     sigmoid_gate = jax.nn.sigmoid(pre_gate)
@@ -160,7 +237,9 @@
     slope = pre_up * sigmoid_gate * (1.0 + pre_gate * (1.0 - sigmoid_gate))
 
     def phase(own_rows, base):
-        grad_rows = both_cores((weight * own_rows).astype(BF))
+        own_grads = (weight * own_rows).astype(BF)
+        grads_both = (own_grads, swap_cores(own_grads))
+        grad_rows = jnp.concatenate(grads_both)
         grad_hidden = times(grad_rows, down, 1, 1)
         grad_gate = (grad_hidden * slope).astype(BF)
         grad_up = (grad_hidden * silu_gate).astype(BF)
@@ -178,7 +257,7 @@
             lax.Precision.HIGHEST,
         )
         part = (base.astype(F32) + share).astype(BF)
-        return part, grad_rows, grad_gate, grad_up
+        return part, grads_both, grad_gate, grad_up
 
     top_part = lax.dynamic_slice(
         top_grad, (major, 0, minor * columns), (1, tokens, columns)
@@ -190,37 +269,35 @@
     pieces = jnp.broadcast_to(listed, (EXPERTS, copies, CAP, columns))
     own_rows = exchange(pieces.reshape(peers, CAP, columns))
     own_rows = own_rows.reshape(MICRO, copies, CAP, columns).transpose(0, 2, 1, 3)
-    part, grad_rows, grad_gate, grad_up = phase(own_rows.reshape(slots, D).astype(F32), base)
+    part, grads_both, grad_gate, grad_up = phase(own_rows.reshape(slots, D).astype(F32), base)
     produced = exchange(jnp.broadcast_to(part, (peers, tokens, columns)))
     produced = side_by_side(produced.reshape(MICRO, copies, tokens, columns))
 
     sums = jnp.concatenate(
         [times(grad_gate, right[0]) + times(grad_up, right[1]), times(hidden, right[2])], axis=1
     )
-    other = swap_cores(sums)
-    sums = sums + jnp.concatenate([other[slots:], other[:slots]])
-    sums = add_copies(sums, copies).astype(BF)
-    factor = times(inputs, sums[:, :R], 0, 0) + times(grad_rows, sums[:, R:], 0, 0)
-    gram_matrix = times(factor, factor, 0, 0, lax.Precision.HIGHEST)
-    inverse = inverse_lower(gram_matrix)
-    ortho = times(factor, inverse, 1, 1, lax.Precision.HIGHEST)
-    ortho16 = ortho.astype(BF)
-    along_inputs = times(inputs, ortho16).astype(BF)
-    along_grads = times(grad_rows, ortho16).astype(BF)
-    scale = 1.0 / math.sqrt(float(replicas * rows))
-    q_next = jnp.stack(
-        [
-            times(grad_gate, along_inputs, 0, 0),
-            times(grad_up, along_inputs, 0, 0),
-            times(hidden, along_grads, 0, 0),
-        ]
-    )
-    row_count = D // replicas
-    basis = lax.dynamic_slice_in_dim(ortho, dp_index * row_count, row_count, 0)
+    rounded = sums.astype(BF)
+    other = swap_cores(rounded)
+    sums = rounded.astype(F32) + jnp.concatenate([other[slots:], other[:slots]]).astype(F32)
+    sums = add_copies(sums, copies)
+    grad_rows = jnp.concatenate(grads_both)
+    squares = (
+        times(inputs, inputs, 1, 1),
+        times(grad_rows, inputs, 1, 1),
+        times(grad_rows, grad_rows, 1, 1),
+    )
+    q_next, basis = finish(
+        dp_index,
+        sums,
+        squares,
+        (*inputs_both, *grads_both),
+        (grad_gate, grad_up, hidden),
+        replicas * rows,
+    )
     return (
         produced.reshape(1, MICRO, tokens, D),
-        (basis * math.sqrt(float(D)))[None, None, None],
-        (q_next * scale)[None, None, None],
+        basis.T[None, None, None],
+        q_next.transpose(0, 2, 1)[None, None, None],
     )
 
 

time: 226 us -> 179 us (0.79)
  Pallas kernels: 55.6 us -> 13.1 us
  waiting for transfers between devices: 54.9 us -> 69.1 us
  matrix products: 41.8 us -> 33.1 us
  other arithmetic: 11.4 us -> 4.32 us
  starting transfers between devices: 30.2 us -> 27.5 us
    pallas_call x2, Pallas kernels: 55.6 us -> 13.1 us  [the longest x1 9.48 us: finish(): pl.pallas_call(kernel, out_shape=(jax.ShapeDtypeStruct((3, R, units), F32...]
    all_to_all x3, waiting for transfers between devices: 20.2 us -> 37.6 us  [exchange(): return lax.all_to_all(pieces, 'expert', 0, 0, tiled=True)]
    dot_general x24 -> x19, matrix products: 41.8 us -> 33.1 us  [times(): lax.dot_general(a, b, (((ca,), (cb,)), ((), ())), preferred_element_type=...]
    ppermute x3, waiting for transfers between devices: 21.7 us -> 16.8 us  [add_copies(): other = lax.ppermute(rounded, 'expert', route)]
    all_to_all x3, starting transfers between devices: 22.5 us -> 18.3 us  [exchange(): return lax.all_to_all(pieces, 'expert', 0, 0, tiled=True)]
    add x3 -> x1, other arithmetic: 2.53 us -> 0.02 us  [add_copies(): values = rounded.astype(F32) + other.astype(F32)]
  transfers between devices with their start and end apart: 13 -> 13, of which waited for: 10 -> 10; matrix products, arithmetic and copies ran while one was open for 16% -> 12% of each run, Pallas kernels for 3% -> 5%
where the time goes in v3:
time: 179 us; the launch traced here: 178 us
  waiting for transfers between devices  69.1 us (39%)
  matrix products  33.1 us (18%)
  starting transfers between devices  27.5 us (15%)
  blocking collectives  20.8 us (12%)
  Pallas kernels  13.1 us (7%)
  local copies, waits for them, and re-layouts  8.43 us (5%)
  other arithmetic  4.32 us (2%)
    all_to_all x3, waiting for transfers between devices, exchange(): return lax.all_to_all(pieces, 'expert', 0, 0, tiled=True)  37.6 us
    dot_general x19, matrix products, times(): lax.dot_general(a, b, (((ca,), (cb,)), ((), ())), preferred_element_type=...  33.1 us
    all_to_all x1, blocking collectives, exchange(): return lax.all_to_all(pieces, 'expert', 0, 0, tiled=True)  20.8 us
    all_to_all x3, starting transfers between devices, exchange(): return lax.all_to_all(pieces, 'expert', 0, 0, tiled=True)  18.3 us
    ppermute x3, waiting for transfers between devices, add_copies(): other = lax.ppermute(rounded, 'expert', route)  16.8 us
    pallas_call x1, Pallas kernels, finish(): pl.pallas_call(kernel, out_shape=(jax.ShapeDtypeStruct((3, R, units), F32...  9.48 us
    ppermute x6, waiting for transfers between devices, swap_cores(): return lax.ppermute(value, 'dp', [(0, 1), (1, 0)])  8.5 us
    ppermute x1, waiting for transfers between devices, shards(): lax.ppermute(part, 'pipe', [(i, i - 1) for i in range(1, sections)])  6.18 us
  transfers between devices with their start and end apart: 13, of which 10 were waited for; matrix products, arithmetic and copies ran while one was open for 12% of the time, Pallas kernels for 5%

profile of v3, /device:TPU:0, one launch (start us, length us, event | category | flops | bytes accessed | tf_op | source)
XLA Modules:
  0.0 177.7 jit_solution(14222253052807354999)
XLA Ops:
  0.7 0.9 copy.44
  1.7 0.7 broadcast_compare_fusion
  3.2 2.9 %convolution_convert_fusion.refs_3_ = bf16[192,3072]{1,0:T(8,128)(2,1)} fusion(bf16[256,3072]{1,0:T(8,128)(2,1)} %bitcast.112, s32[256]{0:T(256)S(1)} %bitcast.122, s32[256]{0:T(256)S(1)} %bitcast.119), kind=kOutput, calls=%fused_computation.4 | convolution fusion | flops 302727168 | bytes 2754560 | tf_op jit(solution)/shard_map/dot_general | solution.py:29
  6.3 1.9 %fusion = bf16[192,3072]{1,0:T(8,128)(2,1)S(1)} fusion(bf16[256,3072]{1,0:T(8,128)(2,1)} %bitcast.111, f32[192]{0:T(256)S(1)} %add_reduce_fusion, s32[256]{0:T(256)S(1)} %bitcast.124, s32[256]{0:T(256)S(1)} %bitcast.121), kind=kOutput, calls=%fused_computation.3 | convolution fusion | flops 303316992 | bytes 2755328 | tf_op jit(solution)/shard_map/dot_general | solution.py:29
  8.3 0.6 collective-permute-start
  8.8 0.5 collective-permute-done.1.refs_4_
  9.3 3.0 %fusion.5 = f32[384,512]{1,0:T(8,128)S(1)} fusion(bf16[1,1,1,3072,512]{4,3,2,1,0:T(8,128)(2,1)S(1)} %copy-done, bf16[192,3072]{1,0:T(8,128)(2,1)} %collective-permute-done.1.refs_4_, bf16[192,3072]{1,0:T(8,128)(2,1)} %convolution_convert_fusion.refs_3_), kind=kOutput, calls=%fused_computation.9 | convolution fusion | flops 1212678144 | bytes 6291456 | tf_op jit(solution)/shard_map/dot_general | solution.py:29
  12.3 3.4 %fusion.9 = f32[384,512]{1,0:T(8,128)S(1)} fusion(bf16[1,1,1,3072,512]{4,3,2,1,0:T(8,128)(2,1)S(1)} %copy-done.11, bf16[192,3072]{1,0:T(8,128)(2,1)} %collective-permute-done.1.refs_4_, bf16[192,3072]{1,0:T(8,128)(2,1)} %convolution_convert_fusion.refs_3_), kind=kOutput, calls=%fused_computation.13 | convolution fusion | flops 1212678144 | bytes 6291456 | tf_op jit(solution)/shard_map/dot_general | solution.py:29
  15.7 1.4 fusion.13
  17.2 1.5 fusion.3
  18.7 1.5 convolution_add_fusion.1
  20.4 0.5 collective-permute-start.2
  20.9 2.5 %collective-permute-done.2 = bf16[192,3072]{1,0:T(8,128)(2,1)S(1)} collective-permute-done((bf16[192,3072]{1,0:T(8,128)(2,1)S(1)}, bf16[192,3072]{1,0:T(8,128)(2,1)S(1)}, u32[]{:S(2)}, u32[]{:S(2)}) %collective-permute-start.2) | collective-permute-done | bytes 1179680 | tf_op jit(solution)/shard_map/ppermute | solution.py:21
  23.3 0.3 fusion.16
  23.9 1.2 copy.53
  25.0 9.5 %all-to-all-start = ((bf16[32,48,384]{2,1,0:T(8,128)(2,1)}), bf16[32,48,384]{2,1,0:T(8,128)(2,1)}, u32[]{:S(2)}, u32[]{:S(2)}) async-start(bf16[32,48,384]{2,1,0:T(8,128)(2,1)} %bitcast.105), calls=%async_computation | async-start | bytes 2359296 | tf_op jit(solution)/shard_map/all_to_all | solution.py:25
  35.0 19.3 %all-to-all-done = bf16[32,48,384]{2,1,0:T(8,128)(2,1)} async-done(((bf16[32,48,384]{2,1,0:T(8,128)(2,1)}), bf16[32,48,384]{2,1,0:T(8,128)(2,1)}, u32[]{:S(2)}, u32[]{:S(2)}) %all-to-all-start) | async-done | bytes 1179680 | tf_op jit(solution)/shard_map/all_to_all | solution.py:25
  54.3 1.5 convert_reduce_fusion.1
  55.8 1.1 fusion.20
  56.9 1.3 collective-permute-start.3
  58.2 6.2 %collective-permute-done.3 = bf16[64,384]{1,0:T(8,128)(2,1)S(1)} collective-permute-done((bf16[64,384]{1,0:T(8,128)(2,1)S(1)}, bf16[64,384]{1,0:T(8,128)(2,1)S(1)}, u32[]{:S(2)}, u32[]{:S(2)}) %collective-permute-start.3) | collective-permute-done | bytes 49184 | tf_op jit(solution)/shard_map/ppermute | solution.py:266
  64.4 1.0 convolution_convert_fusion.1
  65.5 20.8 %all_to_all.20 = bf16[32,48,384]{2,1,0:T(8,128)(2,1)S(1)} all-to-all(bf16[32,48,384]{2,1,0:T(8,128)(2,1)S(1)} %bitcast.107), channel_id=1, replica_groups=mesh['dp'=2,'pipe'=2,'expert'=32] {'expert'}, dimensions={0} | all-to-all | bytes 2359296 | tf_op jit(solution)/shard_map/all_to_all | solution.py:25
  86.5 0.7 copy.54
  87.2 0.4 copy.59
  88.2 2.8 %collective-permute-done.4.refs_6_ = bf16[192,3072]{1,0:T(8,128)(2,1)S(1)} collective-permute-done((bf16[192,3072]{1,0:T(8,128)(2,1)S(1)}, bf16[192,3072]{1,0:T(8,128)(2,1)S(1)}, u32[]{:S(2)}, u32[]{:S(2)}) %collective-permute-start.4) | collective-permute-done | bytes 1179680 | tf_op jit(solution)/shard_map/ppermute | solution.py:21
  91.1 2.4 %multiply_convert_fusion.1 = (bf16[384,512]{1,0:T(8,128)(2,1)}, bf16[384,512]{1,0:T(8,128)(2,1)S(1)}, bf16[384,512]{1,0:T(8,128)(2,1)S(1)}) fusion(f32[384,512]{1,0:T(8,128)S(1)} %copy-done.16, f32[384,512]{1,0:T(8,128)S(1)} %copy-done.14, bf16[1,1,1,512,3072]{4,3,2,1,0:T(8,128)(2,1)S(1)} %copy-done.22, ...), kind=kOutput, calls=%fused_computation.39 | convolution fusion | flops 1215627264 | bytes 8257536 | tf_op jit(solution)/shard_map/dot_general | solution.py:29
  93.5 1.4 fusion.1
  94.9 0.6 copy-done.12
  95.5 1.6 convolution_add_fusion
  97.5 2.7 %collective-permute-done.5 = bf16[192,3072]{1,0:T(8,128)(2,1)S(1)} collective-permute-done((bf16[192,3072]{1,0:T(8,128)(2,1)S(1)}, bf16[192,3072]{1,0:T(8,128)(2,1)S(1)}, u32[]{:S(2)}, u32[]{:S(2)}) %collective-permute-start.5) | collective-permute-done | bytes 1179680 | tf_op jit(solution)/shard_map/ppermute | solution.py:21
  100.2 0.3 fusion.15
  100.7 1.2 copy.55
  101.9 4.1 %all-to-all-start.2 = ((bf16[32,48,384]{2,1,0:T(8,128)(2,1)}), bf16[32,48,384]{2,1,0:T(8,128)(2,1)S(1)}, u32[]{:S(2)}, u32[]{:S(2)}) async-start(bf16[32,48,384]{2,1,0:T(8,128)(2,1)} %bitcast.25), calls=%async_computation.2 | async-start | bytes 2359296 | tf_op jit(solution)/shard_map/all_to_all | solution.py:25
  107.5 18.3 %all-to-all-done.2 = bf16[32,48,384]{2,1,0:T(8,128)(2,1)S(1)} async-done(((bf16[32,48,384]{2,1,0:T(8,128)(2,1)}), bf16[32,48,384]{2,1,0:T(8,128)(2,1)S(1)}, u32[]{:S(2)}, u32[]{:S(2)}) %all-to-all-start.2) | async-done | bytes 1179680 | tf_op jit(solution)/shard_map/all_to_all | solution.py:25
  126.0 1.1 add_convert_fusion.3
  127.1 1.4 broadcast_in_dim.53
  128.5 4.7 %all-to-all-start.3 = ((bf16[32,64,384]{2,1,0:T(8,128)(2,1)}), bf16[32,64,384]{2,1,0:T(8,128)(2,1)}, u32[]{:S(2)}, u32[]{:S(2)}) async-start(bf16[32,64,384]{2,1,0:T(8,128)(2,1)} %broadcast_in_dim.53), calls=%async_computation.3 | async-start | bytes 3145728 | tf_op jit(solution)/shard_map/all_to_all | solution.py:25
  133.3 1.7 collective-permute-start.7
  135.0 3.7 %fusion.50.refs_0_ = f32[384,384]{1,0:T(8,128)S(1)} fusion(bf16[192,3072]{1,0:T(8,128)(2,1)} %collective-permute-done.1.refs_4_, bf16[192,3072]{1,0:T(8,128)(2,1)} %convolution_convert_fusion.refs_3_), kind=kOutput, calls=%fused_computation.92 | convolution fusion | flops 910688256 | bytes 2949120 | tf_op jit(solution)/shard_map/dot_general | solution.py:29
  138.8 14.8 %collective-permute-done.7 = bf16[384,128]{1,0:T(8,128)(2,1)S(1)} collective-permute-done((bf16[384,128]{1,0:T(8,128)(2,1)S(1)}, bf16[384,128]{1,0:T(8,128)(2,1)S(1)}, u32[]{:S(2)}, u32[]{:S(2)}) %collective-permute-start.7) | collective-permute-done | bytes 98336 | tf_op jit(solution)/shard_map/ppermute | solution.py:63
  153.6 1.5 collective-permute-start.8
  155.2 3.0 %fusion.23.refs_1_ = f32[384,384]{1,0:T(8,128)S(1)} fusion(bf16[192,3072]{1,0:T(8,128)(2,1)S(1)} %copy-done.10, bf16[192,3072]{1,0:T(8,128)(2,1)S(1)} %copy-done.3, bf16[192,3072]{1,0:T(8,128)(2,1)} %collective-permute-done.1.refs_4_, bf16[192,3072]{1,0:T(8,128)(2,1)} %convolution_convert_fusion.refs_3_), kind=kOutput, calls=%fused_computation.48 | convolution fusion | flops 915406848 | bytes 5308416 | tf_op jit(solution)/shard_map/dot_general | solution.py:29
  158.4 2.9 %collective-permute-start.9 = (bf16[384,128]{1,0:T(8,128)(2,1)S(1)}, bf16[384,128]{1,0:T(8,128)(2,1)S(1)}, u32[]{:S(2)}, u32[]{:S(2)}) collective-permute-start(bf16[384,128]{1,0:T(8,128)(2,1)S(1)} %add_convert_fusion), channel_id=1, source_target_pairs={{0,6},{1,7},{2,4},{3,5},{4,2},{5,3},{6,0},{7,1},{8,14},{9,15},{10,... | collective-permute-start | bytes 294920 | tf_op jit(solution)/shard_map/ppermute | solution.py:63
  161.3 1.4 fusion.22.refs_2_
  162.7 1.8 %collective-permute-done.9 = bf16[384,128]{1,0:T(8,128)(2,1)S(1)} collective-permute-done((bf16[384,128]{1,0:T(8,128)(2,1)S(1)}, bf16[384,128]{1,0:T(8,128)(2,1)S(1)}, u32[]{:S(2)}, u32[]{:S(2)}) %collective-permute-start.9) | collective-permute-done | bytes 98336 | tf_op jit(solution)/shard_map/ppermute | solution.py:63
  164.6 9.5 %finish.1 = (f32[3,64,512]{2,1,0:T(8,128)}, f32[64,1536]{1,0:T(8,128)}) custom-call(s32[1]{0:T(128)} %bitcast.30.dp_ref, f32[384,128]{1,0:T(8,128)S(1)} %convert_add_fusion.sums_ref, f32[384,384]{1,0:T(8,128)S(1)} %fusion.50.refs_0_, f32[384,384]{1,0:T(8,128)S(1)} %fusion.23.refs_1_, f32[384,384]{1,0:T(8,128)S(1)} %fusion.22.refs_2_, ...), custom_call_target="tpu_custom_call" | custom-call | tf_op jit(solution)/shard_map/finish/pallas_call | solution.py:157
  174.1 3.6 %side_by_side.1 = bf16[4,64,3072]{2,1,0:T(8,128)(2,1)} custom-call(bf16[4,8,64,384]{3,2,1,0:T(8,128)(2,1)} %bitcast.28.pieces_ref), custom_call_target="tpu_custom_call" | custom-call | tf_op jit(solution)/shard_map/side_by_side/pallas_call | solution.py:186
  (94 shorter events, 5.2 us)
Async XLA Ops:
  0.6 8.7 %copy-start = (bf16[1,1,1,3072,512]{4,3,2,1,0:T(8,128)(2,1)S(1)}, bf16[1,1,1,3072,512]{4,3,2,1,0:T(8,128)(2,1)}, u32[]{:S(2)}) copy-start(bf16[1,1,1,3072,512]{4,3,2,1,0:T(8,128)(2,1)} %param.12) | copy-start | bytes 9437188
  0.6 5.5 %copy-start.20 = (f32[1,4,64,2]{2,3,1,0:T(2,128)S(1)}, f32[1,4,64,2]{2,3,1,0:T(2,128)}, u32[]{:S(2)}) copy-start(f32[1,4,64,2]{2,3,1,0:T(2,128)} %param.11) | copy-start | bytes 6148
  6.1 3.2 %collective-permute-start.1 = (bf16[192,3072]{1,0:T(8,128)(2,1)}, bf16[192,3072]{1,0:T(8,128)(2,1)}, u32[]{:S(2)}, u32[]{:S(2)}) collective-permute-start(bf16[192,3072]{1,0:T(8,128)(2,1)} %convolution_convert_fusion.refs_3_), channel_id=1, source_target_pairs={{0,64},{64,0},{1,65},{65,1},{2,66},{66,2},{3,67},{67,3},{4,68},{68... | collective-permute-start | bytes 3538952 | tf_op jit(solution)/shard_map/ppermute | solution.py:21
  8.2 4.1 %copy-start.11 = (bf16[1,1,1,3072,512]{4,3,2,1,0:T(8,128)(2,1)S(1)}, bf16[1,1,1,3072,512]{4,3,2,1,0:T(8,128)(2,1)}, u32[]{:S(2)}) copy-start(bf16[1,1,1,3072,512]{4,3,2,1,0:T(8,128)(2,1)} %param.13) | copy-start | bytes 9437188
  8.3 7.5 %collective-permute-start = (bf16[192,3072]{1,0:T(8,128)(2,1)S(1)}, bf16[192,3072]{1,0:T(8,128)(2,1)S(1)}, u32[]{:S(2)}, u32[]{:S(2)}) collective-permute-start(bf16[192,3072]{1,0:T(8,128)(2,1)S(1)} %fusion), channel_id=1, source_target_pairs={{0,64},{64,0},{1,65},{65,1},{2,66},{66,2},{3,67},{67,3},{4,68},{68... | collective-permute-start | bytes 3538952 | tf_op jit(solution)/shard_map/ppermute | solution.py:21
  12.3 6.4 %copy-start.13 = (f32[384,512]{1,0:T(8,128)}, f32[384,512]{1,0:T(8,128)S(1)}, u32[]{:S(2)}) copy-start(f32[384,512]{1,0:T(8,128)S(1)} %fusion.5) | copy-start | bytes 2359300
  12.3 3.4 %copy-start.21 = (bf16[1,1,1,512,3072]{4,3,2,1,0:T(8,128)(2,1)S(1)}, bf16[1,1,1,512,3072]{4,3,2,1,0:T(8,128)(2,1)}, u32[]{:S(2)}) copy-start(bf16[1,1,1,512,3072]{4,3,2,1,0:T(8,128)(2,1)} %param.14) | copy-start | bytes 9437188
  15.7 1.5 copy-start.15
  20.4 2.9 %collective-permute-start.2 = (bf16[192,3072]{1,0:T(8,128)(2,1)S(1)}, bf16[192,3072]{1,0:T(8,128)(2,1)S(1)}, u32[]{:S(2)}, u32[]{:S(2)}) collective-permute-start(bf16[192,3072]{1,0:T(8,128)(2,1)S(1)} %slice.95), channel_id=1, source_target_pairs={{0,64},{64,0},{1,65},{65,1},{2,66},{66,2},{3,67},{67,3},{4,68},{68... | collective-permute-start | bytes 3538952 | tf_op jit(solution)/shard_map/ppermute | solution.py:21
  25.0 29.3 %all-to-all-start = ((bf16[32,48,384]{2,1,0:T(8,128)(2,1)}), bf16[32,48,384]{2,1,0:T(8,128)(2,1)}, u32[]{:S(2)}, u32[]{:S(2)}) async-start(bf16[32,48,384]{2,1,0:T(8,128)(2,1)} %bitcast.105), calls=%async_computation | async-start | bytes 2359296 | tf_op jit(solution)/shard_map/all_to_all | solution.py:25
  56.9 7.5 %collective-permute-start.3 = (bf16[64,384]{1,0:T(8,128)(2,1)S(1)}, bf16[64,384]{1,0:T(8,128)(2,1)S(1)}, u32[]{:S(2)}, u32[]{:S(2)}) collective-permute-start(bf16[64,384]{1,0:T(8,128)(2,1)S(1)} %fusion.20), channel_id=1, source_target_pairs={{32,0},{33,1},{34,2},{35,3},{36,4},{37,5},{38,6},{39,7},{40,8},{41... | collective-permute-start | bytes 147464 | tf_op jit(solution)/shard_map/ppermute | solution.py:266
  64.4 22.1 %copy-start.18 = (bf16[64,384]{1,0:T(8,128)(2,1)}, bf16[64,384]{1,0:T(8,128)(2,1)S(1)}, u32[]{:S(2)}) copy-start(bf16[64,384]{1,0:T(8,128)(2,1)S(1)} %collective-permute-done.3) | copy-start | bytes 147460
  87.2 3.8 %copy-start.22 = (bf16[1,1,1,512,3072]{4,3,2,1,0:T(8,128)(2,1)S(1)}, bf16[1,1,1,512,3072]{4,3,2,1,0:T(8,128)(2,1)}, u32[]{:S(2)}) copy-start(bf16[1,1,1,512,3072]{4,3,2,1,0:T(8,128)(2,1)} %param.14) | copy-start | bytes 9437188
  87.7 3.4 %copy-start.14 = (f32[384,512]{1,0:T(8,128)S(1)}, f32[384,512]{1,0:T(8,128)}, u32[]{:S(2)}) copy-start(f32[384,512]{1,0:T(8,128)} %copy-done.13) | copy-start | bytes 2359300
  87.7 3.4 %copy-start.16 = (f32[384,512]{1,0:T(8,128)S(1)}, f32[384,512]{1,0:T(8,128)}, u32[]{:S(2)}) copy-start(f32[384,512]{1,0:T(8,128)} %copy-done.15) | copy-start | bytes 2359300
  87.9 5.5 %copy-start.2 = (bf16[192,3072]{1,0:T(8,128)(2,1)}, bf16[192,3072]{1,0:T(8,128)(2,1)S(1)}, u32[]{:S(2)}) copy-start(bf16[192,3072]{1,0:T(8,128)(2,1)S(1)} %multiply_convert_fusion.refs_5_) | copy-start | bytes 3538948
  88.0 3.1 %collective-permute-start.4 = (bf16[192,3072]{1,0:T(8,128)(2,1)S(1)}, bf16[192,3072]{1,0:T(8,128)(2,1)S(1)}, u32[]{:S(2)}, u32[]{:S(2)}) collective-permute-start(bf16[192,3072]{1,0:T(8,128)(2,1)S(1)} %multiply_convert_fusion.refs_5_), channel_id=1, source_target_pairs={{0,64},{64,0},{1,65},{65,1},{2,66},{66,2},{3,67},{67,3},{4,68},{68... | collective-permute-start | bytes 3538952 | tf_op jit(solution)/shard_map/ppermute | solution.py:21
  91.1 2.4 %copy-start.9 = (bf16[192,3072]{1,0:T(8,128)(2,1)}, bf16[192,3072]{1,0:T(8,128)(2,1)S(1)}, u32[]{:S(2)}) copy-start(bf16[192,3072]{1,0:T(8,128)(2,1)S(1)} %collective-permute-done.4.refs_6_) | copy-start | bytes 3538948
  93.5 1.4 copy-start.4
  93.5 2.0 %copy-start.12 = (bf16[1,1,1,3072,512]{4,3,2,1,0:T(8,128)(2,1)S(1)}, bf16[1,1,1,3072,512]{4,3,2,1,0:T(8,128)(2,1)}, u32[]{:S(2)}) copy-start(bf16[1,1,1,3072,512]{4,3,2,1,0:T(8,128)(2,1)} %param.13) | copy-start | bytes 9437188
  97.3 2.9 %collective-permute-start.5 = (bf16[192,3072]{1,0:T(8,128)(2,1)S(1)}, bf16[192,3072]{1,0:T(8,128)(2,1)S(1)}, u32[]{:S(2)}, u32[]{:S(2)}) collective-permute-start(bf16[192,3072]{1,0:T(8,128)(2,1)S(1)} %slice.94), channel_id=1, source_target_pairs={{0,64},{64,0},{1,65},{65,1},{2,66},{66,2},{3,67},{67,3},{4,68},{68... | collective-permute-start | bytes 3538952 | tf_op jit(solution)/shard_map/ppermute | solution.py:21
  100.7 5.3 %copy-start.5 = (bf16[384,512]{1,0:T(8,128)(2,1)S(1)}, bf16[384,512]{1,0:T(8,128)(2,1)}, u32[]{:S(2)}) copy-start(bf16[384,512]{1,0:T(8,128)(2,1)} %copy-done.4) | copy-start | bytes 1179652
  101.9 4.1 %copy-start.17 = (f32[1,1,1,3,512,64]{4,5,3,2,1,0:T(8,128)S(1)}, f32[1,1,1,3,512,64]{4,5,3,2,1,0:T(8,128)}, u32[]{:S(2)}) copy-start(f32[1,1,1,3,512,64]{4,5,3,2,1,0:T(8,128)} %param.15) | copy-start | bytes 1179652
  101.9 4.8 %copy-start.7 = (bf16[384,512]{1,0:T(8,128)(2,1)S(1)}, bf16[384,512]{1,0:T(8,128)(2,1)}, u32[]{:S(2)}) copy-start(bf16[384,512]{1,0:T(8,128)(2,1)} %get-tuple-element.7.refs_9_) | copy-start | bytes 1179652
  101.9 23.9 %all-to-all-start.2 = ((bf16[32,48,384]{2,1,0:T(8,128)(2,1)}), bf16[32,48,384]{2,1,0:T(8,128)(2,1)S(1)}, u32[]{:S(2)}, u32[]{:S(2)}) async-start(bf16[32,48,384]{2,1,0:T(8,128)(2,1)} %bitcast.25), calls=%async_computation.2 | async-start | bytes 2359296 | tf_op jit(solution)/shard_map/all_to_all | solution.py:25
  106.0 20.0 %copy-start.19 = (bf16[64,384]{1,0:T(8,128)(2,1)S(1)}, bf16[64,384]{1,0:T(8,128)(2,1)}, u32[]{:S(2)}) copy-start(bf16[64,384]{1,0:T(8,128)(2,1)} %copy-done.18) | copy-start | bytes 147460
  107.2 25.9 %collective-permute-start.6 = (bf16[384,128]{1,0:T(8,128)(2,1)S(1)}, bf16[384,128]{1,0:T(8,128)(2,1)S(1)}, u32[]{:S(2)}, u32[]{:S(2)}) collective-permute-start(bf16[384,128]{1,0:T(8,128)(2,1)S(1)} %pad_maximum_fusion.5), channel_id=1, source_target_pairs={{0,64},{64,0},{1,65},{65,1},{2,66},{66,2},{3,67},{67,3},{4,68},{68... | collective-permute-start | bytes 294920 | tf_op jit(solution)/shard_map/ppermute | solution.py:21
  128.5 45.6 %all-to-all-start.3 = ((bf16[32,64,384]{2,1,0:T(8,128)(2,1)}), bf16[32,64,384]{2,1,0:T(8,128)(2,1)}, u32[]{:S(2)}, u32[]{:S(2)}) async-start(bf16[32,64,384]{2,1,0:T(8,128)(2,1)} %broadcast_in_dim.53), calls=%async_computation.3 | async-start | bytes 3145728 | tf_op jit(solution)/shard_map/all_to_all | solution.py:25
  133.3 21.9 %copy-start.3 = (bf16[192,3072]{1,0:T(8,128)(2,1)S(1)}, bf16[192,3072]{1,0:T(8,128)(2,1)}, u32[]{:S(2)}) copy-start(bf16[192,3072]{1,0:T(8,128)(2,1)} %copy-done.2) | copy-start | bytes 3538948
  133.3 21.9 %copy-start.10 = (bf16[192,3072]{1,0:T(8,128)(2,1)S(1)}, bf16[192,3072]{1,0:T(8,128)(2,1)}, u32[]{:S(2)}) copy-start(bf16[192,3072]{1,0:T(8,128)(2,1)} %copy-done.9) | copy-start | bytes 3538948
  133.3 20.3 %collective-permute-start.7 = (bf16[384,128]{1,0:T(8,128)(2,1)S(1)}, bf16[384,128]{1,0:T(8,128)(2,1)S(1)}, u32[]{:S(2)}, u32[]{:S(2)}) collective-permute-start(bf16[384,128]{1,0:T(8,128)(2,1)S(1)} %add_convert_fusion.2), channel_id=1, source_target_pairs={{0,1},{1,0},{2,3},{3,2},{4,5},{5,4},{6,7},{7,6},{8,9},{9,8},{10,11... | collective-permute-start | bytes 294920 | tf_op jit(solution)/shard_map/ppermute | solution.py:63
  153.6 4.7 %collective-permute-start.8 = (bf16[384,128]{1,0:T(8,128)(2,1)S(1)}, bf16[384,128]{1,0:T(8,128)(2,1)S(1)}, u32[]{:S(2)}, u32[]{:S(2)}) collective-permute-start(bf16[384,128]{1,0:T(8,128)(2,1)S(1)} %add_convert_fusion.1), channel_id=1, source_target_pairs={{0,2},{1,3},{2,0},{3,1},{4,6},{5,7},{6,4},{7,5},{8,10},{9,11},{10,... | collective-permute-start | bytes 294920 | tf_op jit(solution)/shard_map/ppermute | solution.py:63
  158.4 6.2 %copy-start.6 = (bf16[384,512]{1,0:T(8,128)(2,1)S(1)}, bf16[384,512]{1,0:T(8,128)(2,1)}, u32[]{:S(2)}) copy-start(bf16[384,512]{1,0:T(8,128)(2,1)} %copy-done.4) | copy-start | bytes 1179652
  158.4 6.2 %copy-start.8 = (bf16[384,512]{1,0:T(8,128)(2,1)S(1)}, bf16[384,512]{1,0:T(8,128)(2,1)}, u32[]{:S(2)}) copy-start(bf16[384,512]{1,0:T(8,128)(2,1)} %get-tuple-element.7.refs_9_) | copy-start | bytes 1179652
  158.4 6.1 %collective-permute-start.9 = (bf16[384,128]{1,0:T(8,128)(2,1)S(1)}, bf16[384,128]{1,0:T(8,128)(2,1)S(1)}, u32[]{:S(2)}, u32[]{:S(2)}) collective-permute-start(bf16[384,128]{1,0:T(8,128)(2,1)S(1)} %add_convert_fusion), channel_id=1, source_target_pairs={{0,6},{1,7},{2,4},{3,5},{4,2},{5,3},{6,0},{7,1},{8,14},{9,15},{10,... | collective-permute-start | bytes 294920 | tf_op jit(solution)/shard_map/ppermute | solution.py:63
  164.6 13.1 %copy-start.1 = (bf16[1,1,1,3072,512]{4,3,2,1,0:T(8,128)(2,1)S(1)}, bf16[1,1,1,3072,512]{4,3,2,1,0:T(8,128)(2,1)}, u32[]{:S(2)}) copy-start(bf16[1,1,1,3072,512]{4,3,2,1,0:T(8,128)(2,1)} %param.12) | copy-start | bytes 9437188

commit v4 on v3

--- a/solution.py
+++ b/solution.py
@@ -171,9 +171,224 @@
             pltpu.VMEM((3, count, units), BF),
             pltpu.SemaphoreType.DMA((10,)),
         ],
-        compiler_params=pltpu.CompilerParams(vmem_limit_bytes=32 << 20),
+        compiler_params=pltpu.CompilerParams(vmem_limit_bytes=20 << 20),
         name="finish",
     )(dp_index.reshape(1), sums, *squares, *rows16, *grads)
+
+
+ANYWHERE = pl.BlockSpec(memory_space=pl.ANY)
+IN_SMEM = pl.BlockSpec(memory_space=pltpu.SMEM)
+
+
+def pick_slots(own_expert, routes, mix, inputs, grads):
+    micro, _, tokens = routes.shape
+    width = inputs.shape[1]
+    block = width // 4
+
+    def kernel(expert_ref, routes_ref, mix_ref, inputs_ref, grads_ref, picked_ref, scaled_ref, w_ref):
+        expert = expert_ref[0]
+        filler = jnp.zeros((8 - micro, tokens), F32)
+        first = routes_ref[:, 0, :] == expert
+        second = routes_ref[:, 1, :] == expert
+        hit = jnp.where(first | second, 1.0, 0.0)
+        weight = jnp.where(first, mix_ref[:, 0, :], 0.0) + jnp.where(second, mix_ref[:, 1, :], 0.0)
+        earlier = lax.broadcasted_iota(jnp.int32, (tokens, tokens), 0) < lax.broadcasted_iota(
+            jnp.int32, (tokens, tokens), 1
+        )
+        counted = jnp.concatenate([hit, filler]).astype(BF)
+        rank = times(counted, jnp.where(earlier, 1.0, 0.0).astype(BF))[:micro]
+        place = jnp.where(hit > 0.0, rank, -1.0)
+        slot = lax.broadcasted_iota(jnp.int32, (CAP, tokens), 0).astype(F32)
+        for m in range(micro):
+            chosen = slot == place[m : m + 1]
+            pick = jnp.where(chosen, 1.0, 0.0).astype(BF)
+            by_slot = jnp.sum(jnp.where(chosen, weight[m : m + 1], 0.0), axis=1, keepdims=True)
+            source = pl.ds(m * tokens, tokens)
+            target = pl.ds(m * CAP, CAP)
+            picked_ref[target, :] = times(pick, inputs_ref[source, :]).astype(BF)
+            scaled_ref[target, :] = (by_slot * times(pick, grads_ref[source, :])).astype(BF)
+            w_ref[target, :] = jnp.broadcast_to(by_slot, (CAP, 128))
+
+    def whole(shape):
+        return pl.BlockSpec(shape, lambda d: (0,) * len(shape))
+
+    return pl.pallas_call(
+        kernel,
+        grid=(width // block,),
+        out_shape=(
+            jax.ShapeDtypeStruct((micro * CAP, width), BF),
+            jax.ShapeDtypeStruct((micro * CAP, width), BF),
+            jax.ShapeDtypeStruct((micro * CAP, 128), F32),
+        ),
+        in_specs=[
+            IN_SMEM,
+            whole(routes.shape),
+            whole(mix.shape),
+            pl.BlockSpec((micro * tokens, block), lambda d: (0, d)),
+            pl.BlockSpec((micro * tokens, block), lambda d: (0, d)),
+        ],
+        out_specs=(
+            pl.BlockSpec((micro * CAP, block), lambda d: (0, d)),
+            pl.BlockSpec((micro * CAP, block), lambda d: (0, d)),
+            whole((micro * CAP, 128)),
+        ),
+        name="pick_slots",
+    )(own_expert.reshape(1), routes, mix, inputs, grads)
+
+
+def experts(gate, up, down, grads_both, copies, inputs_both=None, forward=None, right=None):
+    fresh = forward is None
+    slots, width = grads_both[0].shape
+    count = 2 * slots
+    units = gate.shape[1]
+    columns = width // copies
+    cuts = 3
+    part = width // cuts
+    operands = [*grads_both, down, gate, up] + ([*inputs_both] if fresh else [*forward, right])
+    halves_shape = (MICRO, copies, CAP, columns)
+    square = (count, units)
+    if fresh:
+        results = [(square, F32), (square, F32), (square, BF)]
+    else:
+        results = [(square, BF), (square, BF), ((count, 2 * R), BF)]
+    results += [(halves_shape, F32), (halves_shape, BF)]
+
+    def kernel(*refs):
+        ins, outs = (refs[: len(operands)], refs[len(operands) : len(operands) + len(results)])
+        rest = list(refs[len(operands) + len(results) :])
+        grads_v, down_v, gate_v, up_v, gg_v, gu_v, own_v, par_v = rest[:8]
+        in_done, out_done = rest[8:10]
+        more = rest[10:]
+        moves = {}
+        used = [0]
+
+        def load(key, source, target):
+            moves[key] = pltpu.make_async_copy(source, target, in_done.at[used[0]])
+            moves[key].start()
+            used[0] += 1
+
+        def load_rows(name, pair, target, d):
+            for i in range(2):
+                load(
+                    (name, i, d),
+                    pair[i].at[:, pl.ds(d * part, part)],
+                    target.at[d, pl.ds(i * slots, slots)],
+                )
+
+        def load_grads(d):
+            load_rows("grads", ins[:2], grads_v, d)
+            load(("down", 0, d), ins[2].at[:, pl.ds(d * part, part)], down_v.at[d])
+
+        def load_weight(name, source, target, d):
+            load((name, 0, d), source.at[pl.ds(d * part, part)], target.at[pl.ds(d * part, part)])
+
+        if fresh:
+            rows_v, slope_v, silu_v, hidden_v = more
+            for d in range(cuts):
+                load_rows("rows", ins[5:7], rows_v, d)
+                load_weight("gate", ins[3], gate_v, d)
+                load_weight("up", ins[4], up_v, d)
+            for d in range(cuts):
+                load_grads(d)
+        else:
+            slope_v, silu_v, hidden_v, right_v, sums_v = more
+            for d in range(cuts):
+                load_grads(d)
+            for i, target in enumerate((slope_v, silu_v, hidden_v, right_v)):
+                load(("forward", i, 0), ins[5 + i], target)
+            for d in range(cuts):
+                load_weight("gate", ins[3], gate_v, d)
+                load_weight("up", ins[4], up_v, d)
+
+        def arrive(*keys):
+            for key in keys:
+                moves[key].wait()
+
+        stores = []
+
+        def store(source, target):
+            move = pltpu.make_async_copy(source, target, out_done.at[len(stores)])
+            move.start()
+            stores.append(move)
+
+        if fresh:
+            for d in range(cuts):
+                arrive(("rows", 0, d), ("rows", 1, d), ("gate", 0, d))
+                held = pl.ds(d * part, part)
+                term = times(rows_v[d], gate_v[held, :])
+                slope_v[...] = term if d == 0 else slope_v[...] + term
+                arrive(("up", 0, d))
+                term = times(rows_v[d], up_v[held, :])
+                silu_v[...] = term if d == 0 else silu_v[...] + term
+            pre_gate, pre_up = (slope_v[...], silu_v[...])
+            sigmoid = 1.0 / (1.0 + jnp.exp(-pre_gate))
+            silu = pre_gate * sigmoid
+            hidden_v[...] = (silu * pre_up).astype(BF)
+            slope_v[...] = pre_up * sigmoid * (1.0 + pre_gate * (1.0 - sigmoid))
+            silu_v[...] = silu
+            store(slope_v, outs[0])
+            store(silu_v, outs[1])
+            store(hidden_v, outs[2])
+        grad_hidden = None
+        for d in range(cuts):
+            arrive(("grads", 0, d), ("grads", 1, d), ("down", 0, d))
+            term = times(grads_v[d], down_v[d], 1, 1)
+            grad_hidden = term if d == 0 else grad_hidden + term
+        if not fresh:
+            arrive(*[("forward", i, 0) for i in range(4)])
+        gg_v[...] = (grad_hidden * slope_v[...]).astype(BF)
+        gu_v[...] = (grad_hidden * silu_v[...]).astype(BF)
+        if not fresh:
+            store(gg_v, outs[0])
+            store(gu_v, outs[1])
+            right16 = right_v[...].astype(BF)
+            of_inputs = times(gg_v[...], right16[0], 1, 1) + times(gu_v[...], right16[1], 1, 1)
+            of_grads = times(hidden_v[...], right16[2], 1, 1)
+            sums_v[...] = jnp.concatenate([of_inputs, of_grads], axis=1).astype(BF)
+            store(sums_v, outs[2])
+            for d in range(cuts):
+                arrive(("gate", 0, d), ("up", 0, d))
+
+        def column(c, carry):
+            held = pl.ds(pl.multiple_of(c * columns, columns), columns)
+            total = times(gg_v[...], gate_v[held, :], 1, 1) + times(gu_v[...], up_v[held, :], 1, 1)
+            for m in range(MICRO):
+                own_v[m, c] = total[m * CAP : (m + 1) * CAP]
+                par_v[m, c] = total[slots + m * CAP : slots + (m + 1) * CAP].astype(BF)
+            return carry
+
+        lax.fori_loop(0, copies, column, 0)
+        store(own_v, outs[3])
+        store(par_v, outs[4])
+        for move in stores:
+            move.wait()
+
+    scratch = [
+        pltpu.VMEM((cuts, count, part), BF),
+        pltpu.VMEM((cuts, units, part), BF),
+        pltpu.VMEM((width, units), BF),
+        pltpu.VMEM((width, units), BF),
+        pltpu.VMEM(square, BF),
+        pltpu.VMEM(square, BF),
+        pltpu.VMEM(halves_shape, F32),
+        pltpu.VMEM(halves_shape, BF),
+        pltpu.SemaphoreType.DMA((10 * cuts,)),
+        pltpu.SemaphoreType.DMA((5,)),
+    ]
+    if fresh:
+        scratch += [pltpu.VMEM((cuts, count, part), BF)]
+    scratch += [pltpu.VMEM(square, F32), pltpu.VMEM(square, F32), pltpu.VMEM(square, BF)]
+    if not fresh:
+        scratch += [pltpu.VMEM(right.shape, F32), pltpu.VMEM((count, 2 * R), BF)]
+    return pl.pallas_call(
+        kernel,
+        out_shape=tuple(jax.ShapeDtypeStruct(*result) for result in results),
+        in_specs=[ANYWHERE] * len(operands),
+        out_specs=(ANYWHERE,) * len(results),
+        scratch_shapes=scratch,
+        compiler_params=pltpu.CompilerParams(vmem_limit_bytes=44 << 20),
+        name="experts_first" if fresh else "experts_last",
+    )(*operands)
 
 
 def side_by_side(pieces):
@@ -185,10 +400,10 @@
 
     return pl.pallas_call(
         kernel,
-        grid=(micro,),
+        grid=(micro, 2),
         out_shape=jax.ShapeDtypeStruct((micro, tokens, copies * columns), pieces.dtype),
-        in_specs=[pl.BlockSpec((1, copies, tokens, columns), lambda m: (m, 0, 0, 0))],
-        out_specs=pl.BlockSpec((1, tokens, copies * columns), lambda m: (m, 0, 0)),
+        in_specs=[pl.BlockSpec((1, copies, tokens // 2, columns), lambda m, h: (m, 0, h, 0))],
+        out_specs=pl.BlockSpec((1, tokens // 2, copies * columns), lambda m, h: (m, h, 0)),
         name="side_by_side",
     )(pieces)
 
@@ -201,7 +416,7 @@
     replicas = lax.axis_size("dp")
     dp_index = lax.axis_index("dp")
     gate, up, down = (w_gate[0, 0, 0], w_up[0, 0, 0], w_down[0, 0, 0])
-    right = q_prev[0, 0, 0].astype(BF)
+    right = q_prev[0, 0, 0].transpose(0, 2, 1)
     copies = peers // EXPERTS
     tokens = saved_inputs.shape[2]
     rows = MICRO * tokens
@@ -212,41 +427,25 @@
     own_inputs = saved_inputs[0].reshape(rows, D)
     top_rows = top_grad.reshape(rows, D)
     rank = slots_of(routes[0])
-    mix = mix_weights[0].reshape(rows, 2)
-    micro_start = (jnp.arange(MICRO, dtype=jnp.int32) * CAP)[:, None, None]
-    own_ids = jnp.where(routes[0] == major, micro_start + rank, -1).reshape(rows, 2)
-    first, second = hit_table(own_ids, slots)
-    own_pick = (first | second).astype(BF)
-    weight = jnp.sum(
-        jnp.where(first, mix[None, :, 0], 0.0) + jnp.where(second, mix[None, :, 1], 0.0),
-        axis=1,
-        keepdims=True,
-    )
     part_ids = lax.dynamic_index_in_dim(routes[0] * CAP + rank, major, 0, keepdims=False)
     first, second = hit_table(part_ids, EXPERTS * CAP)
     part_pick = (first | second).astype(BF)
 
-    own_slots = times(own_pick, own_inputs).astype(BF)
+    own_slots, own_grads, slot_weights = pick_slots(
+        major,
+        routes[0].transpose(0, 2, 1),
+        mix_weights[0].transpose(0, 2, 1),
+        own_inputs,
+        top_rows,
+    )
     inputs_both = (own_slots, swap_cores(own_slots))
-    inputs = jnp.concatenate(inputs_both)
-    pre_gate = times(inputs, gate)
-    pre_up = times(inputs, up)
-    sigmoid_gate = jax.nn.sigmoid(pre_gate)
-    silu_gate = pre_gate * sigmoid_gate
-    hidden = (silu_gate * pre_up).astype(BF)
-    slope = pre_up * sigmoid_gate * (1.0 + pre_gate * (1.0 - sigmoid_gate))
-
-    def phase(own_rows, base):
-        own_grads = (weight * own_rows).astype(BF)
-        grads_both = (own_grads, swap_cores(own_grads))
-        grad_rows = jnp.concatenate(grads_both)
-        grad_hidden = times(grad_rows, down, 1, 1)
-        grad_gate = (grad_hidden * slope).astype(BF)
-        grad_up = (grad_hidden * silu_gate).astype(BF)
-        partial = times(grad_gate, gate, 1, 1) + times(grad_up, up, 1, 1)
-        other = swap_cores(partial[slots:].astype(BF))
-        mine = partial[:slots] + other.astype(F32)
-        mine = mine.astype(BF).reshape(MICRO, CAP, copies, columns).transpose(0, 2, 1, 3)
+    *forward, own_half, other_half = experts(
+        gate, up, down, (own_grads, swap_cores(own_grads)), copies, inputs_both=inputs_both
+    )
+
+    def reduced(own_half, other_half, base):
+        other = swap_cores(other_half)
+        mine = (own_half + other.astype(F32)).astype(BF)
         pieces = exchange(mine.reshape(peers, CAP, columns))
         summed = jnp.sum(pieces.astype(F32).reshape(EXPERTS, copies, CAP, columns), axis=1)
         share = times(
@@ -257,29 +456,31 @@
             lax.Precision.HIGHEST,
         )
         part = (base.astype(F32) + share).astype(BF)
-        return part, grads_both, grad_gate, grad_up
+        return part
 
     top_part = lax.dynamic_slice(
         top_grad, (major, 0, minor * columns), (1, tokens, columns)
     ).reshape(tokens, columns)
-    part, _, _, _ = phase(times(own_pick, top_rows), top_part)
+    part = reduced(own_half, other_half, top_part)
     incoming = lax.ppermute(part, "pipe", [(i, i - 1) for i in range(1, sections)])
     base = jnp.where(last, top_part, incoming)
     listed = times(part_pick, base).astype(BF).reshape(EXPERTS, 1, CAP, columns)
     pieces = jnp.broadcast_to(listed, (EXPERTS, copies, CAP, columns))
     own_rows = exchange(pieces.reshape(peers, CAP, columns))
     own_rows = own_rows.reshape(MICRO, copies, CAP, columns).transpose(0, 2, 1, 3)
-    part, grads_both, grad_gate, grad_up = phase(own_rows.reshape(slots, D).astype(F32), base)
+    own_grads = (slot_weights[:, :1] * own_rows.reshape(slots, D).astype(F32)).astype(BF)
+    grads_both = (own_grads, swap_cores(own_grads))
+    grad_gate, grad_up, sums, own_half, other_half = experts(
+        gate, up, down, grads_both, copies, forward=forward, right=right
+    )
+    part = reduced(own_half, other_half, base)
     produced = exchange(jnp.broadcast_to(part, (peers, tokens, columns)))
     produced = side_by_side(produced.reshape(MICRO, copies, tokens, columns))
 
-    sums = jnp.concatenate(
-        [times(grad_gate, right[0]) + times(grad_up, right[1]), times(hidden, right[2])], axis=1
-    )
-    rounded = sums.astype(BF)
-    other = swap_cores(rounded)
-    sums = rounded.astype(F32) + jnp.concatenate([other[slots:], other[:slots]]).astype(F32)
+    other = swap_cores(sums)
+    sums = sums.astype(F32) + jnp.concatenate([other[slots:], other[:slots]]).astype(F32)
     sums = add_copies(sums, copies)
+    inputs = jnp.concatenate(inputs_both)
     grad_rows = jnp.concatenate(grads_both)
     squares = (
         times(inputs, inputs, 1, 1),
@@ -291,7 +492,7 @@
         sums,
         squares,
         (*inputs_both, *grads_both),
-        (grad_gate, grad_up, hidden),
+        (grad_gate, grad_up, forward[2]),
         replicas * rows,
     )
     return (

time: 179 us -> 191 us (1.067)
  Pallas kernels: 13.1 us -> 42.8 us
  matrix products: 33.1 us -> 9.95 us
  blocking collectives: 20.8 us -> 0 us
  waiting for transfers between devices: 69.1 us -> 80.4 us
  local copies, waits for them, and re-layouts: 8.43 us -> 16.7 us
  other arithmetic: 4.32 us -> 8.23 us
  starting transfers between devices: 27.5 us -> 31 us
    pallas_call x1 -> x4, Pallas kernels: 3.59 us -> 33.2 us  [the longest x2 22.9 us: experts(): pl.pallas_call(kernel, out_shape=tuple((jax.ShapeDtypeStruct(*result) for...]
    dot_general x19 -> x6, matrix products: 33.1 us -> 9.95 us  [times(): lax.dot_general(a, b, (((ca,), (cb,)), ((), ())), preferred_element_type=...]
    all_to_all x1 -> x0, blocking collectives: 20.8 us -> none  [exchange(): return lax.all_to_all(pieces, 'expert', 0, 0, tiled=True)]
    all_to_all x3 -> x4, waiting for transfers between devices: 37.6 us -> 46.8 us  [exchange(): return lax.all_to_all(pieces, 'expert', 0, 0, tiled=True)]
    unnamed x51 -> x46, local copies, waits for them, and re-layouts: 2.5 us -> 9.08 us
    ppermute x6, waiting for transfers between devices: 8.5 us -> 13.8 us  [swap_cores(): return lax.ppermute(value, 'dp', [(0, 1), (1, 0)])]
    all_to_all x3 -> x4, starting transfers between devices: 18.3 us -> 22.9 us  [exchange(): return lax.all_to_all(pieces, 'expert', 0, 0, tiled=True)]
    convert_element_type x4 -> x3, other arithmetic: 0.89 us -> 4.47 us  [the longest x2 4.22 us: reduced(): mine = (own_half + other.astype(F32)).astype(BF)]
  transfers between devices with their start and end apart: 13 -> 14, of which waited for: 10 -> 12; matrix products, arithmetic and copies ran while one was open for 12% -> 10% of each run, Pallas kernels for 5% -> 5%
where the time goes in v4:
time: 191 us; the launch traced here: 190 us
  waiting for transfers between devices  80.4 us (42%)
  Pallas kernels  42.8 us (22%)
  starting transfers between devices  31 us (16%)
  local copies, waits for them, and re-layouts  16.7 us (9%)
  matrix products  9.95 us (5%)
  other arithmetic  8.23 us (4%)
    all_to_all x4, waiting for transfers between devices, exchange(): return lax.all_to_all(pieces, 'expert', 0, 0, tiled=True)  46.8 us
    pallas_call x2, Pallas kernels, experts(): pl.pallas_call(kernel, out_shape=tuple((jax.ShapeDtypeStruct(*result) for...  22.9 us
    all_to_all x4, starting transfers between devices, exchange(): return lax.all_to_all(pieces, 'expert', 0, 0, tiled=True)  22.9 us
    ppermute x6, waiting for transfers between devices, swap_cores(): return lax.ppermute(value, 'dp', [(0, 1), (1, 0)])  13.8 us
    ppermute x3, waiting for transfers between devices, add_copies(): other = lax.ppermute(rounded, 'expert', route)  13.6 us
    dot_general x6, matrix products, times(): lax.dot_general(a, b, (((ca,), (cb,)), ((), ())), preferred_element_type=...  9.95 us
    pallas_call x1, Pallas kernels, finish(): pl.pallas_call(kernel, out_shape=(jax.ShapeDtypeStruct((3, R, units), F32...  9.56 us
    unnamed x46, local copies, waits for them, and re-layouts  9.08 us
  transfers between devices with their start and end apart: 14, of which 12 were waited for; matrix products, arithmetic and copies ran while one was open for 10% of the time, Pallas kernels for 5%

profile of v4, /device:TPU:0, one launch (start us, length us, event | category | flops | bytes accessed | tf_op | source)
XLA Modules:
  0.0 190.0 jit_solution(11055695300194900379)
XLA Ops:
  0.6 4.8 %pick_slots.1 = (bf16[192,3072]{1,0:T(8,128)(2,1)}, bf16[192,3072]{1,0:T(8,128)(2,1)}, f32[192,128]{1,0:T(8,128)}) custom-call(s32[1]{0:T(128)} %bitcast.7.expert_ref, s32[4,2,64]{2,1,0:T(2,128)} %bitcast.83, f32[4,2,64]{2,1,0:T(2,128)} %bitcast.85, bf16[256,3072]{1,0:T(8,128)(2,1)} %bitcast.77, bf16[256,3072]{1,0:T(8,128)(2,1)} %bitcast.75), custom_call_target="tpu_custom_call" | custom-call | tf_op jit(solution)/shard_map/pick_slots/pallas_call | solution.py:215
  6.0 2.5 %collective-permute-done.refs_1_ = bf16[192,3072]{1,0:T(8,128)(2,1)S(1)} collective-permute-done((bf16[192,3072]{1,0:T(8,128)(2,1)}, bf16[192,3072]{1,0:T(8,128)(2,1)S(1)}, u32[]{:S(2)}, u32[]{:S(2)}) %collective-permute-start) | collective-permute-done | bytes 1179680 | tf_op jit(solution)/shard_map/ppermute | solution.py:21
  8.5 1.7 collective-permute-done.1.refs_6_.refs_4_
  10.2 1.3 copy-done
  11.5 1.3 copy-done.7
  12.7 11.9 %experts_first.1 = (f32[384,512]{1,0:T(8,128)S(1)}, f32[384,512]{1,0:T(8,128)S(1)}, bf16[384,512]{1,0:T(8,128)(2,1)S(1)}, f32[4,8,48,384]{3,2,1,0:T(8,128)S(1)}, bf16[4,8,48,384]{3,2,1,0:T(8,128)(2,1)S(1)}) custom-call(bf16[192,3072]{1,0:T(8,128)(2,1)S(1)} %copy-done.7, bf16[192,3072]{1,0:T(8,128)(2,1)S(1)} %collective-permute-done.refs_1_, ...), custom_call_target="tpu_custom_call" | custom-call | tf_op jit(solution)/shard_map/experts_first/pallas_call | solution.py:383
  24.9 2.7 %collective-permute-done.2 = bf16[4,8,48,384]{3,2,1,0:T(8,128)(2,1)S(1)} collective-permute-done((bf16[4,8,48,384]{3,2,1,0:T(8,128)(2,1)S(1)}, bf16[4,8,48,384]{3,2,1,0:T(8,128)(2,1)S(1)}, u32[]{:S(2)}, u32[]{:S(2)}) %collective-permute-start.2) | collective-permute-done | bytes 1179680 | tf_op jit(solution)/shard_map/ppermute | solution.py:21
  27.6 1.3 add_convert_fusion.1
  28.9 9.5 %all-to-all-start = ((bf16[32,48,384]{2,1,0:T(8,128)(2,1)}), bf16[32,48,384]{2,1,0:T(8,128)(2,1)S(1)}, u32[]{:S(2)}, u32[]{:S(2)}) async-start(bf16[32,48,384]{2,1,0:T(8,128)(2,1)} %bitcast.73), calls=%async_computation | async-start | bytes 2359296 | tf_op jit(solution)/shard_map/all_to_all | solution.py:25
  39.1 0.9 copy.17
  40.3 0.8 copy.19
  41.0 1.6 constant_dynamic-slice_fusion
  42.6 0.9 copy.22
  43.6 14.3 %all-to-all-done = bf16[32,48,384]{2,1,0:T(8,128)(2,1)S(1)} async-done(((bf16[32,48,384]{2,1,0:T(8,128)(2,1)}), bf16[32,48,384]{2,1,0:T(8,128)(2,1)S(1)}, u32[]{:S(2)}, u32[]{:S(2)}) %all-to-all-start) | async-done | bytes 1179680 | tf_op jit(solution)/shard_map/all_to_all | solution.py:25
  58.1 1.1 fusion.2
  59.2 1.3 collective-permute-start.3
  60.5 6.2 %collective-permute-done.3 = bf16[64,384]{1,0:T(8,128)(2,1)S(1)} collective-permute-done((bf16[64,384]{1,0:T(8,128)(2,1)S(1)}, bf16[64,384]{1,0:T(8,128)(2,1)S(1)}, u32[]{:S(2)}, u32[]{:S(2)}) %collective-permute-start.3) | collective-permute-done | bytes 49184 | tf_op jit(solution)/shard_map/ppermute | solution.py:465
  66.7 1.0 convolution_convert_fusion
  67.7 1.1 broadcast_in_dim.18
  68.8 3.9 %all-to-all-start.1 = ((bf16[32,48,384]{2,1,0:T(8,128)(2,1)}), bf16[32,48,384]{2,1,0:T(8,128)(2,1)S(1)}, u32[]{:S(2)}, u32[]{:S(2)}) async-start(bf16[32,48,384]{2,1,0:T(8,128)(2,1)} %bitcast.72), calls=%async_computation.1 | async-start | bytes 2359296 | tf_op jit(solution)/shard_map/all_to_all | solution.py:25
  72.7 1.0 slice_reduce_fusion
  73.7 16.3 %all-to-all-done.1 = bf16[32,48,384]{2,1,0:T(8,128)(2,1)S(1)} async-done(((bf16[32,48,384]{2,1,0:T(8,128)(2,1)}), bf16[32,48,384]{2,1,0:T(8,128)(2,1)S(1)}, u32[]{:S(2)}, u32[]{:S(2)}) %all-to-all-start.1) | async-done | bytes 1179680 | tf_op jit(solution)/shard_map/all_to_all | solution.py:25
  92.0 2.8 %collective-permute-done.4.refs_1_.refs_6_ = bf16[192,3072]{1,0:T(8,128)(2,1)S(1)} collective-permute-done((bf16[192,3072]{1,0:T(8,128)(2,1)S(1)}, bf16[192,3072]{1,0:T(8,128)(2,1)S(1)}, u32[]{:S(2)}, u32[]{:S(2)}) %collective-permute-start.4) | collective-permute-done | bytes 1179680 | tf_op jit(solution)/shard_map/ppermute | solution.py:21
  94.8 11.1 %experts_last.1 = (bf16[384,512]{1,0:T(8,128)(2,1)S(1)}, bf16[384,512]{1,0:T(8,128)(2,1)S(1)}, bf16[384,128]{1,0:T(8,128)(2,1)S(1)}, f32[4,8,48,384]{3,2,1,0:T(8,128)S(1)}, bf16[4,8,48,384]{3,2,1,0:T(8,128)(2,1)}) custom-call(bf16[192,3072]{1,0:T(8,128)(2,1)S(1)} %multiply_convert_fusion.refs_0_.refs_5_, ...), custom_call_target="tpu_custom_call" | custom-call | tf_op jit(solution)/shard_map/experts_last/pallas_call | solution.py:383
  105.9 1.4 copy-done.4
  107.3 0.7 copy-done.11
  108.1 0.7 copy-done.13
  109.6 2.9 %collective-permute-done.5 = bf16[4,8,48,384]{3,2,1,0:T(8,128)(2,1)S(1)} collective-permute-done((bf16[4,8,48,384]{3,2,1,0:T(8,128)(2,1)}, bf16[4,8,48,384]{3,2,1,0:T(8,128)(2,1)S(1)}, u32[]{:S(2)}, u32[]{:S(2)}) %collective-permute-start.5) | collective-permute-done | bytes 1179680 | tf_op jit(solution)/shard_map/ppermute | solution.py:21
  112.5 2.9 %add_convert_fusion = bf16[4,8,48,384]{3,2,1,0:T(8,128)(2,1)} fusion(f32[4,8,48,384]{3,2,1,0:T(8,128)} %copy-done.4, bf16[4,8,48,384]{3,2,1,0:T(8,128)(2,1)S(1)} %collective-permute-done.5), kind=kLoop, calls=%fused_computation.4 | loop fusion | flops 1769472 | bytes 4718592 | tf_op jit(solution)/shard_map/convert_element_type | solution.py:448
  115.5 4.8 %all-to-all-start.2 = ((bf16[32,48,384]{2,1,0:T(8,128)(2,1)}), bf16[32,48,384]{2,1,0:T(8,128)(2,1)}, u32[]{:S(2)}, u32[]{:S(2)}) async-start(bf16[32,48,384]{2,1,0:T(8,128)(2,1)} %bitcast.74), calls=%async_computation.2 | async-start | bytes 2359296 | tf_op jit(solution)/shard_map/all_to_all | solution.py:25
  120.4 0.8 copy-done.16
  121.4 1.1 collective-permute-done.6
  123.1 1.6 collective-permute-start.7
  124.8 16.1 %all-to-all-done.2 = bf16[32,48,384]{2,1,0:T(8,128)(2,1)} async-done(((bf16[32,48,384]{2,1,0:T(8,128)(2,1)}), bf16[32,48,384]{2,1,0:T(8,128)(2,1)}, u32[]{:S(2)}, u32[]{:S(2)}) %all-to-all-start.2) | async-done | bytes 1179680 | tf_op jit(solution)/shard_map/all_to_all | solution.py:25
  140.9 1.5 convert_reduce_fusion
  142.4 1.1 add_convert_fusion.5
  143.5 1.4 broadcast_in_dim.19
  144.9 4.7 %all-to-all-start.3 = ((bf16[32,64,384]{2,1,0:T(8,128)(2,1)}), bf16[32,64,384]{2,1,0:T(8,128)(2,1)}, u32[]{:S(2)}, u32[]{:S(2)}) async-start(bf16[32,64,384]{2,1,0:T(8,128)(2,1)} %broadcast_in_dim.19), calls=%async_computation.3 | async-start | bytes 3145728 | tf_op jit(solution)/shard_map/all_to_all | solution.py:25
  149.6 3.9 %fusion.22.refs_0_ = f32[384,384]{1,0:T(8,128)S(1)} fusion(bf16[384,3072]{1,0:T(8,128)(2,1)} %copy-done.17), kind=kOutput, calls=%fused_computation.43 | convolution fusion | flops 905969664 | bytes 2949120 | tf_op jit(solution)/shard_map/dot_general | solution.py:29
  153.5 1.0 add_convert_fusion.3
  154.5 1.7 collective-permute-start.8
  156.2 1.4 fusion.1.refs_1_
  157.6 11.3 %collective-permute-done.8 = bf16[384,128]{1,0:T(8,128)(2,1)S(1)} collective-permute-done((bf16[384,128]{1,0:T(8,128)(2,1)S(1)}, bf16[384,128]{1,0:T(8,128)(2,1)S(1)}, u32[]{:S(2)}, u32[]{:S(2)}) %collective-permute-start.8) | collective-permute-done | bytes 98336 | tf_op jit(solution)/shard_map/ppermute | solution.py:63
  169.0 2.2 %collective-permute-start.9 = (bf16[384,128]{1,0:T(8,128)(2,1)S(1)}, bf16[384,128]{1,0:T(8,128)(2,1)S(1)}, u32[]{:S(2)}, u32[]{:S(2)}) collective-permute-start(bf16[384,128]{1,0:T(8,128)(2,1)S(1)} %add_convert_fusion.2), channel_id=1, source_target_pairs={{0,6},{1,7},{2,4},{3,5},{4,2},{5,3},{6,0},{7,1},{8,14},{9,15},{10,... | collective-permute-start | bytes 294920 | tf_op jit(solution)/shard_map/ppermute | solution.py:63
  171.2 1.4 fusion.refs_2_
  172.6 2.3 %collective-permute-done.9 = bf16[384,128]{1,0:T(8,128)(2,1)S(1)} collective-permute-done((bf16[384,128]{1,0:T(8,128)(2,1)S(1)}, bf16[384,128]{1,0:T(8,128)(2,1)S(1)}, u32[]{:S(2)}, u32[]{:S(2)}) %collective-permute-start.9) | collective-permute-done | bytes 98336 | tf_op jit(solution)/shard_map/ppermute | solution.py:63
  175.0 9.6 %finish.1 = (f32[3,64,512]{2,1,0:T(8,128)}, f32[64,1536]{1,0:T(8,128)}) custom-call(s32[1]{0:T(128)} %bitcast.30.dp_ref, f32[384,128]{1,0:T(8,128)S(1)} %convert_add_fusion.sums_ref, f32[384,384]{1,0:T(8,128)S(1)} %fusion.22.refs_0_, f32[384,384]{1,0:T(8,128)S(1)} %fusion.1.refs_1_, f32[384,384]{1,0:T(8,128)S(1)} %fusion.refs_2_, ...), custom_call_target="tpu_custom_call" | custom-call | tf_op jit(solution)/shard_map/finish/pallas_call | solution.py:157
  184.6 5.5 %side_by_side.1 = bf16[4,64,3072]{2,1,0:T(8,128)(2,1)} custom-call(bf16[4,8,64,384]{3,2,1,0:T(8,128)(2,1)} %bitcast.28.pieces_ref), custom_call_target="tpu_custom_call" | custom-call | tf_op jit(solution)/shard_map/side_by_side/pallas_call | solution.py:401
  (60 shorter events, 5.6 us)
Async XLA Ops:
  5.5 3.1 %collective-permute-start = (bf16[192,3072]{1,0:T(8,128)(2,1)}, bf16[192,3072]{1,0:T(8,128)(2,1)S(1)}, u32[]{:S(2)}, u32[]{:S(2)}) collective-permute-start(bf16[192,3072]{1,0:T(8,128)(2,1)} %get-tuple-element.18.refs_0_), channel_id=1, source_target_pairs={{0,64},{64,0},{1,65},{65,1},{2,66},{66,2},{3,67},{67,3},{4,68},{68... | collective-permute-start | bytes 3538952 | tf_op jit(solution)/shard_map/ppermute | solution.py:21
  5.5 4.7 %collective-permute-start.1 = (bf16[192,3072]{1,0:T(8,128)(2,1)}, bf16[192,3072]{1,0:T(8,128)(2,1)S(1)}, u32[]{:S(2)}, u32[]{:S(2)}) collective-permute-start(bf16[192,3072]{1,0:T(8,128)(2,1)} %get-tuple-element.19.refs_5_.refs_3_), channel_id=1, source_target_pairs={{0,64},{64,0},{1,65},{65,1},{2,66},{66,2},{3,67},{67,3},{4,68},{68... | collective-permute-start | bytes 3538952 | tf_op jit(solution)/shard_map/ppermute | solution.py:21
  10.2 1.3 copy-start
  11.5 1.3 copy-start.7
  24.6 4.2 %copy-start.8 = (f32[384,512]{1,0:T(8,128)}, f32[384,512]{1,0:T(8,128)S(1)}, u32[]{:S(2)}) copy-start(f32[384,512]{1,0:T(8,128)S(1)} %get-tuple-element.24.refs_6_) | copy-start | bytes 2359300
  24.6 70.2 %copy-start.5 = (bf16[384,512]{1,0:T(8,128)(2,1)}, bf16[384,512]{1,0:T(8,128)(2,1)S(1)}, u32[]{:S(2)}) copy-start(bf16[384,512]{1,0:T(8,128)(2,1)S(1)} %get-tuple-element.25.refs_7_.refs_9_) | copy-start | bytes 1179652
  24.6 2.9 %collective-permute-start.2 = (bf16[4,8,48,384]{3,2,1,0:T(8,128)(2,1)S(1)}, bf16[4,8,48,384]{3,2,1,0:T(8,128)(2,1)S(1)}, u32[]{:S(2)}, u32[]{:S(2)}) collective-permute-start(bf16[4,8,48,384]{3,2,1,0:T(8,128)(2,1)S(1)} %get-tuple-element.21), channel_id=1, source_target_pairs={{0,64},{64,0},{1,65},{65,1},{2,66},{66,2},{3,67},{67,3},{4,68},{68... | collective-permute-start | bytes 3538952 | tf_op jit(solution)/shard_map/ppermute | solution.py:21
  28.9 9.5 %copy-start.20 = (s32[1,4,64,2]{2,3,1,0:T(2,128)S(1)}, s32[1,4,64,2]{2,3,1,0:T(2,128)}, u32[]{:S(2)}) copy-start(s32[1,4,64,2]{2,3,1,0:T(2,128)} %param.10) | copy-start | bytes 6148
  28.9 29.0 %all-to-all-start = ((bf16[32,48,384]{2,1,0:T(8,128)(2,1)}), bf16[32,48,384]{2,1,0:T(8,128)(2,1)S(1)}, u32[]{:S(2)}, u32[]{:S(2)}) async-start(bf16[32,48,384]{2,1,0:T(8,128)(2,1)} %bitcast.73), calls=%async_computation | async-start | bytes 2359296 | tf_op jit(solution)/shard_map/all_to_all | solution.py:25
  59.2 7.5 %collective-permute-start.3 = (bf16[64,384]{1,0:T(8,128)(2,1)S(1)}, bf16[64,384]{1,0:T(8,128)(2,1)S(1)}, u32[]{:S(2)}, u32[]{:S(2)}) collective-permute-start(bf16[64,384]{1,0:T(8,128)(2,1)S(1)} %fusion.2), channel_id=1, source_target_pairs={{32,0},{33,1},{34,2},{35,3},{36,4},{37,5},{38,6},{39,7},{40,8},{41... | collective-permute-start | bytes 147464 | tf_op jit(solution)/shard_map/ppermute | solution.py:465
  66.7 2.1 %copy-start.19 = (bf16[64,384]{1,0:T(8,128)(2,1)}, bf16[64,384]{1,0:T(8,128)(2,1)S(1)}, u32[]{:S(2)}) copy-start(bf16[64,384]{1,0:T(8,128)(2,1)S(1)} %collective-permute-done.3) | copy-start | bytes 147460
  68.8 21.3 %all-to-all-start.1 = ((bf16[32,48,384]{2,1,0:T(8,128)(2,1)}), bf16[32,48,384]{2,1,0:T(8,128)(2,1)S(1)}, u32[]{:S(2)}, u32[]{:S(2)}) async-start(bf16[32,48,384]{2,1,0:T(8,128)(2,1)} %bitcast.72), calls=%async_computation.1 | async-start | bytes 2359296 | tf_op jit(solution)/shard_map/all_to_all | solution.py:25
  91.4 3.4 %copy-start.9 = (f32[384,512]{1,0:T(8,128)S(1)}, f32[384,512]{1,0:T(8,128)}, u32[]{:S(2)}) copy-start(f32[384,512]{1,0:T(8,128)} %copy-done.8) | copy-start | bytes 2359300
  91.4 3.4 %copy-start.10 = (f32[1,1,1,3,512,64]{4,5,3,2,1,0:T(8,128)S(1)}, f32[1,1,1,3,512,64]{4,5,3,2,1,0:T(8,128)}, u32[]{:S(2)}) copy-start(f32[1,1,1,3,512,64]{4,5,3,2,1,0:T(8,128)} %param.15) | copy-start | bytes 1179652
  91.7 3.1 %collective-permute-start.4 = (bf16[192,3072]{1,0:T(8,128)(2,1)S(1)}, bf16[192,3072]{1,0:T(8,128)(2,1)S(1)}, u32[]{:S(2)}, u32[]{:S(2)}) collective-permute-start(bf16[192,3072]{1,0:T(8,128)(2,1)S(1)} %multiply_convert_fusion.refs_0_.refs_5_), channel_id=1, source_target_pairs={{0,64},{64,0},{1,65},{65,1},{2,66},{66,2},{3,67},{67,3},{4,68},{68... | collective-permute-start | bytes 3538952 | tf_op jit(solution)/shard_map/ppermute | solution.py:21
  94.8 11.1 %copy-start.2 = (bf16[192,3072]{1,0:T(8,128)(2,1)}, bf16[192,3072]{1,0:T(8,128)(2,1)S(1)}, u32[]{:S(2)}) copy-start(bf16[192,3072]{1,0:T(8,128)(2,1)S(1)} %collective-permute-done.4.refs_1_.refs_6_) | copy-start | bytes 3538948
  105.9 1.4 copy-start.4
  107.3 0.7 copy-start.11
  108.1 0.7 copy-start.13
  108.8 0.6 copy-start.15
  109.4 3.1 %collective-permute-start.5 = (bf16[4,8,48,384]{3,2,1,0:T(8,128)(2,1)}, bf16[4,8,48,384]{3,2,1,0:T(8,128)(2,1)S(1)}, u32[]{:S(2)}, u32[]{:S(2)}) collective-permute-start(bf16[4,8,48,384]{3,2,1,0:T(8,128)(2,1)} %get-tuple-element.27), channel_id=1, source_target_pairs={{0,64},{64,0},{1,65},{65,1},{2,66},{66,2},{3,67},{67,3},{4,68},{68... | collective-permute-start | bytes 3538952 | tf_op jit(solution)/shard_map/ppermute | solution.py:21
  115.4 4.8 %copy-start.1 = (bf16[192,3072]{1,0:T(8,128)(2,1)S(1)}, bf16[192,3072]{1,0:T(8,128)(2,1)}, u32[]{:S(2)}) copy-start(bf16[192,3072]{1,0:T(8,128)(2,1)} %get-tuple-element.19.refs_5_.refs_3_) | copy-start | bytes 3538948
  115.5 25.5 %all-to-all-start.2 = ((bf16[32,48,384]{2,1,0:T(8,128)(2,1)}), bf16[32,48,384]{2,1,0:T(8,128)(2,1)}, u32[]{:S(2)}, u32[]{:S(2)}) async-start(bf16[32,48,384]{2,1,0:T(8,128)(2,1)} %bitcast.74), calls=%async_computation.2 | async-start | bytes 2359296 | tf_op jit(solution)/shard_map/all_to_all | solution.py:25
  120.3 0.9 copy-start.16
  121.2 1.3 collective-permute-start.6
  121.4 1.8 copy-start.17
  123.1 30.4 %collective-permute-start.7 = (bf16[384,128]{1,0:T(8,128)(2,1)}, bf16[384,128]{1,0:T(8,128)(2,1)}, u32[]{:S(2)}, u32[]{:S(2)}) collective-permute-start(bf16[384,128]{1,0:T(8,128)(2,1)} %add_convert_fusion.4), channel_id=1, source_target_pairs={{0,1},{1,0},{2,3},{3,2},{4,5},{5,4},{6,7},{7,6},{8,9},{9,8},{10,11... | collective-permute-start | bytes 294920 | tf_op jit(solution)/shard_map/ppermute | solution.py:63
  144.9 39.7 %all-to-all-start.3 = ((bf16[32,64,384]{2,1,0:T(8,128)(2,1)}), bf16[32,64,384]{2,1,0:T(8,128)(2,1)}, u32[]{:S(2)}, u32[]{:S(2)}) async-start(bf16[32,64,384]{2,1,0:T(8,128)(2,1)} %broadcast_in_dim.19), calls=%async_computation.3 | async-start | bytes 3145728 | tf_op jit(solution)/shard_map/all_to_all | solution.py:25
  149.6 6.6 %copy-start.3 = (bf16[192,3072]{1,0:T(8,128)(2,1)S(1)}, bf16[192,3072]{1,0:T(8,128)(2,1)}, u32[]{:S(2)}) copy-start(bf16[192,3072]{1,0:T(8,128)(2,1)} %copy-done.2) | copy-start | bytes 3538948
  149.6 6.6 %copy-start.18 = (bf16[384,3072]{1,0:T(8,128)(2,1)S(1)}, bf16[384,3072]{1,0:T(8,128)(2,1)}, u32[]{:S(2)}) copy-start(bf16[384,3072]{1,0:T(8,128)(2,1)} %copy-done.17) | copy-start | bytes 7077892
  154.5 14.4 %collective-permute-start.8 = (bf16[384,128]{1,0:T(8,128)(2,1)S(1)}, bf16[384,128]{1,0:T(8,128)(2,1)S(1)}, u32[]{:S(2)}, u32[]{:S(2)}) collective-permute-start(bf16[384,128]{1,0:T(8,128)(2,1)S(1)} %add_convert_fusion.3), channel_id=1, source_target_pairs={{0,2},{1,3},{2,0},{3,1},{4,6},{5,7},{6,4},{7,5},{8,10},{9,11},{10,... | collective-permute-start | bytes 294920 | tf_op jit(solution)/shard_map/ppermute | solution.py:63
  169.0 6.0 %copy-start.6 = (bf16[384,512]{1,0:T(8,128)(2,1)S(1)}, bf16[384,512]{1,0:T(8,128)(2,1)}, u32[]{:S(2)}) copy-start(bf16[384,512]{1,0:T(8,128)(2,1)} %copy-done.5) | copy-start | bytes 1179652
  169.0 6.0 %copy-start.12 = (bf16[384,512]{1,0:T(8,128)(2,1)S(1)}, bf16[384,512]{1,0:T(8,128)(2,1)}, u32[]{:S(2)}) copy-start(bf16[384,512]{1,0:T(8,128)(2,1)} %copy-done.11) | copy-start | bytes 1179652
  169.0 6.0 %copy-start.14 = (bf16[384,512]{1,0:T(8,128)(2,1)S(1)}, bf16[384,512]{1,0:T(8,128)(2,1)}, u32[]{:S(2)}) copy-start(bf16[384,512]{1,0:T(8,128)(2,1)} %copy-done.13) | copy-start | bytes 1179652
  169.0 5.9 %collective-permute-start.9 = (bf16[384,128]{1,0:T(8,128)(2,1)S(1)}, bf16[384,128]{1,0:T(8,128)(2,1)S(1)}, u32[]{:S(2)}, u32[]{:S(2)}) collective-permute-start(bf16[384,128]{1,0:T(8,128)(2,1)S(1)} %add_convert_fusion.2), channel_id=1, source_target_pairs={{0,6},{1,7},{2,4},{3,5},{4,2},{5,3},{6,0},{7,1},{8,14},{9,15},{10,... | collective-permute-start | bytes 294920 | tf_op jit(solution)/shard_map/ppermute | solution.py:63

commit v5 on v4

--- a/solution.py
+++ b/solution.py
@@ -15,6 +15,7 @@
 
 BF = jnp.bfloat16
 F32 = jnp.float32
+IN_SMEM = pl.BlockSpec(memory_space=pltpu.SMEM)
 
 
 def swap_cores(value):
@@ -96,41 +97,20 @@
 def finish(dp_index, sums, squares, rows16, grads, token_total):
     wide = rows16[0].shape[1]
     half = wide // 2
-    count = sums.shape[0]
     units = grads[0].shape[1]
-    height = rows16[0].shape[0]
 
     def kernel(dp_ref, sums_ref, *refs):
-        squares_hbm, rows_hbm, grads_hbm = (refs[:3], refs[3:7], refs[7:10])
+        squares_ref, rows_ref, grads_ref = (refs[:3], refs[3:7], refs[7:10])
         q_ref, basis_ref = refs[10:12]
-        squares_ref, rows_ref, grads_ref, done = refs[12:]
-        moves = [
-            pltpu.make_async_copy(squares_hbm[i], squares_ref.at[i], done.at[i]) for i in range(3)
-        ]
-        moves += [
-            pltpu.make_async_copy(grads_hbm[i], grads_ref.at[i], done.at[3 + i]) for i in range(3)
-        ]
         start = pl.multiple_of(dp_ref[0] * half, half)
-        moves += [
-            pltpu.make_async_copy(
-                rows_hbm[i].at[:, pl.ds(start, half)],
-                rows_ref.at[pl.ds(i * height, height)],
-                done.at[6 + i],
-            )
-            for i in range(4)
-        ]
-        for move in moves:
-            move.start()
         turned = sums_ref[...].T
         of_inputs, of_grads = (turned[:R].astype(BF), turned[R:].astype(BF))
-        for move in moves[:3]:
-            move.wait()
 
         def twice(left, right, cb):
             high, low = halves(right)
             return times(left, high, 1, cb) + times(left, low, 1, cb)
 
-        inputs_inputs, grads_inputs, grads_grads = (squares_ref[i] for i in range(3))
+        inputs_inputs, grads_inputs, grads_grads = (ref[...] for ref in squares_ref)
         along_inputs = twice(of_inputs, inputs_inputs, 0) + twice(of_grads, grads_inputs, 0)
         along_grads = twice(of_inputs, grads_inputs, 1) + twice(of_grads, grads_grads, 0)
         gram = twice(of_inputs, along_inputs, 1) + twice(of_grads, along_grads, 1)
@@ -146,38 +126,22 @@
         scale = 1.0 / math.sqrt(float(token_total))
         along_inputs = times(inverse, along_inputs, 1, 0, exact).astype(BF)
         along_grads = times(inverse, along_grads, 1, 0, exact).astype(BF)
-        for move in moves[3:]:
-            move.wait()
-        q_ref[0] = times(along_inputs, grads_ref[0]) * scale
-        q_ref[1] = times(along_inputs, grads_ref[1]) * scale
-        q_ref[2] = times(along_grads, grads_ref[2]) * scale
-        basis_ref[...] = times(weights, rows_ref[...]) * math.sqrt(float(wide))
-
-    anywhere = pl.BlockSpec(memory_space=pl.ANY)
+        q_ref[0] = times(along_inputs, grads_ref[0][...]) * scale
+        q_ref[1] = times(along_inputs, grads_ref[1][...]) * scale
+        q_ref[2] = times(along_grads, grads_ref[2][...]) * scale
+        rows = jnp.concatenate([ref[:, pl.ds(start, half)] for ref in rows_ref])
+        basis_ref[...] = times(weights, rows) * math.sqrt(float(wide))
+
     return pl.pallas_call(
         kernel,
         out_shape=(
             jax.ShapeDtypeStruct((3, R, units), F32),
             jax.ShapeDtypeStruct((R, half), F32),
         ),
-        in_specs=[
-            pl.BlockSpec(memory_space=pltpu.SMEM),
-            pl.BlockSpec(memory_space=pltpu.VMEM),
-            *[anywhere] * 10,
-        ],
-        scratch_shapes=[
-            pltpu.VMEM((3, count, count), F32),
-            pltpu.VMEM((4 * height, half), BF),
-            pltpu.VMEM((3, count, units), BF),
-            pltpu.SemaphoreType.DMA((10,)),
-        ],
+        in_specs=[IN_SMEM] + [pl.BlockSpec(memory_space=pltpu.VMEM)] * 11,
         compiler_params=pltpu.CompilerParams(vmem_limit_bytes=20 << 20),
         name="finish",
     )(dp_index.reshape(1), sums, *squares, *rows16, *grads)
-
-
-ANYWHERE = pl.BlockSpec(memory_space=pl.ANY)
-IN_SMEM = pl.BlockSpec(memory_space=pltpu.SMEM)
 
 
 def pick_slots(own_expert, routes, mix, inputs, grads):
@@ -197,17 +161,17 @@
         )
         counted = jnp.concatenate([hit, filler]).astype(BF)
         rank = times(counted, jnp.where(earlier, 1.0, 0.0).astype(BF))[:micro]
-        place = jnp.where(hit > 0.0, rank, -1.0)
-        slot = lax.broadcasted_iota(jnp.int32, (CAP, tokens), 0).astype(F32)
-        for m in range(micro):
-            chosen = slot == place[m : m + 1]
-            pick = jnp.where(chosen, 1.0, 0.0).astype(BF)
-            by_slot = jnp.sum(jnp.where(chosen, weight[m : m + 1], 0.0), axis=1, keepdims=True)
-            source = pl.ds(m * tokens, tokens)
-            target = pl.ds(m * CAP, CAP)
-            picked_ref[target, :] = times(pick, inputs_ref[source, :]).astype(BF)
-            scaled_ref[target, :] = (by_slot * times(pick, grads_ref[source, :])).astype(BF)
-            w_ref[target, :] = jnp.broadcast_to(by_slot, (CAP, 128))
+        base = lax.broadcasted_iota(jnp.int32, (micro, tokens), 0).astype(F32) * CAP
+        place = jnp.where(hit > 0.0, rank + base, -1.0)
+        place = jnp.concatenate([place[m : m + 1] for m in range(micro)], axis=1)
+        weight = jnp.concatenate([weight[m : m + 1] for m in range(micro)], axis=1)
+        slot = lax.broadcasted_iota(jnp.int32, (micro * CAP, micro * tokens), 0).astype(F32)
+        chosen = slot == place
+        pick = jnp.where(chosen, 1.0, 0.0).astype(BF)
+        by_slot = jnp.sum(jnp.where(chosen, weight, 0.0), axis=1, keepdims=True)
+        picked_ref[...] = times(pick, inputs_ref[...]).astype(BF)
+        scaled_ref[...] = (by_slot * times(pick, grads_ref[...])).astype(BF)
+        w_ref[...] = jnp.broadcast_to(by_slot, (micro * CAP, 128))
 
     def whole(shape):
         return pl.BlockSpec(shape, lambda d: (0,) * len(shape))
@@ -242,11 +206,9 @@
     count = 2 * slots
     units = gate.shape[1]
     columns = width // copies
-    cuts = 3
-    part = width // cuts
-    operands = [*grads_both, down, gate, up] + ([*inputs_both] if fresh else [*forward, right])
     halves_shape = (MICRO, copies, CAP, columns)
     square = (count, units)
+    operands = [*grads_both, down, gate, up] + ([*inputs_both] if fresh else [*forward, right])
     if fresh:
         results = [(square, F32), (square, F32), (square, BF)]
     else:
@@ -255,138 +217,51 @@
 
     def kernel(*refs):
         ins, outs = (refs[: len(operands)], refs[len(operands) : len(operands) + len(results)])
-        rest = list(refs[len(operands) + len(results) :])
-        grads_v, down_v, gate_v, up_v, gg_v, gu_v, own_v, par_v = rest[:8]
-        in_done, out_done = rest[8:10]
-        more = rest[10:]
-        moves = {}
-        used = [0]
-
-        def load(key, source, target):
-            moves[key] = pltpu.make_async_copy(source, target, in_done.at[used[0]])
-            moves[key].start()
-            used[0] += 1
-
-        def load_rows(name, pair, target, d):
-            for i in range(2):
-                load(
-                    (name, i, d),
-                    pair[i].at[:, pl.ds(d * part, part)],
-                    target.at[d, pl.ds(i * slots, slots)],
-                )
-
-        def load_grads(d):
-            load_rows("grads", ins[:2], grads_v, d)
-            load(("down", 0, d), ins[2].at[:, pl.ds(d * part, part)], down_v.at[d])
-
-        def load_weight(name, source, target, d):
-            load((name, 0, d), source.at[pl.ds(d * part, part)], target.at[pl.ds(d * part, part)])
+        down_ref, gate_ref, up_ref = ins[2:5]
+        own_ref, par_ref = outs[3:]
+
+        def both(pair):
+            return jnp.concatenate([pair[0][...], pair[1][...]])
 
         if fresh:
-            rows_v, slope_v, silu_v, hidden_v = more
-            for d in range(cuts):
-                load_rows("rows", ins[5:7], rows_v, d)
-                load_weight("gate", ins[3], gate_v, d)
-                load_weight("up", ins[4], up_v, d)
-            for d in range(cuts):
-                load_grads(d)
-        else:
-            slope_v, silu_v, hidden_v, right_v, sums_v = more
-            for d in range(cuts):
-                load_grads(d)
-            for i, target in enumerate((slope_v, silu_v, hidden_v, right_v)):
-                load(("forward", i, 0), ins[5 + i], target)
-            for d in range(cuts):
-                load_weight("gate", ins[3], gate_v, d)
-                load_weight("up", ins[4], up_v, d)
-
-        def arrive(*keys):
-            for key in keys:
-                moves[key].wait()
-
-        stores = []
-
-        def store(source, target):
-            move = pltpu.make_async_copy(source, target, out_done.at[len(stores)])
-            move.start()
-            stores.append(move)
-
-        if fresh:
-            for d in range(cuts):
-                arrive(("rows", 0, d), ("rows", 1, d), ("gate", 0, d))
-                held = pl.ds(d * part, part)
-                term = times(rows_v[d], gate_v[held, :])
-                slope_v[...] = term if d == 0 else slope_v[...] + term
-                arrive(("up", 0, d))
-                term = times(rows_v[d], up_v[held, :])
-                silu_v[...] = term if d == 0 else silu_v[...] + term
-            pre_gate, pre_up = (slope_v[...], silu_v[...])
+            gg_ref, gu_ref = refs[len(operands) + len(results) :]
+            inputs = both(ins[5:7])
+            pre_gate = times(inputs, gate_ref[...])
+            pre_up = times(inputs, up_ref[...])
             sigmoid = 1.0 / (1.0 + jnp.exp(-pre_gate))
             silu = pre_gate * sigmoid
-            hidden_v[...] = (silu * pre_up).astype(BF)
-            slope_v[...] = pre_up * sigmoid * (1.0 + pre_gate * (1.0 - sigmoid))
-            silu_v[...] = silu
-            store(slope_v, outs[0])
-            store(silu_v, outs[1])
-            store(hidden_v, outs[2])
-        grad_hidden = None
-        for d in range(cuts):
-            arrive(("grads", 0, d), ("grads", 1, d), ("down", 0, d))
-            term = times(grads_v[d], down_v[d], 1, 1)
-            grad_hidden = term if d == 0 else grad_hidden + term
+            outs[0][...] = pre_up * sigmoid * (1.0 + pre_gate * (1.0 - sigmoid))
+            outs[1][...] = silu
+            outs[2][...] = (silu * pre_up).astype(BF)
+            slope_ref, silu_ref = outs[:2]
+        else:
+            gg_ref, gu_ref, sums_ref = outs[:3]
+            slope_ref, silu_ref, hidden_ref, right_ref = ins[5:9]
+        grad_hidden = times(both(ins[:2]), down_ref[...], 1, 1)
+        gg_ref[...] = (grad_hidden * slope_ref[...]).astype(BF)
+        gu_ref[...] = (grad_hidden * silu_ref[...]).astype(BF)
         if not fresh:
-            arrive(*[("forward", i, 0) for i in range(4)])
-        gg_v[...] = (grad_hidden * slope_v[...]).astype(BF)
-        gu_v[...] = (grad_hidden * silu_v[...]).astype(BF)
-        if not fresh:
-            store(gg_v, outs[0])
-            store(gu_v, outs[1])
-            right16 = right_v[...].astype(BF)
-            of_inputs = times(gg_v[...], right16[0], 1, 1) + times(gu_v[...], right16[1], 1, 1)
-            of_grads = times(hidden_v[...], right16[2], 1, 1)
-            sums_v[...] = jnp.concatenate([of_inputs, of_grads], axis=1).astype(BF)
-            store(sums_v, outs[2])
-            for d in range(cuts):
-                arrive(("gate", 0, d), ("up", 0, d))
+            right16 = right_ref[...].astype(BF)
+            of_inputs = times(gg_ref[...], right16[0], 1, 1) + times(gu_ref[...], right16[1], 1, 1)
+            of_grads = times(hidden_ref[...], right16[2], 1, 1)
+            sums_ref[...] = jnp.concatenate([of_inputs, of_grads], axis=1).astype(BF)
 
         def column(c, carry):
             held = pl.ds(pl.multiple_of(c * columns, columns), columns)
-            total = times(gg_v[...], gate_v[held, :], 1, 1) + times(gu_v[...], up_v[held, :], 1, 1)
+            total = times(gg_ref[...], gate_ref[held, :], 1, 1)
+            total = total + times(gu_ref[...], up_ref[held, :], 1, 1)
             for m in range(MICRO):
-                own_v[m, c] = total[m * CAP : (m + 1) * CAP]
-                par_v[m, c] = total[slots + m * CAP : slots + (m + 1) * CAP].astype(BF)
+                own_ref[m, c] = total[m * CAP : (m + 1) * CAP]
+                par_ref[m, c] = total[slots + m * CAP : slots + (m + 1) * CAP].astype(BF)
             return carry
 
         lax.fori_loop(0, copies, column, 0)
-        store(own_v, outs[3])
-        store(par_v, outs[4])
-        for move in stores:
-            move.wait()
-
-    scratch = [
-        pltpu.VMEM((cuts, count, part), BF),
-        pltpu.VMEM((cuts, units, part), BF),
-        pltpu.VMEM((width, units), BF),
-        pltpu.VMEM((width, units), BF),
-        pltpu.VMEM(square, BF),
-        pltpu.VMEM(square, BF),
-        pltpu.VMEM(halves_shape, F32),
-        pltpu.VMEM(halves_shape, BF),
-        pltpu.SemaphoreType.DMA((10 * cuts,)),
-        pltpu.SemaphoreType.DMA((5,)),
-    ]
-    if fresh:
-        scratch += [pltpu.VMEM((cuts, count, part), BF)]
-    scratch += [pltpu.VMEM(square, F32), pltpu.VMEM(square, F32), pltpu.VMEM(square, BF)]
-    if not fresh:
-        scratch += [pltpu.VMEM(right.shape, F32), pltpu.VMEM((count, 2 * R), BF)]
+
     return pl.pallas_call(
         kernel,
         out_shape=tuple(jax.ShapeDtypeStruct(*result) for result in results),
-        in_specs=[ANYWHERE] * len(operands),
-        out_specs=(ANYWHERE,) * len(results),
-        scratch_shapes=scratch,
-        compiler_params=pltpu.CompilerParams(vmem_limit_bytes=44 << 20),
+        scratch_shapes=[pltpu.VMEM(square, BF), pltpu.VMEM(square, BF)] if fresh else [],
+        compiler_params=pltpu.CompilerParams(vmem_limit_bytes=32 << 20),
         name="experts_first" if fresh else "experts_last",
     )(*operands)
 
@@ -396,14 +271,12 @@
 
     def kernel(pieces_ref, out_ref):
         for c in range(copies):
-            out_ref[0, :, c * columns : (c + 1) * columns] = pieces_ref[0, c]
+            out_ref[:, :, c * columns : (c + 1) * columns] = pieces_ref[:, c]
 
     return pl.pallas_call(
         kernel,
-        grid=(micro, 2),
         out_shape=jax.ShapeDtypeStruct((micro, tokens, copies * columns), pieces.dtype),
-        in_specs=[pl.BlockSpec((1, copies, tokens // 2, columns), lambda m, h: (m, 0, h, 0))],
-        out_specs=pl.BlockSpec((1, tokens // 2, copies * columns), lambda m, h: (m, h, 0)),
+        compiler_params=pltpu.CompilerParams(vmem_limit_bytes=8 << 20),
         name="side_by_side",
     )(pieces)
 

time: 191 us -> 189 us (0.990)
  Pallas kernels: 42.8 us -> 32.2 us
  local copies, waits for them, and re-layouts: 16.7 us -> 20.6 us
  other arithmetic: 8.23 us -> 10.2 us
    pallas_call x2, Pallas kernels: 22.9 us -> 16.3 us  [experts(): pl.pallas_call(kernel, out_shape=tuple((jax.ShapeDtypeStruct(*result) for...]
    unnamed x46 -> x66, local copies, waits for them, and re-layouts: 9.08 us -> 13 us
    pallas_call x1, Pallas kernels: 5.46 us -> 2.7 us  [side_by_side(): pl.pallas_call(kernel, out_shape=jax.ShapeDtypeStruct((micro, tokens, cop...]
  transfers between devices with their start and end apart: 14 -> 14, of which waited for: 12 -> 12; matrix products, arithmetic and copies ran while one was open for 10% -> 10% of each run, Pallas kernels for 5% -> 4%
where the time goes in v5:
time: 189 us; the launch traced here: 188 us
  waiting for transfers between devices  81.8 us (43%)
  Pallas kernels  32.2 us (17%)
  starting transfers between devices  31.6 us (17%)
  local copies, waits for them, and re-layouts  20.6 us (11%)
  matrix products  10.6 us (6%)
  other arithmetic  10.2 us (5%)
    all_to_all x4, waiting for transfers between devices, exchange(): return lax.all_to_all(pieces, 'expert', 0, 0, tiled=True)  47.8 us
    all_to_all x4, starting transfers between devices, exchange(): return lax.all_to_all(pieces, 'expert', 0, 0, tiled=True)  23.8 us
    pallas_call x2, Pallas kernels, experts(): pl.pallas_call(kernel, out_shape=tuple((jax.ShapeDtypeStruct(*result) for...  16.3 us
    ppermute x6, waiting for transfers between devices, swap_cores(): return lax.ppermute(value, 'dp', [(0, 1), (1, 0)])  13.9 us
    ppermute x3, waiting for transfers between devices, add_copies(): other = lax.ppermute(rounded, 'expert', route)  13.6 us
    unnamed x66, local copies, waits for them, and re-layouts  13 us
    dot_general x6, matrix products, times(): lax.dot_general(a, b, (((ca,), (cb,)), ((), ())), preferred_element_type=...  10.6 us
    pallas_call x1, Pallas kernels, finish(): pl.pallas_call(kernel, out_shape=(jax.ShapeDtypeStruct((3, R, units), F32...  8.22 us
  transfers between devices with their start and end apart: 14, of which 12 were waited for; matrix products, arithmetic and copies ran while one was open for 10% of the time, Pallas kernels for 4%

profile of v5, /device:TPU:0, one launch (start us, length us, event | category | flops | bytes accessed | tf_op | source)
XLA Modules:
  0.0 188.1 jit_solution(7548351394535451452)
XLA Ops:
  0.7 5.0 %pick_slots.1 = (bf16[192,3072]{1,0:T(8,128)(2,1)}, bf16[192,3072]{1,0:T(8,128)(2,1)}, f32[192,128]{1,0:T(8,128)}) custom-call(s32[1]{0:T(128)} %bitcast.7.expert_ref, s32[4,2,64]{2,1,0:T(2,128)} %bitcast.82, f32[4,2,64]{2,1,0:T(2,128)} %bitcast.84, bf16[256,3072]{1,0:T(8,128)(2,1)} %bitcast.76, bf16[256,3072]{1,0:T(8,128)(2,1)} %bitcast.74), custom_call_target="tpu_custom_call" | custom-call | tf_op jit(solution)/shard_map/pick_slots/pallas_call | solution.py:179
  6.1 2.5 %collective-permute-done.refs_1_ = bf16[192,3072]{1,0:T(8,128)(2,1)S(1)} collective-permute-done((bf16[192,3072]{1,0:T(8,128)(2,1)}, bf16[192,3072]{1,0:T(8,128)(2,1)S(1)}, u32[]{:S(2)}, u32[]{:S(2)}) %collective-permute-start) | collective-permute-done | bytes 1179680 | tf_op jit(solution)/shard_map/ppermute | solution.py:22
  8.7 1.7 collective-permute-done.1.refs_6_.refs_4_
  10.4 2.3 %copy-done.1 = bf16[1,1,1,3072,512]{4,3,2,1,0:T(8,128)(2,1)S(1)} copy-done((bf16[1,1,1,3072,512]{4,3,2,1,0:T(8,128)(2,1)S(1)}, bf16[1,1,1,3072,512]{4,3,2,1,0:T(8,128)(2,1)}, u32[]{:S(2)}) %copy-start.1) | copy-done | bytes 3145752
  12.7 1.9 %copy-done.3 = bf16[1,1,1,3072,512]{4,3,2,1,0:T(8,128)(2,1)S(1)} copy-done((bf16[1,1,1,3072,512]{4,3,2,1,0:T(8,128)(2,1)S(1)}, bf16[1,1,1,3072,512]{4,3,2,1,0:T(8,128)(2,1)}, u32[]{:S(2)}) %copy-start.3) | copy-done | bytes 3145752
  14.6 1.3 copy-done.5
  15.9 1.3 copy-done.16
  17.1 8.6 %experts_first.1 = (f32[384,512]{1,0:T(8,128)S(1)}, f32[384,512]{1,0:T(8,128)S(1)}, bf16[384,512]{1,0:T(8,128)(2,1)S(1)}, f32[4,8,48,384]{3,2,1,0:T(8,128)S(1)}, bf16[4,8,48,384]{3,2,1,0:T(8,128)(2,1)S(1)}) custom-call(bf16[192,3072]{1,0:T(8,128)(2,1)S(1)} %copy-done.16, bf16[192,3072]{1,0:T(8,128)(2,1)S(1)} %collective-permute-done.refs_1_, ...), custom_call_target="tpu_custom_call" | custom-call | tf_op jit(solution)/shard_map/experts_first/pallas_call | solution.py:260
  26.0 2.7 %collective-permute-done.2 = bf16[4,8,48,384]{3,2,1,0:T(8,128)(2,1)S(1)} collective-permute-done((bf16[4,8,48,384]{3,2,1,0:T(8,128)(2,1)S(1)}, bf16[4,8,48,384]{3,2,1,0:T(8,128)(2,1)S(1)}, u32[]{:S(2)}, u32[]{:S(2)}) %collective-permute-start.2) | collective-permute-done | bytes 1179680 | tf_op jit(solution)/shard_map/ppermute | solution.py:22
  28.7 1.4 add_convert_fusion.1
  30.1 9.6 %all-to-all-start = ((bf16[32,48,384]{2,1,0:T(8,128)(2,1)}), bf16[32,48,384]{2,1,0:T(8,128)(2,1)}, u32[]{:S(2)}, u32[]{:S(2)}) async-start(bf16[32,48,384]{2,1,0:T(8,128)(2,1)} %bitcast.72), calls=%async_computation | async-start | bytes 2359296 | tf_op jit(solution)/shard_map/all_to_all | solution.py:26
  40.5 0.9 copy.17
  42.4 1.6 constant_dynamic-slice_fusion
  44.0 0.9 copy.22
  45.0 14.3 %all-to-all-done = bf16[32,48,384]{2,1,0:T(8,128)(2,1)} async-done(((bf16[32,48,384]{2,1,0:T(8,128)(2,1)}), bf16[32,48,384]{2,1,0:T(8,128)(2,1)}, u32[]{:S(2)}, u32[]{:S(2)}) %all-to-all-start) | async-done | bytes 1179680 | tf_op jit(solution)/shard_map/all_to_all | solution.py:26
  59.3 1.5 convert_reduce_fusion.1
  60.8 1.7 fusion.2
  62.5 1.3 collective-permute-start.3
  63.8 6.5 %collective-permute-done.3 = bf16[64,384]{1,0:T(8,128)(2,1)} collective-permute-done((bf16[64,384]{1,0:T(8,128)(2,1)}, bf16[64,384]{1,0:T(8,128)(2,1)}, u32[]{:S(2)}, u32[]{:S(2)}) %collective-permute-start.3) | collective-permute-done | bytes 49184 | tf_op jit(solution)/shard_map/ppermute | solution.py:338
  70.3 1.0 convolution_convert_fusion
  71.3 1.1 broadcast_in_dim.18
  72.4 4.7 %all-to-all-start.1 = ((bf16[32,48,384]{2,1,0:T(8,128)(2,1)}), bf16[32,48,384]{2,1,0:T(8,128)(2,1)}, u32[]{:S(2)}, u32[]{:S(2)}) async-start(bf16[32,48,384]{2,1,0:T(8,128)(2,1)} %bitcast.71), calls=%async_computation.1 | async-start | bytes 2359296 | tf_op jit(solution)/shard_map/all_to_all | solution.py:26
  77.1 1.0 slice_reduce_fusion
  78.1 16.3 %all-to-all-done.1 = bf16[32,48,384]{2,1,0:T(8,128)(2,1)} async-done(((bf16[32,48,384]{2,1,0:T(8,128)(2,1)}), bf16[32,48,384]{2,1,0:T(8,128)(2,1)}, u32[]{:S(2)}, u32[]{:S(2)}) %all-to-all-start.1) | async-done | bytes 1179680 | tf_op jit(solution)/shard_map/all_to_all | solution.py:26
  94.4 1.5 convert_bitcast_fusion
  97.4 2.8 %collective-permute-done.4.refs_1_.refs_6_ = bf16[192,3072]{1,0:T(8,128)(2,1)S(1)} collective-permute-done((bf16[192,3072]{1,0:T(8,128)(2,1)S(1)}, bf16[192,3072]{1,0:T(8,128)(2,1)S(1)}, u32[]{:S(2)}, u32[]{:S(2)}) %collective-permute-start.4) | collective-permute-done | bytes 1179680 | tf_op jit(solution)/shard_map/ppermute | solution.py:22
  100.4 7.7 %experts_last.1 = (bf16[384,512]{1,0:T(8,128)(2,1)S(1)}, bf16[384,512]{1,0:T(8,128)(2,1)S(1)}, bf16[384,128]{1,0:T(8,128)(2,1)S(1)}, f32[4,8,48,384]{3,2,1,0:T(8,128)S(1)}, bf16[4,8,48,384]{3,2,1,0:T(8,128)(2,1)}) custom-call(bf16[192,3072]{1,0:T(8,128)(2,1)S(1)} %multiply_convert_fusion.refs_0_.refs_5_, ...), custom_call_target="tpu_custom_call" | custom-call | tf_op jit(solution)/shard_map/experts_last/pallas_call | solution.py:260
  108.1 1.4 copy-done.15
  111.7 3.1 %collective-permute-done.5 = bf16[4,8,48,384]{3,2,1,0:T(8,128)(2,1)S(1)} collective-permute-done((bf16[4,8,48,384]{3,2,1,0:T(8,128)(2,1)}, bf16[4,8,48,384]{3,2,1,0:T(8,128)(2,1)S(1)}, u32[]{:S(2)}, u32[]{:S(2)}) %collective-permute-start.5) | collective-permute-done | bytes 1179680 | tf_op jit(solution)/shard_map/ppermute | solution.py:22
  114.7 2.9 %add_convert_fusion = bf16[4,8,48,384]{3,2,1,0:T(8,128)(2,1)} fusion(f32[4,8,48,384]{3,2,1,0:T(8,128)} %copy-done.15, bf16[4,8,48,384]{3,2,1,0:T(8,128)(2,1)S(1)} %collective-permute-done.5), kind=kLoop, calls=%fused_computation.4 | loop fusion | flops 1769472 | bytes 4718592 | tf_op jit(solution)/shard_map/convert_element_type | solution.py:321
  117.6 4.8 %all-to-all-start.2 = ((bf16[32,48,384]{2,1,0:T(8,128)(2,1)}), bf16[32,48,384]{2,1,0:T(8,128)(2,1)}, u32[]{:S(2)}, u32[]{:S(2)}) async-start(bf16[32,48,384]{2,1,0:T(8,128)(2,1)} %bitcast.73), calls=%async_computation.2 | async-start | bytes 2359296 | tf_op jit(solution)/shard_map/all_to_all | solution.py:26
  123.1 1.1 collective-permute-done.6
  124.5 1.5 collective-permute-start.7
  126.0 17.1 %all-to-all-done.2 = bf16[32,48,384]{2,1,0:T(8,128)(2,1)} async-done(((bf16[32,48,384]{2,1,0:T(8,128)(2,1)}), bf16[32,48,384]{2,1,0:T(8,128)(2,1)}, u32[]{:S(2)}, u32[]{:S(2)}) %all-to-all-start.2) | async-done | bytes 1179680 | tf_op jit(solution)/shard_map/all_to_all | solution.py:26
  143.1 1.5 convert_reduce_fusion
  144.6 1.1 add_convert_fusion.5
  145.7 1.4 broadcast_in_dim.19
  147.1 4.7 %all-to-all-start.3 = ((bf16[32,64,384]{2,1,0:T(8,128)(2,1)}), bf16[32,64,384]{2,1,0:T(8,128)(2,1)}, u32[]{:S(2)}, u32[]{:S(2)}) async-start(bf16[32,64,384]{2,1,0:T(8,128)(2,1)} %broadcast_in_dim.19), calls=%async_computation.3 | async-start | bytes 3145728 | tf_op jit(solution)/shard_map/all_to_all | solution.py:26
  151.8 3.9 %fusion.22.refs_0_ = f32[384,384]{1,0:T(8,128)S(1)} fusion(bf16[384,3072]{1,0:T(8,128)(2,1)} %copy-done.28), kind=kOutput, calls=%fused_computation.43 | convolution fusion | flops 905969664 | bytes 2949120 | tf_op jit(solution)/shard_map/dot_general | solution.py:30
  155.8 0.9 add_convert_fusion.3
  156.7 1.7 collective-permute-start.8
  158.4 1.4 fusion.1.refs_1_
  159.8 11.3 %collective-permute-done.8 = bf16[384,128]{1,0:T(8,128)(2,1)S(1)} collective-permute-done((bf16[384,128]{1,0:T(8,128)(2,1)S(1)}, bf16[384,128]{1,0:T(8,128)(2,1)S(1)}, u32[]{:S(2)}, u32[]{:S(2)}) %collective-permute-start.8) | collective-permute-done | bytes 98336 | tf_op jit(solution)/shard_map/ppermute | solution.py:64
  171.2 2.2 %collective-permute-start.9 = (bf16[384,128]{1,0:T(8,128)(2,1)S(1)}, bf16[384,128]{1,0:T(8,128)(2,1)S(1)}, u32[]{:S(2)}, u32[]{:S(2)}) collective-permute-start(bf16[384,128]{1,0:T(8,128)(2,1)S(1)} %add_convert_fusion.2), channel_id=1, source_target_pairs={{0,6},{1,7},{2,4},{3,5},{4,2},{5,3},{6,0},{7,1},{8,14},{9,15},{10,... | collective-permute-start | bytes 294920 | tf_op jit(solution)/shard_map/ppermute | solution.py:64
  173.4 1.4 fusion.refs_2_
  174.8 2.3 %collective-permute-done.9 = bf16[384,128]{1,0:T(8,128)(2,1)S(1)} collective-permute-done((bf16[384,128]{1,0:T(8,128)(2,1)S(1)}, bf16[384,128]{1,0:T(8,128)(2,1)S(1)}, u32[]{:S(2)}, u32[]{:S(2)}) %collective-permute-start.9) | collective-permute-done | bytes 98336 | tf_op jit(solution)/shard_map/ppermute | solution.py:64
  177.2 8.2 %finish.1 = (f32[3,64,512]{2,1,0:T(8,128)}, f32[64,1536]{1,0:T(8,128)}) custom-call(s32[1]{0:T(128)} %bitcast.30.dp_ref, f32[384,128]{1,0:T(8,128)S(1)} %convert_add_fusion.sums_ref, f32[384,384]{1,0:T(8,128)S(1)} %fusion.22.refs_0_, f32[384,384]{1,0:T(8,128)S(1)} %fusion.1.refs_1_, f32[384,384]{1,0:T(8,128)S(1)} %fusion.refs_2_, ...), custom_call_target="tpu_custom_call" | custom-call | tf_op jit(solution)/shard_map/finish/pallas_call | solution.py:135
  185.4 2.7 %side_by_side.1 = bf16[4,64,3072]{2,1,0:T(8,128)(2,1)} custom-call(bf16[4,8,64,384]{3,2,1,0:T(8,128)(2,1)} %bitcast.28.pieces_ref), custom_call_target="tpu_custom_call" | custom-call | tf_op jit(solution)/shard_map/side_by_side/pallas_call | solution.py:276
  (80 shorter events, 7.3 us)
Async XLA Ops:
  0.6 9.8 %copy-start = (bf16[1,1,1,512,3072]{4,3,2,1,0:T(8,128)(2,1)S(1)}, bf16[1,1,1,512,3072]{4,3,2,1,0:T(8,128)(2,1)}, u32[]{:S(2)}) copy-start(bf16[1,1,1,512,3072]{4,3,2,1,0:T(8,128)(2,1)} %param.14) | copy-start | bytes 9437188
  5.6 3.1 %collective-permute-start = (bf16[192,3072]{1,0:T(8,128)(2,1)}, bf16[192,3072]{1,0:T(8,128)(2,1)S(1)}, u32[]{:S(2)}, u32[]{:S(2)}) collective-permute-start(bf16[192,3072]{1,0:T(8,128)(2,1)} %get-tuple-element.18.refs_0_), channel_id=1, source_target_pairs={{0,64},{64,0},{1,65},{65,1},{2,66},{66,2},{3,67},{67,3},{4,68},{68... | collective-permute-start | bytes 3538952 | tf_op jit(solution)/shard_map/ppermute | solution.py:22
  5.6 4.7 %collective-permute-start.1 = (bf16[192,3072]{1,0:T(8,128)(2,1)}, bf16[192,3072]{1,0:T(8,128)(2,1)S(1)}, u32[]{:S(2)}, u32[]{:S(2)}) collective-permute-start(bf16[192,3072]{1,0:T(8,128)(2,1)} %get-tuple-element.19.refs_5_.refs_3_), channel_id=1, source_target_pairs={{0,64},{64,0},{1,65},{65,1},{2,66},{66,2},{3,67},{67,3},{4,68},{68... | collective-permute-start | bytes 3538952 | tf_op jit(solution)/shard_map/ppermute | solution.py:22
  10.4 15.4 %copy-start.8 = (bf16[192,3072]{1,0:T(8,128)(2,1)}, bf16[192,3072]{1,0:T(8,128)(2,1)S(1)}, u32[]{:S(2)}) copy-start(bf16[192,3072]{1,0:T(8,128)(2,1)S(1)} %collective-permute-done.1.refs_6_.refs_4_) | copy-start | bytes 3538948
  10.4 2.3 %copy-start.1 = (bf16[1,1,1,3072,512]{4,3,2,1,0:T(8,128)(2,1)S(1)}, bf16[1,1,1,3072,512]{4,3,2,1,0:T(8,128)(2,1)}, u32[]{:S(2)}) copy-start(bf16[1,1,1,3072,512]{4,3,2,1,0:T(8,128)(2,1)} %param.12) | copy-start | bytes 9437188
  12.7 1.9 %copy-start.3 = (bf16[1,1,1,3072,512]{4,3,2,1,0:T(8,128)(2,1)S(1)}, bf16[1,1,1,3072,512]{4,3,2,1,0:T(8,128)(2,1)}, u32[]{:S(2)}) copy-start(bf16[1,1,1,3072,512]{4,3,2,1,0:T(8,128)(2,1)} %param.13) | copy-start | bytes 9437188
  14.6 1.3 copy-start.5
  15.9 1.3 copy-start.16
  25.8 4.3 %copy-start.17 = (f32[384,512]{1,0:T(8,128)}, f32[384,512]{1,0:T(8,128)S(1)}, u32[]{:S(2)}) copy-start(f32[384,512]{1,0:T(8,128)S(1)} %get-tuple-element.23.refs_5_) | copy-start | bytes 2359300
  25.8 4.3 %copy-start.19 = (f32[384,512]{1,0:T(8,128)}, f32[384,512]{1,0:T(8,128)S(1)}, u32[]{:S(2)}) copy-start(f32[384,512]{1,0:T(8,128)S(1)} %get-tuple-element.24.refs_6_) | copy-start | bytes 2359300
  25.8 2.9 %collective-permute-start.2 = (bf16[4,8,48,384]{3,2,1,0:T(8,128)(2,1)S(1)}, bf16[4,8,48,384]{3,2,1,0:T(8,128)(2,1)S(1)}, u32[]{:S(2)}, u32[]{:S(2)}) collective-permute-start(bf16[4,8,48,384]{3,2,1,0:T(8,128)(2,1)S(1)} %get-tuple-element.21), channel_id=1, source_target_pairs={{0,64},{64,0},{1,65},{65,1},{2,66},{66,2},{3,67},{67,3},{4,68},{68... | collective-permute-start | bytes 3538952 | tf_op jit(solution)/shard_map/ppermute | solution.py:22
  30.1 9.6 %copy-start.30 = (s32[1,4,64,2]{2,3,1,0:T(2,128)S(1)}, s32[1,4,64,2]{2,3,1,0:T(2,128)}, u32[]{:S(2)}) copy-start(s32[1,4,64,2]{2,3,1,0:T(2,128)} %param.10) | copy-start | bytes 6148
  30.1 29.2 %all-to-all-start = ((bf16[32,48,384]{2,1,0:T(8,128)(2,1)}), bf16[32,48,384]{2,1,0:T(8,128)(2,1)}, u32[]{:S(2)}, u32[]{:S(2)}) async-start(bf16[32,48,384]{2,1,0:T(8,128)(2,1)} %bitcast.72), calls=%async_computation | async-start | bytes 2359296 | tf_op jit(solution)/shard_map/all_to_all | solution.py:26
  62.5 7.8 %collective-permute-start.3 = (bf16[64,384]{1,0:T(8,128)(2,1)}, bf16[64,384]{1,0:T(8,128)(2,1)}, u32[]{:S(2)}, u32[]{:S(2)}) collective-permute-start(bf16[64,384]{1,0:T(8,128)(2,1)} %fusion.2), channel_id=1, source_target_pairs={{32,0},{33,1},{34,2},{35,3},{36,4},{37,5},{38,6},{39,7},{40,8},{41... | collective-permute-start | bytes 147464 | tf_op jit(solution)/shard_map/ppermute | solution.py:338
  72.4 22.0 %all-to-all-start.1 = ((bf16[32,48,384]{2,1,0:T(8,128)(2,1)}), bf16[32,48,384]{2,1,0:T(8,128)(2,1)}, u32[]{:S(2)}, u32[]{:S(2)}) async-start(bf16[32,48,384]{2,1,0:T(8,128)(2,1)} %bitcast.71), calls=%async_computation.1 | async-start | bytes 2359296 | tf_op jit(solution)/shard_map/all_to_all | solution.py:26
  96.6 3.7 %copy-start.4 = (bf16[1,1,1,3072,512]{4,3,2,1,0:T(8,128)(2,1)S(1)}, bf16[1,1,1,3072,512]{4,3,2,1,0:T(8,128)(2,1)}, u32[]{:S(2)}) copy-start(bf16[1,1,1,3072,512]{4,3,2,1,0:T(8,128)(2,1)} %param.13) | copy-start | bytes 9437188
  96.6 3.7 %copy-start.18 = (f32[384,512]{1,0:T(8,128)S(1)}, f32[384,512]{1,0:T(8,128)}, u32[]{:S(2)}) copy-start(f32[384,512]{1,0:T(8,128)} %copy-done.17) | copy-start | bytes 2359300
  96.6 3.7 %copy-start.20 = (f32[384,512]{1,0:T(8,128)S(1)}, f32[384,512]{1,0:T(8,128)}, u32[]{:S(2)}) copy-start(f32[384,512]{1,0:T(8,128)} %copy-done.19) | copy-start | bytes 2359300
  97.0 3.4 %copy-start.2 = (bf16[1,1,1,3072,512]{4,3,2,1,0:T(8,128)(2,1)S(1)}, bf16[1,1,1,3072,512]{4,3,2,1,0:T(8,128)(2,1)}, u32[]{:S(2)}) copy-start(bf16[1,1,1,3072,512]{4,3,2,1,0:T(8,128)(2,1)} %param.12) | copy-start | bytes 9437188
  97.0 3.4 %copy-start.21 = (f32[1,1,1,3,512,64]{4,5,3,2,1,0:T(8,128)S(1)}, f32[1,1,1,3,512,64]{4,5,3,2,1,0:T(8,128)}, u32[]{:S(2)}) copy-start(f32[1,1,1,3,512,64]{4,5,3,2,1,0:T(8,128)} %param.15) | copy-start | bytes 1179652
  97.3 10.8 %copy-start.11 = (bf16[192,3072]{1,0:T(8,128)(2,1)}, bf16[192,3072]{1,0:T(8,128)(2,1)S(1)}, u32[]{:S(2)}) copy-start(bf16[192,3072]{1,0:T(8,128)(2,1)S(1)} %multiply_convert_fusion.refs_0_.refs_5_) | copy-start | bytes 3538948
  97.3 2.9 %collective-permute-start.4 = (bf16[192,3072]{1,0:T(8,128)(2,1)S(1)}, bf16[192,3072]{1,0:T(8,128)(2,1)S(1)}, u32[]{:S(2)}, u32[]{:S(2)}) collective-permute-start(bf16[192,3072]{1,0:T(8,128)(2,1)S(1)} %multiply_convert_fusion.refs_0_.refs_5_), channel_id=1, source_target_pairs={{0,64},{64,0},{1,65},{65,1},{2,66},{66,2},{3,67},{67,3},{4,68},{68... | collective-permute-start | bytes 3538952 | tf_op jit(solution)/shard_map/ppermute | solution.py:22
  100.2 7.9 %copy-start.13 = (bf16[192,3072]{1,0:T(8,128)(2,1)}, bf16[192,3072]{1,0:T(8,128)(2,1)S(1)}, u32[]{:S(2)}) copy-start(bf16[192,3072]{1,0:T(8,128)(2,1)S(1)} %collective-permute-done.4.refs_1_.refs_6_) | copy-start | bytes 3538948
  108.1 1.4 copy-start.15
  109.5 0.7 copy-start.22
  110.3 0.7 copy-start.24
  111.0 0.6 copy-start.26
  111.7 3.1 %collective-permute-start.5 = (bf16[4,8,48,384]{3,2,1,0:T(8,128)(2,1)}, bf16[4,8,48,384]{3,2,1,0:T(8,128)(2,1)S(1)}, u32[]{:S(2)}, u32[]{:S(2)}) collective-permute-start(bf16[4,8,48,384]{3,2,1,0:T(8,128)(2,1)} %get-tuple-element.27), channel_id=1, source_target_pairs={{0,64},{64,0},{1,65},{65,1},{2,66},{66,2},{3,67},{67,3},{4,68},{68... | collective-permute-start | bytes 3538952 | tf_op jit(solution)/shard_map/ppermute | solution.py:22
  117.6 4.8 %copy-start.6 = (bf16[192,3072]{1,0:T(8,128)(2,1)S(1)}, bf16[192,3072]{1,0:T(8,128)(2,1)}, u32[]{:S(2)}) copy-start(bf16[192,3072]{1,0:T(8,128)(2,1)} %get-tuple-element.19.refs_5_.refs_3_) | copy-start | bytes 3538948
  117.6 4.9 %copy-start.27 = (bf16[384,128]{1,0:T(8,128)(2,1)S(1)}, bf16[384,128]{1,0:T(8,128)(2,1)}, u32[]{:S(2)}) copy-start(bf16[384,128]{1,0:T(8,128)(2,1)} %copy-done.26) | copy-start | bytes 294916
  117.6 5.3 %copy-start.9 = (bf16[192,3072]{1,0:T(8,128)(2,1)S(1)}, bf16[192,3072]{1,0:T(8,128)(2,1)}, u32[]{:S(2)}) copy-start(bf16[192,3072]{1,0:T(8,128)(2,1)} %copy-done.8) | copy-start | bytes 3538948
  117.6 25.4 %all-to-all-start.2 = ((bf16[32,48,384]{2,1,0:T(8,128)(2,1)}), bf16[32,48,384]{2,1,0:T(8,128)(2,1)}, u32[]{:S(2)}, u32[]{:S(2)}) async-start(bf16[32,48,384]{2,1,0:T(8,128)(2,1)} %bitcast.73), calls=%async_computation.2 | async-start | bytes 2359296 | tf_op jit(solution)/shard_map/all_to_all | solution.py:26
  122.6 1.6 collective-permute-start.6
  123.0 1.4 copy-start.28
  124.5 31.3 %collective-permute-start.7 = (bf16[384,128]{1,0:T(8,128)(2,1)S(1)}, bf16[384,128]{1,0:T(8,128)(2,1)}, u32[]{:S(2)}, u32[]{:S(2)}) collective-permute-start(bf16[384,128]{1,0:T(8,128)(2,1)S(1)} %add_convert_fusion.4), channel_id=1, source_target_pairs={{0,1},{1,0},{2,3},{3,2},{4,5},{5,4},{6,7},{7,6},{8,9},{9,8},{10,11... | collective-permute-start | bytes 294920 | tf_op jit(solution)/shard_map/ppermute | solution.py:64
  147.1 38.3 %all-to-all-start.3 = ((bf16[32,64,384]{2,1,0:T(8,128)(2,1)}), bf16[32,64,384]{2,1,0:T(8,128)(2,1)}, u32[]{:S(2)}, u32[]{:S(2)}) async-start(bf16[32,64,384]{2,1,0:T(8,128)(2,1)} %broadcast_in_dim.19), calls=%async_computation.3 | async-start | bytes 3145728 | tf_op jit(solution)/shard_map/all_to_all | solution.py:26
  151.8 6.6 %copy-start.12 = (bf16[192,3072]{1,0:T(8,128)(2,1)S(1)}, bf16[192,3072]{1,0:T(8,128)(2,1)}, u32[]{:S(2)}) copy-start(bf16[192,3072]{1,0:T(8,128)(2,1)} %copy-done.11) | copy-start | bytes 3538948
  151.8 6.6 %copy-start.14 = (bf16[192,3072]{1,0:T(8,128)(2,1)S(1)}, bf16[192,3072]{1,0:T(8,128)(2,1)}, u32[]{:S(2)}) copy-start(bf16[192,3072]{1,0:T(8,128)(2,1)} %copy-done.13) | copy-start | bytes 3538948
  151.8 6.6 %copy-start.29 = (bf16[384,3072]{1,0:T(8,128)(2,1)S(1)}, bf16[384,3072]{1,0:T(8,128)(2,1)}, u32[]{:S(2)}) copy-start(bf16[384,3072]{1,0:T(8,128)(2,1)} %copy-done.28) | copy-start | bytes 7077892
  156.7 14.5 %collective-permute-start.8 = (bf16[384,128]{1,0:T(8,128)(2,1)S(1)}, bf16[384,128]{1,0:T(8,128)(2,1)S(1)}, u32[]{:S(2)}, u32[]{:S(2)}) collective-permute-start(bf16[384,128]{1,0:T(8,128)(2,1)S(1)} %add_convert_fusion.3), channel_id=1, source_target_pairs={{0,2},{1,3},{2,0},{3,1},{4,6},{5,7},{6,4},{7,5},{8,10},{9,11},{10,... | collective-permute-start | bytes 294920 | tf_op jit(solution)/shard_map/ppermute | solution.py:64
  171.2 6.0 %copy-start.7 = (bf16[192,3072]{1,0:T(8,128)(2,1)S(1)}, bf16[192,3072]{1,0:T(8,128)(2,1)}, u32[]{:S(2)}) copy-start(bf16[192,3072]{1,0:T(8,128)(2,1)} %get-tuple-element.19.refs_5_.refs_3_) | copy-start | bytes 3538948
  171.2 6.0 %copy-start.10 = (bf16[192,3072]{1,0:T(8,128)(2,1)S(1)}, bf16[192,3072]{1,0:T(8,128)(2,1)}, u32[]{:S(2)}) copy-start(bf16[192,3072]{1,0:T(8,128)(2,1)} %copy-done.8) | copy-start | bytes 3538948
  171.2 6.0 %copy-start.23 = (bf16[384,512]{1,0:T(8,128)(2,1)S(1)}, bf16[384,512]{1,0:T(8,128)(2,1)}, u32[]{:S(2)}) copy-start(bf16[384,512]{1,0:T(8,128)(2,1)} %copy-done.22) | copy-start | bytes 1179652
  171.2 6.0 %copy-start.25 = (bf16[384,512]{1,0:T(8,128)(2,1)S(1)}, bf16[384,512]{1,0:T(8,128)(2,1)}, u32[]{:S(2)}) copy-start(bf16[384,512]{1,0:T(8,128)(2,1)} %copy-done.24) | copy-start | bytes 1179652
  171.2 5.9 %collective-permute-start.9 = (bf16[384,128]{1,0:T(8,128)(2,1)S(1)}, bf16[384,128]{1,0:T(8,128)(2,1)S(1)}, u32[]{:S(2)}, u32[]{:S(2)}) collective-permute-start(bf16[384,128]{1,0:T(8,128)(2,1)S(1)} %add_convert_fusion.2), channel_id=1, source_target_pairs={{0,6},{1,7},{2,4},{3,5},{4,2},{5,3},{6,0},{7,1},{8,14},{9,15},{10,... | collective-permute-start | bytes 294920 | tf_op jit(solution)/shard_map/ppermute | solution.py:64

commit v6 on v5

--- a/solution.py
+++ b/solution.py
@@ -16,6 +16,12 @@
 BF = jnp.bfloat16
 F32 = jnp.float32
 IN_SMEM = pl.BlockSpec(memory_space=pltpu.SMEM)
+IN_VMEM = pl.BlockSpec(memory_space=pltpu.VMEM)
+IN_HBM = pl.BlockSpec(memory_space=pltpu.HBM)
+
+
+def cost(flops, moved):
+    return pl.CostEstimate(flops=int(flops), bytes_accessed=int(moved), transcendentals=0)
 
 
 def swap_cores(value):
@@ -95,22 +101,38 @@
 
 
 def finish(dp_index, sums, squares, rows16, grads, token_total):
-    wide = rows16[0].shape[1]
+    count, wide = rows16[0].shape
     half = wide // 2
-    units = grads[0].shape[1]
+    units = grads.shape[2]
 
     def kernel(dp_ref, sums_ref, *refs):
-        squares_ref, rows_ref, grads_ref = (refs[:3], refs[3:7], refs[7:10])
-        q_ref, basis_ref = refs[10:12]
+        squares_hbm, rows_hbm, grads_hbm = (refs[:3], refs[3:5], refs[5])
+        q_ref, basis_ref, squares_ref, rows_ref, grads_ref, done = refs[6:]
         start = pl.multiple_of(dp_ref[0] * half, half)
+        moves = [
+            pltpu.make_async_copy(squares_hbm[i], squares_ref.at[i], done.at[i]) for i in range(3)
+        ]
+        moves.append(pltpu.make_async_copy(grads_hbm, grads_ref, done.at[3]))
+        moves += [
+            pltpu.make_async_copy(
+                rows_hbm[i].at[:, pl.ds(start, half)],
+                rows_ref.at[pl.ds(i * count, count)],
+                done.at[4 + i],
+            )
+            for i in range(2)
+        ]
+        for move in moves:
+            move.start()
         turned = sums_ref[...].T
         of_inputs, of_grads = (turned[:R].astype(BF), turned[R:].astype(BF))
+        for move in moves[:3]:
+            move.wait()
 
         def twice(left, right, cb):
             high, low = halves(right)
             return times(left, high, 1, cb) + times(left, low, 1, cb)
 
-        inputs_inputs, grads_inputs, grads_grads = (ref[...] for ref in squares_ref)
+        inputs_inputs, grads_inputs, grads_grads = (squares_ref[i] for i in range(3))
         along_inputs = twice(of_inputs, inputs_inputs, 0) + twice(of_grads, grads_inputs, 0)
         along_grads = twice(of_inputs, grads_inputs, 1) + twice(of_grads, grads_grads, 0)
         gram = twice(of_inputs, along_inputs, 1) + twice(of_grads, along_grads, 1)
@@ -126,11 +148,12 @@
         scale = 1.0 / math.sqrt(float(token_total))
         along_inputs = times(inverse, along_inputs, 1, 0, exact).astype(BF)
         along_grads = times(inverse, along_grads, 1, 0, exact).astype(BF)
-        q_ref[0] = times(along_inputs, grads_ref[0][...]) * scale
-        q_ref[1] = times(along_inputs, grads_ref[1][...]) * scale
-        q_ref[2] = times(along_grads, grads_ref[2][...]) * scale
-        rows = jnp.concatenate([ref[:, pl.ds(start, half)] for ref in rows_ref])
-        basis_ref[...] = times(weights, rows) * math.sqrt(float(wide))
+        for move in moves[3:]:
+            move.wait()
+        q_ref[0] = times(along_inputs, grads_ref[0]) * scale
+        q_ref[1] = times(along_inputs, grads_ref[1]) * scale
+        q_ref[2] = times(along_grads, grads_ref[2]) * scale
+        basis_ref[...] = times(weights, rows_ref[...]) * math.sqrt(float(wide))
 
     return pl.pallas_call(
         kernel,
@@ -138,16 +161,24 @@
             jax.ShapeDtypeStruct((3, R, units), F32),
             jax.ShapeDtypeStruct((R, half), F32),
         ),
-        in_specs=[IN_SMEM] + [pl.BlockSpec(memory_space=pltpu.VMEM)] * 11,
-        compiler_params=pltpu.CompilerParams(vmem_limit_bytes=20 << 20),
+        in_specs=[IN_SMEM, IN_VMEM] + [IN_HBM] * 6,
+        scratch_shapes=[
+            pltpu.VMEM((3, count, count), F32),
+            pltpu.VMEM((2 * count, half), BF),
+            pltpu.VMEM((3, count, units), BF),
+            pltpu.SemaphoreType.DMA((6,)),
+        ],
+        compiler_params=pltpu.CompilerParams(vmem_limit_bytes=61 << 20),
+        cost_estimate=cost(4 * R * count * wide, 2 * count * (wide + 3 * units) + 12 * count**2),
         name="finish",
-    )(dp_index.reshape(1), sums, *squares, *rows16, *grads)
+    )(dp_index.reshape(1), sums, *squares, *rows16, grads)
 
 
 def pick_slots(own_expert, routes, mix, inputs, grads):
     micro, _, tokens = routes.shape
     width = inputs.shape[1]
     block = width // 4
+    count = micro * CAP
 
     def kernel(expert_ref, routes_ref, mix_ref, inputs_ref, grads_ref, picked_ref, scaled_ref, w_ref):
         expert = expert_ref[0]
@@ -169,35 +200,94 @@
         chosen = slot == place
         pick = jnp.where(chosen, 1.0, 0.0).astype(BF)
         by_slot = jnp.sum(jnp.where(chosen, weight, 0.0), axis=1, keepdims=True)
-        picked_ref[...] = times(pick, inputs_ref[...]).astype(BF)
-        scaled_ref[...] = (by_slot * times(pick, grads_ref[...])).astype(BF)
-        w_ref[...] = jnp.broadcast_to(by_slot, (micro * CAP, 128))
-
-    def whole(shape):
-        return pl.BlockSpec(shape, lambda d: (0,) * len(shape))
-
-    return pl.pallas_call(
-        kernel,
-        grid=(width // block,),
+        w_ref[...] = jnp.broadcast_to(by_slot, (count, 128))
+        for at in range(0, width, block):
+            held = pl.ds(at, block)
+            picked_ref[:, held] = times(pick, inputs_ref[:, held]).astype(BF)
+            scaled_ref[:, held] = (by_slot * times(pick, grads_ref[:, held])).astype(BF)
+
+    return pl.pallas_call(
+        kernel,
         out_shape=(
-            jax.ShapeDtypeStruct((micro * CAP, width), BF),
-            jax.ShapeDtypeStruct((micro * CAP, width), BF),
-            jax.ShapeDtypeStruct((micro * CAP, 128), F32),
+            jax.ShapeDtypeStruct((count, width), BF),
+            jax.ShapeDtypeStruct((count, width), BF),
+            jax.ShapeDtypeStruct((count, 128), F32),
         ),
-        in_specs=[
-            IN_SMEM,
-            whole(routes.shape),
-            whole(mix.shape),
-            pl.BlockSpec((micro * tokens, block), lambda d: (0, d)),
-            pl.BlockSpec((micro * tokens, block), lambda d: (0, d)),
-        ],
-        out_specs=(
-            pl.BlockSpec((micro * CAP, block), lambda d: (0, d)),
-            pl.BlockSpec((micro * CAP, block), lambda d: (0, d)),
-            whole((micro * CAP, 128)),
-        ),
+        in_specs=[IN_SMEM] + [IN_VMEM] * 4,
+        compiler_params=pltpu.CompilerParams(vmem_limit_bytes=14 << 20),
+        cost_estimate=cost(4 * count * micro * tokens * width, 60 << 20),
         name="pick_slots",
     )(own_expert.reshape(1), routes, mix, inputs, grads)
+
+
+def scale_rows(pieces, slot_weights):
+    micro, copies, cap, columns = pieces.shape
+
+    def kernel(pieces_ref, w_ref, out_ref):
+        for m in range(micro):
+            held = pl.ds(m * cap, cap)
+            weight = w_ref[held, :1]
+            for c in range(copies):
+                scaled = weight * pieces_ref[m, c].astype(F32)
+                out_ref[held, c * columns : (c + 1) * columns] = scaled.astype(BF)
+
+    return pl.pallas_call(
+        kernel,
+        out_shape=jax.ShapeDtypeStruct((micro * cap, copies * columns), BF),
+        compiler_params=pltpu.CompilerParams(vmem_limit_bytes=8 << 20),
+        name="scale_rows",
+    )(pieces, slot_weights)
+
+
+def combine(pieces, pick, base, peers):
+    experts_count, copies, _, columns = pieces.shape
+    tokens = base.shape[0]
+
+    def kernel(pieces_ref, pick_ref, base_ref, out_ref):
+        share = base_ref[...].astype(F32)
+        for e in range(experts_count):
+            total = pieces_ref[e, 0].astype(F32)
+            for c in range(1, copies):
+                total = total + pieces_ref[e, c].astype(F32)
+            for term in halves(total):
+                share = share + times(pick_ref[e], term)
+        part = share.astype(BF)
+        for peer in range(peers):
+            out_ref[peer] = part
+
+    return pl.pallas_call(
+        kernel,
+        out_shape=jax.ShapeDtypeStruct((peers, tokens, columns), BF),
+        compiler_params=pltpu.CompilerParams(vmem_limit_bytes=8 << 20),
+        name="combine",
+    )(pieces, pick, base)
+
+
+def deal(last, top_part, incoming, pick, copies):
+    tokens, columns = incoming.shape
+    slots = pick.shape[0]
+    cap = slots // EXPERTS
+
+    def kernel(last_ref, top_ref, incoming_ref, pick_ref, base_ref, out_ref):
+        base = jnp.where(last_ref[0] == 1, top_ref[...].astype(F32), incoming_ref[...].astype(F32))
+        base = base.astype(BF)
+        base_ref[...] = base
+        listed = times(pick_ref[...], base).astype(BF)
+        for e in range(EXPERTS):
+            for c in range(copies):
+                out_ref[e, c] = listed[e * cap : (e + 1) * cap]
+
+    return pl.pallas_call(
+        kernel,
+        out_shape=(
+            jax.ShapeDtypeStruct((tokens, columns), BF),
+            jax.ShapeDtypeStruct((EXPERTS, copies, cap, columns), BF),
+        ),
+        in_specs=[IN_SMEM] + [IN_VMEM] * 3,
+        compiler_params=pltpu.CompilerParams(vmem_limit_bytes=8 << 20),
+        cost_estimate=cost(2 * slots * tokens * columns, 60 << 20),
+        name="deal",
+    )(last.astype(jnp.int32).reshape(1), top_part, incoming, pick)
 
 
 def experts(gate, up, down, grads_both, copies, inputs_both=None, forward=None, right=None):
@@ -209,22 +299,36 @@
     halves_shape = (MICRO, copies, CAP, columns)
     square = (count, units)
     operands = [*grads_both, down, gate, up] + ([*inputs_both] if fresh else [*forward, right])
+    made = [(halves_shape, F32), (halves_shape, BF)]
     if fresh:
-        results = [(square, F32), (square, F32), (square, BF)]
+        made = [(square, F32), (square, F32), (square, BF)] + made
+        kept = []
     else:
-        results = [(square, BF), (square, BF), ((count, 2 * R), BF)]
-    results += [(halves_shape, F32), (halves_shape, BF)]
+        made = [((count, 2 * R), BF)] + made
+        kept = [((3, *square), BF)]
+    kept += [((count, width), BF)]
 
     def kernel(*refs):
-        ins, outs = (refs[: len(operands)], refs[len(operands) : len(operands) + len(results)])
+        ins, refs = (refs[: len(operands)], refs[len(operands) :])
+        outs, refs = (refs[: len(made)], refs[len(made) :])
+        keeps, (gg_ref, gu_ref, done) = (refs[: len(kept)], refs[len(kept) :])
         down_ref, gate_ref, up_ref = ins[2:5]
-        own_ref, par_ref = outs[3:]
+        own_ref, par_ref = outs[-2:]
+        moves = []
+
+        def keep(source, target):
+            move = pltpu.make_async_copy(source, target, done.at[len(moves)])
+            move.start()
+            moves.append(move)
+
+        rows_refs = ins[5:7] if fresh else ins[:2]
+        for i in range(2):
+            keep(rows_refs[i], keeps[-1].at[pl.ds(i * slots, slots)])
 
         def both(pair):
             return jnp.concatenate([pair[0][...], pair[1][...]])
 
         if fresh:
-            gg_ref, gu_ref = refs[len(operands) + len(results) :]
             inputs = both(ins[5:7])
             pre_gate = times(inputs, gate_ref[...])
             pre_up = times(inputs, up_ref[...])
@@ -235,16 +339,18 @@
             outs[2][...] = (silu * pre_up).astype(BF)
             slope_ref, silu_ref = outs[:2]
         else:
-            gg_ref, gu_ref, sums_ref = outs[:3]
             slope_ref, silu_ref, hidden_ref, right_ref = ins[5:9]
+            keep(hidden_ref, keeps[0].at[2])
         grad_hidden = times(both(ins[:2]), down_ref[...], 1, 1)
         gg_ref[...] = (grad_hidden * slope_ref[...]).astype(BF)
         gu_ref[...] = (grad_hidden * silu_ref[...]).astype(BF)
         if not fresh:
+            keep(gg_ref, keeps[0].at[0])
+            keep(gu_ref, keeps[0].at[1])
             right16 = right_ref[...].astype(BF)
             of_inputs = times(gg_ref[...], right16[0], 1, 1) + times(gu_ref[...], right16[1], 1, 1)
             of_grads = times(hidden_ref[...], right16[2], 1, 1)
-            sums_ref[...] = jnp.concatenate([of_inputs, of_grads], axis=1).astype(BF)
+            outs[0][...] = jnp.concatenate([of_inputs, of_grads], axis=1).astype(BF)
 
         def column(c, carry):
             held = pl.ds(pl.multiple_of(c * columns, columns), columns)
@@ -256,12 +362,23 @@
             return carry
 
         lax.fori_loop(0, copies, column, 0)
-
-    return pl.pallas_call(
-        kernel,
-        out_shape=tuple(jax.ShapeDtypeStruct(*result) for result in results),
-        scratch_shapes=[pltpu.VMEM(square, BF), pltpu.VMEM(square, BF)] if fresh else [],
-        compiler_params=pltpu.CompilerParams(vmem_limit_bytes=32 << 20),
+        for move in moves:
+            move.wait()
+
+    return pl.pallas_call(
+        kernel,
+        out_shape=tuple(jax.ShapeDtypeStruct(*result) for result in made + kept),
+        in_specs=[IN_VMEM] * len(operands),
+        out_specs=(*[IN_VMEM] * len(made), *[IN_HBM] * len(kept)),
+        scratch_shapes=[
+            pltpu.VMEM(square, BF),
+            pltpu.VMEM(square, BF),
+            pltpu.SemaphoreType.DMA((5,)),
+        ],
+        compiler_params=pltpu.CompilerParams(vmem_limit_bytes=30 << 20),
+        cost_estimate=cost(
+            2 * count * width * units * (5 if fresh else 3), 2 * width * (3 * units + 4 * count)
+        ),
         name="experts_first" if fresh else "experts_last",
     )(*operands)
 
@@ -302,7 +419,8 @@
     rank = slots_of(routes[0])
     part_ids = lax.dynamic_index_in_dim(routes[0] * CAP + rank, major, 0, keepdims=False)
     first, second = hit_table(part_ids, EXPERTS * CAP)
-    part_pick = (first | second).astype(BF)
+    deal_pick = (first | second).astype(BF)
+    part_pick = deal_pick.reshape(EXPERTS, CAP, tokens).transpose(0, 2, 1)
 
     own_slots, own_grads, slot_weights = pick_slots(
         major,
@@ -312,49 +430,42 @@
         top_rows,
     )
     inputs_both = (own_slots, swap_cores(own_slots))
-    *forward, own_half, other_half = experts(
+    *forward, own_half, other_half, inputs = experts(
         gate, up, down, (own_grads, swap_cores(own_grads)), copies, inputs_both=inputs_both
     )
 
-    def reduced(own_half, other_half, base):
+    def reduced(own_half, other_half, base, targets):
         other = swap_cores(other_half)
         mine = (own_half + other.astype(F32)).astype(BF)
         pieces = exchange(mine.reshape(peers, CAP, columns))
-        summed = jnp.sum(pieces.astype(F32).reshape(EXPERTS, copies, CAP, columns), axis=1)
-        share = times(
-            part_pick.astype(F32),
-            summed.reshape(EXPERTS * CAP, columns),
-            0,
-            0,
-            lax.Precision.HIGHEST,
+        return combine(
+            pieces.reshape(EXPERTS, copies, CAP, columns), part_pick, base, targets
         )
-        part = (base.astype(F32) + share).astype(BF)
-        return part
 
     top_part = lax.dynamic_slice(
         top_grad, (major, 0, minor * columns), (1, tokens, columns)
     ).reshape(tokens, columns)
-    part = reduced(own_half, other_half, top_part)
+    part = reduced(own_half, other_half, top_part, 1)[0]
     incoming = lax.ppermute(part, "pipe", [(i, i - 1) for i in range(1, sections)])
-    base = jnp.where(last, top_part, incoming)
-    listed = times(part_pick, base).astype(BF).reshape(EXPERTS, 1, CAP, columns)
-    pieces = jnp.broadcast_to(listed, (EXPERTS, copies, CAP, columns))
+    base, pieces = deal(last, top_part, incoming, deal_pick, copies)
     own_rows = exchange(pieces.reshape(peers, CAP, columns))
-    own_rows = own_rows.reshape(MICRO, copies, CAP, columns).transpose(0, 2, 1, 3)
-    own_grads = (slot_weights[:, :1] * own_rows.reshape(slots, D).astype(F32)).astype(BF)
-    grads_both = (own_grads, swap_cores(own_grads))
-    grad_gate, grad_up, sums, own_half, other_half = experts(
-        gate, up, down, grads_both, copies, forward=forward, right=right
-    )
-    part = reduced(own_half, other_half, base)
-    produced = exchange(jnp.broadcast_to(part, (peers, tokens, columns)))
+    own_grads = scale_rows(own_rows.reshape(MICRO, copies, CAP, columns), slot_weights)
+    sums, own_half, other_half, grads, grad_rows = experts(
+        gate,
+        up,
+        down,
+        (own_grads, swap_cores(own_grads)),
+        copies,
+        forward=forward,
+        right=right,
+    )
+    parts = reduced(own_half, other_half, base, peers)
+    produced = exchange(parts)
     produced = side_by_side(produced.reshape(MICRO, copies, tokens, columns))
 
     other = swap_cores(sums)
     sums = sums.astype(F32) + jnp.concatenate([other[slots:], other[:slots]]).astype(F32)
     sums = add_copies(sums, copies)
-    inputs = jnp.concatenate(inputs_both)
-    grad_rows = jnp.concatenate(grads_both)
     squares = (
         times(inputs, inputs, 1, 1),
         times(grad_rows, inputs, 1, 1),
@@ -364,8 +475,8 @@
         dp_index,
         sums,
         squares,
-        (*inputs_both, *grads_both),
-        (grad_gate, grad_up, forward[2]),
+        (inputs, grad_rows),
+        grads,
         replicas * rows,
     )
     return (

time: 189 us -> 175 us (0.926)
  blocking collectives: 0 us -> 20.8 us
  waiting for transfers between devices: 81.8 us -> 66.9 us
  other arithmetic: 10.2 us -> 3.73 us
  starting transfers between devices: 31.6 us -> 25.8 us
  local copies, waits for them, and re-layouts: 20.6 us -> 15.1 us
    all_to_all x0 -> x1, blocking collectives: none -> 20.8 us  [exchange(): return lax.all_to_all(pieces, 'expert', 0, 0, tiled=True)]
    all_to_all x4 -> x3, waiting for transfers between devices: 47.8 us -> 35.2 us  [exchange(): return lax.all_to_all(pieces, 'expert', 0, 0, tiled=True)]
    all_to_all x4 -> x3, starting transfers between devices: 23.8 us -> 17.5 us  [exchange(): return lax.all_to_all(pieces, 'expert', 0, 0, tiled=True)]
    reduce_sum x2 -> x0, other arithmetic: 2.91 us -> none  [reduced(): jnp.sum(pieces.astype(F32).reshape(EXPERTS, copies, CAP, columns), axis=1)]
    pallas_call x1 -> x5, Pallas kernels: 4.98 us -> 2.35 us  [the longest x1 0.96 us: pick_slots(): pl.pallas_call(kernel, out_shape=(jax.ShapeDtypeStruct((count, width), BF...]
    broadcast_in_dim x2 -> x0, local copies, waits for them, and re-layouts: 2.5 us -> none  [the longest x1 1.38 us: shards(): produced = exchange(jnp.broadcast_to(part, (peers, tokens, columns)))]
    pallas_call x1, Pallas kernels: 8.22 us -> 10.7 us  [finish(): pl.pallas_call(kernel, out_shape=(jax.ShapeDtypeStruct((3, R, units), F32...]
    dot_general x6 -> x3, matrix products: 10.6 us -> 9.23 us  [times(): lax.dot_general(a, b, (((ca,), (cb,)), ((), ())), preferred_element_type=...]
  transfers between devices with their start and end apart: 14 -> 13, of which waited for: 12 -> 11; matrix products, arithmetic and copies ran while one was open for 10% -> 7% of each run, Pallas kernels for 4% -> 6%
where the time goes in v6:
time: 175 us; the launch traced here: 174 us
  waiting for transfers between devices  66.9 us (38%)
  Pallas kernels  31.4 us (18%)
  starting transfers between devices  25.8 us (15%)
  blocking collectives  20.8 us (12%)
  local copies, waits for them, and re-layouts  15.1 us (9%)
  matrix products  9.23 us (5%)
  other arithmetic  3.73 us (2%)
    all_to_all x3, waiting for transfers between devices, exchange(): return lax.all_to_all(pieces, 'expert', 0, 0, tiled=True)  35.2 us
    all_to_all x1, blocking collectives, exchange(): return lax.all_to_all(pieces, 'expert', 0, 0, tiled=True)  20.8 us
    all_to_all x3, starting transfers between devices, exchange(): return lax.all_to_all(pieces, 'expert', 0, 0, tiled=True)  17.5 us
    pallas_call x2, Pallas kernels, experts(): pl.pallas_call(kernel, out_shape=tuple((jax.ShapeDtypeStruct(*result) for...  17.1 us
    unnamed x50, local copies, waits for them, and re-layouts  13.9 us
    ppermute x6, waiting for transfers between devices, swap_cores(): return lax.ppermute(value, 'dp', [(0, 1), (1, 0)])  13.4 us
    ppermute x3, waiting for transfers between devices, add_copies(): other = lax.ppermute(rounded, 'expert', route)  12.1 us
    pallas_call x1, Pallas kernels, finish(): pl.pallas_call(kernel, out_shape=(jax.ShapeDtypeStruct((3, R, units), F32...  10.7 us
  transfers between devices with their start and end apart: 13, of which 11 were waited for; matrix products, arithmetic and copies ran while one was open for 7% of the time, Pallas kernels for 6%

profile of v6, /device:TPU:0, one launch (start us, length us, event | category | flops | bytes accessed | tf_op | source)
XLA Modules:
  0.0 173.9 jit_solution(2023592287416986219)
XLA Ops:
  0.7 1.5 copy-done.11
  2.2 1.4 copy-done.12
  3.6 0.7 copy-done.21
  4.3 0.7 copy-done.23
  5.0 1.0 pick_slots.1
  6.0 0.6 copy-done.19
  6.6 0.5 collective-permute-start.1
  7.1 2.3 %collective-permute-done.refs_1_ = bf16[192,3072]{1,0:T(8,128)(2,1)S(1)} collective-permute-done((bf16[192,3072]{1,0:T(8,128)(2,1)S(1)}, bf16[192,3072]{1,0:T(8,128)(2,1)S(1)}, u32[]{:S(2)}, u32[]{:S(2)}) %collective-permute-start) | collective-permute-done | bytes 1179680 | tf_op jit(solution)/shard_map/ppermute | solution.py:28
  9.5 1.7 collective-permute-done.1.refs_6_
  11.2 1.9 %copy-done.3 = bf16[1,1,1,3072,512]{4,3,2,1,0:T(8,128)(2,1)S(1)} copy-done((bf16[1,1,1,3072,512]{4,3,2,1,0:T(8,128)(2,1)S(1)}, bf16[1,1,1,3072,512]{4,3,2,1,0:T(8,128)(2,1)}, u32[]{:S(2)}) %copy-start.3) | copy-done | bytes 3145752
  13.0 1.9 %copy-done.5 = bf16[1,1,1,3072,512]{4,3,2,1,0:T(8,128)(2,1)S(1)} copy-done((bf16[1,1,1,3072,512]{4,3,2,1,0:T(8,128)(2,1)S(1)}, bf16[1,1,1,3072,512]{4,3,2,1,0:T(8,128)(2,1)}, u32[]{:S(2)}) %copy-start.5) | copy-done | bytes 3145752
  14.9 9.2 %experts_first.1 = (f32[384,512]{1,0:T(8,128)S(1)}, f32[384,512]{1,0:T(8,128)S(1)}, bf16[384,512]{1,0:T(8,128)(2,1)S(1)}, f32[4,8,48,384]{3,2,1,0:T(8,128)S(1)},...) custom-call(bf16[192,3072]{1,0:T(8,128)(2,1)S(1)} %get-tuple-element.21.refs_0_, ...), custom_call_target="tpu_custom_call" | custom-call | flops 6039797760 | bytes 18874368 | tf_op jit(solution)/shard_map/experts_first/pallas_call | solution.py:368
  24.1 0.2 collective-permute-start.2
  24.4 2.7 %collective-permute-done.2 = bf16[4,8,48,384]{3,2,1,0:T(8,128)(2,1)S(1)} collective-permute-done((bf16[4,8,48,384]{3,2,1,0:T(8,128)(2,1)S(1)}, bf16[4,8,48,384]{3,2,1,0:T(8,128)(2,1)S(1)}, u32[]{:S(2)}, u32[]{:S(2)}) %collective-permute-start.2) | collective-permute-done | bytes 1179680 | tf_op jit(solution)/shard_map/ppermute | solution.py:28
  27.1 1.3 add_convert_fusion.1
  28.4 9.4 %all-to-all-start = ((bf16[32,48,384]{2,1,0:T(8,128)(2,1)}), bf16[32,48,384]{2,1,0:T(8,128)(2,1)S(1)}, u32[]{:S(2)}, u32[]{:S(2)}) async-start(bf16[32,48,384]{2,1,0:T(8,128)(2,1)} %bitcast.12), calls=%async_computation | async-start | bytes 2359296 | tf_op jit(solution)/shard_map/all_to_all | solution.py:32
  38.0 0.3 convert_reduce_fusion
  38.6 0.8 dynamic-slice_bitcast_fusion.base_ref.top_ref
  39.5 17.8 %all-to-all-done = bf16[32,48,384]{2,1,0:T(8,128)(2,1)S(1)} async-done(((bf16[32,48,384]{2,1,0:T(8,128)(2,1)}), bf16[32,48,384]{2,1,0:T(8,128)(2,1)S(1)}, u32[]{:S(2)}, u32[]{:S(2)}) %all-to-all-start) | async-done | bytes 1179680 | tf_op jit(solution)/shard_map/all_to_all | solution.py:32
  57.3 0.3 combine.2
  57.6 1.3 collective-permute-start.3
  59.0 6.2 %collective-permute-done.3.incoming_ref = bf16[64,384]{1,0:T(8,128)(2,1)S(1)} collective-permute-done((bf16[64,384]{1,0:T(8,128)(2,1)S(1)}, bf16[64,384]{1,0:T(8,128)(2,1)S(1)}, u32[]{:S(2)}, u32[]{:S(2)}) %collective-permute-start.3) | collective-permute-done | bytes 49184 | tf_op jit(solution)/shard_map/ppermute | solution.py:449
  65.1 0.2 deal.1
  65.4 20.8 %all_to_all.20 = bf16[32,48,384]{2,1,0:T(8,128)(2,1)S(1)} all-to-all(bf16[32,48,384]{2,1,0:T(8,128)(2,1)S(1)} %bitcast.60), channel_id=1, replica_groups=mesh['dp'=2,'pipe'=2,'expert'=32] {'expert'}, dimensions={0} | all-to-all | bytes 2359296 | tf_op jit(solution)/shard_map/all_to_all | solution.py:32
  86.2 0.3 scale_rows.1.refs_0_
  86.5 2.8 %collective-permute-done.4.refs_1_ = bf16[192,3072]{1,0:T(8,128)(2,1)S(1)} collective-permute-done((bf16[192,3072]{1,0:T(8,128)(2,1)S(1)}, bf16[192,3072]{1,0:T(8,128)(2,1)S(1)}, u32[]{:S(2)}, u32[]{:S(2)}) %collective-permute-start.4) | collective-permute-done | bytes 1179680 | tf_op jit(solution)/shard_map/ppermute | solution.py:28
  89.4 1.9 %copy-done.4 = bf16[1,1,1,3072,512]{4,3,2,1,0:T(8,128)(2,1)S(1)} copy-done((bf16[1,1,1,3072,512]{4,3,2,1,0:T(8,128)(2,1)S(1)}, bf16[1,1,1,3072,512]{4,3,2,1,0:T(8,128)(2,1)}, u32[]{:S(2)}) %copy-start.4) | copy-done | bytes 3145752
  91.3 1.9 %copy-done.6 = bf16[1,1,1,3072,512]{4,3,2,1,0:T(8,128)(2,1)S(1)} copy-done((bf16[1,1,1,3072,512]{4,3,2,1,0:T(8,128)(2,1)S(1)}, bf16[1,1,1,3072,512]{4,3,2,1,0:T(8,128)(2,1)}, u32[]{:S(2)}) %copy-start.6) | copy-done | bytes 3145752
  93.2 7.9 %experts_last.1 = (bf16[384,128]{1,0:T(8,128)(2,1)S(1)}, f32[4,8,48,384]{3,2,1,0:T(8,128)S(1)}, bf16[4,8,48,384]{3,2,1,0:T(8,128)(2,1)S(1)}, bf16[3,384,512]{2,1,0:T(8,128)(2,1)S(1)}, bf16[384,3072]{1,0:T(8,128)(2,1)S(1)}) custom-call(bf16[192,3072]{1,0:T(8,128)(2,1)S(1)} %scale_rows.1.refs_0_, bf16[192,3072]{1,0:T(8,128)(2,1)S(1)} %collective-permute-done.4.refs_1_, ...), custom_call_target="tpu_custom_call" | custom-call | flops 3623878656 | bytes 18874368 | tf_op jit(solution)/shard_map/experts_last/pallas_call | solution.py:368
  101.3 2.7 %collective-permute-done.5 = bf16[4,8,48,384]{3,2,1,0:T(8,128)(2,1)S(1)} collective-permute-done((bf16[4,8,48,384]{3,2,1,0:T(8,128)(2,1)S(1)}, bf16[4,8,48,384]{3,2,1,0:T(8,128)(2,1)S(1)}, u32[]{:S(2)}, u32[]{:S(2)}) %collective-permute-start.5) | collective-permute-done | bytes 1179680 | tf_op jit(solution)/shard_map/ppermute | solution.py:28
  104.1 1.3 add_convert_fusion
  105.3 3.9 %all-to-all-start.2 = ((bf16[32,48,384]{2,1,0:T(8,128)(2,1)}), bf16[32,48,384]{2,1,0:T(8,128)(2,1)S(1)}, u32[]{:S(2)}, u32[]{:S(2)}) async-start(bf16[32,48,384]{2,1,0:T(8,128)(2,1)} %bitcast.24), calls=%async_computation.2 | async-start | bytes 2359296 | tf_op jit(solution)/shard_map/all_to_all | solution.py:32
  109.5 1.2 collective-permute-done.6
  110.7 1.8 %collective-permute-start.7 = (bf16[384,128]{1,0:T(8,128)(2,1)S(1)}, bf16[384,128]{1,0:T(8,128)(2,1)S(1)}, u32[]{:S(2)}, u32[]{:S(2)}) collective-permute-start(bf16[384,128]{1,0:T(8,128)(2,1)S(1)} %add_convert_fusion.4), channel_id=1, source_target_pairs={{0,1},{1,0},{2,3},{3,2},{4,5},{5,4},{6,7},{7,6},{8,9},{9,8},{10,11... | collective-permute-start | bytes 294920 | tf_op jit(solution)/shard_map/ppermute | solution.py:70
  112.5 17.5 %all-to-all-done.2 = bf16[32,48,384]{2,1,0:T(8,128)(2,1)S(1)} async-done(((bf16[32,48,384]{2,1,0:T(8,128)(2,1)}), bf16[32,48,384]{2,1,0:T(8,128)(2,1)S(1)}, u32[]{:S(2)}, u32[]{:S(2)}) %all-to-all-start.2) | async-done | bytes 1179680 | tf_op jit(solution)/shard_map/all_to_all | solution.py:32
  129.9 0.5 combine.3
  130.5 1.1 copy-done
  131.6 4.2 %all-to-all-start.3 = ((bf16[32,64,384]{2,1,0:T(8,128)(2,1)}), bf16[32,64,384]{2,1,0:T(8,128)(2,1)S(1)}, u32[]{:S(2)}, u32[]{:S(2)}) async-start(bf16[32,64,384]{2,1,0:T(8,128)(2,1)} %copy-done), calls=%async_computation.3 | async-start | bytes 3145728 | tf_op jit(solution)/shard_map/all_to_all | solution.py:32
  135.8 4.8 %fusion.5.refs_0_ = f32[384,384]{1,0:T(8,128)} fusion(bf16[384,3072]{1,0:T(8,128)(2,1)} %copy-done.7), kind=kOutput, calls=%fused_computation.22 | convolution fusion | flops 905969664 | bytes 2949120 | tf_op jit(solution)/shard_map/dot_general | solution.py:36
  140.6 1.8 %collective-permute-start.8 = (bf16[384,128]{1,0:T(8,128)(2,1)S(1)}, bf16[384,128]{1,0:T(8,128)(2,1)S(1)}, u32[]{:S(2)}, u32[]{:S(2)}) collective-permute-start(bf16[384,128]{1,0:T(8,128)(2,1)S(1)} %add_convert_fusion.3), channel_id=1, source_target_pairs={{0,2},{1,3},{2,0},{3,1},{4,6},{5,7},{6,4},{7,5},{8,10},{9,11},{10,... | collective-permute-start | bytes 294920 | tf_op jit(solution)/shard_map/ppermute | solution.py:70
  142.4 2.2 %fusion.6.refs_1_ = f32[384,384]{1,0:T(8,128)} fusion(bf16[384,3072]{1,0:T(8,128)(2,1)S(1)} %copy-done.10, bf16[384,3072]{1,0:T(8,128)(2,1)S(1)} %copy-done.8), kind=kOutput, calls=%fused_computation.23 | convolution fusion | flops 905969664 | bytes 5308416 | tf_op jit(solution)/shard_map/dot_general | solution.py:36
  144.6 10.7 %collective-permute-done.8 = bf16[384,128]{1,0:T(8,128)(2,1)S(1)} collective-permute-done((bf16[384,128]{1,0:T(8,128)(2,1)S(1)}, bf16[384,128]{1,0:T(8,128)(2,1)S(1)}, u32[]{:S(2)}, u32[]{:S(2)}) %collective-permute-start.8) | collective-permute-done | bytes 98336 | tf_op jit(solution)/shard_map/ppermute | solution.py:70
  155.3 2.2 %collective-permute-start.9 = (bf16[384,128]{1,0:T(8,128)(2,1)S(1)}, bf16[384,128]{1,0:T(8,128)(2,1)S(1)}, u32[]{:S(2)}, u32[]{:S(2)}) collective-permute-start(bf16[384,128]{1,0:T(8,128)(2,1)S(1)} %add_convert_fusion.2), channel_id=1, source_target_pairs={{0,6},{1,7},{2,4},{3,5},{4,2},{5,3},{6,0},{7,1},{8,14},{9,15},{10,... | collective-permute-start | bytes 294920 | tf_op jit(solution)/shard_map/ppermute | solution.py:70
  157.5 2.2 %fusion.7.refs_2_ = f32[384,384]{1,0:T(8,128)} fusion(bf16[384,3072]{1,0:T(8,128)(2,1)S(1)} %copy-done.10), kind=kOutput, calls=%fused_computation.24 | convolution fusion | flops 905969664 | bytes 2949120 | tf_op jit(solution)/shard_map/dot_general | solution.py:36
  159.8 1.4 collective-permute-done.9
  161.2 0.7 convert_add_fusion.sums_ref
  161.9 10.7 %finish.1 = (f32[3,64,512]{2,1,0:T(8,128)}, f32[64,1536]{1,0:T(8,128)}) custom-call(s32[1]{0:T(128)} %bitcast.28.dp_ref, f32[384,128]{1,0:T(8,128)} %convert_add_fusion.sums_ref, f32[384,384]{1,0:T(8,128)} %fusion.5.refs_0_, f32[384,384]{1,0:T(8,128)} %fusion.6.refs_1_, f32[384,384]{1,0:T(8,128)} %fusion.7.refs_2_, bf16[384,3072]{1,0:T(8,128)(2,1)} %copy-done.7, ...), custom_call_target="tpu_custom_call" | custom-call | flops 301989888 | bytes 5308416 | tf_op jit(solution)/shard_map/finish/pallas_call | solution.py:158
  172.6 1.3 side_by_side.1
  (59 shorter events, 1.3 us)
Async XLA Ops:
  0.6 10.5 %copy-start.1 = (bf16[1,1,1,512,3072]{4,3,2,1,0:T(8,128)(2,1)S(1)}, bf16[1,1,1,512,3072]{4,3,2,1,0:T(8,128)(2,1)}, u32[]{:S(2)}) copy-start(bf16[1,1,1,512,3072]{4,3,2,1,0:T(8,128)(2,1)} %param.14) | copy-start | bytes 9437188
  0.7 1.6 copy-start.11
  2.2 1.4 copy-start.12
  3.6 0.7 copy-start.21
  4.3 0.7 copy-start.23
  6.0 0.6 copy-start.19
  6.6 2.8 %collective-permute-start = (bf16[192,3072]{1,0:T(8,128)(2,1)S(1)}, bf16[192,3072]{1,0:T(8,128)(2,1)S(1)}, u32[]{:S(2)}, u32[]{:S(2)}) collective-permute-start(bf16[192,3072]{1,0:T(8,128)(2,1)S(1)} %get-tuple-element.21.refs_0_), channel_id=1, source_target_pairs={{0,64},{64,0},{1,65},{65,1},{2,66},{66,2},{3,67},{67,3},{4,68},{68... | collective-permute-start | bytes 3538952 | tf_op jit(solution)/shard_map/ppermute | solution.py:28
  6.6 4.5 %collective-permute-start.1 = (bf16[192,3072]{1,0:T(8,128)(2,1)S(1)}, bf16[192,3072]{1,0:T(8,128)(2,1)S(1)}, u32[]{:S(2)}, u32[]{:S(2)}) collective-permute-start(bf16[192,3072]{1,0:T(8,128)(2,1)S(1)} %get-tuple-element.22.refs_5_), channel_id=1, source_target_pairs={{0,64},{64,0},{1,65},{65,1},{2,66},{66,2},{3,67},{67,3},{4,68},{68... | collective-permute-start | bytes 3538952 | tf_op jit(solution)/shard_map/ppermute | solution.py:28
  11.2 1.9 %copy-start.3 = (bf16[1,1,1,3072,512]{4,3,2,1,0:T(8,128)(2,1)S(1)}, bf16[1,1,1,3072,512]{4,3,2,1,0:T(8,128)(2,1)}, u32[]{:S(2)}) copy-start(bf16[1,1,1,3072,512]{4,3,2,1,0:T(8,128)(2,1)} %param.12) | copy-start | bytes 9437188
  13.0 1.9 %copy-start.5 = (bf16[1,1,1,3072,512]{4,3,2,1,0:T(8,128)(2,1)S(1)}, bf16[1,1,1,3072,512]{4,3,2,1,0:T(8,128)(2,1)}, u32[]{:S(2)}) copy-start(bf16[1,1,1,3072,512]{4,3,2,1,0:T(8,128)(2,1)} %param.13) | copy-start | bytes 9437188
  24.1 4.2 %copy-start.7 = (bf16[384,3072]{1,0:T(8,128)(2,1)}, bf16[384,3072]{1,0:T(8,128)(2,1)S(1)}, u32[]{:S(2)}) copy-start(bf16[384,3072]{1,0:T(8,128)(2,1)S(1)} %get-tuple-element.34.refs_3_) | copy-start | bytes 7077892
  24.1 4.2 %copy-start.14 = (f32[384,512]{1,0:T(8,128)}, f32[384,512]{1,0:T(8,128)S(1)}, u32[]{:S(2)}) copy-start(f32[384,512]{1,0:T(8,128)S(1)} %get-tuple-element.27.refs_5_) | copy-start | bytes 2359300
  24.1 4.2 %copy-start.16 = (f32[384,512]{1,0:T(8,128)}, f32[384,512]{1,0:T(8,128)S(1)}, u32[]{:S(2)}) copy-start(f32[384,512]{1,0:T(8,128)S(1)} %get-tuple-element.28.refs_6_) | copy-start | bytes 2359300
  24.1 2.9 %collective-permute-start.2 = (bf16[4,8,48,384]{3,2,1,0:T(8,128)(2,1)S(1)}, bf16[4,8,48,384]{3,2,1,0:T(8,128)(2,1)S(1)}, u32[]{:S(2)}, u32[]{:S(2)}) collective-permute-start(bf16[4,8,48,384]{3,2,1,0:T(8,128)(2,1)S(1)} %get-tuple-element.24), channel_id=1, source_target_pairs={{0,64},{64,0},{1,65},{65,1},{2,66},{66,2},{3,67},{67,3},{4,68},{68... | collective-permute-start | bytes 3538952 | tf_op jit(solution)/shard_map/ppermute | solution.py:28
  28.3 9.5 %copy-start.22 = (s32[1,4,64,2]{2,3,1,0:T(2,128)S(1)}, s32[1,4,64,2]{2,3,1,0:T(2,128)}, u32[]{:S(2)}) copy-start(s32[1,4,64,2]{2,3,1,0:T(2,128)} %param.10) | copy-start | bytes 6148
  28.4 28.9 %all-to-all-start = ((bf16[32,48,384]{2,1,0:T(8,128)(2,1)}), bf16[32,48,384]{2,1,0:T(8,128)(2,1)S(1)}, u32[]{:S(2)}, u32[]{:S(2)}) async-start(bf16[32,48,384]{2,1,0:T(8,128)(2,1)} %bitcast.12), calls=%async_computation | async-start | bytes 2359296 | tf_op jit(solution)/shard_map/all_to_all | solution.py:32
  37.8 48.4 %copy-start.20 = (f32[192,128]{1,0:T(8,128)S(1)}, f32[192,128]{1,0:T(8,128)}, u32[]{:S(2)}) copy-start(f32[192,128]{1,0:T(8,128)} %copy-done.19) | copy-start | bytes 294916
  57.3 32.1 %copy-start.18 = (f32[1,1,1,3,512,64]{4,5,3,2,1,0:T(8,128)S(1)}, f32[1,1,1,3,512,64]{4,5,3,2,1,0:T(8,128)}, u32[]{:S(2)}) copy-start(f32[1,1,1,3,512,64]{4,5,3,2,1,0:T(8,128)} %param.15) | copy-start | bytes 1179652
  57.6 7.5 %collective-permute-start.3 = (bf16[64,384]{1,0:T(8,128)(2,1)S(1)}, bf16[64,384]{1,0:T(8,128)(2,1)S(1)}, u32[]{:S(2)}, u32[]{:S(2)}) collective-permute-start(bf16[64,384]{1,0:T(8,128)(2,1)S(1)} %bitcast.62), channel_id=1, source_target_pairs={{32,0},{33,1},{34,2},{35,3},{36,4},{37,5},{38,6},{39,7},{40,8},{41... | collective-permute-start | bytes 147464 | tf_op jit(solution)/shard_map/ppermute | solution.py:449
  65.4 24.0 %copy-start.2 = (bf16[1,1,1,512,3072]{4,3,2,1,0:T(8,128)(2,1)S(1)}, bf16[1,1,1,512,3072]{4,3,2,1,0:T(8,128)(2,1)}, u32[]{:S(2)}) copy-start(bf16[1,1,1,512,3072]{4,3,2,1,0:T(8,128)(2,1)} %param.14) | copy-start | bytes 9437188
  65.4 24.0 %copy-start.15 = (f32[384,512]{1,0:T(8,128)S(1)}, f32[384,512]{1,0:T(8,128)}, u32[]{:S(2)}) copy-start(f32[384,512]{1,0:T(8,128)} %copy-done.14) | copy-start | bytes 2359300
  65.4 24.0 %copy-start.17 = (f32[384,512]{1,0:T(8,128)S(1)}, f32[384,512]{1,0:T(8,128)}, u32[]{:S(2)}) copy-start(f32[384,512]{1,0:T(8,128)} %copy-done.16) | copy-start | bytes 2359300
  86.4 2.9 %collective-permute-start.4 = (bf16[192,3072]{1,0:T(8,128)(2,1)S(1)}, bf16[192,3072]{1,0:T(8,128)(2,1)S(1)}, u32[]{:S(2)}, u32[]{:S(2)}) collective-permute-start(bf16[192,3072]{1,0:T(8,128)(2,1)S(1)} %scale_rows.1.refs_0_), channel_id=1, source_target_pairs={{0,64},{64,0},{1,65},{65,1},{2,66},{66,2},{3,67},{67,3},{4,68},{68... | collective-permute-start | bytes 3538952 | tf_op jit(solution)/shard_map/ppermute | solution.py:28
  89.4 1.9 %copy-start.4 = (bf16[1,1,1,3072,512]{4,3,2,1,0:T(8,128)(2,1)S(1)}, bf16[1,1,1,3072,512]{4,3,2,1,0:T(8,128)(2,1)}, u32[]{:S(2)}) copy-start(bf16[1,1,1,3072,512]{4,3,2,1,0:T(8,128)(2,1)} %param.12) | copy-start | bytes 9437188
  91.3 1.9 %copy-start.6 = (bf16[1,1,1,3072,512]{4,3,2,1,0:T(8,128)(2,1)S(1)}, bf16[1,1,1,3072,512]{4,3,2,1,0:T(8,128)(2,1)}, u32[]{:S(2)}) copy-start(bf16[1,1,1,3072,512]{4,3,2,1,0:T(8,128)(2,1)} %param.13) | copy-start | bytes 9437188
  101.1 4.2 %copy-start.9 = (bf16[384,3072]{1,0:T(8,128)(2,1)}, bf16[384,3072]{1,0:T(8,128)(2,1)S(1)}, u32[]{:S(2)}) copy-start(bf16[384,3072]{1,0:T(8,128)(2,1)S(1)} %get-tuple-element.35.refs_4_) | copy-start | bytes 7077892
  101.1 4.2 %copy-start.13 = (bf16[3,384,512]{2,1,0:T(8,128)(2,1)}, bf16[3,384,512]{2,1,0:T(8,128)(2,1)S(1)}, u32[]{:S(2)}) copy-start(bf16[3,384,512]{2,1,0:T(8,128)(2,1)S(1)} %get-tuple-element.36.refs_5_) | copy-start | bytes 3538948
  101.1 2.9 %collective-permute-start.5 = (bf16[4,8,48,384]{3,2,1,0:T(8,128)(2,1)S(1)}, bf16[4,8,48,384]{3,2,1,0:T(8,128)(2,1)S(1)}, u32[]{:S(2)}, u32[]{:S(2)}) collective-permute-start(bf16[4,8,48,384]{3,2,1,0:T(8,128)(2,1)S(1)} %get-tuple-element.31), channel_id=1, source_target_pairs={{0,64},{64,0},{1,65},{65,1},{2,66},{66,2},{3,67},{67,3},{4,68},{68... | collective-permute-start | bytes 3538952 | tf_op jit(solution)/shard_map/ppermute | solution.py:28
  105.3 24.6 %all-to-all-start.2 = ((bf16[32,48,384]{2,1,0:T(8,128)(2,1)}), bf16[32,48,384]{2,1,0:T(8,128)(2,1)S(1)}, u32[]{:S(2)}, u32[]{:S(2)}) async-start(bf16[32,48,384]{2,1,0:T(8,128)(2,1)} %bitcast.24), calls=%async_computation.2 | async-start | bytes 2359296 | tf_op jit(solution)/shard_map/all_to_all | solution.py:32
  109.3 1.4 collective-permute-start.6
  110.7 29.9 %collective-permute-start.7 = (bf16[384,128]{1,0:T(8,128)(2,1)S(1)}, bf16[384,128]{1,0:T(8,128)(2,1)S(1)}, u32[]{:S(2)}, u32[]{:S(2)}) collective-permute-start(bf16[384,128]{1,0:T(8,128)(2,1)S(1)} %add_convert_fusion.4), channel_id=1, source_target_pairs={{0,1},{1,0},{2,3},{3,2},{4,5},{5,4},{6,7},{7,6},{8,9},{9,8},{10,11... | collective-permute-start | bytes 294920 | tf_op jit(solution)/shard_map/ppermute | solution.py:70
  130.5 1.1 copy-start
  131.6 40.9 %all-to-all-start.3 = ((bf16[32,64,384]{2,1,0:T(8,128)(2,1)}), bf16[32,64,384]{2,1,0:T(8,128)(2,1)S(1)}, u32[]{:S(2)}, u32[]{:S(2)}) async-start(bf16[32,64,384]{2,1,0:T(8,128)(2,1)} %copy-done), calls=%async_computation.3 | async-start | bytes 3145728 | tf_op jit(solution)/shard_map/all_to_all | solution.py:32
  135.8 6.6 %copy-start.8 = (bf16[384,3072]{1,0:T(8,128)(2,1)S(1)}, bf16[384,3072]{1,0:T(8,128)(2,1)}, u32[]{:S(2)}) copy-start(bf16[384,3072]{1,0:T(8,128)(2,1)} %copy-done.7) | copy-start | bytes 7077892
  135.8 6.6 %copy-start.10 = (bf16[384,3072]{1,0:T(8,128)(2,1)S(1)}, bf16[384,3072]{1,0:T(8,128)(2,1)}, u32[]{:S(2)}) copy-start(bf16[384,3072]{1,0:T(8,128)(2,1)} %copy-done.9) | copy-start | bytes 7077892
  140.6 14.7 %collective-permute-start.8 = (bf16[384,128]{1,0:T(8,128)(2,1)S(1)}, bf16[384,128]{1,0:T(8,128)(2,1)S(1)}, u32[]{:S(2)}, u32[]{:S(2)}) collective-permute-start(bf16[384,128]{1,0:T(8,128)(2,1)S(1)} %add_convert_fusion.3), channel_id=1, source_target_pairs={{0,2},{1,3},{2,0},{3,1},{4,6},{5,7},{6,4},{7,5},{8,10},{9,11},{10,... | collective-permute-start | bytes 294920 | tf_op jit(solution)/shard_map/ppermute | solution.py:70
  155.3 5.9 %collective-permute-start.9 = (bf16[384,128]{1,0:T(8,128)(2,1)S(1)}, bf16[384,128]{1,0:T(8,128)(2,1)S(1)}, u32[]{:S(2)}, u32[]{:S(2)}) collective-permute-start(bf16[384,128]{1,0:T(8,128)(2,1)S(1)} %add_convert_fusion.2), channel_id=1, source_target_pairs={{0,6},{1,7},{2,4},{3,5},{4,2},{5,3},{6,0},{7,1},{8,14},{9,15},{10,... | collective-permute-start | bytes 294920 | tf_op jit(solution)/shard_map/ppermute | solution.py:70

commit v7 on v6

--- a/solution.py
+++ b/solution.py
@@ -174,19 +174,20 @@
     )(dp_index.reshape(1), sums, *squares, *rows16, grads)
 
 
-def pick_slots(own_expert, routes, mix, inputs, grads):
+def pick_slots(own_expert, routes, values, mix=None):
     micro, _, tokens = routes.shape
-    width = inputs.shape[1]
+    width = values.shape[1]
     block = width // 4
     count = micro * CAP
-
-    def kernel(expert_ref, routes_ref, mix_ref, inputs_ref, grads_ref, picked_ref, scaled_ref, w_ref):
+    weighted = mix is not None
+
+    def kernel(expert_ref, routes_ref, *refs):
+        values_ref, slots_ref = (refs[weighted], refs[weighted + 1])
         expert = expert_ref[0]
         filler = jnp.zeros((8 - micro, tokens), F32)
         first = routes_ref[:, 0, :] == expert
         second = routes_ref[:, 1, :] == expert
         hit = jnp.where(first | second, 1.0, 0.0)
-        weight = jnp.where(first, mix_ref[:, 0, :], 0.0) + jnp.where(second, mix_ref[:, 1, :], 0.0)
         earlier = lax.broadcasted_iota(jnp.int32, (tokens, tokens), 0) < lax.broadcasted_iota(
             jnp.int32, (tokens, tokens), 1
         )
@@ -195,29 +196,33 @@
         base = lax.broadcasted_iota(jnp.int32, (micro, tokens), 0).astype(F32) * CAP
         place = jnp.where(hit > 0.0, rank + base, -1.0)
         place = jnp.concatenate([place[m : m + 1] for m in range(micro)], axis=1)
-        weight = jnp.concatenate([weight[m : m + 1] for m in range(micro)], axis=1)
-        slot = lax.broadcasted_iota(jnp.int32, (micro * CAP, micro * tokens), 0).astype(F32)
+        slot = lax.broadcasted_iota(jnp.int32, (count, micro * tokens), 0).astype(F32)
         chosen = slot == place
         pick = jnp.where(chosen, 1.0, 0.0).astype(BF)
-        by_slot = jnp.sum(jnp.where(chosen, weight, 0.0), axis=1, keepdims=True)
-        w_ref[...] = jnp.broadcast_to(by_slot, (count, 128))
+        by_slot = 1.0
+        if weighted:
+            mix_ref, w_ref = (refs[0], refs[3])
+            weight = jnp.where(first, mix_ref[:, 0, :], 0.0)
+            weight = weight + jnp.where(second, mix_ref[:, 1, :], 0.0)
+            weight = jnp.concatenate([weight[m : m + 1] for m in range(micro)], axis=1)
+            by_slot = jnp.sum(jnp.where(chosen, weight, 0.0), axis=1, keepdims=True)
+            w_ref[...] = jnp.broadcast_to(by_slot, (count, 128))
         for at in range(0, width, block):
             held = pl.ds(at, block)
-            picked_ref[:, held] = times(pick, inputs_ref[:, held]).astype(BF)
-            scaled_ref[:, held] = (by_slot * times(pick, grads_ref[:, held])).astype(BF)
-
-    return pl.pallas_call(
-        kernel,
-        out_shape=(
-            jax.ShapeDtypeStruct((count, width), BF),
-            jax.ShapeDtypeStruct((count, width), BF),
-            jax.ShapeDtypeStruct((count, 128), F32),
-        ),
-        in_specs=[IN_SMEM] + [IN_VMEM] * 4,
-        compiler_params=pltpu.CompilerParams(vmem_limit_bytes=14 << 20),
-        cost_estimate=cost(4 * count * micro * tokens * width, 60 << 20),
-        name="pick_slots",
-    )(own_expert.reshape(1), routes, mix, inputs, grads)
+            slots_ref[:, held] = (by_slot * times(pick, values_ref[:, held])).astype(BF)
+
+    slots_shape = jax.ShapeDtypeStruct((count, width), BF)
+    operands = (own_expert.reshape(1), routes, *([mix] if weighted else []), values)
+    return pl.pallas_call(
+        kernel,
+        out_shape=(slots_shape, jax.ShapeDtypeStruct((count, 128), F32))
+        if weighted
+        else slots_shape,
+        in_specs=[IN_SMEM] + [IN_VMEM] * (len(operands) - 1),
+        compiler_params=pltpu.CompilerParams(vmem_limit_bytes=12 << 20),
+        cost_estimate=cost(2 * count * micro * tokens * width, 2 * (count + micro * tokens) * width),
+        name="pick_weighted" if weighted else "pick_slots",
+    )(*operands)
 
 
 def scale_rows(pieces, slot_weights):
@@ -290,67 +295,157 @@
     )(last.astype(jnp.int32).reshape(1), top_part, incoming, pick)
 
 
-def experts(gate, up, down, grads_both, copies, inputs_both=None, forward=None, right=None):
-    fresh = forward is None
+def fetch(arrays):
+    count = len(arrays)
+
+    def kernel(*refs):
+        done = refs[-1]
+        moves = [
+            pltpu.make_async_copy(refs[i], refs[count + i], done.at[i]) for i in range(count)
+        ]
+        for move in moves:
+            move.start()
+        for move in moves:
+            move.wait()
+
+    return pl.pallas_call(
+        kernel,
+        out_shape=tuple(jax.ShapeDtypeStruct(a.shape, a.dtype) for a in arrays),
+        in_specs=[IN_HBM] * count,
+        out_specs=(IN_VMEM,) * count,
+        scratch_shapes=[pltpu.SemaphoreType.DMA((count,))],
+        compiler_params=pltpu.CompilerParams(vmem_limit_bytes=12 << 20),
+    )(*arrays)
+
+
+def expert_slopes(down, grads_both, forward, right):
+    slots, width = grads_both[0].shape
+    count = 2 * slots
+    units = right.shape[2]
+    square = (count, units)
+
+    def kernel(*refs):
+        own_ref, partner_ref, down_ref, slope_ref, silu_ref, hidden_ref, right_ref = refs[:7]
+        sums_ref, gg_ref, gu_ref, grads_hbm, rows_hbm, done = refs[7:]
+        moves = []
+
+        def keep(source, target):
+            move = pltpu.make_async_copy(source, target, done.at[len(moves)])
+            move.start()
+            moves.append(move)
+
+        keep(own_ref, rows_hbm.at[pl.ds(0, slots)])
+        keep(partner_ref, rows_hbm.at[pl.ds(slots, slots)])
+        keep(hidden_ref, grads_hbm.at[2])
+        rows = jnp.concatenate([own_ref[...], partner_ref[...]])
+        grad_hidden = times(rows, down_ref[...], 1, 1)
+        gg_ref[...] = (grad_hidden * slope_ref[...]).astype(BF)
+        gu_ref[...] = (grad_hidden * silu_ref[...]).astype(BF)
+        keep(gg_ref, grads_hbm.at[0])
+        keep(gu_ref, grads_hbm.at[1])
+        right16 = right_ref[...].astype(BF)
+        of_inputs = times(gg_ref[...], right16[0], 1, 1) + times(gu_ref[...], right16[1], 1, 1)
+        of_grads = times(hidden_ref[...], right16[2], 1, 1)
+        sums_ref[...] = jnp.concatenate([of_inputs, of_grads], axis=1).astype(BF)
+        for move in moves:
+            move.wait()
+
+    return pl.pallas_call(
+        kernel,
+        out_shape=(
+            jax.ShapeDtypeStruct((count, 2 * R), BF),
+            jax.ShapeDtypeStruct(square, BF),
+            jax.ShapeDtypeStruct(square, BF),
+            jax.ShapeDtypeStruct((3, *square), BF),
+            jax.ShapeDtypeStruct((count, width), BF),
+        ),
+        in_specs=[IN_VMEM] * 7,
+        out_specs=(*[IN_VMEM] * 3, *[IN_HBM] * 2),
+        scratch_shapes=[pltpu.SemaphoreType.DMA((5,))],
+        compiler_params=pltpu.CompilerParams(vmem_limit_bytes=20 << 20),
+        cost_estimate=cost(
+            2 * count * width * units, 2 * width * (units + 2 * count) + 12 * count * units
+        ),
+        name="expert_slopes",
+    )(*grads_both, down, *forward, right)
+
+
+def expert_rows(gate, up, grad_gate, grad_up, copies):
+    width, units = gate.shape
+    count = grad_gate.shape[0]
+    slots = count // 2
+    columns = width // copies
+    shape = (MICRO, copies, CAP, columns)
+
+    def kernel(gg_ref, gu_ref, gate_hbm, up_hbm, own_ref, par_ref, gate_ref, up_ref, done):
+        def arrival(c, which):
+            source, target = ((gate_hbm, gate_ref), (up_hbm, up_ref))[which]
+            held = pl.ds(c * columns, columns)
+            return pltpu.make_async_copy(source.at[held], target.at[c], done.at[which, c])
+
+        for c in range(copies):
+            arrival(c, 0).start()
+            arrival(c, 1).start()
+        for c in range(copies):
+            arrival(c, 0).wait()
+            total = times(gg_ref[...], gate_ref[c], 1, 1)
+            arrival(c, 1).wait()
+            total = total + times(gu_ref[...], up_ref[c], 1, 1)
+            for m in range(MICRO):
+                own_ref[m, c] = total[m * CAP : (m + 1) * CAP]
+                par_ref[m, c] = total[slots + m * CAP : slots + (m + 1) * CAP].astype(BF)
+
+    return pl.pallas_call(
+        kernel,
+        out_shape=(jax.ShapeDtypeStruct(shape, F32), jax.ShapeDtypeStruct(shape, BF)),
+        in_specs=[IN_VMEM] * 2 + [IN_HBM] * 2,
+        scratch_shapes=[
+            pltpu.VMEM((copies, columns, units), BF),
+            pltpu.VMEM((copies, columns, units), BF),
+            pltpu.SemaphoreType.DMA((2, copies)),
+        ],
+        compiler_params=pltpu.CompilerParams(vmem_limit_bytes=24 << 20),
+        cost_estimate=cost(
+            4 * count * width * units, 4 * width * units + 6 * count * width
+        ),
+        name="expert_rows",
+    )(grad_gate, grad_up, gate, up)
+
+
+def experts(gate, up, down, grads_both, copies, inputs_both):
     slots, width = grads_both[0].shape
     count = 2 * slots
     units = gate.shape[1]
     columns = width // copies
     halves_shape = (MICRO, copies, CAP, columns)
     square = (count, units)
-    operands = [*grads_both, down, gate, up] + ([*inputs_both] if fresh else [*forward, right])
-    made = [(halves_shape, F32), (halves_shape, BF)]
-    if fresh:
-        made = [(square, F32), (square, F32), (square, BF)] + made
-        kept = []
-    else:
-        made = [((count, 2 * R), BF)] + made
-        kept = [((3, *square), BF)]
-    kept += [((count, width), BF)]
+    made = [(square, F32), (square, F32), (square, BF), (halves_shape, F32), (halves_shape, BF)]
 
     def kernel(*refs):
-        ins, refs = (refs[: len(operands)], refs[len(operands) :])
-        outs, refs = (refs[: len(made)], refs[len(made) :])
-        keeps, (gg_ref, gu_ref, done) = (refs[: len(kept)], refs[len(kept) :])
-        down_ref, gate_ref, up_ref = ins[2:5]
-        own_ref, par_ref = outs[-2:]
-        moves = []
-
-        def keep(source, target):
-            move = pltpu.make_async_copy(source, target, done.at[len(moves)])
+        grads_refs, (down_ref, gate_ref, up_ref), rows_refs = (refs[:2], refs[2:5], refs[5:7])
+        slope_ref, silu_ref, hidden_ref, own_ref, par_ref, rows_hbm = refs[7:13]
+        gg_ref, gu_ref, done = refs[13:]
+        moves = [
+            pltpu.make_async_copy(rows_refs[i], rows_hbm.at[pl.ds(i * slots, slots)], done.at[i])
+            for i in range(2)
+        ]
+        for move in moves:
             move.start()
-            moves.append(move)
-
-        rows_refs = ins[5:7] if fresh else ins[:2]
-        for i in range(2):
-            keep(rows_refs[i], keeps[-1].at[pl.ds(i * slots, slots)])
 
         def both(pair):
             return jnp.concatenate([pair[0][...], pair[1][...]])
 
-        if fresh:
-            inputs = both(ins[5:7])
-            pre_gate = times(inputs, gate_ref[...])
-            pre_up = times(inputs, up_ref[...])
-            sigmoid = 1.0 / (1.0 + jnp.exp(-pre_gate))
-            silu = pre_gate * sigmoid
-            outs[0][...] = pre_up * sigmoid * (1.0 + pre_gate * (1.0 - sigmoid))
-            outs[1][...] = silu
-            outs[2][...] = (silu * pre_up).astype(BF)
-            slope_ref, silu_ref = outs[:2]
-        else:
-            slope_ref, silu_ref, hidden_ref, right_ref = ins[5:9]
-            keep(hidden_ref, keeps[0].at[2])
-        grad_hidden = times(both(ins[:2]), down_ref[...], 1, 1)
+        inputs = both(rows_refs)
+        pre_gate = times(inputs, gate_ref[...])
+        pre_up = times(inputs, up_ref[...])
+        sigmoid = 1.0 / (1.0 + jnp.exp(-pre_gate))
+        silu = pre_gate * sigmoid
+        slope_ref[...] = pre_up * sigmoid * (1.0 + pre_gate * (1.0 - sigmoid))
+        silu_ref[...] = silu
+        hidden_ref[...] = (silu * pre_up).astype(BF)
+        grad_hidden = times(both(grads_refs), down_ref[...], 1, 1)
         gg_ref[...] = (grad_hidden * slope_ref[...]).astype(BF)
         gu_ref[...] = (grad_hidden * silu_ref[...]).astype(BF)
-        if not fresh:
-            keep(gg_ref, keeps[0].at[0])
-            keep(gu_ref, keeps[0].at[1])
-            right16 = right_ref[...].astype(BF)
-            of_inputs = times(gg_ref[...], right16[0], 1, 1) + times(gu_ref[...], right16[1], 1, 1)
-            of_grads = times(hidden_ref[...], right16[2], 1, 1)
-            outs[0][...] = jnp.concatenate([of_inputs, of_grads], axis=1).astype(BF)
 
         def column(c, carry):
             held = pl.ds(pl.multiple_of(c * columns, columns), columns)
@@ -367,20 +462,21 @@
 
     return pl.pallas_call(
         kernel,
-        out_shape=tuple(jax.ShapeDtypeStruct(*result) for result in made + kept),
-        in_specs=[IN_VMEM] * len(operands),
-        out_specs=(*[IN_VMEM] * len(made), *[IN_HBM] * len(kept)),
+        out_shape=(
+            *[jax.ShapeDtypeStruct(*result) for result in made],
+            jax.ShapeDtypeStruct((count, width), BF),
+        ),
+        in_specs=[IN_VMEM] * 7,
+        out_specs=(*[IN_VMEM] * 5, IN_HBM),
         scratch_shapes=[
             pltpu.VMEM(square, BF),
             pltpu.VMEM(square, BF),
-            pltpu.SemaphoreType.DMA((5,)),
+            pltpu.SemaphoreType.DMA((2,)),
         ],
         compiler_params=pltpu.CompilerParams(vmem_limit_bytes=30 << 20),
-        cost_estimate=cost(
-            2 * count * width * units * (5 if fresh else 3), 2 * width * (3 * units + 4 * count)
-        ),
-        name="experts_first" if fresh else "experts_last",
-    )(*operands)
+        cost_estimate=cost(10 * count * width * units, 2 * width * (3 * units + 4 * count)),
+        name="experts_first",
+    )(*grads_both, down, gate, up, *inputs_both)
 
 
 def side_by_side(pieces):
@@ -422,16 +518,15 @@
     deal_pick = (first | second).astype(BF)
     part_pick = deal_pick.reshape(EXPERTS, CAP, tokens).transpose(0, 2, 1)
 
-    own_slots, own_grads, slot_weights = pick_slots(
-        major,
-        routes[0].transpose(0, 2, 1),
-        mix_weights[0].transpose(0, 2, 1),
-        own_inputs,
-        top_rows,
-    )
+    routes_by_choice = routes[0].transpose(0, 2, 1)
+    own_slots = pick_slots(major, routes_by_choice, own_inputs)
     inputs_both = (own_slots, swap_cores(own_slots))
+    own_grads, slot_weights = pick_slots(
+        major, routes_by_choice, top_rows, mix_weights[0].transpose(0, 2, 1)
+    )
+    gate_first, up_first = fetch((gate, up))
     *forward, own_half, other_half, inputs = experts(
-        gate, up, down, (own_grads, swap_cores(own_grads)), copies, inputs_both=inputs_both
+        gate_first, up_first, down, (own_grads, swap_cores(own_grads)), copies, inputs_both=inputs_both
     )
 
     def reduced(own_half, other_half, base, targets):
@@ -450,21 +545,16 @@
     base, pieces = deal(last, top_part, incoming, deal_pick, copies)
     own_rows = exchange(pieces.reshape(peers, CAP, columns))
     own_grads = scale_rows(own_rows.reshape(MICRO, copies, CAP, columns), slot_weights)
-    sums, own_half, other_half, grads, grad_rows = experts(
-        gate,
-        up,
-        down,
-        (own_grads, swap_cores(own_grads)),
-        copies,
-        forward=forward,
-        right=right,
-    )
+    sums, grad_gate, grad_up, grads, grad_rows = expert_slopes(
+        down, (own_grads, swap_cores(own_grads)), forward, right
+    )
+    other_sums = swap_cores(sums)
+    own_half, other_half = expert_rows(gate, up, grad_gate, grad_up, copies)
     parts = reduced(own_half, other_half, base, peers)
     produced = exchange(parts)
     produced = side_by_side(produced.reshape(MICRO, copies, tokens, columns))
 
-    other = swap_cores(sums)
-    sums = sums.astype(F32) + jnp.concatenate([other[slots:], other[:slots]]).astype(F32)
+    sums = sums.astype(F32) + jnp.concatenate([other_sums[slots:], other_sums[:slots]]).astype(F32)
     sums = add_copies(sums, copies)
     squares = (
         times(inputs, inputs, 1, 1),

time: 175 us -> 172 us (0.983)
  Pallas kernels: 31.4 us -> 35.7 us
  waiting for transfers between devices: 66.9 us -> 63.2 us
  local copies, waits for them, and re-layouts: 15.1 us -> 11.5 us
    pallas_call x3 -> x6, Pallas kernels: 18.1 us -> 22.4 us  [the longest x1 9.15 us: experts(): pl.pallas_call(kernel, out_shape=(*[jax.ShapeDtypeStruct(*result) for res...]
    ppermute x6, waiting for transfers between devices: 13.4 us -> 9.66 us  [swap_cores(): return lax.ppermute(value, 'dp', [(0, 1), (1, 0)])]
    unnamed x50 -> x38, local copies, waits for them, and re-layouts: 13.9 us -> 10.3 us
  transfers between devices with their start and end apart: 13 -> 13, of which waited for: 11 -> 10; matrix products, arithmetic and copies ran while one was open for 7% -> 7% of each run, Pallas kernels for 6% -> 7%
where the time goes in v7:
time: 172 us; the launch traced here: 171 us
  waiting for transfers between devices  63.2 us (37%)
  Pallas kernels  35.7 us (21%)
  starting transfers between devices  26.1 us (15%)
  blocking collectives  20.8 us (12%)
  local copies, waits for them, and re-layouts  11.5 us (7%)
  matrix products  9.19 us (5%)
  other arithmetic  3.85 us (2%)
    all_to_all x3, waiting for transfers between devices, exchange(): return lax.all_to_all(pieces, 'expert', 0, 0, tiled=True)  35.2 us
    all_to_all x1, blocking collectives, exchange(): return lax.all_to_all(pieces, 'expert', 0, 0, tiled=True)  20.8 us
    all_to_all x3, starting transfers between devices, exchange(): return lax.all_to_all(pieces, 'expert', 0, 0, tiled=True)  17.4 us
    ppermute x3, waiting for transfers between devices, add_copies(): other = lax.ppermute(rounded, 'expert', route)  12.2 us
    pallas_call x1, Pallas kernels, finish(): pl.pallas_call(kernel, out_shape=(jax.ShapeDtypeStruct((3, R, units), F32...  10.7 us
    unnamed x38, local copies, waits for them, and re-layouts  10.3 us
    ppermute x6, waiting for transfers between devices, swap_cores(): return lax.ppermute(value, 'dp', [(0, 1), (1, 0)])  9.66 us
    dot_general x3, matrix products, times(): lax.dot_general(a, b, (((ca,), (cb,)), ((), ())), preferred_element_type=...  9.19 us
  transfers between devices with their start and end apart: 13, of which 10 were waited for; matrix products, arithmetic and copies ran while one was open for 7% of the time, Pallas kernels for 7%

profile of v7, /device:TPU:0, one launch (start us, length us, event | category | flops | bytes accessed | tf_op | source)
XLA Modules:
  0.0 171.3 jit_solution(12036231471563824197)
XLA Ops:
  0.7 1.5 copy-done.11
  2.2 0.7 copy-done.15
  2.9 0.7 copy-done.17
  3.6 0.7 pick_weighted.1
  4.4 1.4 copy-done.12
  5.8 0.7 pick_slots.1.refs_5_
  6.4 0.6 collective-permute-start.1
  7.0 1.9 %copy-done.3 = bf16[1,1,1,3072,512]{4,3,2,1,0:T(8,128)(2,1)S(1)} copy-done((bf16[1,1,1,3072,512]{4,3,2,1,0:T(8,128)(2,1)S(1)}, bf16[1,1,1,3072,512]{4,3,2,1,0:T(8,128)(2,1)}, u32[]{:S(2)}) %copy-start.3) | copy-done | bytes 3145752
  8.9 0.4 shard_map.103
  9.5 1.3 copy-done.5
  10.8 9.2 %experts_first.1 = (f32[384,512]{1,0:T(8,128)S(1)}, f32[384,512]{1,0:T(8,128)S(1)}, bf16[384,512]{1,0:T(8,128)(2,1)S(1)}, f32[4,8,48,384]{3,2,1,0:T(8,128)S(1)},...) custom-call(bf16[192,3072]{1,0:T(8,128)(2,1)S(1)} %get-tuple-element.24.refs_0_, ...), custom_call_target="tpu_custom_call" | custom-call | flops 6039797760 | bytes 18874368 | tf_op jit(solution)/shard_map/experts_first/pallas_call | solution.py:463
  20.1 2.8 %collective-permute-done.2 = bf16[4,8,48,384]{3,2,1,0:T(8,128)(2,1)S(1)} collective-permute-done((bf16[4,8,48,384]{3,2,1,0:T(8,128)(2,1)S(1)}, bf16[4,8,48,384]{3,2,1,0:T(8,128)(2,1)S(1)}, u32[]{:S(2)}, u32[]{:S(2)}) %collective-permute-start.2) | collective-permute-done | bytes 1179680 | tf_op jit(solution)/shard_map/ppermute | solution.py:28
  22.9 1.3 add_convert_fusion.1
  24.2 9.5 %all-to-all-start = ((bf16[32,48,384]{2,1,0:T(8,128)(2,1)}), bf16[32,48,384]{2,1,0:T(8,128)(2,1)S(1)}, u32[]{:S(2)}, u32[]{:S(2)}) async-start(bf16[32,48,384]{2,1,0:T(8,128)(2,1)} %bitcast.67), calls=%async_computation | async-start | bytes 2359296 | tf_op jit(solution)/shard_map/all_to_all | solution.py:32
  33.9 0.3 convert_reduce_fusion
  34.5 0.8 dynamic-slice_bitcast_fusion.base_ref.top_ref
  35.4 17.8 %all-to-all-done = bf16[32,48,384]{2,1,0:T(8,128)(2,1)S(1)} async-done(((bf16[32,48,384]{2,1,0:T(8,128)(2,1)}), bf16[32,48,384]{2,1,0:T(8,128)(2,1)S(1)}, u32[]{:S(2)}, u32[]{:S(2)}) %all-to-all-start) | async-done | bytes 1179680 | tf_op jit(solution)/shard_map/all_to_all | solution.py:32
  53.2 0.3 combine.2
  53.5 1.3 collective-permute-start.3
  54.9 6.2 %collective-permute-done.3.incoming_ref = bf16[64,384]{1,0:T(8,128)(2,1)S(1)} collective-permute-done((bf16[64,384]{1,0:T(8,128)(2,1)S(1)}, bf16[64,384]{1,0:T(8,128)(2,1)S(1)}, u32[]{:S(2)}, u32[]{:S(2)}) %collective-permute-start.3) | collective-permute-done | bytes 49184 | tf_op jit(solution)/shard_map/ppermute | solution.py:544
  61.0 0.2 deal.1
  61.3 20.8 %all_to_all.20 = bf16[32,48,384]{2,1,0:T(8,128)(2,1)S(1)} all-to-all(bf16[32,48,384]{2,1,0:T(8,128)(2,1)S(1)} %bitcast.60), channel_id=1, replica_groups=mesh['dp'=2,'pipe'=2,'expert'=32] {'expert'}, dimensions={0} | all-to-all | bytes 2359296 | tf_op jit(solution)/shard_map/all_to_all | solution.py:32
  82.0 0.3 scale_rows.1.refs_0_
  82.3 0.3 collective-permute-start.4
  82.6 2.8 %collective-permute-done.4.refs_1_ = bf16[192,3072]{1,0:T(8,128)(2,1)S(1)} collective-permute-done((bf16[192,3072]{1,0:T(8,128)(2,1)S(1)}, bf16[192,3072]{1,0:T(8,128)(2,1)S(1)}, u32[]{:S(2)}, u32[]{:S(2)}) %collective-permute-start.4) | collective-permute-done | bytes 1179680 | tf_op jit(solution)/shard_map/ppermute | solution.py:28
  85.4 3.2 %expert_slopes.1 = (bf16[384,128]{1,0:T(8,128)(2,1)S(1)}, bf16[384,512]{1,0:T(8,128)(2,1)S(1)}, bf16[384,512]{1,0:T(8,128)(2,1)S(1)}, bf16[3,384,512]{2,1,0:T(8,128)(2,1)S(1)}, bf16[384,3072]{1,0:T(8,128)(2,1)S(1)}) custom-call(bf16[192,3072]{1,0:T(8,128)(2,1)S(1)} %scale_rows.1.refs_0_, bf16[192,3072]{1,0:T(8,128)(2,1)S(1)} %collective-permute-done.4.refs_1_, ...), custom_call_target="tpu_custom_call" | custom-call | flops 1207959552 | bytes 10223616 | tf_op jit(solution)/shard_map/expert_slopes/pallas_call | solution.py:353
  88.6 1.4 copy-done.9
  90.1 8.3 %expert_rows.1 = (f32[4,8,48,384]{3,2,1,0:T(8,128)S(1)}, bf16[4,8,48,384]{3,2,1,0:T(8,128)(2,1)S(1)}) custom-call(bf16[384,512]{1,0:T(8,128)(2,1)S(1)} %get-tuple-element.34.gg_ref, bf16[384,512]{1,0:T(8,128)(2,1)S(1)} %get-tuple-element.35.gu_ref, bf16[3072,512]{1,0:T(8,128)(2,1)S(1)} %bitcast.53, bf16[3072,512]{1,0:T(8,128)(2,1)S(1)} %bitcast.55), custom_call_target="tpu_custom_call" | custom-call | flops 2415919104 | bytes 13369344 | tf_op jit(solution)/shard_map/expert_rows/pallas_call | solution.py:398
  98.6 2.7 %collective-permute-done.5 = bf16[4,8,48,384]{3,2,1,0:T(8,128)(2,1)S(1)} collective-permute-done((bf16[4,8,48,384]{3,2,1,0:T(8,128)(2,1)S(1)}, bf16[4,8,48,384]{3,2,1,0:T(8,128)(2,1)S(1)}, u32[]{:S(2)}, u32[]{:S(2)}) %collective-permute-start.5) | collective-permute-done | bytes 1179680 | tf_op jit(solution)/shard_map/ppermute | solution.py:28
  101.3 1.4 add_convert_fusion
  102.7 3.9 %all-to-all-start.2 = ((bf16[32,48,384]{2,1,0:T(8,128)(2,1)}), bf16[32,48,384]{2,1,0:T(8,128)(2,1)S(1)}, u32[]{:S(2)}, u32[]{:S(2)}) async-start(bf16[32,48,384]{2,1,0:T(8,128)(2,1)} %bitcast.25), calls=%async_computation.2 | async-start | bytes 2359296 | tf_op jit(solution)/shard_map/all_to_all | solution.py:32
  106.6 0.2 collective-permute-start.6
  106.8 1.2 collective-permute-done.6
  108.0 1.8 %collective-permute-start.7 = (bf16[384,128]{1,0:T(8,128)(2,1)S(1)}, bf16[384,128]{1,0:T(8,128)(2,1)S(1)}, u32[]{:S(2)}, u32[]{:S(2)}) collective-permute-start(bf16[384,128]{1,0:T(8,128)(2,1)S(1)} %add_convert_fusion.4), channel_id=1, source_target_pairs={{0,1},{1,0},{2,3},{3,2},{4,5},{5,4},{6,7},{7,6},{8,9},{9,8},{10,11... | collective-permute-start | bytes 294920 | tf_op jit(solution)/shard_map/ppermute | solution.py:70
  109.8 17.5 %all-to-all-done.2 = bf16[32,48,384]{2,1,0:T(8,128)(2,1)S(1)} async-done(((bf16[32,48,384]{2,1,0:T(8,128)(2,1)}), bf16[32,48,384]{2,1,0:T(8,128)(2,1)S(1)}, u32[]{:S(2)}, u32[]{:S(2)}) %all-to-all-start.2) | async-done | bytes 1179680 | tf_op jit(solution)/shard_map/all_to_all | solution.py:32
  127.3 0.6 combine.3
  127.8 1.1 copy-done
  129.0 4.0 %all-to-all-start.3 = ((bf16[32,64,384]{2,1,0:T(8,128)(2,1)}), bf16[32,64,384]{2,1,0:T(8,128)(2,1)S(1)}, u32[]{:S(2)}, u32[]{:S(2)}) async-start(bf16[32,64,384]{2,1,0:T(8,128)(2,1)} %copy-done), calls=%async_computation.3 | async-start | bytes 3145728 | tf_op jit(solution)/shard_map/all_to_all | solution.py:32
  133.0 4.7 %fusion.5.refs_0_ = f32[384,384]{1,0:T(8,128)} fusion(bf16[384,3072]{1,0:T(8,128)(2,1)} %copy-done.7), kind=kOutput, calls=%fused_computation.22 | convolution fusion | flops 905969664 | bytes 2949120 | tf_op jit(solution)/shard_map/dot_general | solution.py:36
  137.7 1.8 %collective-permute-start.8 = (bf16[384,128]{1,0:T(8,128)(2,1)S(1)}, bf16[384,128]{1,0:T(8,128)(2,1)S(1)}, u32[]{:S(2)}, u32[]{:S(2)}) collective-permute-start(bf16[384,128]{1,0:T(8,128)(2,1)S(1)} %add_convert_fusion.3), channel_id=1, source_target_pairs={{0,2},{1,3},{2,0},{3,1},{4,6},{5,7},{6,4},{7,5},{8,10},{9,11},{10,... | collective-permute-start | bytes 294920 | tf_op jit(solution)/shard_map/ppermute | solution.py:70
  139.5 2.2 %fusion.6.refs_1_ = f32[384,384]{1,0:T(8,128)} fusion(bf16[384,3072]{1,0:T(8,128)(2,1)S(1)} %copy-done.10, bf16[384,3072]{1,0:T(8,128)(2,1)S(1)} %copy-done.8), kind=kOutput, calls=%fused_computation.23 | convolution fusion | flops 905969664 | bytes 5308416 | tf_op jit(solution)/shard_map/dot_general | solution.py:36
  141.7 10.7 %collective-permute-done.8 = bf16[384,128]{1,0:T(8,128)(2,1)S(1)} collective-permute-done((bf16[384,128]{1,0:T(8,128)(2,1)S(1)}, bf16[384,128]{1,0:T(8,128)(2,1)S(1)}, u32[]{:S(2)}, u32[]{:S(2)}) %collective-permute-start.8) | collective-permute-done | bytes 98336 | tf_op jit(solution)/shard_map/ppermute | solution.py:70
  152.4 2.4 %collective-permute-start.9 = (bf16[384,128]{1,0:T(8,128)(2,1)S(1)}, bf16[384,128]{1,0:T(8,128)(2,1)S(1)}, u32[]{:S(2)}, u32[]{:S(2)}) collective-permute-start(bf16[384,128]{1,0:T(8,128)(2,1)S(1)} %add_convert_fusion.2), channel_id=1, source_target_pairs={{0,6},{1,7},{2,4},{3,5},{4,2},{5,3},{6,0},{7,1},{8,14},{9,15},{10,... | collective-permute-start | bytes 294920 | tf_op jit(solution)/shard_map/ppermute | solution.py:70
  154.9 2.2 %fusion.7.refs_2_ = f32[384,384]{1,0:T(8,128)} fusion(bf16[384,3072]{1,0:T(8,128)(2,1)S(1)} %copy-done.10), kind=kOutput, calls=%fused_computation.24 | convolution fusion | flops 905969664 | bytes 2949120 | tf_op jit(solution)/shard_map/dot_general | solution.py:36
  157.1 1.5 collective-permute-done.9
  158.6 0.7 convert_add_fusion.sums_ref
  159.3 10.7 %finish.1 = (f32[3,64,512]{2,1,0:T(8,128)}, f32[64,1536]{1,0:T(8,128)}) custom-call(s32[1]{0:T(128)} %bitcast.29.dp_ref, f32[384,128]{1,0:T(8,128)} %convert_add_fusion.sums_ref, f32[384,384]{1,0:T(8,128)} %fusion.5.refs_0_, f32[384,384]{1,0:T(8,128)} %fusion.6.refs_1_, f32[384,384]{1,0:T(8,128)} %fusion.7.refs_2_, bf16[384,3072]{1,0:T(8,128)(2,1)} %copy-done.7, ...), custom_call_target="tpu_custom_call" | custom-call | flops 301989888 | bytes 5308416 | tf_op jit(solution)/shard_map/finish/pallas_call | solution.py:158
  170.0 1.3 side_by_side.1
  (50 shorter events, 1.3 us)
Async XLA Ops:
  0.6 6.4 %copy-start.1 = (bf16[1,1,1,3072,512]{4,3,2,1,0:T(8,128)(2,1)S(1)}, bf16[1,1,1,3072,512]{4,3,2,1,0:T(8,128)(2,1)}, u32[]{:S(2)}) copy-start(bf16[1,1,1,3072,512]{4,3,2,1,0:T(8,128)(2,1)} %param.12) | copy-start | bytes 9437188
  0.7 1.6 copy-start.11
  2.2 0.7 copy-start.15
  2.9 0.7 copy-start.17
  4.3 5.1 %collective-permute-start = (bf16[192,3072]{1,0:T(8,128)(2,1)S(1)}, bf16[192,3072]{1,0:T(8,128)(2,1)S(1)}, u32[]{:S(2)}, u32[]{:S(2)}) collective-permute-start(bf16[192,3072]{1,0:T(8,128)(2,1)S(1)} %get-tuple-element.24.refs_0_), channel_id=1, source_target_pairs={{0,64},{64,0},{1,65},{65,1},{2,66},{66,2},{3,67},{67,3},{4,68},{68... | collective-permute-start | bytes 3538952 | tf_op jit(solution)/shard_map/ppermute | solution.py:28
  4.4 1.4 copy-start.12
  6.4 3.1 %collective-permute-start.1 = (bf16[192,3072]{1,0:T(8,128)(2,1)S(1)}, bf16[192,3072]{1,0:T(8,128)(2,1)S(1)}, u32[]{:S(2)}, u32[]{:S(2)}) collective-permute-start(bf16[192,3072]{1,0:T(8,128)(2,1)S(1)} %pick_slots.1.refs_5_), channel_id=1, source_target_pairs={{0,64},{64,0},{1,65},{65,1},{2,66},{66,2},{3,67},{67,3},{4,68},{68... | collective-permute-start | bytes 3538952 | tf_op jit(solution)/shard_map/ppermute | solution.py:28
  7.0 1.9 %copy-start.3 = (bf16[1,1,1,3072,512]{4,3,2,1,0:T(8,128)(2,1)S(1)}, bf16[1,1,1,3072,512]{4,3,2,1,0:T(8,128)(2,1)}, u32[]{:S(2)}) copy-start(bf16[1,1,1,3072,512]{4,3,2,1,0:T(8,128)(2,1)} %param.13) | copy-start | bytes 9437188
  8.9 1.9 %copy-start.5 = (bf16[1,1,1,512,3072]{4,3,2,1,0:T(8,128)(2,1)S(1)}, bf16[1,1,1,512,3072]{4,3,2,1,0:T(8,128)(2,1)}, u32[]{:S(2)}) copy-start(bf16[1,1,1,512,3072]{4,3,2,1,0:T(8,128)(2,1)} %param.14) | copy-start | bytes 9437188
  19.9 4.2 %copy-start.7 = (bf16[384,3072]{1,0:T(8,128)(2,1)}, bf16[384,3072]{1,0:T(8,128)(2,1)S(1)}, u32[]{:S(2)}) copy-start(bf16[384,3072]{1,0:T(8,128)(2,1)S(1)} %get-tuple-element.40.refs_3_) | copy-start | bytes 7077892
  20.0 2.9 %collective-permute-start.2 = (bf16[4,8,48,384]{3,2,1,0:T(8,128)(2,1)S(1)}, bf16[4,8,48,384]{3,2,1,0:T(8,128)(2,1)S(1)}, u32[]{:S(2)}, u32[]{:S(2)}) collective-permute-start(bf16[4,8,48,384]{3,2,1,0:T(8,128)(2,1)S(1)} %get-tuple-element.28), channel_id=1, source_target_pairs={{0,64},{64,0},{1,65},{65,1},{2,66},{66,2},{3,67},{67,3},{4,68},{68... | collective-permute-start | bytes 3538952 | tf_op jit(solution)/shard_map/ppermute | solution.py:28
  24.2 9.5 %copy-start.16 = (s32[1,4,64,2]{2,3,1,0:T(2,128)S(1)}, s32[1,4,64,2]{2,3,1,0:T(2,128)}, u32[]{:S(2)}) copy-start(s32[1,4,64,2]{2,3,1,0:T(2,128)} %param.10) | copy-start | bytes 6148
  24.2 29.0 %all-to-all-start = ((bf16[32,48,384]{2,1,0:T(8,128)(2,1)}), bf16[32,48,384]{2,1,0:T(8,128)(2,1)S(1)}, u32[]{:S(2)}, u32[]{:S(2)}) async-start(bf16[32,48,384]{2,1,0:T(8,128)(2,1)} %bitcast.67), calls=%async_computation | async-start | bytes 2359296 | tf_op jit(solution)/shard_map/all_to_all | solution.py:32
  53.5 7.5 %collective-permute-start.3 = (bf16[64,384]{1,0:T(8,128)(2,1)S(1)}, bf16[64,384]{1,0:T(8,128)(2,1)S(1)}, u32[]{:S(2)}, u32[]{:S(2)}) collective-permute-start(bf16[64,384]{1,0:T(8,128)(2,1)S(1)} %bitcast.62), channel_id=1, source_target_pairs={{32,0},{33,1},{34,2},{35,3},{36,4},{37,5},{38,6},{39,7},{40,8},{41... | collective-permute-start | bytes 147464 | tf_op jit(solution)/shard_map/ppermute | solution.py:544
  61.3 24.2 %copy-start.6 = (bf16[1,1,1,512,3072]{4,3,2,1,0:T(8,128)(2,1)S(1)}, bf16[1,1,1,512,3072]{4,3,2,1,0:T(8,128)(2,1)}, u32[]{:S(2)}) copy-start(bf16[1,1,1,512,3072]{4,3,2,1,0:T(8,128)(2,1)} %param.14) | copy-start | bytes 9437188
  61.3 24.2 %copy-start.14 = (f32[1,1,1,3,512,64]{4,5,3,2,1,0:T(8,128)S(1)}, f32[1,1,1,3,512,64]{4,5,3,2,1,0:T(8,128)}, u32[]{:S(2)}) copy-start(f32[1,1,1,3,512,64]{4,5,3,2,1,0:T(8,128)} %param.15) | copy-start | bytes 1179652
  82.3 3.1 %collective-permute-start.4 = (bf16[192,3072]{1,0:T(8,128)(2,1)S(1)}, bf16[192,3072]{1,0:T(8,128)(2,1)S(1)}, u32[]{:S(2)}, u32[]{:S(2)}) collective-permute-start(bf16[192,3072]{1,0:T(8,128)(2,1)S(1)} %scale_rows.1.refs_0_), channel_id=1, source_target_pairs={{0,64},{64,0},{1,65},{65,1},{2,66},{66,2},{3,67},{67,3},{4,68},{68... | collective-permute-start | bytes 3538952 | tf_op jit(solution)/shard_map/ppermute | solution.py:28
  85.4 4.6 %copy-start.2 = (bf16[1,1,1,3072,512]{4,3,2,1,0:T(8,128)(2,1)S(1)}, bf16[1,1,1,3072,512]{4,3,2,1,0:T(8,128)(2,1)}, u32[]{:S(2)}) copy-start(bf16[1,1,1,3072,512]{4,3,2,1,0:T(8,128)(2,1)} %param.12) | copy-start | bytes 9437188
  85.4 4.6 %copy-start.4 = (bf16[1,1,1,3072,512]{4,3,2,1,0:T(8,128)(2,1)S(1)}, bf16[1,1,1,3072,512]{4,3,2,1,0:T(8,128)(2,1)}, u32[]{:S(2)}) copy-start(bf16[1,1,1,3072,512]{4,3,2,1,0:T(8,128)(2,1)} %param.13) | copy-start | bytes 9437188
  88.6 1.4 copy-start.9
  90.1 8.3 %copy-start.13 = (bf16[3,384,512]{2,1,0:T(8,128)(2,1)}, bf16[3,384,512]{2,1,0:T(8,128)(2,1)S(1)}, u32[]{:S(2)}) copy-start(bf16[3,384,512]{2,1,0:T(8,128)(2,1)S(1)} %get-tuple-element.42.refs_5_) | copy-start | bytes 3538948
  98.4 2.9 %collective-permute-start.5 = (bf16[4,8,48,384]{3,2,1,0:T(8,128)(2,1)S(1)}, bf16[4,8,48,384]{3,2,1,0:T(8,128)(2,1)S(1)}, u32[]{:S(2)}, u32[]{:S(2)}) collective-permute-start(bf16[4,8,48,384]{3,2,1,0:T(8,128)(2,1)S(1)} %get-tuple-element.37), channel_id=1, source_target_pairs={{0,64},{64,0},{1,65},{65,1},{2,66},{66,2},{3,67},{67,3},{4,68},{68... | collective-permute-start | bytes 3538952 | tf_op jit(solution)/shard_map/ppermute | solution.py:28
  102.7 24.6 %all-to-all-start.2 = ((bf16[32,48,384]{2,1,0:T(8,128)(2,1)}), bf16[32,48,384]{2,1,0:T(8,128)(2,1)S(1)}, u32[]{:S(2)}, u32[]{:S(2)}) async-start(bf16[32,48,384]{2,1,0:T(8,128)(2,1)} %bitcast.25), calls=%async_computation.2 | async-start | bytes 2359296 | tf_op jit(solution)/shard_map/all_to_all | solution.py:32
  106.6 1.4 collective-permute-start.6
  108.0 29.7 %collective-permute-start.7 = (bf16[384,128]{1,0:T(8,128)(2,1)S(1)}, bf16[384,128]{1,0:T(8,128)(2,1)S(1)}, u32[]{:S(2)}, u32[]{:S(2)}) collective-permute-start(bf16[384,128]{1,0:T(8,128)(2,1)S(1)} %add_convert_fusion.4), channel_id=1, source_target_pairs={{0,1},{1,0},{2,3},{3,2},{4,5},{5,4},{6,7},{7,6},{8,9},{9,8},{10,11... | collective-permute-start | bytes 294920 | tf_op jit(solution)/shard_map/ppermute | solution.py:70
  127.8 1.1 copy-start
  129.0 41.0 %all-to-all-start.3 = ((bf16[32,64,384]{2,1,0:T(8,128)(2,1)}), bf16[32,64,384]{2,1,0:T(8,128)(2,1)S(1)}, u32[]{:S(2)}, u32[]{:S(2)}) async-start(bf16[32,64,384]{2,1,0:T(8,128)(2,1)} %copy-done), calls=%async_computation.3 | async-start | bytes 3145728 | tf_op jit(solution)/shard_map/all_to_all | solution.py:32
  132.9 6.6 %copy-start.8 = (bf16[384,3072]{1,0:T(8,128)(2,1)S(1)}, bf16[384,3072]{1,0:T(8,128)(2,1)}, u32[]{:S(2)}) copy-start(bf16[384,3072]{1,0:T(8,128)(2,1)} %copy-done.7) | copy-start | bytes 7077892
  133.0 6.6 %copy-start.10 = (bf16[384,3072]{1,0:T(8,128)(2,1)S(1)}, bf16[384,3072]{1,0:T(8,128)(2,1)}, u32[]{:S(2)}) copy-start(bf16[384,3072]{1,0:T(8,128)(2,1)} %copy-done.9) | copy-start | bytes 7077892
  137.7 14.7 %collective-permute-start.8 = (bf16[384,128]{1,0:T(8,128)(2,1)S(1)}, bf16[384,128]{1,0:T(8,128)(2,1)S(1)}, u32[]{:S(2)}, u32[]{:S(2)}) collective-permute-start(bf16[384,128]{1,0:T(8,128)(2,1)S(1)} %add_convert_fusion.3), channel_id=1, source_target_pairs={{0,2},{1,3},{2,0},{3,1},{4,6},{5,7},{6,4},{7,5},{8,10},{9,11},{10,... | collective-permute-start | bytes 294920 | tf_op jit(solution)/shard_map/ppermute | solution.py:70
  152.4 6.1 %collective-permute-start.9 = (bf16[384,128]{1,0:T(8,128)(2,1)S(1)}, bf16[384,128]{1,0:T(8,128)(2,1)S(1)}, u32[]{:S(2)}, u32[]{:S(2)}) collective-permute-start(bf16[384,128]{1,0:T(8,128)(2,1)S(1)} %add_convert_fusion.2), channel_id=1, source_target_pairs={{0,6},{1,7},{2,4},{3,5},{4,2},{5,3},{6,0},{7,1},{8,14},{9,15},{10,... | collective-permute-start | bytes 294920 | tf_op jit(solution)/shard_map/ppermute | solution.py:70

commit v8 on v7

--- a/solution.py
+++ b/solution.py
@@ -326,7 +326,7 @@
 
     def kernel(*refs):
         own_ref, partner_ref, down_ref, slope_ref, silu_ref, hidden_ref, right_ref = refs[:7]
-        sums_ref, gg_ref, gu_ref, grads_hbm, rows_hbm, done = refs[7:]
+        sums_ref, gg_ref, gu_ref, rows_hbm, done = refs[7:]
         moves = []
 
         def keep(source, target):
@@ -336,13 +336,10 @@
 
         keep(own_ref, rows_hbm.at[pl.ds(0, slots)])
         keep(partner_ref, rows_hbm.at[pl.ds(slots, slots)])
-        keep(hidden_ref, grads_hbm.at[2])
         rows = jnp.concatenate([own_ref[...], partner_ref[...]])
         grad_hidden = times(rows, down_ref[...], 1, 1)
         gg_ref[...] = (grad_hidden * slope_ref[...]).astype(BF)
         gu_ref[...] = (grad_hidden * silu_ref[...]).astype(BF)
-        keep(gg_ref, grads_hbm.at[0])
-        keep(gu_ref, grads_hbm.at[1])
         right16 = right_ref[...].astype(BF)
         of_inputs = times(gg_ref[...], right16[0], 1, 1) + times(gu_ref[...], right16[1], 1, 1)
         of_grads = times(hidden_ref[...], right16[2], 1, 1)
@@ -356,12 +353,11 @@
             jax.ShapeDtypeStruct((count, 2 * R), BF),
             jax.ShapeDtypeStruct(square, BF),
             jax.ShapeDtypeStruct(square, BF),
-            jax.ShapeDtypeStruct((3, *square), BF),
             jax.ShapeDtypeStruct((count, width), BF),
         ),
         in_specs=[IN_VMEM] * 7,
-        out_specs=(*[IN_VMEM] * 3, *[IN_HBM] * 2),
-        scratch_shapes=[pltpu.SemaphoreType.DMA((5,))],
+        out_specs=(*[IN_VMEM] * 3, IN_HBM),
+        scratch_shapes=[pltpu.SemaphoreType.DMA((2,))],
         compiler_params=pltpu.CompilerParams(vmem_limit_bytes=20 << 20),
         cost_estimate=cost(
             2 * count * width * units, 2 * width * (units + 2 * count) + 12 * count * units
@@ -370,46 +366,48 @@
     )(*grads_both, down, *forward, right)
 
 
-def expert_rows(gate, up, grad_gate, grad_up, copies):
+def expert_rows(gate, up, grad_gate, grad_up, hidden, copies):
     width, units = gate.shape
     count = grad_gate.shape[0]
     slots = count // 2
     columns = width // copies
     shape = (MICRO, copies, CAP, columns)
 
-    def kernel(gg_ref, gu_ref, gate_hbm, up_hbm, own_ref, par_ref, gate_ref, up_ref, done):
-        def arrival(c, which):
-            source, target = ((gate_hbm, gate_ref), (up_hbm, up_ref))[which]
-            held = pl.ds(c * columns, columns)
-            return pltpu.make_async_copy(source.at[held], target.at[c], done.at[which, c])
-
-        for c in range(copies):
-            arrival(c, 0).start()
-            arrival(c, 1).start()
-        for c in range(copies):
-            arrival(c, 0).wait()
-            total = times(gg_ref[...], gate_ref[c], 1, 1)
-            arrival(c, 1).wait()
-            total = total + times(gu_ref[...], up_ref[c], 1, 1)
+    def kernel(gg_ref, gu_ref, hidden_ref, gate_ref, up_ref, own_ref, par_ref, grads_hbm, done):
+        moves = [
+            pltpu.make_async_copy(source, grads_hbm.at[i], done.at[i])
+            for i, source in enumerate((gg_ref, gu_ref, hidden_ref))
+        ]
+        for move in moves:
+            move.start()
+
+        def column(c, carry):
+            held = pl.ds(pl.multiple_of(c * columns, columns), columns)
+            total = times(gg_ref[...], gate_ref[held, :], 1, 1)
+            total = total + times(gu_ref[...], up_ref[held, :], 1, 1)
             for m in range(MICRO):
                 own_ref[m, c] = total[m * CAP : (m + 1) * CAP]
                 par_ref[m, c] = total[slots + m * CAP : slots + (m + 1) * CAP].astype(BF)
-
-    return pl.pallas_call(
-        kernel,
-        out_shape=(jax.ShapeDtypeStruct(shape, F32), jax.ShapeDtypeStruct(shape, BF)),
-        in_specs=[IN_VMEM] * 2 + [IN_HBM] * 2,
-        scratch_shapes=[
-            pltpu.VMEM((copies, columns, units), BF),
-            pltpu.VMEM((copies, columns, units), BF),
-            pltpu.SemaphoreType.DMA((2, copies)),
-        ],
+            return carry
+
+        lax.fori_loop(0, copies, column, 0)
+        for move in moves:
+            move.wait()
+
+    return pl.pallas_call(
+        kernel,
+        out_shape=(
+            jax.ShapeDtypeStruct(shape, F32),
+            jax.ShapeDtypeStruct(shape, BF),
+            jax.ShapeDtypeStruct((3, count, units), BF),
+        ),
+        in_specs=[IN_VMEM] * 5,
+        out_specs=(IN_VMEM, IN_VMEM, IN_HBM),
+        scratch_shapes=[pltpu.SemaphoreType.DMA((3,))],
         compiler_params=pltpu.CompilerParams(vmem_limit_bytes=24 << 20),
-        cost_estimate=cost(
-            4 * count * width * units, 4 * width * units + 6 * count * width
-        ),
+        cost_estimate=cost(4 * count * width * units, 4 * width * units + 6 * count * width),
         name="expert_rows",
-    )(grad_gate, grad_up, gate, up)
+    )(grad_gate, grad_up, hidden, gate, up)
 
 
 def experts(gate, up, down, grads_both, copies, inputs_both):
@@ -545,11 +543,13 @@
     base, pieces = deal(last, top_part, incoming, deal_pick, copies)
     own_rows = exchange(pieces.reshape(peers, CAP, columns))
     own_grads = scale_rows(own_rows.reshape(MICRO, copies, CAP, columns), slot_weights)
-    sums, grad_gate, grad_up, grads, grad_rows = expert_slopes(
+    sums, grad_gate, grad_up, grad_rows = expert_slopes(
         down, (own_grads, swap_cores(own_grads)), forward, right
     )
     other_sums = swap_cores(sums)
-    own_half, other_half = expert_rows(gate, up, grad_gate, grad_up, copies)
+    own_half, other_half, grads = expert_rows(
+        gate, up, grad_gate, grad_up, forward[2], copies
+    )
     parts = reduced(own_half, other_half, base, peers)
     produced = exchange(parts)
     produced = side_by_side(produced.reshape(MICRO, copies, tokens, columns))

time: 172 us -> 168 us (0.977)
  Pallas kernels: 35.7 us -> 32 us
    pallas_call x1, Pallas kernels: 8.28 us -> 5.36 us  [expert_rows(): pl.pallas_call(kernel, out_shape=(jax.ShapeDtypeStruct(shape, F32), jax.S...]
where the time goes in v8:
time: 168 us; the launch traced here: 167 us
  waiting for transfers between devices  63.2 us (38%)
  Pallas kernels  32 us (19%)
  starting transfers between devices  25.9 us (15%)
  blocking collectives  20.8 us (12%)
  local copies, waits for them, and re-layouts  11.5 us (7%)
  matrix products  9.18 us (5%)
  other arithmetic  3.85 us (2%)
    all_to_all x3, waiting for transfers between devices, exchange(): return lax.all_to_all(pieces, 'expert', 0, 0, tiled=True)  35.2 us
    all_to_all x1, blocking collectives, exchange(): return lax.all_to_all(pieces, 'expert', 0, 0, tiled=True)  20.8 us
    all_to_all x3, starting transfers between devices, exchange(): return lax.all_to_all(pieces, 'expert', 0, 0, tiled=True)  17.6 us
    ppermute x3, waiting for transfers between devices, add_copies(): other = lax.ppermute(rounded, 'expert', route)  12.2 us
    pallas_call x1, Pallas kernels, finish(): pl.pallas_call(kernel, out_shape=(jax.ShapeDtypeStruct((3, R, units), F32...  10.7 us
    unnamed x38, local copies, waits for them, and re-layouts  10.3 us
    ppermute x6, waiting for transfers between devices, swap_cores(): return lax.ppermute(value, 'dp', [(0, 1), (1, 0)])  9.66 us
    dot_general x3, matrix products, times(): lax.dot_general(a, b, (((ca,), (cb,)), ((), ())), preferred_element_type=...  9.18 us
  transfers between devices with their start and end apart: 13, of which 10 were waited for; matrix products, arithmetic and copies ran while one was open for 7% of the time, Pallas kernels for 7%

profile of v8, /device:TPU:0, one launch (start us, length us, event | category | flops | bytes accessed | tf_op | source)
XLA Modules:
  0.0 167.3 jit_solution(2724294868024376667)
XLA Ops:
  0.7 1.5 copy-done.11
  2.2 0.7 copy-done.15
  2.9 0.7 copy-done.17
  3.6 0.7 pick_weighted.1
  4.4 1.4 copy-done.12
  5.8 0.7 pick_slots.1.refs_5_
  6.4 0.6 collective-permute-start.1
  7.0 1.9 %copy-done.3 = bf16[1,1,1,3072,512]{4,3,2,1,0:T(8,128)(2,1)S(1)} copy-done((bf16[1,1,1,3072,512]{4,3,2,1,0:T(8,128)(2,1)S(1)}, bf16[1,1,1,3072,512]{4,3,2,1,0:T(8,128)(2,1)}, u32[]{:S(2)}) %copy-start.3) | copy-done | bytes 3145752
  8.9 0.4 shard_map.103
  9.5 1.3 copy-done.5
  10.8 9.2 %experts_first.1 = (f32[384,512]{1,0:T(8,128)S(1)}, f32[384,512]{1,0:T(8,128)S(1)}, bf16[384,512]{1,0:T(8,128)(2,1)S(1)}, f32[4,8,48,384]{3,2,1,0:T(8,128)S(1)},...) custom-call(bf16[192,3072]{1,0:T(8,128)(2,1)S(1)} %get-tuple-element.24.refs_0_, ...), custom_call_target="tpu_custom_call" | custom-call | flops 6039797760 | bytes 18874368 | tf_op jit(solution)/shard_map/experts_first/pallas_call | solution.py:461
  20.1 2.8 %collective-permute-done.2 = bf16[4,8,48,384]{3,2,1,0:T(8,128)(2,1)S(1)} collective-permute-done((bf16[4,8,48,384]{3,2,1,0:T(8,128)(2,1)S(1)}, bf16[4,8,48,384]{3,2,1,0:T(8,128)(2,1)S(1)}, u32[]{:S(2)}, u32[]{:S(2)}) %collective-permute-start.2) | collective-permute-done | bytes 1179680 | tf_op jit(solution)/shard_map/ppermute | solution.py:28
  22.9 1.3 add_convert_fusion.1
  24.2 9.5 %all-to-all-start = ((bf16[32,48,384]{2,1,0:T(8,128)(2,1)}), bf16[32,48,384]{2,1,0:T(8,128)(2,1)S(1)}, u32[]{:S(2)}, u32[]{:S(2)}) async-start(bf16[32,48,384]{2,1,0:T(8,128)(2,1)} %bitcast.67), calls=%async_computation | async-start | bytes 2359296 | tf_op jit(solution)/shard_map/all_to_all | solution.py:32
  33.9 0.3 convert_reduce_fusion
  34.5 0.8 dynamic-slice_bitcast_fusion.base_ref.top_ref
  35.4 17.8 %all-to-all-done = bf16[32,48,384]{2,1,0:T(8,128)(2,1)S(1)} async-done(((bf16[32,48,384]{2,1,0:T(8,128)(2,1)}), bf16[32,48,384]{2,1,0:T(8,128)(2,1)S(1)}, u32[]{:S(2)}, u32[]{:S(2)}) %all-to-all-start) | async-done | bytes 1179680 | tf_op jit(solution)/shard_map/all_to_all | solution.py:32
  53.2 0.3 combine.2
  53.5 1.3 collective-permute-start.3
  54.9 6.2 %collective-permute-done.3.incoming_ref = bf16[64,384]{1,0:T(8,128)(2,1)S(1)} collective-permute-done((bf16[64,384]{1,0:T(8,128)(2,1)S(1)}, bf16[64,384]{1,0:T(8,128)(2,1)S(1)}, u32[]{:S(2)}, u32[]{:S(2)}) %collective-permute-start.3) | collective-permute-done | bytes 49184 | tf_op jit(solution)/shard_map/ppermute | solution.py:542
  61.0 0.2 deal.1
  61.3 20.8 %all_to_all.20 = bf16[32,48,384]{2,1,0:T(8,128)(2,1)S(1)} all-to-all(bf16[32,48,384]{2,1,0:T(8,128)(2,1)S(1)} %bitcast.60), channel_id=1, replica_groups=mesh['dp'=2,'pipe'=2,'expert'=32] {'expert'}, dimensions={0} | all-to-all | bytes 2359296 | tf_op jit(solution)/shard_map/all_to_all | solution.py:32
  82.0 0.3 scale_rows.1.refs_0_
  82.4 2.8 %collective-permute-done.4.refs_1_ = bf16[192,3072]{1,0:T(8,128)(2,1)S(1)} collective-permute-done((bf16[192,3072]{1,0:T(8,128)(2,1)S(1)}, bf16[192,3072]{1,0:T(8,128)(2,1)S(1)}, u32[]{:S(2)}, u32[]{:S(2)}) %collective-permute-start.4) | collective-permute-done | bytes 1179680 | tf_op jit(solution)/shard_map/ppermute | solution.py:28
  85.3 2.4 %expert_slopes.1 = (bf16[384,128]{1,0:T(8,128)(2,1)S(1)}, bf16[384,512]{1,0:T(8,128)(2,1)S(1)}, bf16[384,512]{1,0:T(8,128)(2,1)S(1)}, bf16[384,3072]{1,0:T(8,128)(2,1)S(1)}) custom-call(bf16[192,3072]{1,0:T(8,128)(2,1)S(1)} %scale_rows.1.refs_0_, bf16[192,3072]{1,0:T(8,128)(2,1)S(1)} %collective-permute-done.4.refs_1_, bf16[512,3072]{1,0:T(8,128)(2,1)S(1)} %bitcast.57, ...), custom_call_target="tpu_custom_call" | custom-call | flops 1207959552 | bytes 10223616 | tf_op jit(solution)/shard_map/expert_slopes/pallas_call | solution.py:350
  87.6 1.4 copy-done.9
  89.1 5.4 %expert_rows.1 = (f32[4,8,48,384]{3,2,1,0:T(8,128)S(1)}, bf16[4,8,48,384]{3,2,1,0:T(8,128)(2,1)S(1)}, bf16[3,384,512]{2,1,0:T(8,128)(2,1)S(1)}) custom-call(bf16[384,512]{1,0:T(8,128)(2,1)S(1)} %get-tuple-element.34.gg_ref, bf16[384,512]{1,0:T(8,128)(2,1)S(1)} %get-tuple-element.35.gu_ref, bf16[384,512]{1,0:T(8,128)(2,1)S(1)} %get-tuple-element.33.refs_5_.hidden_ref, ...), custom_call_target="tpu_custom_call" | custom-call | flops 2415919104 | bytes 13369344 | tf_op jit(solution)/shard_map/expert_rows/pallas_call | solution.py:397
  94.5 0.2 collective-permute-start.5
  94.7 2.7 %collective-permute-done.5 = bf16[4,8,48,384]{3,2,1,0:T(8,128)(2,1)S(1)} collective-permute-done((bf16[4,8,48,384]{3,2,1,0:T(8,128)(2,1)S(1)}, bf16[4,8,48,384]{3,2,1,0:T(8,128)(2,1)S(1)}, u32[]{:S(2)}, u32[]{:S(2)}) %collective-permute-start.5) | collective-permute-done | bytes 1179680 | tf_op jit(solution)/shard_map/ppermute | solution.py:28
  97.4 1.4 add_convert_fusion
  98.8 3.9 %all-to-all-start.2 = ((bf16[32,48,384]{2,1,0:T(8,128)(2,1)}), bf16[32,48,384]{2,1,0:T(8,128)(2,1)S(1)}, u32[]{:S(2)}, u32[]{:S(2)}) async-start(bf16[32,48,384]{2,1,0:T(8,128)(2,1)} %bitcast.25), calls=%async_computation.2 | async-start | bytes 2359296 | tf_op jit(solution)/shard_map/all_to_all | solution.py:32
  102.7 0.2 collective-permute-start.6
  102.9 1.2 collective-permute-done.6
  104.1 1.8 %collective-permute-start.7 = (bf16[384,128]{1,0:T(8,128)(2,1)S(1)}, bf16[384,128]{1,0:T(8,128)(2,1)S(1)}, u32[]{:S(2)}, u32[]{:S(2)}) collective-permute-start(bf16[384,128]{1,0:T(8,128)(2,1)S(1)} %add_convert_fusion.4), channel_id=1, source_target_pairs={{0,1},{1,0},{2,3},{3,2},{4,5},{5,4},{6,7},{7,6},{8,9},{9,8},{10,11... | collective-permute-start | bytes 294920 | tf_op jit(solution)/shard_map/ppermute | solution.py:70
  105.9 17.5 %all-to-all-done.2 = bf16[32,48,384]{2,1,0:T(8,128)(2,1)S(1)} async-done(((bf16[32,48,384]{2,1,0:T(8,128)(2,1)}), bf16[32,48,384]{2,1,0:T(8,128)(2,1)S(1)}, u32[]{:S(2)}, u32[]{:S(2)}) %all-to-all-start.2) | async-done | bytes 1179680 | tf_op jit(solution)/shard_map/all_to_all | solution.py:32
  123.4 0.5 combine.3
  123.9 1.1 copy-done
  125.1 4.2 %all-to-all-start.3 = ((bf16[32,64,384]{2,1,0:T(8,128)(2,1)}), bf16[32,64,384]{2,1,0:T(8,128)(2,1)S(1)}, u32[]{:S(2)}, u32[]{:S(2)}) async-start(bf16[32,64,384]{2,1,0:T(8,128)(2,1)} %copy-done), calls=%async_computation.3 | async-start | bytes 3145728 | tf_op jit(solution)/shard_map/all_to_all | solution.py:32
  129.2 4.7 %fusion.5.refs_0_ = f32[384,384]{1,0:T(8,128)} fusion(bf16[384,3072]{1,0:T(8,128)(2,1)} %copy-done.7), kind=kOutput, calls=%fused_computation.22 | convolution fusion | flops 905969664 | bytes 2949120 | tf_op jit(solution)/shard_map/dot_general | solution.py:36
  134.0 1.8 %collective-permute-start.8 = (bf16[384,128]{1,0:T(8,128)(2,1)S(1)}, bf16[384,128]{1,0:T(8,128)(2,1)S(1)}, u32[]{:S(2)}, u32[]{:S(2)}) collective-permute-start(bf16[384,128]{1,0:T(8,128)(2,1)S(1)} %add_convert_fusion.3), channel_id=1, source_target_pairs={{0,2},{1,3},{2,0},{3,1},{4,6},{5,7},{6,4},{7,5},{8,10},{9,11},{10,... | collective-permute-start | bytes 294920 | tf_op jit(solution)/shard_map/ppermute | solution.py:70
  135.8 2.2 %fusion.6.refs_1_ = f32[384,384]{1,0:T(8,128)} fusion(bf16[384,3072]{1,0:T(8,128)(2,1)S(1)} %copy-done.10, bf16[384,3072]{1,0:T(8,128)(2,1)S(1)} %copy-done.8), kind=kOutput, calls=%fused_computation.23 | convolution fusion | flops 905969664 | bytes 5308416 | tf_op jit(solution)/shard_map/dot_general | solution.py:36
  138.0 10.7 %collective-permute-done.8 = bf16[384,128]{1,0:T(8,128)(2,1)S(1)} collective-permute-done((bf16[384,128]{1,0:T(8,128)(2,1)S(1)}, bf16[384,128]{1,0:T(8,128)(2,1)S(1)}, u32[]{:S(2)}, u32[]{:S(2)}) %collective-permute-start.8) | collective-permute-done | bytes 98336 | tf_op jit(solution)/shard_map/ppermute | solution.py:70
  148.7 2.2 %collective-permute-start.9 = (bf16[384,128]{1,0:T(8,128)(2,1)S(1)}, bf16[384,128]{1,0:T(8,128)(2,1)S(1)}, u32[]{:S(2)}, u32[]{:S(2)}) collective-permute-start(bf16[384,128]{1,0:T(8,128)(2,1)S(1)} %add_convert_fusion.2), channel_id=1, source_target_pairs={{0,6},{1,7},{2,4},{3,5},{4,2},{5,3},{6,0},{7,1},{8,14},{9,15},{10,... | collective-permute-start | bytes 294920 | tf_op jit(solution)/shard_map/ppermute | solution.py:70
  150.9 2.2 %fusion.7.refs_2_ = f32[384,384]{1,0:T(8,128)} fusion(bf16[384,3072]{1,0:T(8,128)(2,1)S(1)} %copy-done.10), kind=kOutput, calls=%fused_computation.24 | convolution fusion | flops 905969664 | bytes 2949120 | tf_op jit(solution)/shard_map/dot_general | solution.py:36
  153.2 1.5 collective-permute-done.9
  154.6 0.7 convert_add_fusion.sums_ref
  155.3 10.7 %finish.1 = (f32[3,64,512]{2,1,0:T(8,128)}, f32[64,1536]{1,0:T(8,128)}) custom-call(s32[1]{0:T(128)} %bitcast.29.dp_ref, f32[384,128]{1,0:T(8,128)} %convert_add_fusion.sums_ref, f32[384,384]{1,0:T(8,128)} %fusion.5.refs_0_, f32[384,384]{1,0:T(8,128)} %fusion.6.refs_1_, f32[384,384]{1,0:T(8,128)} %fusion.7.refs_2_, bf16[384,3072]{1,0:T(8,128)(2,1)} %copy-done.7, ...), custom_call_target="tpu_custom_call" | custom-call | flops 301989888 | bytes 5308416 | tf_op jit(solution)/shard_map/finish/pallas_call | solution.py:158
  166.0 1.3 side_by_side.1
  (50 shorter events, 1.2 us)
Async XLA Ops:
  0.6 6.4 %copy-start.1 = (bf16[1,1,1,3072,512]{4,3,2,1,0:T(8,128)(2,1)S(1)}, bf16[1,1,1,3072,512]{4,3,2,1,0:T(8,128)(2,1)}, u32[]{:S(2)}) copy-start(bf16[1,1,1,3072,512]{4,3,2,1,0:T(8,128)(2,1)} %param.12) | copy-start | bytes 9437188
  0.7 1.6 copy-start.11
  2.2 0.7 copy-start.15
  2.9 0.7 copy-start.17
  4.3 5.1 %collective-permute-start = (bf16[192,3072]{1,0:T(8,128)(2,1)S(1)}, bf16[192,3072]{1,0:T(8,128)(2,1)S(1)}, u32[]{:S(2)}, u32[]{:S(2)}) collective-permute-start(bf16[192,3072]{1,0:T(8,128)(2,1)S(1)} %get-tuple-element.24.refs_0_), channel_id=1, source_target_pairs={{0,64},{64,0},{1,65},{65,1},{2,66},{66,2},{3,67},{67,3},{4,68},{68... | collective-permute-start | bytes 3538952 | tf_op jit(solution)/shard_map/ppermute | solution.py:28
  4.4 1.4 copy-start.12
  6.4 3.1 %collective-permute-start.1 = (bf16[192,3072]{1,0:T(8,128)(2,1)S(1)}, bf16[192,3072]{1,0:T(8,128)(2,1)S(1)}, u32[]{:S(2)}, u32[]{:S(2)}) collective-permute-start(bf16[192,3072]{1,0:T(8,128)(2,1)S(1)} %pick_slots.1.refs_5_), channel_id=1, source_target_pairs={{0,64},{64,0},{1,65},{65,1},{2,66},{66,2},{3,67},{67,3},{4,68},{68... | collective-permute-start | bytes 3538952 | tf_op jit(solution)/shard_map/ppermute | solution.py:28
  7.0 1.9 %copy-start.3 = (bf16[1,1,1,3072,512]{4,3,2,1,0:T(8,128)(2,1)S(1)}, bf16[1,1,1,3072,512]{4,3,2,1,0:T(8,128)(2,1)}, u32[]{:S(2)}) copy-start(bf16[1,1,1,3072,512]{4,3,2,1,0:T(8,128)(2,1)} %param.13) | copy-start | bytes 9437188
  8.9 1.9 %copy-start.5 = (bf16[1,1,1,512,3072]{4,3,2,1,0:T(8,128)(2,1)S(1)}, bf16[1,1,1,512,3072]{4,3,2,1,0:T(8,128)(2,1)}, u32[]{:S(2)}) copy-start(bf16[1,1,1,512,3072]{4,3,2,1,0:T(8,128)(2,1)} %param.14) | copy-start | bytes 9437188
  19.9 4.2 %copy-start.7 = (bf16[384,3072]{1,0:T(8,128)(2,1)}, bf16[384,3072]{1,0:T(8,128)(2,1)S(1)}, u32[]{:S(2)}) copy-start(bf16[384,3072]{1,0:T(8,128)(2,1)S(1)} %get-tuple-element.40.refs_3_) | copy-start | bytes 7077892
  20.0 2.9 %collective-permute-start.2 = (bf16[4,8,48,384]{3,2,1,0:T(8,128)(2,1)S(1)}, bf16[4,8,48,384]{3,2,1,0:T(8,128)(2,1)S(1)}, u32[]{:S(2)}, u32[]{:S(2)}) collective-permute-start(bf16[4,8,48,384]{3,2,1,0:T(8,128)(2,1)S(1)} %get-tuple-element.28), channel_id=1, source_target_pairs={{0,64},{64,0},{1,65},{65,1},{2,66},{66,2},{3,67},{67,3},{4,68},{68... | collective-permute-start | bytes 3538952 | tf_op jit(solution)/shard_map/ppermute | solution.py:28
  24.2 9.5 %copy-start.16 = (s32[1,4,64,2]{2,3,1,0:T(2,128)S(1)}, s32[1,4,64,2]{2,3,1,0:T(2,128)}, u32[]{:S(2)}) copy-start(s32[1,4,64,2]{2,3,1,0:T(2,128)} %param.10) | copy-start | bytes 6148
  24.2 29.0 %all-to-all-start = ((bf16[32,48,384]{2,1,0:T(8,128)(2,1)}), bf16[32,48,384]{2,1,0:T(8,128)(2,1)S(1)}, u32[]{:S(2)}, u32[]{:S(2)}) async-start(bf16[32,48,384]{2,1,0:T(8,128)(2,1)} %bitcast.67), calls=%async_computation | async-start | bytes 2359296 | tf_op jit(solution)/shard_map/all_to_all | solution.py:32
  53.5 7.5 %collective-permute-start.3 = (bf16[64,384]{1,0:T(8,128)(2,1)S(1)}, bf16[64,384]{1,0:T(8,128)(2,1)S(1)}, u32[]{:S(2)}, u32[]{:S(2)}) collective-permute-start(bf16[64,384]{1,0:T(8,128)(2,1)S(1)} %bitcast.62), channel_id=1, source_target_pairs={{32,0},{33,1},{34,2},{35,3},{36,4},{37,5},{38,6},{39,7},{40,8},{41... | collective-permute-start | bytes 147464 | tf_op jit(solution)/shard_map/ppermute | solution.py:542
  61.3 24.0 %copy-start.6 = (bf16[1,1,1,512,3072]{4,3,2,1,0:T(8,128)(2,1)S(1)}, bf16[1,1,1,512,3072]{4,3,2,1,0:T(8,128)(2,1)}, u32[]{:S(2)}) copy-start(bf16[1,1,1,512,3072]{4,3,2,1,0:T(8,128)(2,1)} %param.14) | copy-start | bytes 9437188
  61.3 24.0 %copy-start.14 = (f32[1,1,1,3,512,64]{4,5,3,2,1,0:T(8,128)S(1)}, f32[1,1,1,3,512,64]{4,5,3,2,1,0:T(8,128)}, u32[]{:S(2)}) copy-start(f32[1,1,1,3,512,64]{4,5,3,2,1,0:T(8,128)} %param.15) | copy-start | bytes 1179652
  82.3 2.9 %collective-permute-start.4 = (bf16[192,3072]{1,0:T(8,128)(2,1)S(1)}, bf16[192,3072]{1,0:T(8,128)(2,1)S(1)}, u32[]{:S(2)}, u32[]{:S(2)}) collective-permute-start(bf16[192,3072]{1,0:T(8,128)(2,1)S(1)} %scale_rows.1.refs_0_), channel_id=1, source_target_pairs={{0,64},{64,0},{1,65},{65,1},{2,66},{66,2},{3,67},{67,3},{4,68},{68... | collective-permute-start | bytes 3538952 | tf_op jit(solution)/shard_map/ppermute | solution.py:28
  85.3 3.8 %copy-start.2 = (bf16[1,1,1,3072,512]{4,3,2,1,0:T(8,128)(2,1)S(1)}, bf16[1,1,1,3072,512]{4,3,2,1,0:T(8,128)(2,1)}, u32[]{:S(2)}) copy-start(bf16[1,1,1,3072,512]{4,3,2,1,0:T(8,128)(2,1)} %param.12) | copy-start | bytes 9437188
  85.3 3.8 %copy-start.4 = (bf16[1,1,1,3072,512]{4,3,2,1,0:T(8,128)(2,1)S(1)}, bf16[1,1,1,3072,512]{4,3,2,1,0:T(8,128)(2,1)}, u32[]{:S(2)}) copy-start(bf16[1,1,1,3072,512]{4,3,2,1,0:T(8,128)(2,1)} %param.13) | copy-start | bytes 9437188
  87.6 1.4 copy-start.9
  94.4 4.3 %copy-start.13 = (bf16[3,384,512]{2,1,0:T(8,128)(2,1)}, bf16[3,384,512]{2,1,0:T(8,128)(2,1)S(1)}, u32[]{:S(2)}) copy-start(bf16[3,384,512]{2,1,0:T(8,128)(2,1)S(1)} %get-tuple-element.42.refs_5_) | copy-start | bytes 3538948
  94.5 2.9 %collective-permute-start.5 = (bf16[4,8,48,384]{3,2,1,0:T(8,128)(2,1)S(1)}, bf16[4,8,48,384]{3,2,1,0:T(8,128)(2,1)S(1)}, u32[]{:S(2)}, u32[]{:S(2)}) collective-permute-start(bf16[4,8,48,384]{3,2,1,0:T(8,128)(2,1)S(1)} %get-tuple-element.37), channel_id=1, source_target_pairs={{0,64},{64,0},{1,65},{65,1},{2,66},{66,2},{3,67},{67,3},{4,68},{68... | collective-permute-start | bytes 3538952 | tf_op jit(solution)/shard_map/ppermute | solution.py:28
  98.8 24.6 %all-to-all-start.2 = ((bf16[32,48,384]{2,1,0:T(8,128)(2,1)}), bf16[32,48,384]{2,1,0:T(8,128)(2,1)S(1)}, u32[]{:S(2)}, u32[]{:S(2)}) async-start(bf16[32,48,384]{2,1,0:T(8,128)(2,1)} %bitcast.25), calls=%async_computation.2 | async-start | bytes 2359296 | tf_op jit(solution)/shard_map/all_to_all | solution.py:32
  102.7 1.4 collective-permute-start.6
  104.1 29.8 %collective-permute-start.7 = (bf16[384,128]{1,0:T(8,128)(2,1)S(1)}, bf16[384,128]{1,0:T(8,128)(2,1)S(1)}, u32[]{:S(2)}, u32[]{:S(2)}) collective-permute-start(bf16[384,128]{1,0:T(8,128)(2,1)S(1)} %add_convert_fusion.4), channel_id=1, source_target_pairs={{0,1},{1,0},{2,3},{3,2},{4,5},{5,4},{6,7},{7,6},{8,9},{9,8},{10,11... | collective-permute-start | bytes 294920 | tf_op jit(solution)/shard_map/ppermute | solution.py:70
  123.9 1.1 copy-start
  125.1 41.0 %all-to-all-start.3 = ((bf16[32,64,384]{2,1,0:T(8,128)(2,1)}), bf16[32,64,384]{2,1,0:T(8,128)(2,1)S(1)}, u32[]{:S(2)}, u32[]{:S(2)}) async-start(bf16[32,64,384]{2,1,0:T(8,128)(2,1)} %copy-done), calls=%async_computation.3 | async-start | bytes 3145728 | tf_op jit(solution)/shard_map/all_to_all | solution.py:32
  129.2 6.6 %copy-start.8 = (bf16[384,3072]{1,0:T(8,128)(2,1)S(1)}, bf16[384,3072]{1,0:T(8,128)(2,1)}, u32[]{:S(2)}) copy-start(bf16[384,3072]{1,0:T(8,128)(2,1)} %copy-done.7) | copy-start | bytes 7077892
  129.2 6.6 %copy-start.10 = (bf16[384,3072]{1,0:T(8,128)(2,1)S(1)}, bf16[384,3072]{1,0:T(8,128)(2,1)}, u32[]{:S(2)}) copy-start(bf16[384,3072]{1,0:T(8,128)(2,1)} %copy-done.9) | copy-start | bytes 7077892
  134.0 14.7 %collective-permute-start.8 = (bf16[384,128]{1,0:T(8,128)(2,1)S(1)}, bf16[384,128]{1,0:T(8,128)(2,1)S(1)}, u32[]{:S(2)}, u32[]{:S(2)}) collective-permute-start(bf16[384,128]{1,0:T(8,128)(2,1)S(1)} %add_convert_fusion.3), channel_id=1, source_target_pairs={{0,2},{1,3},{2,0},{3,1},{4,6},{5,7},{6,4},{7,5},{8,10},{9,11},{10,... | collective-permute-start | bytes 294920 | tf_op jit(solution)/shard_map/ppermute | solution.py:70
  148.7 5.9 %collective-permute-start.9 = (bf16[384,128]{1,0:T(8,128)(2,1)S(1)}, bf16[384,128]{1,0:T(8,128)(2,1)S(1)}, u32[]{:S(2)}, u32[]{:S(2)}) collective-permute-start(bf16[384,128]{1,0:T(8,128)(2,1)S(1)} %add_convert_fusion.2), channel_id=1, source_target_pairs={{0,6},{1,7},{2,4},{3,5},{4,2},{5,3},{6,0},{7,1},{8,14},{9,15},{10,... | collective-permute-start | bytes 294920 | tf_op jit(solution)/shard_map/ppermute | solution.py:70

commit v9 on v8

--- a/solution.py
+++ b/solution.py
@@ -69,7 +69,7 @@
         rounded = values.astype(BF)
         other = lax.ppermute(rounded, "expert", route)
         values = rounded.astype(F32) + other.astype(F32)
-    return values
+    return rounded, other
 
 
 def inverse_lower(gram):
@@ -105,7 +105,7 @@
     half = wide // 2
     units = grads.shape[2]
 
-    def kernel(dp_ref, sums_ref, *refs):
+    def kernel(dp_ref, sums_ref, others_ref, *refs):
         squares_hbm, rows_hbm, grads_hbm = (refs[:3], refs[3:5], refs[5])
         q_ref, basis_ref, squares_ref, rows_ref, grads_ref, done = refs[6:]
         start = pl.multiple_of(dp_ref[0] * half, half)
@@ -123,7 +123,7 @@
         ]
         for move in moves:
             move.start()
-        turned = sums_ref[...].T
+        turned = (sums_ref[...].astype(F32) + others_ref[...].astype(F32)).T
         of_inputs, of_grads = (turned[:R].astype(BF), turned[R:].astype(BF))
         for move in moves[:3]:
             move.wait()
@@ -161,7 +161,7 @@
             jax.ShapeDtypeStruct((3, R, units), F32),
             jax.ShapeDtypeStruct((R, half), F32),
         ),
-        in_specs=[IN_SMEM, IN_VMEM] + [IN_HBM] * 6,
+        in_specs=[IN_SMEM, IN_VMEM, IN_VMEM] + [IN_HBM] * 6,
         scratch_shapes=[
             pltpu.VMEM((3, count, count), F32),
             pltpu.VMEM((2 * count, half), BF),
@@ -171,7 +171,7 @@
         compiler_params=pltpu.CompilerParams(vmem_limit_bytes=61 << 20),
         cost_estimate=cost(4 * R * count * wide, 2 * count * (wide + 3 * units) + 12 * count**2),
         name="finish",
-    )(dp_index.reshape(1), sums, *squares, *rows16, grads)
+    )(dp_index.reshape(1), *sums, *squares, *rows16, grads)
 
 
 def pick_slots(own_expert, routes, values, mix=None):
@@ -240,6 +240,7 @@
         kernel,
         out_shape=jax.ShapeDtypeStruct((micro * cap, copies * columns), BF),
         compiler_params=pltpu.CompilerParams(vmem_limit_bytes=8 << 20),
+        cost_estimate=cost(0, 8 * micro * cap * copies * columns),
         name="scale_rows",
     )(pieces, slot_weights)
 
@@ -248,22 +249,43 @@
     experts_count, copies, _, columns = pieces.shape
     tokens = base.shape[0]
 
-    def kernel(pieces_ref, pick_ref, base_ref, out_ref):
+    def kernel(pieces_hbm, pick_ref, base_ref, out_hbm, pieces_ref, part_ref, arrived, sent):
+        arrivals = [
+            pltpu.make_async_copy(pieces_hbm.at[e], pieces_ref.at[e], arrived.at[e])
+            for e in range(experts_count)
+        ]
+        for arrival in arrivals:
+            arrival.start()
         share = base_ref[...].astype(F32)
         for e in range(experts_count):
+            arrivals[e].wait()
             total = pieces_ref[e, 0].astype(F32)
             for c in range(1, copies):
                 total = total + pieces_ref[e, c].astype(F32)
             for term in halves(total):
                 share = share + times(pick_ref[e], term)
-        part = share.astype(BF)
-        for peer in range(peers):
-            out_ref[peer] = part
+        part_ref[...] = share.astype(BF)
+        sends = [
+            pltpu.make_async_copy(part_ref, out_hbm.at[peer], sent.at[peer])
+            for peer in range(peers)
+        ]
+        for send in sends:
+            send.start()
+        for send in sends:
+            send.wait()
 
     return pl.pallas_call(
         kernel,
         out_shape=jax.ShapeDtypeStruct((peers, tokens, columns), BF),
-        compiler_params=pltpu.CompilerParams(vmem_limit_bytes=8 << 20),
+        in_specs=[IN_HBM, IN_VMEM, IN_VMEM],
+        out_specs=IN_HBM,
+        scratch_shapes=[
+            pltpu.VMEM(pieces.shape, BF),
+            pltpu.VMEM((tokens, columns), BF),
+            pltpu.SemaphoreType.DMA((experts_count,)),
+            pltpu.SemaphoreType.DMA((peers,)),
+        ],
+        compiler_params=pltpu.CompilerParams(vmem_limit_bytes=61 << 20),
         name="combine",
     )(pieces, pick, base)
 

time: 168 us -> 175 us (1.042)
  Pallas kernels: 32 us -> 37.8 us
  local copies, waits for them, and re-layouts: 11.5 us -> 13.4 us
    pallas_call x2, Pallas kernels: 0.88 us -> 6.73 us  [combine(): pl.pallas_call(kernel, out_shape=jax.ShapeDtypeStruct((peers, tokens, col...]
    unnamed x38 -> x46, local copies, waits for them, and re-layouts: 10.3 us -> 11.7 us
  transfers between devices with their start and end apart: 13 -> 13, of which waited for: 10 -> 10; matrix products, arithmetic and copies ran while one was open for 7% -> 7% of each run, Pallas kernels for 7% -> 9%
where the time goes in v9:
time: 175 us; the launch traced here: 174 us
  waiting for transfers between devices  62.1 us (35%)
  Pallas kernels  37.8 us (22%)
  starting transfers between devices  26.1 us (15%)
  blocking collectives  20.7 us (12%)
  local copies, waits for them, and re-layouts  13.4 us (8%)
  matrix products  9.23 us (5%)
  other arithmetic  3.76 us (2%)
    all_to_all x3, waiting for transfers between devices, exchange(): return lax.all_to_all(pieces, 'expert', 0, 0, tiled=True)  34 us
    all_to_all x1, blocking collectives, exchange(): return lax.all_to_all(pieces, 'expert', 0, 0, tiled=True)  20.7 us
    all_to_all x3, starting transfers between devices, exchange(): return lax.all_to_all(pieces, 'expert', 0, 0, tiled=True)  17.7 us
    ppermute x3, waiting for transfers between devices, add_copies(): other = lax.ppermute(rounded, 'expert', route)  12.2 us
    unnamed x46, local copies, waits for them, and re-layouts  11.7 us
    pallas_call x1, Pallas kernels, finish(): pl.pallas_call(kernel, out_shape=(jax.ShapeDtypeStruct((3, R, units), F32...  10.7 us
    ppermute x6, waiting for transfers between devices, swap_cores(): return lax.ppermute(value, 'dp', [(0, 1), (1, 0)])  9.6 us
    dot_general x3, matrix products, times(): lax.dot_general(a, b, (((ca,), (cb,)), ((), ())), preferred_element_type=...  9.23 us
  transfers between devices with their start and end apart: 13, of which 10 were waited for; matrix products, arithmetic and copies ran while one was open for 7% of the time, Pallas kernels for 9%

profile of v9, /device:TPU:0, one launch (start us, length us, event | category | flops | bytes accessed | tf_op | source)
XLA Modules:
  0.0 174.1 jit_solution(4703928918762307011)
XLA Ops:
  0.7 1.5 copy-done.10
  2.2 0.7 copy-done.16
  2.9 0.7 copy-done.18
  3.6 0.7 pick_weighted.1
  4.4 1.4 copy-done.11
  5.8 0.7 pick_slots.1.refs_5_
  6.4 0.6 collective-permute-start.1
  7.0 1.9 %copy-done.2 = bf16[1,1,1,3072,512]{4,3,2,1,0:T(8,128)(2,1)S(1)} copy-done((bf16[1,1,1,3072,512]{4,3,2,1,0:T(8,128)(2,1)S(1)}, bf16[1,1,1,3072,512]{4,3,2,1,0:T(8,128)(2,1)}, u32[]{:S(2)}) %copy-start.2) | copy-done | bytes 3145752
  8.9 0.4 shard_map.103
  9.5 1.3 copy-done.4
  10.8 9.2 %experts_first.1 = (f32[384,512]{1,0:T(8,128)S(1)}, f32[384,512]{1,0:T(8,128)S(1)}, bf16[384,512]{1,0:T(8,128)(2,1)S(1)}, f32[4,8,48,384]{3,2,1,0:T(8,128)S(1)},...) custom-call(bf16[192,3072]{1,0:T(8,128)(2,1)S(1)} %get-tuple-element.24.refs_0_, ...), custom_call_target="tpu_custom_call" | custom-call | flops 6039797760 | bytes 18874368 | tf_op jit(solution)/shard_map/experts_first/pallas_call | solution.py:483
  20.1 2.8 %collective-permute-done.2 = bf16[4,8,48,384]{3,2,1,0:T(8,128)(2,1)S(1)} collective-permute-done((bf16[4,8,48,384]{3,2,1,0:T(8,128)(2,1)S(1)}, bf16[4,8,48,384]{3,2,1,0:T(8,128)(2,1)S(1)}, u32[]{:S(2)}, u32[]{:S(2)}) %collective-permute-start.2) | collective-permute-done | bytes 1179680 | tf_op jit(solution)/shard_map/ppermute | solution.py:28
  22.9 1.3 add_convert_fusion.1
  24.1 9.6 %all-to-all-start = ((bf16[32,48,384]{2,1,0:T(8,128)(2,1)}), bf16[32,48,384]{2,1,0:T(8,128)(2,1)}, u32[]{:S(2)}, u32[]{:S(2)}) async-start(bf16[32,48,384]{2,1,0:T(8,128)(2,1)} %bitcast.64), calls=%async_computation | async-start | bytes 2359296 | tf_op jit(solution)/shard_map/all_to_all | solution.py:32
  34.0 0.3 convert_reduce_fusion
  34.6 1.4 dynamic-slice_bitcast_fusion.base_ref.top_ref
  36.1 0.7 or_convert_fusion.pick_ref
  36.8 16.5 %all-to-all-done = bf16[32,48,384]{2,1,0:T(8,128)(2,1)} async-done(((bf16[32,48,384]{2,1,0:T(8,128)(2,1)}), bf16[32,48,384]{2,1,0:T(8,128)(2,1)}, u32[]{:S(2)}, u32[]{:S(2)}) %all-to-all-start) | async-done | bytes 1179680 | tf_op jit(solution)/shard_map/all_to_all | solution.py:32
  53.3 3.0 %combine.2 = bf16[1,64,384]{2,1,0:T(8,128)(2,1)} custom-call(bf16[4,8,48,384]{3,2,1,0:T(8,128)(2,1)} %bitcast.14.pieces_hbm, bf16[4,64,48]{2,1,0:T(8,128)(2,1)} %or_convert_fusion.pick_ref, bf16[64,384]{1,0:T(8,128)(2,1)} %dynamic-slice_bitcast_fusion.base_ref.top_ref), custom_call_target="tpu_custom_call" | custom-call | tf_op jit(solution)/shard_map/combine/pallas_call | solution.py:277
  56.3 1.3 collective-permute-start.3
  57.6 6.4 %collective-permute-done.3.incoming_ref = bf16[64,384]{1,0:T(8,128)(2,1)S(1)} collective-permute-done((bf16[64,384]{1,0:T(8,128)(2,1)}, bf16[64,384]{1,0:T(8,128)(2,1)S(1)}, u32[]{:S(2)}, u32[]{:S(2)}) %collective-permute-start.3) | collective-permute-done | bytes 49184 | tf_op jit(solution)/shard_map/ppermute | solution.py:564
  64.0 0.8 copy-done.13
  65.1 20.7 %all_to_all.20 = bf16[32,48,384]{2,1,0:T(8,128)(2,1)S(1)} all-to-all(bf16[32,48,384]{2,1,0:T(8,128)(2,1)S(1)} %bitcast.58), channel_id=1, replica_groups=mesh['dp'=2,'pipe'=2,'expert'=32] {'expert'}, dimensions={0} | all-to-all | bytes 2359296 | tf_op jit(solution)/shard_map/all_to_all | solution.py:32
  85.8 0.3 scale_rows.1.refs_0_
  86.2 2.8 %collective-permute-done.4.refs_1_ = bf16[192,3072]{1,0:T(8,128)(2,1)S(1)} collective-permute-done((bf16[192,3072]{1,0:T(8,128)(2,1)S(1)}, bf16[192,3072]{1,0:T(8,128)(2,1)S(1)}, u32[]{:S(2)}, u32[]{:S(2)}) %collective-permute-start.4) | collective-permute-done | bytes 1179680 | tf_op jit(solution)/shard_map/ppermute | solution.py:28
  89.0 2.4 %expert_slopes.1 = (bf16[384,128]{1,0:T(8,128)(2,1)S(1)}, bf16[384,512]{1,0:T(8,128)(2,1)S(1)}, bf16[384,512]{1,0:T(8,128)(2,1)S(1)}, bf16[384,3072]{1,0:T(8,128)(2,1)S(1)}) custom-call(bf16[192,3072]{1,0:T(8,128)(2,1)S(1)} %scale_rows.1.refs_0_, bf16[192,3072]{1,0:T(8,128)(2,1)S(1)} %collective-permute-done.4.refs_1_, bf16[512,3072]{1,0:T(8,128)(2,1)S(1)} %bitcast.55, ...), custom_call_target="tpu_custom_call" | custom-call | flops 1207959552 | bytes 10223616 | tf_op jit(solution)/shard_map/expert_slopes/pallas_call | solution.py:372
  91.4 1.4 copy-done.8
  92.9 5.3 %expert_rows.1 = (f32[4,8,48,384]{3,2,1,0:T(8,128)S(1)}, bf16[4,8,48,384]{3,2,1,0:T(8,128)(2,1)S(1)}, bf16[3,384,512]{2,1,0:T(8,128)(2,1)S(1)}) custom-call(bf16[384,512]{1,0:T(8,128)(2,1)S(1)} %get-tuple-element.34.gg_ref, bf16[384,512]{1,0:T(8,128)(2,1)S(1)} %get-tuple-element.35.gu_ref, bf16[384,512]{1,0:T(8,128)(2,1)S(1)} %get-tuple-element.33.refs_5_.hidden_ref, ...), custom_call_target="tpu_custom_call" | custom-call | flops 2415919104 | bytes 13369344 | tf_op jit(solution)/shard_map/expert_rows/pallas_call | solution.py:419
  98.2 0.2 collective-permute-start.5
  98.5 2.7 %collective-permute-done.5 = bf16[4,8,48,384]{3,2,1,0:T(8,128)(2,1)S(1)} collective-permute-done((bf16[4,8,48,384]{3,2,1,0:T(8,128)(2,1)S(1)}, bf16[4,8,48,384]{3,2,1,0:T(8,128)(2,1)S(1)}, u32[]{:S(2)}, u32[]{:S(2)}) %collective-permute-start.5) | collective-permute-done | bytes 1179680 | tf_op jit(solution)/shard_map/ppermute | solution.py:28
  101.2 1.4 add_convert_fusion
  102.5 3.9 %all-to-all-start.2 = ((bf16[32,48,384]{2,1,0:T(8,128)(2,1)}), bf16[32,48,384]{2,1,0:T(8,128)(2,1)S(1)}, u32[]{:S(2)}, u32[]{:S(2)}) async-start(bf16[32,48,384]{2,1,0:T(8,128)(2,1)} %bitcast.25), calls=%async_computation.2 | async-start | bytes 2359296 | tf_op jit(solution)/shard_map/all_to_all | solution.py:32
  106.7 1.1 collective-permute-done.6
  107.9 1.8 %collective-permute-start.7 = (bf16[384,128]{1,0:T(8,128)(2,1)S(1)}, bf16[384,128]{1,0:T(8,128)(2,1)S(1)}, u32[]{:S(2)}, u32[]{:S(2)}) collective-permute-start(bf16[384,128]{1,0:T(8,128)(2,1)S(1)} %add_convert_fusion.4), channel_id=1, source_target_pairs={{0,1},{1,0},{2,3},{3,2},{4,5},{5,4},{6,7},{7,6},{8,9},{9,8},{10,11... | collective-permute-start | bytes 294920 | tf_op jit(solution)/shard_map/ppermute | solution.py:70
  109.7 17.5 %all-to-all-done.2 = bf16[32,48,384]{2,1,0:T(8,128)(2,1)S(1)} async-done(((bf16[32,48,384]{2,1,0:T(8,128)(2,1)}), bf16[32,48,384]{2,1,0:T(8,128)(2,1)S(1)}, u32[]{:S(2)}, u32[]{:S(2)}) %all-to-all-start.2) | async-done | bytes 1179680 | tf_op jit(solution)/shard_map/all_to_all | solution.py:32
  127.1 1.0 copy-done.19
  128.1 3.7 %combine.3 = bf16[32,64,384]{2,1,0:T(8,128)(2,1)} custom-call(bf16[4,8,48,384]{3,2,1,0:T(8,128)(2,1)} %bitcast.65, bf16[4,64,48]{2,1,0:T(8,128)(2,1)} %or_convert_fusion.pick_ref, bf16[64,384]{1,0:T(8,128)(2,1)} %copy-done.15), custom_call_target="tpu_custom_call" | custom-call | tf_op jit(solution)/shard_map/combine/pallas_call | solution.py:277
  131.9 4.2 %all-to-all-start.3 = ((bf16[32,64,384]{2,1,0:T(8,128)(2,1)}), bf16[32,64,384]{2,1,0:T(8,128)(2,1)S(1)}, u32[]{:S(2)}, u32[]{:S(2)}) async-start(bf16[32,64,384]{2,1,0:T(8,128)(2,1)} %combine.3), calls=%async_computation.3 | async-start | bytes 3145728 | tf_op jit(solution)/shard_map/all_to_all | solution.py:32
  136.1 4.8 %fusion.5.refs_0_ = f32[384,384]{1,0:T(8,128)} fusion(bf16[384,3072]{1,0:T(8,128)(2,1)} %copy-done.6), kind=kOutput, calls=%fused_computation.21 | convolution fusion | flops 905969664 | bytes 2949120 | tf_op jit(solution)/shard_map/dot_general | solution.py:36
  140.9 1.8 %collective-permute-start.8 = (bf16[384,128]{1,0:T(8,128)(2,1)S(1)}, bf16[384,128]{1,0:T(8,128)(2,1)S(1)}, u32[]{:S(2)}, u32[]{:S(2)}) collective-permute-start(bf16[384,128]{1,0:T(8,128)(2,1)S(1)} %add_convert_fusion.3), channel_id=1, source_target_pairs={{0,2},{1,3},{2,0},{3,1},{4,6},{5,7},{6,4},{7,5},{8,10},{9,11},{10,... | collective-permute-start | bytes 294920 | tf_op jit(solution)/shard_map/ppermute | solution.py:70
  142.7 2.2 %fusion.6.refs_1_ = f32[384,384]{1,0:T(8,128)} fusion(bf16[384,3072]{1,0:T(8,128)(2,1)S(1)} %copy-done.9, bf16[384,3072]{1,0:T(8,128)(2,1)S(1)} %copy-done.7), kind=kOutput, calls=%fused_computation.22 | convolution fusion | flops 905969664 | bytes 5308416 | tf_op jit(solution)/shard_map/dot_general | solution.py:36
  144.9 10.7 %collective-permute-done.8 = bf16[384,128]{1,0:T(8,128)(2,1)S(1)} collective-permute-done((bf16[384,128]{1,0:T(8,128)(2,1)S(1)}, bf16[384,128]{1,0:T(8,128)(2,1)S(1)}, u32[]{:S(2)}, u32[]{:S(2)}) %collective-permute-start.8) | collective-permute-done | bytes 98336 | tf_op jit(solution)/shard_map/ppermute | solution.py:70
  155.6 2.2 %collective-permute-start.9 = (bf16[384,128]{1,0:T(8,128)(2,1)S(1)}, bf16[384,128]{1,0:T(8,128)(2,1)S(1)}, u32[]{:S(2)}, u32[]{:S(2)}) collective-permute-start(bf16[384,128]{1,0:T(8,128)(2,1)S(1)} %add_convert_fusion.2.sums_ref), channel_id=1, source_target_pairs={{0,6},{1,7},{2,4},{3,5},{4,2},{5,3},{6,0},{7,1},{8,14},{9,15},{10,... | collective-permute-start | bytes 294920 | tf_op jit(solution)/shard_map/ppermute | solution.py:70
  157.8 2.2 %fusion.7.refs_2_ = f32[384,384]{1,0:T(8,128)} fusion(bf16[384,3072]{1,0:T(8,128)(2,1)S(1)} %copy-done.9), kind=kOutput, calls=%fused_computation.23 | convolution fusion | flops 905969664 | bytes 2949120 | tf_op jit(solution)/shard_map/dot_general | solution.py:36
  160.1 1.4 collective-permute-done.9.others_ref
  161.5 0.6 copy-done.21
  162.2 10.7 %finish.1 = (f32[3,64,512]{2,1,0:T(8,128)}, f32[64,1536]{1,0:T(8,128)}) custom-call(s32[1]{0:T(128)} %bitcast.29.dp_ref, bf16[384,128]{1,0:T(8,128)(2,1)} %copy-done.20, bf16[384,128]{1,0:T(8,128)(2,1)} %copy-done.21, f32[384,384]{1,0:T(8,128)} %fusion.5.refs_0_, f32[384,384]{1,0:T(8,128)} %fusion.6.refs_1_, f32[384,384]{1,0:T(8,128)} %fusion.7.refs_2_, ...), custom_call_target="tpu_custom_call" | custom-call | flops 301989888 | bytes 5308416 | tf_op jit(solution)/shard_map/finish/pallas_call | solution.py:158
  172.9 1.3 side_by_side.1
  (57 shorter events, 1.6 us)
Async XLA Ops:
  0.6 6.4 %copy-start = (bf16[1,1,1,3072,512]{4,3,2,1,0:T(8,128)(2,1)S(1)}, bf16[1,1,1,3072,512]{4,3,2,1,0:T(8,128)(2,1)}, u32[]{:S(2)}) copy-start(bf16[1,1,1,3072,512]{4,3,2,1,0:T(8,128)(2,1)} %param.12) | copy-start | bytes 9437188
  0.7 1.6 copy-start.10
  2.2 0.7 copy-start.16
  2.9 0.7 copy-start.18
  4.3 5.1 %collective-permute-start = (bf16[192,3072]{1,0:T(8,128)(2,1)S(1)}, bf16[192,3072]{1,0:T(8,128)(2,1)S(1)}, u32[]{:S(2)}, u32[]{:S(2)}) collective-permute-start(bf16[192,3072]{1,0:T(8,128)(2,1)S(1)} %get-tuple-element.24.refs_0_), channel_id=1, source_target_pairs={{0,64},{64,0},{1,65},{65,1},{2,66},{66,2},{3,67},{67,3},{4,68},{68... | collective-permute-start | bytes 3538952 | tf_op jit(solution)/shard_map/ppermute | solution.py:28
  4.3 1.4 copy-start.11
  6.4 3.0 %collective-permute-start.1 = (bf16[192,3072]{1,0:T(8,128)(2,1)S(1)}, bf16[192,3072]{1,0:T(8,128)(2,1)S(1)}, u32[]{:S(2)}, u32[]{:S(2)}) collective-permute-start(bf16[192,3072]{1,0:T(8,128)(2,1)S(1)} %pick_slots.1.refs_5_), channel_id=1, source_target_pairs={{0,64},{64,0},{1,65},{65,1},{2,66},{66,2},{3,67},{67,3},{4,68},{68... | collective-permute-start | bytes 3538952 | tf_op jit(solution)/shard_map/ppermute | solution.py:28
  7.0 1.9 %copy-start.2 = (bf16[1,1,1,3072,512]{4,3,2,1,0:T(8,128)(2,1)S(1)}, bf16[1,1,1,3072,512]{4,3,2,1,0:T(8,128)(2,1)}, u32[]{:S(2)}) copy-start(bf16[1,1,1,3072,512]{4,3,2,1,0:T(8,128)(2,1)} %param.13) | copy-start | bytes 9437188
  8.9 1.9 %copy-start.4 = (bf16[1,1,1,512,3072]{4,3,2,1,0:T(8,128)(2,1)S(1)}, bf16[1,1,1,512,3072]{4,3,2,1,0:T(8,128)(2,1)}, u32[]{:S(2)}) copy-start(bf16[1,1,1,512,3072]{4,3,2,1,0:T(8,128)(2,1)} %param.14) | copy-start | bytes 9437188
  19.9 4.2 %copy-start.6 = (bf16[384,3072]{1,0:T(8,128)(2,1)}, bf16[384,3072]{1,0:T(8,128)(2,1)S(1)}, u32[]{:S(2)}) copy-start(bf16[384,3072]{1,0:T(8,128)(2,1)S(1)} %get-tuple-element.40.refs_3_) | copy-start | bytes 7077892
  19.9 2.9 %collective-permute-start.2 = (bf16[4,8,48,384]{3,2,1,0:T(8,128)(2,1)S(1)}, bf16[4,8,48,384]{3,2,1,0:T(8,128)(2,1)S(1)}, u32[]{:S(2)}, u32[]{:S(2)}) collective-permute-start(bf16[4,8,48,384]{3,2,1,0:T(8,128)(2,1)S(1)} %get-tuple-element.28), channel_id=1, source_target_pairs={{0,64},{64,0},{1,65},{65,1},{2,66},{66,2},{3,67},{67,3},{4,68},{68... | collective-permute-start | bytes 3538952 | tf_op jit(solution)/shard_map/ppermute | solution.py:28
  24.1 9.7 %copy-start.17 = (s32[1,4,64,2]{2,3,1,0:T(2,128)S(1)}, s32[1,4,64,2]{2,3,1,0:T(2,128)}, u32[]{:S(2)}) copy-start(s32[1,4,64,2]{2,3,1,0:T(2,128)} %param.10) | copy-start | bytes 6148
  24.1 29.2 %all-to-all-start = ((bf16[32,48,384]{2,1,0:T(8,128)(2,1)}), bf16[32,48,384]{2,1,0:T(8,128)(2,1)}, u32[]{:S(2)}, u32[]{:S(2)}) async-start(bf16[32,48,384]{2,1,0:T(8,128)(2,1)} %bitcast.64), calls=%async_computation | async-start | bytes 2359296 | tf_op jit(solution)/shard_map/all_to_all | solution.py:32
  56.3 7.7 %collective-permute-start.3 = (bf16[64,384]{1,0:T(8,128)(2,1)}, bf16[64,384]{1,0:T(8,128)(2,1)S(1)}, u32[]{:S(2)}, u32[]{:S(2)}) collective-permute-start(bf16[64,384]{1,0:T(8,128)(2,1)} %bitcast.69), channel_id=1, source_target_pairs={{32,0},{33,1},{34,2},{35,3},{36,4},{37,5},{38,6},{39,7},{40,8},{41... | collective-permute-start | bytes 147464 | tf_op jit(solution)/shard_map/ppermute | solution.py:564
  64.0 0.8 copy-start.13
  65.0 21.1 %copy-start.15 = (bf16[64,384]{1,0:T(8,128)(2,1)}, bf16[64,384]{1,0:T(8,128)(2,1)S(1)}, u32[]{:S(2)}) copy-start(bf16[64,384]{1,0:T(8,128)(2,1)S(1)} %get-tuple-element.38.base_ref) | copy-start | bytes 147460
  65.0 24.0 %copy-start.5 = (bf16[1,1,1,512,3072]{4,3,2,1,0:T(8,128)(2,1)S(1)}, bf16[1,1,1,512,3072]{4,3,2,1,0:T(8,128)(2,1)}, u32[]{:S(2)}) copy-start(bf16[1,1,1,512,3072]{4,3,2,1,0:T(8,128)(2,1)} %param.14) | copy-start | bytes 9437188
  65.1 24.0 %copy-start.14 = (f32[1,1,1,3,512,64]{4,5,3,2,1,0:T(8,128)S(1)}, f32[1,1,1,3,512,64]{4,5,3,2,1,0:T(8,128)}, u32[]{:S(2)}) copy-start(f32[1,1,1,3,512,64]{4,5,3,2,1,0:T(8,128)} %param.15) | copy-start | bytes 1179652
  86.1 2.9 %collective-permute-start.4 = (bf16[192,3072]{1,0:T(8,128)(2,1)S(1)}, bf16[192,3072]{1,0:T(8,128)(2,1)S(1)}, u32[]{:S(2)}, u32[]{:S(2)}) collective-permute-start(bf16[192,3072]{1,0:T(8,128)(2,1)S(1)} %scale_rows.1.refs_0_), channel_id=1, source_target_pairs={{0,64},{64,0},{1,65},{65,1},{2,66},{66,2},{3,67},{67,3},{4,68},{68... | collective-permute-start | bytes 3538952 | tf_op jit(solution)/shard_map/ppermute | solution.py:28
  89.0 3.8 %copy-start.1 = (bf16[1,1,1,3072,512]{4,3,2,1,0:T(8,128)(2,1)S(1)}, bf16[1,1,1,3072,512]{4,3,2,1,0:T(8,128)(2,1)}, u32[]{:S(2)}) copy-start(bf16[1,1,1,3072,512]{4,3,2,1,0:T(8,128)(2,1)} %param.12) | copy-start | bytes 9437188
  89.0 3.8 %copy-start.3 = (bf16[1,1,1,3072,512]{4,3,2,1,0:T(8,128)(2,1)S(1)}, bf16[1,1,1,3072,512]{4,3,2,1,0:T(8,128)(2,1)}, u32[]{:S(2)}) copy-start(bf16[1,1,1,3072,512]{4,3,2,1,0:T(8,128)(2,1)} %param.13) | copy-start | bytes 9437188
  91.4 1.4 copy-start.8
  98.2 4.3 %copy-start.12 = (bf16[3,384,512]{2,1,0:T(8,128)(2,1)}, bf16[3,384,512]{2,1,0:T(8,128)(2,1)S(1)}, u32[]{:S(2)}) copy-start(bf16[3,384,512]{2,1,0:T(8,128)(2,1)S(1)} %get-tuple-element.42.refs_5_) | copy-start | bytes 3538948
  98.2 2.9 %collective-permute-start.5 = (bf16[4,8,48,384]{3,2,1,0:T(8,128)(2,1)S(1)}, bf16[4,8,48,384]{3,2,1,0:T(8,128)(2,1)S(1)}, u32[]{:S(2)}, u32[]{:S(2)}) collective-permute-start(bf16[4,8,48,384]{3,2,1,0:T(8,128)(2,1)S(1)} %get-tuple-element.37), channel_id=1, source_target_pairs={{0,64},{64,0},{1,65},{65,1},{2,66},{66,2},{3,67},{67,3},{4,68},{68... | collective-permute-start | bytes 3538952 | tf_op jit(solution)/shard_map/ppermute | solution.py:28
  102.5 24.6 %all-to-all-start.2 = ((bf16[32,48,384]{2,1,0:T(8,128)(2,1)}), bf16[32,48,384]{2,1,0:T(8,128)(2,1)S(1)}, u32[]{:S(2)}, u32[]{:S(2)}) async-start(bf16[32,48,384]{2,1,0:T(8,128)(2,1)} %bitcast.25), calls=%async_computation.2 | async-start | bytes 2359296 | tf_op jit(solution)/shard_map/all_to_all | solution.py:32
  106.5 1.4 collective-permute-start.6
  107.9 32.9 %collective-permute-start.7 = (bf16[384,128]{1,0:T(8,128)(2,1)S(1)}, bf16[384,128]{1,0:T(8,128)(2,1)S(1)}, u32[]{:S(2)}, u32[]{:S(2)}) collective-permute-start(bf16[384,128]{1,0:T(8,128)(2,1)S(1)} %add_convert_fusion.4), channel_id=1, source_target_pairs={{0,1},{1,0},{2,3},{3,2},{4,5},{5,4},{6,7},{7,6},{8,9},{9,8},{10,11... | collective-permute-start | bytes 294920 | tf_op jit(solution)/shard_map/ppermute | solution.py:70
  127.1 1.0 copy-start.19
  131.9 41.0 %all-to-all-start.3 = ((bf16[32,64,384]{2,1,0:T(8,128)(2,1)}), bf16[32,64,384]{2,1,0:T(8,128)(2,1)S(1)}, u32[]{:S(2)}, u32[]{:S(2)}) async-start(bf16[32,64,384]{2,1,0:T(8,128)(2,1)} %combine.3), calls=%async_computation.3 | async-start | bytes 3145728 | tf_op jit(solution)/shard_map/all_to_all | solution.py:32
  136.1 6.6 %copy-start.7 = (bf16[384,3072]{1,0:T(8,128)(2,1)S(1)}, bf16[384,3072]{1,0:T(8,128)(2,1)}, u32[]{:S(2)}) copy-start(bf16[384,3072]{1,0:T(8,128)(2,1)} %copy-done.6) | copy-start | bytes 7077892
  136.1 6.6 %copy-start.9 = (bf16[384,3072]{1,0:T(8,128)(2,1)S(1)}, bf16[384,3072]{1,0:T(8,128)(2,1)}, u32[]{:S(2)}) copy-start(bf16[384,3072]{1,0:T(8,128)(2,1)} %copy-done.8) | copy-start | bytes 7077892
  140.9 14.7 %collective-permute-start.8 = (bf16[384,128]{1,0:T(8,128)(2,1)S(1)}, bf16[384,128]{1,0:T(8,128)(2,1)S(1)}, u32[]{:S(2)}, u32[]{:S(2)}) collective-permute-start(bf16[384,128]{1,0:T(8,128)(2,1)S(1)} %add_convert_fusion.3), channel_id=1, source_target_pairs={{0,2},{1,3},{2,0},{3,1},{4,6},{5,7},{6,4},{7,5},{8,10},{9,11},{10,... | collective-permute-start | bytes 294920 | tf_op jit(solution)/shard_map/ppermute | solution.py:70
  155.6 4.5 %copy-start.20 = (bf16[384,128]{1,0:T(8,128)(2,1)}, bf16[384,128]{1,0:T(8,128)(2,1)S(1)}, u32[]{:S(2)}) copy-start(bf16[384,128]{1,0:T(8,128)(2,1)S(1)} %add_convert_fusion.2.sums_ref) | copy-start | bytes 294916
  155.6 5.9 %collective-permute-start.9 = (bf16[384,128]{1,0:T(8,128)(2,1)S(1)}, bf16[384,128]{1,0:T(8,128)(2,1)S(1)}, u32[]{:S(2)}, u32[]{:S(2)}) collective-permute-start(bf16[384,128]{1,0:T(8,128)(2,1)S(1)} %add_convert_fusion.2.sums_ref), channel_id=1, source_target_pairs={{0,6},{1,7},{2,4},{3,5},{4,2},{5,3},{6,0},{7,1},{8,14},{9,15},{10,... | collective-permute-start | bytes 294920 | tf_op jit(solution)/shard_map/ppermute | solution.py:70
  161.5 0.6 copy-start.21

commit v10 on v8

--- a/solution.py
+++ b/solution.py
@@ -69,7 +69,7 @@
         rounded = values.astype(BF)
         other = lax.ppermute(rounded, "expert", route)
         values = rounded.astype(F32) + other.astype(F32)
-    return values
+    return rounded, other
 
 
 def inverse_lower(gram):
@@ -105,7 +105,7 @@
     half = wide // 2
     units = grads.shape[2]
 
-    def kernel(dp_ref, sums_ref, *refs):
+    def kernel(dp_ref, sums_ref, others_ref, *refs):
         squares_hbm, rows_hbm, grads_hbm = (refs[:3], refs[3:5], refs[5])
         q_ref, basis_ref, squares_ref, rows_ref, grads_ref, done = refs[6:]
         start = pl.multiple_of(dp_ref[0] * half, half)
@@ -123,7 +123,7 @@
         ]
         for move in moves:
             move.start()
-        turned = sums_ref[...].T
+        turned = (sums_ref[...].astype(F32) + others_ref[...].astype(F32)).T
         of_inputs, of_grads = (turned[:R].astype(BF), turned[R:].astype(BF))
         for move in moves[:3]:
             move.wait()
@@ -161,7 +161,7 @@
             jax.ShapeDtypeStruct((3, R, units), F32),
             jax.ShapeDtypeStruct((R, half), F32),
         ),
-        in_specs=[IN_SMEM, IN_VMEM] + [IN_HBM] * 6,
+        in_specs=[IN_SMEM, IN_VMEM, IN_VMEM] + [IN_HBM] * 6,
         scratch_shapes=[
             pltpu.VMEM((3, count, count), F32),
             pltpu.VMEM((2 * count, half), BF),
@@ -171,7 +171,7 @@
         compiler_params=pltpu.CompilerParams(vmem_limit_bytes=61 << 20),
         cost_estimate=cost(4 * R * count * wide, 2 * count * (wide + 3 * units) + 12 * count**2),
         name="finish",
-    )(dp_index.reshape(1), sums, *squares, *rows16, grads)
+    )(dp_index.reshape(1), *sums, *squares, *rows16, grads)
 
 
 def pick_slots(own_expert, routes, values, mix=None):
@@ -240,6 +240,7 @@
         kernel,
         out_shape=jax.ShapeDtypeStruct((micro * cap, copies * columns), BF),
         compiler_params=pltpu.CompilerParams(vmem_limit_bytes=8 << 20),
+        cost_estimate=cost(0, 8 * micro * cap * copies * columns),
         name="scale_rows",
     )(pieces, slot_weights)
 
@@ -263,7 +264,7 @@
     return pl.pallas_call(
         kernel,
         out_shape=jax.ShapeDtypeStruct((peers, tokens, columns), BF),
-        compiler_params=pltpu.CompilerParams(vmem_limit_bytes=8 << 20),
+        compiler_params=pltpu.CompilerParams(vmem_limit_bytes=61 << 20),
         name="combine",
     )(pieces, pick, base)
 

time: 168 us -> 173 us (1.030)
  Pallas kernels: 32 us -> 36.3 us
  local copies, waits for them, and re-layouts: 11.5 us -> 13.4 us
    pallas_call x2, Pallas kernels: 0.88 us -> 5.28 us  [combine(): pl.pallas_call(kernel, out_shape=jax.ShapeDtypeStruct((peers, tokens, col...]
    unnamed x38 -> x46, local copies, waits for them, and re-layouts: 10.3 us -> 11.7 us
  transfers between devices with their start and end apart: 13 -> 13, of which waited for: 10 -> 10; matrix products, arithmetic and copies ran while one was open for 7% -> 7% of each run, Pallas kernels for 7% -> 9%
where the time goes in v10:
time: 173 us
  waiting for transfers between devices  62.1 us (36%)
  Pallas kernels  36.3 us (21%)
  starting transfers between devices  26.1 us (15%)
  blocking collectives  20.7 us (12%)
  local copies, waits for them, and re-layouts  13.4 us (8%)
  matrix products  9.23 us (5%)
  other arithmetic  3.76 us (2%)
    all_to_all x3, waiting for transfers between devices, exchange(): return lax.all_to_all(pieces, 'expert', 0, 0, tiled=True)  34 us
    all_to_all x1, blocking collectives, exchange(): return lax.all_to_all(pieces, 'expert', 0, 0, tiled=True)  20.7 us
    all_to_all x3, starting transfers between devices, exchange(): return lax.all_to_all(pieces, 'expert', 0, 0, tiled=True)  17.7 us
    ppermute x3, waiting for transfers between devices, add_copies(): other = lax.ppermute(rounded, 'expert', route)  12.2 us
    unnamed x46, local copies, waits for them, and re-layouts  11.7 us
    pallas_call x1, Pallas kernels, finish(): pl.pallas_call(kernel, out_shape=(jax.ShapeDtypeStruct((3, R, units), F32...  10.7 us
    ppermute x6, waiting for transfers between devices, swap_cores(): return lax.ppermute(value, 'dp', [(0, 1), (1, 0)])  9.6 us
    dot_general x3, matrix products, times(): lax.dot_general(a, b, (((ca,), (cb,)), ((), ())), preferred_element_type=...  9.23 us
  transfers between devices with their start and end apart: 13, of which 10 were waited for; matrix products, arithmetic and copies ran while one was open for 7% of the time, Pallas kernels for 9%

profile of v10, /device:TPU:0, one launch (start us, length us, event | category | flops | bytes accessed | tf_op | source)
XLA Modules:
  0.0 172.7 jit_solution(17296941573751245098)
XLA Ops:
  0.7 1.5 copy-done.10
  2.2 0.7 copy-done.16
  2.9 0.7 copy-done.18
  3.6 0.7 pick_weighted.1
  4.4 1.4 copy-done.11
  5.8 0.7 pick_slots.1.refs_5_
  6.4 0.6 collective-permute-start.1
  7.0 1.9 %copy-done.2 = bf16[1,1,1,3072,512]{4,3,2,1,0:T(8,128)(2,1)S(1)} copy-done((bf16[1,1,1,3072,512]{4,3,2,1,0:T(8,128)(2,1)S(1)}, bf16[1,1,1,3072,512]{4,3,2,1,0:T(8,128)(2,1)}, u32[]{:S(2)}) %copy-start.2) | copy-done | bytes 3145752
  8.9 0.4 shard_map.103
  9.5 1.3 copy-done.4
  10.8 9.2 %experts_first.1 = (f32[384,512]{1,0:T(8,128)S(1)}, f32[384,512]{1,0:T(8,128)S(1)}, bf16[384,512]{1,0:T(8,128)(2,1)S(1)}, f32[4,8,48,384]{3,2,1,0:T(8,128)S(1)},...) custom-call(bf16[192,3072]{1,0:T(8,128)(2,1)S(1)} %get-tuple-element.24.refs_0_, ...), custom_call_target="tpu_custom_call" | custom-call | flops 6039797760 | bytes 18874368 | tf_op jit(solution)/shard_map/experts_first/pallas_call | solution.py:462
  20.1 2.8 %collective-permute-done.2 = bf16[4,8,48,384]{3,2,1,0:T(8,128)(2,1)S(1)} collective-permute-done((bf16[4,8,48,384]{3,2,1,0:T(8,128)(2,1)S(1)}, bf16[4,8,48,384]{3,2,1,0:T(8,128)(2,1)S(1)}, u32[]{:S(2)}, u32[]{:S(2)}) %collective-permute-start.2) | collective-permute-done | bytes 1179680 | tf_op jit(solution)/shard_map/ppermute | solution.py:28
  22.9 1.3 add_convert_fusion.1
  24.1 9.6 %all-to-all-start = ((bf16[32,48,384]{2,1,0:T(8,128)(2,1)}), bf16[32,48,384]{2,1,0:T(8,128)(2,1)}, u32[]{:S(2)}, u32[]{:S(2)}) async-start(bf16[32,48,384]{2,1,0:T(8,128)(2,1)} %bitcast.64), calls=%async_computation | async-start | bytes 2359296 | tf_op jit(solution)/shard_map/all_to_all | solution.py:32
  34.0 0.3 convert_reduce_fusion
  34.6 1.4 dynamic-slice_bitcast_fusion.base_ref.top_ref
  36.1 0.7 or_convert_fusion.pick_ref
  36.8 16.5 %all-to-all-done = bf16[32,48,384]{2,1,0:T(8,128)(2,1)} async-done(((bf16[32,48,384]{2,1,0:T(8,128)(2,1)}), bf16[32,48,384]{2,1,0:T(8,128)(2,1)}, u32[]{:S(2)}, u32[]{:S(2)}) %all-to-all-start) | async-done | bytes 1179680 | tf_op jit(solution)/shard_map/all_to_all | solution.py:32
  53.3 2.3 %combine.2 = bf16[1,64,384]{2,1,0:T(8,128)(2,1)} custom-call(bf16[4,8,48,384]{3,2,1,0:T(8,128)(2,1)} %bitcast.14.pieces_ref, bf16[4,64,48]{2,1,0:T(8,128)(2,1)} %or_convert_fusion.pick_ref, bf16[64,384]{1,0:T(8,128)(2,1)} %dynamic-slice_bitcast_fusion.base_ref.top_ref), custom_call_target="tpu_custom_call" | custom-call | tf_op jit(solution)/shard_map/combine/pallas_call | solution.py:264
  55.6 1.3 collective-permute-start.3
  56.9 6.4 %collective-permute-done.3.incoming_ref = bf16[64,384]{1,0:T(8,128)(2,1)S(1)} collective-permute-done((bf16[64,384]{1,0:T(8,128)(2,1)}, bf16[64,384]{1,0:T(8,128)(2,1)S(1)}, u32[]{:S(2)}, u32[]{:S(2)}) %collective-permute-start.3) | collective-permute-done | bytes 49184 | tf_op jit(solution)/shard_map/ppermute | solution.py:543
  63.3 0.8 copy-done.13
  64.3 20.7 %all_to_all.20 = bf16[32,48,384]{2,1,0:T(8,128)(2,1)S(1)} all-to-all(bf16[32,48,384]{2,1,0:T(8,128)(2,1)S(1)} %bitcast.58), channel_id=1, replica_groups=mesh['dp'=2,'pipe'=2,'expert'=32] {'expert'}, dimensions={0} | all-to-all | bytes 2359296 | tf_op jit(solution)/shard_map/all_to_all | solution.py:32
  85.1 0.3 scale_rows.1.refs_0_
  85.5 2.8 %collective-permute-done.4.refs_1_ = bf16[192,3072]{1,0:T(8,128)(2,1)S(1)} collective-permute-done((bf16[192,3072]{1,0:T(8,128)(2,1)S(1)}, bf16[192,3072]{1,0:T(8,128)(2,1)S(1)}, u32[]{:S(2)}, u32[]{:S(2)}) %collective-permute-start.4) | collective-permute-done | bytes 1179680 | tf_op jit(solution)/shard_map/ppermute | solution.py:28
  88.3 2.4 %expert_slopes.1 = (bf16[384,128]{1,0:T(8,128)(2,1)S(1)}, bf16[384,512]{1,0:T(8,128)(2,1)S(1)}, bf16[384,512]{1,0:T(8,128)(2,1)S(1)}, bf16[384,3072]{1,0:T(8,128)(2,1)S(1)}) custom-call(bf16[192,3072]{1,0:T(8,128)(2,1)S(1)} %scale_rows.1.refs_0_, bf16[192,3072]{1,0:T(8,128)(2,1)S(1)} %collective-permute-done.4.refs_1_, bf16[512,3072]{1,0:T(8,128)(2,1)S(1)} %bitcast.55, ...), custom_call_target="tpu_custom_call" | custom-call | flops 1207959552 | bytes 10223616 | tf_op jit(solution)/shard_map/expert_slopes/pallas_call | solution.py:351
  90.7 1.4 copy-done.8
  92.1 5.3 %expert_rows.1 = (f32[4,8,48,384]{3,2,1,0:T(8,128)S(1)}, bf16[4,8,48,384]{3,2,1,0:T(8,128)(2,1)S(1)}, bf16[3,384,512]{2,1,0:T(8,128)(2,1)S(1)}) custom-call(bf16[384,512]{1,0:T(8,128)(2,1)S(1)} %get-tuple-element.34.gg_ref, bf16[384,512]{1,0:T(8,128)(2,1)S(1)} %get-tuple-element.35.gu_ref, bf16[384,512]{1,0:T(8,128)(2,1)S(1)} %get-tuple-element.33.refs_5_.hidden_ref, ...), custom_call_target="tpu_custom_call" | custom-call | flops 2415919104 | bytes 13369344 | tf_op jit(solution)/shard_map/expert_rows/pallas_call | solution.py:398
  97.5 0.2 collective-permute-start.5
  97.7 2.7 %collective-permute-done.5 = bf16[4,8,48,384]{3,2,1,0:T(8,128)(2,1)S(1)} collective-permute-done((bf16[4,8,48,384]{3,2,1,0:T(8,128)(2,1)S(1)}, bf16[4,8,48,384]{3,2,1,0:T(8,128)(2,1)S(1)}, u32[]{:S(2)}, u32[]{:S(2)}) %collective-permute-start.5) | collective-permute-done | bytes 1179680 | tf_op jit(solution)/shard_map/ppermute | solution.py:28
  100.4 1.4 add_convert_fusion
  101.8 3.9 %all-to-all-start.2 = ((bf16[32,48,384]{2,1,0:T(8,128)(2,1)}), bf16[32,48,384]{2,1,0:T(8,128)(2,1)S(1)}, u32[]{:S(2)}, u32[]{:S(2)}) async-start(bf16[32,48,384]{2,1,0:T(8,128)(2,1)} %bitcast.25), calls=%async_computation.2 | async-start | bytes 2359296 | tf_op jit(solution)/shard_map/all_to_all | solution.py:32
  106.0 1.1 collective-permute-done.6
  107.2 1.8 %collective-permute-start.7 = (bf16[384,128]{1,0:T(8,128)(2,1)S(1)}, bf16[384,128]{1,0:T(8,128)(2,1)S(1)}, u32[]{:S(2)}, u32[]{:S(2)}) collective-permute-start(bf16[384,128]{1,0:T(8,128)(2,1)S(1)} %add_convert_fusion.4), channel_id=1, source_target_pairs={{0,1},{1,0},{2,3},{3,2},{4,5},{5,4},{6,7},{7,6},{8,9},{9,8},{10,11... | collective-permute-start | bytes 294920 | tf_op jit(solution)/shard_map/ppermute | solution.py:70
  108.9 17.5 %all-to-all-done.2 = bf16[32,48,384]{2,1,0:T(8,128)(2,1)S(1)} async-done(((bf16[32,48,384]{2,1,0:T(8,128)(2,1)}), bf16[32,48,384]{2,1,0:T(8,128)(2,1)S(1)}, u32[]{:S(2)}, u32[]{:S(2)}) %all-to-all-start.2) | async-done | bytes 1179680 | tf_op jit(solution)/shard_map/all_to_all | solution.py:32
  126.4 1.0 copy-done.19
  127.4 3.0 %combine.3 = bf16[32,64,384]{2,1,0:T(8,128)(2,1)} custom-call(bf16[4,8,48,384]{3,2,1,0:T(8,128)(2,1)} %bitcast.65, bf16[4,64,48]{2,1,0:T(8,128)(2,1)} %or_convert_fusion.pick_ref, bf16[64,384]{1,0:T(8,128)(2,1)} %copy-done.15), custom_call_target="tpu_custom_call" | custom-call | tf_op jit(solution)/shard_map/combine/pallas_call | solution.py:264
  130.4 4.2 %all-to-all-start.3 = ((bf16[32,64,384]{2,1,0:T(8,128)(2,1)}), bf16[32,64,384]{2,1,0:T(8,128)(2,1)S(1)}, u32[]{:S(2)}, u32[]{:S(2)}) async-start(bf16[32,64,384]{2,1,0:T(8,128)(2,1)} %combine.3), calls=%async_computation.3 | async-start | bytes 3145728 | tf_op jit(solution)/shard_map/all_to_all | solution.py:32
  134.6 4.8 %fusion.5.refs_0_ = f32[384,384]{1,0:T(8,128)} fusion(bf16[384,3072]{1,0:T(8,128)(2,1)} %copy-done.6), kind=kOutput, calls=%fused_computation.21 | convolution fusion | flops 905969664 | bytes 2949120 | tf_op jit(solution)/shard_map/dot_general | solution.py:36
  139.4 1.8 %collective-permute-start.8 = (bf16[384,128]{1,0:T(8,128)(2,1)S(1)}, bf16[384,128]{1,0:T(8,128)(2,1)S(1)}, u32[]{:S(2)}, u32[]{:S(2)}) collective-permute-start(bf16[384,128]{1,0:T(8,128)(2,1)S(1)} %add_convert_fusion.3), channel_id=1, source_target_pairs={{0,2},{1,3},{2,0},{3,1},{4,6},{5,7},{6,4},{7,5},{8,10},{9,11},{10,... | collective-permute-start | bytes 294920 | tf_op jit(solution)/shard_map/ppermute | solution.py:70
  141.2 2.2 %fusion.6.refs_1_ = f32[384,384]{1,0:T(8,128)} fusion(bf16[384,3072]{1,0:T(8,128)(2,1)S(1)} %copy-done.9, bf16[384,3072]{1,0:T(8,128)(2,1)S(1)} %copy-done.7), kind=kOutput, calls=%fused_computation.22 | convolution fusion | flops 905969664 | bytes 5308416 | tf_op jit(solution)/shard_map/dot_general | solution.py:36
  143.4 10.7 %collective-permute-done.8 = bf16[384,128]{1,0:T(8,128)(2,1)S(1)} collective-permute-done((bf16[384,128]{1,0:T(8,128)(2,1)S(1)}, bf16[384,128]{1,0:T(8,128)(2,1)S(1)}, u32[]{:S(2)}, u32[]{:S(2)}) %collective-permute-start.8) | collective-permute-done | bytes 98336 | tf_op jit(solution)/shard_map/ppermute | solution.py:70
  154.1 2.2 %collective-permute-start.9 = (bf16[384,128]{1,0:T(8,128)(2,1)S(1)}, bf16[384,128]{1,0:T(8,128)(2,1)S(1)}, u32[]{:S(2)}, u32[]{:S(2)}) collective-permute-start(bf16[384,128]{1,0:T(8,128)(2,1)S(1)} %add_convert_fusion.2.sums_ref), channel_id=1, source_target_pairs={{0,6},{1,7},{2,4},{3,5},{4,2},{5,3},{6,0},{7,1},{8,14},{9,15},{10,... | collective-permute-start | bytes 294920 | tf_op jit(solution)/shard_map/ppermute | solution.py:70
  156.4 2.2 %fusion.7.refs_2_ = f32[384,384]{1,0:T(8,128)} fusion(bf16[384,3072]{1,0:T(8,128)(2,1)S(1)} %copy-done.9), kind=kOutput, calls=%fused_computation.23 | convolution fusion | flops 905969664 | bytes 2949120 | tf_op jit(solution)/shard_map/dot_general | solution.py:36
  158.6 1.4 collective-permute-done.9.others_ref
  160.1 0.6 copy-done.21
  160.7 10.7 %finish.1 = (f32[3,64,512]{2,1,0:T(8,128)}, f32[64,1536]{1,0:T(8,128)}) custom-call(s32[1]{0:T(128)} %bitcast.29.dp_ref, bf16[384,128]{1,0:T(8,128)(2,1)} %copy-done.20, bf16[384,128]{1,0:T(8,128)(2,1)} %copy-done.21, f32[384,384]{1,0:T(8,128)} %fusion.5.refs_0_, f32[384,384]{1,0:T(8,128)} %fusion.6.refs_1_, f32[384,384]{1,0:T(8,128)} %fusion.7.refs_2_, ...), custom_call_target="tpu_custom_call" | custom-call | flops 301989888 | bytes 5308416 | tf_op jit(solution)/shard_map/finish/pallas_call | solution.py:158
  171.4 1.3 side_by_side.1
  (57 shorter events, 1.6 us)
Async XLA Ops:
  0.6 6.4 %copy-start = (bf16[1,1,1,3072,512]{4,3,2,1,0:T(8,128)(2,1)S(1)}, bf16[1,1,1,3072,512]{4,3,2,1,0:T(8,128)(2,1)}, u32[]{:S(2)}) copy-start(bf16[1,1,1,3072,512]{4,3,2,1,0:T(8,128)(2,1)} %param.12) | copy-start | bytes 9437188
  0.7 1.6 copy-start.10
  2.2 0.7 copy-start.16
  2.9 0.7 copy-start.18
  4.3 5.1 %collective-permute-start = (bf16[192,3072]{1,0:T(8,128)(2,1)S(1)}, bf16[192,3072]{1,0:T(8,128)(2,1)S(1)}, u32[]{:S(2)}, u32[]{:S(2)}) collective-permute-start(bf16[192,3072]{1,0:T(8,128)(2,1)S(1)} %get-tuple-element.24.refs_0_), channel_id=1, source_target_pairs={{0,64},{64,0},{1,65},{65,1},{2,66},{66,2},{3,67},{67,3},{4,68},{68... | collective-permute-start | bytes 3538952 | tf_op jit(solution)/shard_map/ppermute | solution.py:28
  4.3 1.4 copy-start.11
  6.4 3.0 %collective-permute-start.1 = (bf16[192,3072]{1,0:T(8,128)(2,1)S(1)}, bf16[192,3072]{1,0:T(8,128)(2,1)S(1)}, u32[]{:S(2)}, u32[]{:S(2)}) collective-permute-start(bf16[192,3072]{1,0:T(8,128)(2,1)S(1)} %pick_slots.1.refs_5_), channel_id=1, source_target_pairs={{0,64},{64,0},{1,65},{65,1},{2,66},{66,2},{3,67},{67,3},{4,68},{68... | collective-permute-start | bytes 3538952 | tf_op jit(solution)/shard_map/ppermute | solution.py:28
  7.0 1.9 %copy-start.2 = (bf16[1,1,1,3072,512]{4,3,2,1,0:T(8,128)(2,1)S(1)}, bf16[1,1,1,3072,512]{4,3,2,1,0:T(8,128)(2,1)}, u32[]{:S(2)}) copy-start(bf16[1,1,1,3072,512]{4,3,2,1,0:T(8,128)(2,1)} %param.13) | copy-start | bytes 9437188
  8.9 1.9 %copy-start.4 = (bf16[1,1,1,512,3072]{4,3,2,1,0:T(8,128)(2,1)S(1)}, bf16[1,1,1,512,3072]{4,3,2,1,0:T(8,128)(2,1)}, u32[]{:S(2)}) copy-start(bf16[1,1,1,512,3072]{4,3,2,1,0:T(8,128)(2,1)} %param.14) | copy-start | bytes 9437188
  19.9 4.2 %copy-start.6 = (bf16[384,3072]{1,0:T(8,128)(2,1)}, bf16[384,3072]{1,0:T(8,128)(2,1)S(1)}, u32[]{:S(2)}) copy-start(bf16[384,3072]{1,0:T(8,128)(2,1)S(1)} %get-tuple-element.40.refs_3_) | copy-start | bytes 7077892
  19.9 2.9 %collective-permute-start.2 = (bf16[4,8,48,384]{3,2,1,0:T(8,128)(2,1)S(1)}, bf16[4,8,48,384]{3,2,1,0:T(8,128)(2,1)S(1)}, u32[]{:S(2)}, u32[]{:S(2)}) collective-permute-start(bf16[4,8,48,384]{3,2,1,0:T(8,128)(2,1)S(1)} %get-tuple-element.28), channel_id=1, source_target_pairs={{0,64},{64,0},{1,65},{65,1},{2,66},{66,2},{3,67},{67,3},{4,68},{68... | collective-permute-start | bytes 3538952 | tf_op jit(solution)/shard_map/ppermute | solution.py:28
  24.1 9.7 %copy-start.17 = (s32[1,4,64,2]{2,3,1,0:T(2,128)S(1)}, s32[1,4,64,2]{2,3,1,0:T(2,128)}, u32[]{:S(2)}) copy-start(s32[1,4,64,2]{2,3,1,0:T(2,128)} %param.10) | copy-start | bytes 6148
  24.1 29.2 %all-to-all-start = ((bf16[32,48,384]{2,1,0:T(8,128)(2,1)}), bf16[32,48,384]{2,1,0:T(8,128)(2,1)}, u32[]{:S(2)}, u32[]{:S(2)}) async-start(bf16[32,48,384]{2,1,0:T(8,128)(2,1)} %bitcast.64), calls=%async_computation | async-start | bytes 2359296 | tf_op jit(solution)/shard_map/all_to_all | solution.py:32
  55.6 7.7 %collective-permute-start.3 = (bf16[64,384]{1,0:T(8,128)(2,1)}, bf16[64,384]{1,0:T(8,128)(2,1)S(1)}, u32[]{:S(2)}, u32[]{:S(2)}) collective-permute-start(bf16[64,384]{1,0:T(8,128)(2,1)} %bitcast.69), channel_id=1, source_target_pairs={{32,0},{33,1},{34,2},{35,3},{36,4},{37,5},{38,6},{39,7},{40,8},{41... | collective-permute-start | bytes 147464 | tf_op jit(solution)/shard_map/ppermute | solution.py:543
  63.3 0.8 copy-start.13
  64.3 21.1 %copy-start.15 = (bf16[64,384]{1,0:T(8,128)(2,1)}, bf16[64,384]{1,0:T(8,128)(2,1)S(1)}, u32[]{:S(2)}) copy-start(bf16[64,384]{1,0:T(8,128)(2,1)S(1)} %get-tuple-element.38.base_ref) | copy-start | bytes 147460
  64.3 24.0 %copy-start.5 = (bf16[1,1,1,512,3072]{4,3,2,1,0:T(8,128)(2,1)S(1)}, bf16[1,1,1,512,3072]{4,3,2,1,0:T(8,128)(2,1)}, u32[]{:S(2)}) copy-start(bf16[1,1,1,512,3072]{4,3,2,1,0:T(8,128)(2,1)} %param.14) | copy-start | bytes 9437188
  64.3 24.0 %copy-start.14 = (f32[1,1,1,3,512,64]{4,5,3,2,1,0:T(8,128)S(1)}, f32[1,1,1,3,512,64]{4,5,3,2,1,0:T(8,128)}, u32[]{:S(2)}) copy-start(f32[1,1,1,3,512,64]{4,5,3,2,1,0:T(8,128)} %param.15) | copy-start | bytes 1179652
  85.4 2.9 %collective-permute-start.4 = (bf16[192,3072]{1,0:T(8,128)(2,1)S(1)}, bf16[192,3072]{1,0:T(8,128)(2,1)S(1)}, u32[]{:S(2)}, u32[]{:S(2)}) collective-permute-start(bf16[192,3072]{1,0:T(8,128)(2,1)S(1)} %scale_rows.1.refs_0_), channel_id=1, source_target_pairs={{0,64},{64,0},{1,65},{65,1},{2,66},{66,2},{3,67},{67,3},{4,68},{68... | collective-permute-start | bytes 3538952 | tf_op jit(solution)/shard_map/ppermute | solution.py:28
  88.3 3.8 %copy-start.1 = (bf16[1,1,1,3072,512]{4,3,2,1,0:T(8,128)(2,1)S(1)}, bf16[1,1,1,3072,512]{4,3,2,1,0:T(8,128)(2,1)}, u32[]{:S(2)}) copy-start(bf16[1,1,1,3072,512]{4,3,2,1,0:T(8,128)(2,1)} %param.12) | copy-start | bytes 9437188
  88.3 3.8 %copy-start.3 = (bf16[1,1,1,3072,512]{4,3,2,1,0:T(8,128)(2,1)S(1)}, bf16[1,1,1,3072,512]{4,3,2,1,0:T(8,128)(2,1)}, u32[]{:S(2)}) copy-start(bf16[1,1,1,3072,512]{4,3,2,1,0:T(8,128)(2,1)} %param.13) | copy-start | bytes 9437188
  90.7 1.4 copy-start.8
  97.5 4.3 %copy-start.12 = (bf16[3,384,512]{2,1,0:T(8,128)(2,1)}, bf16[3,384,512]{2,1,0:T(8,128)(2,1)S(1)}, u32[]{:S(2)}) copy-start(bf16[3,384,512]{2,1,0:T(8,128)(2,1)S(1)} %get-tuple-element.42.refs_5_) | copy-start | bytes 3538948
  97.5 2.9 %collective-permute-start.5 = (bf16[4,8,48,384]{3,2,1,0:T(8,128)(2,1)S(1)}, bf16[4,8,48,384]{3,2,1,0:T(8,128)(2,1)S(1)}, u32[]{:S(2)}, u32[]{:S(2)}) collective-permute-start(bf16[4,8,48,384]{3,2,1,0:T(8,128)(2,1)S(1)} %get-tuple-element.37), channel_id=1, source_target_pairs={{0,64},{64,0},{1,65},{65,1},{2,66},{66,2},{3,67},{67,3},{4,68},{68... | collective-permute-start | bytes 3538952 | tf_op jit(solution)/shard_map/ppermute | solution.py:28
  101.8 24.6 %all-to-all-start.2 = ((bf16[32,48,384]{2,1,0:T(8,128)(2,1)}), bf16[32,48,384]{2,1,0:T(8,128)(2,1)S(1)}, u32[]{:S(2)}, u32[]{:S(2)}) async-start(bf16[32,48,384]{2,1,0:T(8,128)(2,1)} %bitcast.25), calls=%async_computation.2 | async-start | bytes 2359296 | tf_op jit(solution)/shard_map/all_to_all | solution.py:32
  105.7 1.4 collective-permute-start.6
  107.2 32.2 %collective-permute-start.7 = (bf16[384,128]{1,0:T(8,128)(2,1)S(1)}, bf16[384,128]{1,0:T(8,128)(2,1)S(1)}, u32[]{:S(2)}, u32[]{:S(2)}) collective-permute-start(bf16[384,128]{1,0:T(8,128)(2,1)S(1)} %add_convert_fusion.4), channel_id=1, source_target_pairs={{0,1},{1,0},{2,3},{3,2},{4,5},{5,4},{6,7},{7,6},{8,9},{9,8},{10,11... | collective-permute-start | bytes 294920 | tf_op jit(solution)/shard_map/ppermute | solution.py:70
  126.4 1.0 copy-start.19
  130.4 40.9 %all-to-all-start.3 = ((bf16[32,64,384]{2,1,0:T(8,128)(2,1)}), bf16[32,64,384]{2,1,0:T(8,128)(2,1)S(1)}, u32[]{:S(2)}, u32[]{:S(2)}) async-start(bf16[32,64,384]{2,1,0:T(8,128)(2,1)} %combine.3), calls=%async_computation.3 | async-start | bytes 3145728 | tf_op jit(solution)/shard_map/all_to_all | solution.py:32
  134.6 6.6 %copy-start.7 = (bf16[384,3072]{1,0:T(8,128)(2,1)S(1)}, bf16[384,3072]{1,0:T(8,128)(2,1)}, u32[]{:S(2)}) copy-start(bf16[384,3072]{1,0:T(8,128)(2,1)} %copy-done.6) | copy-start | bytes 7077892
  134.6 6.6 %copy-start.9 = (bf16[384,3072]{1,0:T(8,128)(2,1)S(1)}, bf16[384,3072]{1,0:T(8,128)(2,1)}, u32[]{:S(2)}) copy-start(bf16[384,3072]{1,0:T(8,128)(2,1)} %copy-done.8) | copy-start | bytes 7077892
  139.4 14.7 %collective-permute-start.8 = (bf16[384,128]{1,0:T(8,128)(2,1)S(1)}, bf16[384,128]{1,0:T(8,128)(2,1)S(1)}, u32[]{:S(2)}, u32[]{:S(2)}) collective-permute-start(bf16[384,128]{1,0:T(8,128)(2,1)S(1)} %add_convert_fusion.3), channel_id=1, source_target_pairs={{0,2},{1,3},{2,0},{3,1},{4,6},{5,7},{6,4},{7,5},{8,10},{9,11},{10,... | collective-permute-start | bytes 294920 | tf_op jit(solution)/shard_map/ppermute | solution.py:70
  154.1 4.5 %copy-start.20 = (bf16[384,128]{1,0:T(8,128)(2,1)}, bf16[384,128]{1,0:T(8,128)(2,1)S(1)}, u32[]{:S(2)}) copy-start(bf16[384,128]{1,0:T(8,128)(2,1)S(1)} %add_convert_fusion.2.sums_ref) | copy-start | bytes 294916
  154.1 5.9 %collective-permute-start.9 = (bf16[384,128]{1,0:T(8,128)(2,1)S(1)}, bf16[384,128]{1,0:T(8,128)(2,1)S(1)}, u32[]{:S(2)}, u32[]{:S(2)}) collective-permute-start(bf16[384,128]{1,0:T(8,128)(2,1)S(1)} %add_convert_fusion.2.sums_ref), channel_id=1, source_target_pairs={{0,6},{1,7},{2,4},{3,5},{4,2},{5,3},{6,0},{7,1},{8,14},{9,15},{10,... | collective-permute-start | bytes 294920 | tf_op jit(solution)/shard_map/ppermute | solution.py:70
  160.1 0.6 copy-start.21
